TPU v7x, 128 devices: a whole 4x4x4 slice. The times are simulated.
128 devices in a mesh: tm: 8 (over z_hi, x), space: 16 (over y, z_lo, core).
Axes of the slice: x: 4, y: 4, z: 4 (z_hi: 2, z_lo: 2; z = z_hi * 2 + z_lo), core: 2. Of those that a mesh axis runs over, the one named last changes fastest.
Arguments:
- guess: float32 [16, 3, 192, 64, 128], P('tm', None, 'space'), may hold values from -6 to 6
- source: float32 [16, 3, 192, 64, 128], P('tm', None, 'space'), may hold values from -6 to 6
- regions: int32 [192, 64, 128], P('space'), may hold values from 0 to 3
- conductance: float32 [4], replicated, may hold values from 8 to 32
- reluct: float32 [4], replicated, may hold values from 0.25 to 2
Outputs:
- field: float32 [16, 3, 192, 64, 128], P('tm', None, 'space')
- coarse_residual: float32 [8, 3, 192, 64, 128], P('tm', None, 'space')
Inputs may be any that keep to these rules, and one draw needn't show every extreme that they name: `regions`: a region id per cell.
All inputs are finite; a program needn't handle non-finite values.
Results may differ from a plain program's by a relative error of at most 0.0001.
Values sent between devices are 32-bit elements; how exact they have to be, the bound alone decides.
No kernel may reach another device: no remote copies, remote signals or barrier semaphores. Data moves between devices by JAX's collectives and lax.ppermute only.
A program may use at most 128 MiB of HBM per device.

v0:
```python
import jax
import jax.numpy as jnp
from jax import lax
from jax.sharding import PartitionSpec as P

PICARD = 2


def extended_2(x, sides, width):
    for axis, dim in sides:
        count, length = (lax.axis_size(axis), x.shape[dim])
        up = [(i, (i + 1) % count) for i in range(count - 1)]
        down = [(j, i) for i, j in up]
        last = lax.slice_in_dim(x, length - width, length, axis=dim)
        leading = lax.slice_in_dim(x, 0, width, axis=dim)
        before = lax.ppermute(last, axis, up)
        after = lax.ppermute(leading, axis, down)
        x = jnp.concatenate([before, x, after], axis=dim)
    return x


def shifted(block, axis, distance):
    devices = range(lax.axis_size(axis))
    route = [((i - distance) % len(devices), i) for i in devices]
    return lax.ppermute(block, axis, route)


def material(regions, table):
    ids = jnp.arange(table.shape[0]).reshape(-1, 1, 1, 1)
    return jnp.sum(
        jnp.where(regions[None] == ids, table.reshape(-1, 1, 1, 1), jnp.float32(0.0)), axis=0
    )


def neighbour_sum(extended):
    first = extended[:, 2:] + extended[:, :-2]
    centre = extended[:, 1:-1]
    padded = jnp.pad(centre, ((0, 0), (0, 0), (1, 1), (1, 1)))
    second = padded[:, :, 2:, 1:-1] + padded[:, :, :-2, 1:-1]
    third = padded[:, :, 1:-1, 2:] + padded[:, :, 1:-1, :-2]
    return first + second + third


def rim_one(state):
    return extended_2(state, (("space", 1),), 1)


def fine_update(extended, old, force, cond, base_nu):
    centre = extended[:, 1:-1]
    square = jnp.sum(centre * centre, axis=0)
    nu = (base_nu * (1.0 + 0.5 * square / (1.0 + square)))[None]
    return (cond * old + force + nu * neighbour_sum(extended)) / (cond + 6.0 * nu)


def body(guess, source, regions, conductance, reluct):
    steps = guess.shape[0]
    cond = material(regions, conductance)
    base_nu = material(regions, reluct)

    def advance(old, force):
        state = old
        for sweep in range(PICARD):
            state = fine_update(rim_one(state), old, force, cond, base_nu)
        return state

    cond_coarse = cond / steps

    def previous_end(last):
        return shifted(last, "tm", 1)

    points = [guess[i] for i in range(steps)]
    forces = [source[i] for i in range(steps)]

    def relax_f(points):
        points = list(points)
        points[1] = advance(points[0], forces[1])
        return points

    points = relax_f(points)
    points[0] = advance(previous_end(points[steps - 1]), forces[0])
    points = relax_f(points)
    residual = advance(previous_end(points[steps - 1]), forces[0]) - points[0]
    slices = lax.axis_size("tm")
    correction = jnp.zeros_like(residual)
    for k in range(slices):
        flat = shifted(correction, "tm", 1)
        coarse_state = flat
        for coarse_sweep in range(PICARD):
            coarse_state = (cond_coarse * flat + base_nu * neighbour_sum(rim_one(coarse_state))) / (
                cond_coarse + 6.0 * base_nu
            )
        correction = coarse_state + residual
    points[0] = points[0] + correction
    points = relax_f(points)
    return (jnp.stack(points, axis=0), residual[None])


def solution(mesh):
    in_specs = (
        P("tm", None, "space", None, None),
        P("tm", None, "space", None, None),
        P("space", None, None),
        P(),
        P(),
    )
    out_specs = (P("tm", None, "space", None, None), P("tm", None, "space", None, None))
    return jax.shard_map(body, mesh=mesh, in_specs=in_specs, out_specs=out_specs, check_vma=False)
```

profile of v0, /device:TPU:17, one launch (start us, length us, event | category | flops | bytes accessed | tf_op | source)
XLA Modules:
  0.0 573.3 jit_solution(16128213294329222183)
XLA Ops:
  11.1 4.7 collective-permute-start.2
  23.2 26.1 %collective-permute-done.4 = f32[3,12,64,128]{3,2,1,0:T(8,128)S(1)} collective-permute-done((f32[3,12,64,128]{3,2,1,0:T(8,128)S(1)}, f32[3,12,64,128]{3,2,1,0:T(8,128)S(1)}, u32[]{:S(2)}, u32[]{:S(2)}) %collective-permute-start.4) | collective-permute-done | bytes 1179680 | tf_op jit(solution)/shard_map/ppermute | solution.py:25
  49.3 8.9 %collective-permute-start.5 = (f32[3,1,64,128]{3,2,1,0:T(8,128)S(1)}, f32[3,1,64,128]{3,2,1,0:T(8,128)S(1)}, u32[]{:S(2)}, u32[]{:S(2)}) collective-permute-start(f32[3,1,64,128]{3,2,1,0:T(8,128)S(1)} %get-tuple-element.86), channel_id=1, source_target_pairs={{1,0},{2,1},{3,2},{4,3},{5,4},{6,5},{7,6},{8,7},{9,8},{10,9},{11,1... | collective-permute-start | bytes 294920 | tf_op jit(solution)/shard_map/ppermute | solution.py:17
  60.4 20.7 %collective-permute-done.5 = f32[3,1,64,128]{3,2,1,0:T(8,128)S(1)} collective-permute-done((f32[3,1,64,128]{3,2,1,0:T(8,128)S(1)}, f32[3,1,64,128]{3,2,1,0:T(8,128)S(1)}, u32[]{:S(2)}, u32[]{:S(2)}) %collective-permute-start.5) | collective-permute-done | bytes 98336 | tf_op jit(solution)/shard_map/ppermute | solution.py:17
  114.1 22.9 %collective-permute-done.18 = f32[3,12,64,128]{3,2,1,0:T(8,128)S(1)} collective-permute-done((f32[3,12,64,128]{3,2,1,0:T(8,128)S(1)}, f32[3,12,64,128]{3,2,1,0:T(8,128)S(1)}, u32[]{:S(2)}, u32[]{:S(2)}) %collective-permute-start.18) | collective-permute-done | bytes 1179680 | tf_op jit(solution)/shard_map/ppermute | solution.py:25
  137.0 5.6 collective-permute-start.19
  166.5 28.0 %collective-permute-done.23 = f32[3,12,64,128]{3,2,1,0:T(8,128)S(1)} collective-permute-done((f32[3,12,64,128]{3,2,1,0:T(8,128)S(1)}, f32[3,12,64,128]{3,2,1,0:T(8,128)S(1)}, u32[]{:S(2)}, u32[]{:S(2)}) %collective-permute-start.23) | collective-permute-done | bytes 1179680 | tf_op jit(solution)/shard_map/ppermute | solution.py:25
  194.5 5.9 %collective-permute-start.24 = (f32[3,1,64,128]{3,2,1,0:T(8,128)S(1)}, f32[3,1,64,128]{3,2,1,0:T(8,128)S(1)}, u32[]{:S(2)}, u32[]{:S(2)}) collective-permute-start(f32[3,1,64,128]{3,2,1,0:T(8,128)S(1)} %get-tuple-element.70), channel_id=1, source_target_pairs={{1,0},{2,1},{3,2},{4,3},{5,4},{6,5},{7,6},{8,7},{9,8},{10,9},{11,1... | collective-permute-start | bytes 294920 | tf_op jit(solution)/shard_map/ppermute | solution.py:17
  215.7 28.0 %collective-permute-done.28 = f32[3,12,64,128]{3,2,1,0:T(8,128)S(1)} collective-permute-done((f32[3,12,64,128]{3,2,1,0:T(8,128)S(1)}, f32[3,12,64,128]{3,2,1,0:T(8,128)S(1)}, u32[]{:S(2)}, u32[]{:S(2)}) %collective-permute-start.28) | collective-permute-done | bytes 1179680 | tf_op jit(solution)/shard_map/ppermute | solution.py:25
  243.7 5.9 %collective-permute-start.29 = (f32[3,1,64,128]{3,2,1,0:T(8,128)S(1)}, f32[3,1,64,128]{3,2,1,0:T(8,128)S(1)}, u32[]{:S(2)}, u32[]{:S(2)}) collective-permute-start(f32[3,1,64,128]{3,2,1,0:T(8,128)S(1)} %get-tuple-element.66), channel_id=1, source_target_pairs={{1,0},{2,1},{3,2},{4,3},{5,4},{6,5},{7,6},{8,7},{9,8},{10,9},{11,1... | collective-permute-start | bytes 294920 | tf_op jit(solution)/shard_map/ppermute | solution.py:17
  264.8 28.0 %collective-permute-done.33 = f32[3,12,64,128]{3,2,1,0:T(8,128)S(1)} collective-permute-done((f32[3,12,64,128]{3,2,1,0:T(8,128)S(1)}, f32[3,12,64,128]{3,2,1,0:T(8,128)S(1)}, u32[]{:S(2)}, u32[]{:S(2)}) %collective-permute-start.33) | collective-permute-done | bytes 1179680 | tf_op jit(solution)/shard_map/ppermute | solution.py:25
  292.8 5.9 %collective-permute-start.34 = (f32[3,1,64,128]{3,2,1,0:T(8,128)S(1)}, f32[3,1,64,128]{3,2,1,0:T(8,128)S(1)}, u32[]{:S(2)}, u32[]{:S(2)}) collective-permute-start(f32[3,1,64,128]{3,2,1,0:T(8,128)S(1)} %get-tuple-element.62), channel_id=1, source_target_pairs={{1,0},{2,1},{3,2},{4,3},{5,4},{6,5},{7,6},{8,7},{9,8},{10,9},{11,1... | collective-permute-start | bytes 294920 | tf_op jit(solution)/shard_map/ppermute | solution.py:17
  314.0 28.0 %collective-permute-done.38 = f32[3,12,64,128]{3,2,1,0:T(8,128)S(1)} collective-permute-done((f32[3,12,64,128]{3,2,1,0:T(8,128)S(1)}, f32[3,12,64,128]{3,2,1,0:T(8,128)S(1)}, u32[]{:S(2)}, u32[]{:S(2)}) %collective-permute-start.38) | collective-permute-done | bytes 1179680 | tf_op jit(solution)/shard_map/ppermute | solution.py:25
  342.0 5.9 %collective-permute-start.39 = (f32[3,1,64,128]{3,2,1,0:T(8,128)S(1)}, f32[3,1,64,128]{3,2,1,0:T(8,128)S(1)}, u32[]{:S(2)}, u32[]{:S(2)}) collective-permute-start(f32[3,1,64,128]{3,2,1,0:T(8,128)S(1)} %get-tuple-element.58), channel_id=1, source_target_pairs={{1,0},{2,1},{3,2},{4,3},{5,4},{6,5},{7,6},{8,7},{9,8},{10,9},{11,1... | collective-permute-start | bytes 294920 | tf_op jit(solution)/shard_map/ppermute | solution.py:17
  363.1 27.8 %collective-permute-done.43 = f32[3,12,64,128]{3,2,1,0:T(8,128)S(1)} collective-permute-done((f32[3,12,64,128]{3,2,1,0:T(8,128)S(1)}, f32[3,12,64,128]{3,2,1,0:T(8,128)S(1)}, u32[]{:S(2)}, u32[]{:S(2)}) %collective-permute-start.43) | collective-permute-done | bytes 1179680 | tf_op jit(solution)/shard_map/ppermute | solution.py:25
  390.9 6.1 %collective-permute-start.44 = (f32[3,1,64,128]{3,2,1,0:T(8,128)S(1)}, f32[3,1,64,128]{3,2,1,0:T(8,128)S(1)}, u32[]{:S(2)}, u32[]{:S(2)}) collective-permute-start(f32[3,1,64,128]{3,2,1,0:T(8,128)S(1)} %get-tuple-element.54), channel_id=1, source_target_pairs={{1,0},{2,1},{3,2},{4,3},{5,4},{6,5},{7,6},{8,7},{9,8},{10,9},{11,1... | collective-permute-start | bytes 294920 | tf_op jit(solution)/shard_map/ppermute | solution.py:17
  412.3 27.8 %collective-permute-done.48 = f32[3,12,64,128]{3,2,1,0:T(8,128)S(1)} collective-permute-done((f32[3,12,64,128]{3,2,1,0:T(8,128)S(1)}, f32[3,12,64,128]{3,2,1,0:T(8,128)S(1)}, u32[]{:S(2)}, u32[]{:S(2)}) %collective-permute-start.48) | collective-permute-done | bytes 1179680 | tf_op jit(solution)/shard_map/ppermute | solution.py:25
  440.1 6.1 %collective-permute-start.49 = (f32[3,1,64,128]{3,2,1,0:T(8,128)S(1)}, f32[3,1,64,128]{3,2,1,0:T(8,128)S(1)}, u32[]{:S(2)}, u32[]{:S(2)}) collective-permute-start(f32[3,1,64,128]{3,2,1,0:T(8,128)S(1)} %get-tuple-element.50), channel_id=1, source_target_pairs={{1,0},{2,1},{3,2},{4,3},{5,4},{6,5},{7,6},{8,7},{9,8},{10,9},{11,1... | collective-permute-start | bytes 294920 | tf_op jit(solution)/shard_map/ppermute | solution.py:17
  450.9 6.0 %collective-permute-start.51 = (f32[3,1,64,128]{3,2,1,0:T(8,128)S(1)}, f32[3,1,64,128]{3,2,1,0:T(8,128)S(1)}, u32[]{:S(2)}, u32[]{:S(2)}) collective-permute-start(f32[3,1,64,128]{3,2,1,0:T(8,128)S(1)} %get-tuple-element.48), channel_id=1, source_target_pairs={{1,0},{2,1},{3,2},{4,3},{5,4},{6,5},{7,6},{8,7},{9,8},{10,9},{11,1... | collective-permute-start | bytes 294920 | tf_op jit(solution)/shard_map/ppermute | solution.py:17
  461.4 27.8 %collective-permute-done.53 = f32[3,12,64,128]{3,2,1,0:T(8,128)S(1)} collective-permute-done((f32[3,12,64,128]{3,2,1,0:T(8,128)S(1)}, f32[3,12,64,128]{3,2,1,0:T(8,128)S(1)}, u32[]{:S(2)}, u32[]{:S(2)}) %collective-permute-start.53) | collective-permute-done | bytes 1179680 | tf_op jit(solution)/shard_map/ppermute | solution.py:25
  489.2 6.1 %collective-permute-start.54 = (f32[3,1,64,128]{3,2,1,0:T(8,128)S(1)}, f32[3,1,64,128]{3,2,1,0:T(8,128)S(1)}, u32[]{:S(2)}, u32[]{:S(2)}) collective-permute-start(f32[3,1,64,128]{3,2,1,0:T(8,128)S(1)} %get-tuple-element.46), channel_id=1, source_target_pairs={{1,0},{2,1},{3,2},{4,3},{5,4},{6,5},{7,6},{8,7},{9,8},{10,9},{11,1... | collective-permute-start | bytes 294920 | tf_op jit(solution)/shard_map/ppermute | solution.py:17
  495.4 36.4 %collective-permute-start.55 = (f32[3,1,64,128]{3,2,1,0:T(8,128)S(1)}, f32[3,1,64,128]{3,2,1,0:T(8,128)S(1)}, u32[]{:S(2)}, u32[]{:S(2)}) collective-permute-start(f32[3,1,64,128]{3,2,1,0:T(8,128)S(1)} %get-tuple-element.47), channel_id=1, source_target_pairs={{0,1},{1,2},{2,3},{3,4},{4,5},{5,6},{6,7},{7,8},{8,9},{9,10},{10,1... | collective-permute-start | bytes 294920 | tf_op jit(solution)/shard_map/ppermute | solution.py:16
  545.0 14.6 %collective-permute-start.59 = (f32[3,1,64,128]{3,2,1,0:T(8,128)S(1)}, f32[3,1,64,128]{3,2,1,0:T(8,128)S(1)}, u32[]{:S(2)}, u32[]{:S(2)}) collective-permute-start(f32[3,1,64,128]{3,2,1,0:T(8,128)S(1)} %get-tuple-element.43), channel_id=1, source_target_pairs={{0,1},{1,2},{2,3},{3,4},{4,5},{5,6},{6,7},{7,8},{8,9},{9,10},{10,1... | collective-permute-start | bytes 294920 | tf_op jit(solution)/shard_map/ppermute | solution.py:16
  564.0 5.2 collective-permute-start.61
  (180 shorter events, 183.2 us)
Async XLA Ops:
  20.5 28.8 %collective-permute-start.4 = (f32[3,12,64,128]{3,2,1,0:T(8,128)S(1)}, f32[3,12,64,128]{3,2,1,0:T(8,128)S(1)}, u32[]{:S(2)}, u32[]{:S(2)}) collective-permute-start(f32[3,12,64,128]{3,2,1,0:T(8,128)S(1)} %fusion.12), channel_id=1, source_target_pairs={{112,0},{0,16},{16,32},{32,48},{48,64},{64,80},{80,96},{96,112},{1... | collective-permute-start | bytes 3538952 | tf_op jit(solution)/shard_map/ppermute | solution.py:25
  21.9 85.7 %collective-permute-start.9 = (f32[3,12,64,128]{3,2,1,0:T(8,128)S(1)}, f32[3,12,64,128]{3,2,1,0:T(8,128)S(1)}, u32[]{:S(2)}, u32[]{:S(2)}) collective-permute-start(f32[3,12,64,128]{3,2,1,0:T(8,128)S(1)} %broadcast_in_dim.25), channel_id=1, source_target_pairs={{112,0},{0,16},{16,32},{32,48},{48,64},{64,80},{80,96},{96,112},{1... | collective-permute-start | bytes 3538952 | tf_op jit(solution)/shard_map/ppermute | solution.py:25
  49.3 31.8 %collective-permute-start.5 = (f32[3,1,64,128]{3,2,1,0:T(8,128)S(1)}, f32[3,1,64,128]{3,2,1,0:T(8,128)S(1)}, u32[]{:S(2)}, u32[]{:S(2)}) collective-permute-start(f32[3,1,64,128]{3,2,1,0:T(8,128)S(1)} %get-tuple-element.86), channel_id=1, source_target_pairs={{1,0},{2,1},{3,2},{4,3},{5,4},{6,5},{7,6},{8,7},{9,8},{10,9},{11,1... | collective-permute-start | bytes 294920 | tf_op jit(solution)/shard_map/ppermute | solution.py:17
  58.2 22.9 %collective-permute-start.6 = (f32[3,1,64,128]{3,2,1,0:T(8,128)S(1)}, f32[3,1,64,128]{3,2,1,0:T(8,128)S(1)}, u32[]{:S(2)}, u32[]{:S(2)}) collective-permute-start(f32[3,1,64,128]{3,2,1,0:T(8,128)S(1)} %get-tuple-element.87), channel_id=1, source_target_pairs={{0,1},{1,2},{2,3},{3,4},{4,5},{5,6},{6,7},{7,8},{8,9},{9,10},{10,1... | collective-permute-start | bytes 294920 | tf_op jit(solution)/shard_map/ppermute | solution.py:16
  107.5 29.5 %collective-permute-start.18 = (f32[3,12,64,128]{3,2,1,0:T(8,128)S(1)}, f32[3,12,64,128]{3,2,1,0:T(8,128)S(1)}, u32[]{:S(2)}, u32[]{:S(2)}) collective-permute-start(f32[3,12,64,128]{3,2,1,0:T(8,128)S(1)} %fusion.55), channel_id=1, source_target_pairs={{112,0},{0,16},{16,32},{32,48},{48,64},{64,80},{80,96},{96,112},{1... | collective-permute-start | bytes 3538952 | tf_op jit(solution)/shard_map/ppermute | solution.py:25
  107.6 47.5 %collective-permute-start.10 = (f32[3,1,64,128]{3,2,1,0:T(8,128)S(1)}, f32[3,1,64,128]{3,2,1,0:T(8,128)S(1)}, u32[]{:S(2)}, u32[]{:S(2)}) collective-permute-start(f32[3,1,64,128]{3,2,1,0:T(8,128)S(1)} %get-tuple-element.82), channel_id=1, source_target_pairs={{1,0},{2,1},{3,2},{4,3},{5,4},{6,5},{7,6},{8,7},{9,8},{10,9},{11,1... | collective-permute-start | bytes 294920 | tf_op jit(solution)/shard_map/ppermute | solution.py:17
  112.2 42.9 %collective-permute-start.11 = (f32[3,1,64,128]{3,2,1,0:T(8,128)S(1)}, f32[3,1,64,128]{3,2,1,0:T(8,128)S(1)}, u32[]{:S(2)}, u32[]{:S(2)}) collective-permute-start(f32[3,1,64,128]{3,2,1,0:T(8,128)S(1)} %get-tuple-element.83), channel_id=1, source_target_pairs={{0,1},{1,2},{2,3},{3,4},{4,5},{5,6},{6,7},{7,8},{8,9},{9,10},{10,1... | collective-permute-start | bytes 294920 | tf_op jit(solution)/shard_map/ppermute | solution.py:16
  148.6 13.0 %collective-permute-start.21 = (f32[3,1,64,128]{3,2,1,0:T(8,128)S(1)}, f32[3,1,64,128]{3,2,1,0:T(8,128)S(1)}, u32[]{:S(2)}, u32[]{:S(2)}) collective-permute-start(f32[3,1,64,128]{3,2,1,0:T(8,128)S(1)} %get-tuple-element.72), channel_id=1, source_target_pairs={{1,0},{2,1},{3,2},{4,3},{5,4},{6,5},{7,6},{8,7},{9,8},{10,9},{11,1... | collective-permute-start | bytes 294920 | tf_op jit(solution)/shard_map/ppermute | solution.py:17
  166.4 28.1 %collective-permute-start.23 = (f32[3,12,64,128]{3,2,1,0:T(8,128)S(1)}, f32[3,12,64,128]{3,2,1,0:T(8,128)S(1)}, u32[]{:S(2)}, u32[]{:S(2)}) collective-permute-start(f32[3,12,64,128]{3,2,1,0:T(8,128)S(1)} %get-tuple-element.12), channel_id=1, source_target_pairs={{112,0},{0,16},{16,32},{32,48},{48,64},{64,80},{80,96},{96,112},{1... | collective-permute-start | bytes 3538952 | tf_op jit(solution)/shard_map/ppermute | solution.py:25
  194.5 10.2 %collective-permute-start.24 = (f32[3,1,64,128]{3,2,1,0:T(8,128)S(1)}, f32[3,1,64,128]{3,2,1,0:T(8,128)S(1)}, u32[]{:S(2)}, u32[]{:S(2)}) collective-permute-start(f32[3,1,64,128]{3,2,1,0:T(8,128)S(1)} %get-tuple-element.70), channel_id=1, source_target_pairs={{1,0},{2,1},{3,2},{4,3},{5,4},{6,5},{7,6},{8,7},{9,8},{10,9},{11,1... | collective-permute-start | bytes 294920 | tf_op jit(solution)/shard_map/ppermute | solution.py:17
  215.6 28.1 %collective-permute-start.28 = (f32[3,12,64,128]{3,2,1,0:T(8,128)S(1)}, f32[3,12,64,128]{3,2,1,0:T(8,128)S(1)}, u32[]{:S(2)}, u32[]{:S(2)}) collective-permute-start(f32[3,12,64,128]{3,2,1,0:T(8,128)S(1)} %fusion.85), channel_id=1, source_target_pairs={{112,0},{0,16},{16,32},{32,48},{48,64},{64,80},{80,96},{96,112},{1... | collective-permute-start | bytes 3538952 | tf_op jit(solution)/shard_map/ppermute | solution.py:25
  243.7 10.2 %collective-permute-start.29 = (f32[3,1,64,128]{3,2,1,0:T(8,128)S(1)}, f32[3,1,64,128]{3,2,1,0:T(8,128)S(1)}, u32[]{:S(2)}, u32[]{:S(2)}) collective-permute-start(f32[3,1,64,128]{3,2,1,0:T(8,128)S(1)} %get-tuple-element.66), channel_id=1, source_target_pairs={{1,0},{2,1},{3,2},{4,3},{5,4},{6,5},{7,6},{8,7},{9,8},{10,9},{11,1... | collective-permute-start | bytes 294920 | tf_op jit(solution)/shard_map/ppermute | solution.py:17
  264.7 28.1 %collective-permute-start.33 = (f32[3,12,64,128]{3,2,1,0:T(8,128)S(1)}, f32[3,12,64,128]{3,2,1,0:T(8,128)S(1)}, u32[]{:S(2)}, u32[]{:S(2)}) collective-permute-start(f32[3,12,64,128]{3,2,1,0:T(8,128)S(1)} %fusion.100), channel_id=1, source_target_pairs={{112,0},{0,16},{16,32},{32,48},{48,64},{64,80},{80,96},{96,112},{1... | collective-permute-start | bytes 3538952 | tf_op jit(solution)/shard_map/ppermute | solution.py:25
  292.8 10.2 %collective-permute-start.34 = (f32[3,1,64,128]{3,2,1,0:T(8,128)S(1)}, f32[3,1,64,128]{3,2,1,0:T(8,128)S(1)}, u32[]{:S(2)}, u32[]{:S(2)}) collective-permute-start(f32[3,1,64,128]{3,2,1,0:T(8,128)S(1)} %get-tuple-element.62), channel_id=1, source_target_pairs={{1,0},{2,1},{3,2},{4,3},{5,4},{6,5},{7,6},{8,7},{9,8},{10,9},{11,1... | collective-permute-start | bytes 294920 | tf_op jit(solution)/shard_map/ppermute | solution.py:17
  313.9 28.1 %collective-permute-start.38 = (f32[3,12,64,128]{3,2,1,0:T(8,128)S(1)}, f32[3,12,64,128]{3,2,1,0:T(8,128)S(1)}, u32[]{:S(2)}, u32[]{:S(2)}) collective-permute-start(f32[3,12,64,128]{3,2,1,0:T(8,128)S(1)} %fusion.115), channel_id=1, source_target_pairs={{112,0},{0,16},{16,32},{32,48},{48,64},{64,80},{80,96},{96,112},{1... | collective-permute-start | bytes 3538952 | tf_op jit(solution)/shard_map/ppermute | solution.py:25
  342.0 10.2 %collective-permute-start.39 = (f32[3,1,64,128]{3,2,1,0:T(8,128)S(1)}, f32[3,1,64,128]{3,2,1,0:T(8,128)S(1)}, u32[]{:S(2)}, u32[]{:S(2)}) collective-permute-start(f32[3,1,64,128]{3,2,1,0:T(8,128)S(1)} %get-tuple-element.58), channel_id=1, source_target_pairs={{1,0},{2,1},{3,2},{4,3},{5,4},{6,5},{7,6},{8,7},{9,8},{10,9},{11,1... | collective-permute-start | bytes 294920 | tf_op jit(solution)/shard_map/ppermute | solution.py:17
  363.1 27.9 %collective-permute-start.43 = (f32[3,12,64,128]{3,2,1,0:T(8,128)S(1)}, f32[3,12,64,128]{3,2,1,0:T(8,128)S(1)}, u32[]{:S(2)}, u32[]{:S(2)}) collective-permute-start(f32[3,12,64,128]{3,2,1,0:T(8,128)S(1)} %fusion.130), channel_id=1, source_target_pairs={{112,0},{0,16},{16,32},{32,48},{48,64},{64,80},{80,96},{96,112},{1... | collective-permute-start | bytes 3538952 | tf_op jit(solution)/shard_map/ppermute | solution.py:25
  390.9 10.4 %collective-permute-start.44 = (f32[3,1,64,128]{3,2,1,0:T(8,128)S(1)}, f32[3,1,64,128]{3,2,1,0:T(8,128)S(1)}, u32[]{:S(2)}, u32[]{:S(2)}) collective-permute-start(f32[3,1,64,128]{3,2,1,0:T(8,128)S(1)} %get-tuple-element.54), channel_id=1, source_target_pairs={{1,0},{2,1},{3,2},{4,3},{5,4},{6,5},{7,6},{8,7},{9,8},{10,9},{11,1... | collective-permute-start | bytes 294920 | tf_op jit(solution)/shard_map/ppermute | solution.py:17
  412.0 28.1 %collective-permute-start.48 = (f32[3,12,64,128]{3,2,1,0:T(8,128)S(1)}, f32[3,12,64,128]{3,2,1,0:T(8,128)S(1)}, u32[]{:S(2)}, u32[]{:S(2)}) collective-permute-start(f32[3,12,64,128]{3,2,1,0:T(8,128)S(1)} %fusion.145), channel_id=1, source_target_pairs={{112,0},{0,16},{16,32},{32,48},{48,64},{64,80},{80,96},{96,112},{1... | collective-permute-start | bytes 3538952 | tf_op jit(solution)/shard_map/ppermute | solution.py:25
  461.4 27.8 %collective-permute-start.53 = (f32[3,12,64,128]{3,2,1,0:T(8,128)S(1)}, f32[3,12,64,128]{3,2,1,0:T(8,128)S(1)}, u32[]{:S(2)}, u32[]{:S(2)}) collective-permute-start(f32[3,12,64,128]{3,2,1,0:T(8,128)S(1)} %fusion.160), channel_id=1, source_target_pairs={{112,0},{0,16},{16,32},{32,48},{48,64},{64,80},{80,96},{96,112},{1... | collective-permute-start | bytes 3538952 | tf_op jit(solution)/shard_map/ppermute | solution.py:25
  489.2 42.9 %collective-permute-start.54 = (f32[3,1,64,128]{3,2,1,0:T(8,128)S(1)}, f32[3,1,64,128]{3,2,1,0:T(8,128)S(1)}, u32[]{:S(2)}, u32[]{:S(2)}) collective-permute-start(f32[3,1,64,128]{3,2,1,0:T(8,128)S(1)} %get-tuple-element.46), channel_id=1, source_target_pairs={{1,0},{2,1},{3,2},{4,3},{5,4},{6,5},{7,6},{8,7},{9,8},{10,9},{11,1... | collective-permute-start | bytes 294920 | tf_op jit(solution)/shard_map/ppermute | solution.py:17
  495.4 38.1 %collective-permute-start.55 = (f32[3,1,64,128]{3,2,1,0:T(8,128)S(1)}, f32[3,1,64,128]{3,2,1,0:T(8,128)S(1)}, u32[]{:S(2)}, u32[]{:S(2)}) collective-permute-start(f32[3,1,64,128]{3,2,1,0:T(8,128)S(1)} %get-tuple-element.47), channel_id=1, source_target_pairs={{0,1},{1,2},{2,3},{3,4},{4,5},{5,6},{6,7},{7,8},{8,9},{9,10},{10,1... | collective-permute-start | bytes 294920 | tf_op jit(solution)/shard_map/ppermute | solution.py:16
  543.0 16.9 %collective-permute-start.58 = (f32[3,1,64,128]{3,2,1,0:T(8,128)S(1)}, f32[3,1,64,128]{3,2,1,0:T(8,128)S(1)}, u32[]{:S(2)}, u32[]{:S(2)}) collective-permute-start(f32[3,1,64,128]{3,2,1,0:T(8,128)S(1)} %get-tuple-element.42), channel_id=1, source_target_pairs={{1,0},{2,1},{3,2},{4,3},{5,4},{6,5},{7,6},{8,7},{9,8},{10,9},{11,1... | collective-permute-start | bytes 294920 | tf_op jit(solution)/shard_map/ppermute | solution.py:17
  545.0 16.2 %collective-permute-start.59 = (f32[3,1,64,128]{3,2,1,0:T(8,128)S(1)}, f32[3,1,64,128]{3,2,1,0:T(8,128)S(1)}, u32[]{:S(2)}, u32[]{:S(2)}) collective-permute-start(f32[3,1,64,128]{3,2,1,0:T(8,128)S(1)} %get-tuple-element.43), channel_id=1, source_target_pairs={{0,1},{1,2},{2,3},{3,4},{4,5},{5,6},{6,7},{7,8},{8,9},{9,10},{10,1... | collective-permute-start | bytes 294920 | tf_op jit(solution)/shard_map/ppermute | solution.py:16
  (44 other events, 625.7 us)
where the time goes:
time: 583 us; the launch traced here: 573 us
  waiting for transfers between devices  302 us (52%)
  starting transfers between devices  241 us (41%)
  other arithmetic  25.5 us (4%)
    ppermute x10, waiting for transfers between devices, shifted(): return lax.ppermute(block, axis, route)  244 us
    ppermute x26, starting transfers between devices, extended_2(): before = lax.ppermute(last, axis, up)  122 us
    ppermute x26, starting transfers between devices, extended_2(): after = lax.ppermute(leading, axis, down)  116 us
    ppermute x26, waiting for transfers between devices, extended_2(): before = lax.ppermute(last, axis, up)  31.8 us
    ppermute x26, waiting for transfers between devices, extended_2(): after = lax.ppermute(leading, axis, down)  26.3 us
  transfers between devices with their start and end apart: 62, of which 52 were waited for; matrix products, arithmetic and copies ran while one was open for 1% of the time, Pallas kernels for 0%

commit v1 on v0

v1 whole, which is shorter than its diff:
```python
import functools

import jax
import jax.numpy as jnp
from jax import lax
from jax.experimental import pallas as pl
from jax.experimental.pallas import tpu as pltpu
from jax.sharding import PartitionSpec as P

LX, NY, NZ = 12, 64, 128
F32 = jnp.float32
ANY = pl.BlockSpec(memory_space=pl.ANY)
SMEM = pl.BlockSpec(memory_space=pltpu.SMEM)


def planes(*lead):
    return jax.ShapeDtypeStruct(tuple(lead) + (NY, NZ), F32)


def vmem(*lead):
    return pltpu.VMEM(tuple(lead) + (NY, NZ), F32)


def copy_all(pairs, sems, base=0):
    copies = [
        pltpu.make_async_copy(src, dst, sems.at[base + n]) for n, (src, dst) in enumerate(pairs)
    ]
    for copy in copies:
        copy.start()
    return copies


def wait_all(copies):
    for copy in copies:
        copy.wait()


def run_copies(pairs, sems, base=0):
    wait_all(copy_all(pairs, sems, base))


def call(kernel, name, args, outs, scratch, n_sems, flops=0):
    in_specs = [SMEM if a.ndim == 1 else ANY for a in args]
    single = not isinstance(outs, (list, tuple))
    return pl.pallas_call(
        kernel,
        name=name,
        out_shape=outs,
        in_specs=in_specs,
        out_specs=ANY if single else [ANY] * len(outs),
        scratch_shapes=list(scratch) + [pltpu.SemaphoreType.DMA((n_sems,))],
        compiler_params=pltpu.CompilerParams(vmem_limit_bytes=40 * 1024 * 1024),
        cost_estimate=pl.CostEstimate(flops=flops, bytes_accessed=4 << 20, transcendentals=0),
    )(*args)


def neighbours(src, at):
    row = lax.broadcasted_iota(jnp.int32, (NY, NZ), 0)
    lane = lax.broadcasted_iota(jnp.int32, (NY, NZ), 1)
    zero = jnp.float32(0.0)
    def of(*lead_i):
        *lead, i = lead_i
        a = src[(*lead, i)]
        first = src[(*lead, i + 1)] + src[(*lead, i - 1)]
        up = jnp.where(row == 0, zero, pltpu.roll(a, 1, 0))
        down = jnp.where(row == NY - 1, zero, pltpu.roll(a, NY - 1, 0))
        left = jnp.where(lane == 0, zero, pltpu.roll(a, 1, 1))
        right = jnp.where(lane == NZ - 1, zero, pltpu.roll(a, NZ - 1, 1))
        return (first + (up + down)) + (left + right)
    return of(*at)


def fine_sweep(src, store, held, cond, nu, lo, hi, force=None):
    def body(i, carry):
        square = src[0, i] * src[0, i] + src[1, i] * src[1, i] + src[2, i] * src[2, i]
        base = nu[i]
        weight = cond[i]
        grown = 1.0 + square
        strong = base * (1.0 + 1.5 * square)
        scale = 1.0 / (weight * grown + 6.0 * strong)
        keep = grown * scale
        spread = strong * scale
        for c in range(3):
            if force is not None:
                fixed = weight * src[c, i] + force[c, i]
                held[c, i] = fixed
            else:
                fixed = held[c, i]
            store(c, i, fixed * keep + neighbours(src, (c, i)) * spread)
        return carry

    lax.fori_loop(lo, hi, body, 0)


def coarse_sweep(src, store, held, keep, spread, off, lo, hi, first, comps):
    def body(i, carry):
        k = keep[i + off]
        s = spread[i + off]
        for lead in comps:
            at = lead + (i,)
            if first:
                fixed = k * src[at]
                held[at] = fixed
            else:
                fixed = held[at]
            store(at, fixed + s * neighbours(src, at))
        return carry

    lax.fori_loop(lo, hi, body, 0)


def lookup(code, table):
    first = jnp.where(code == 1.0, table[0], table[1])
    second = jnp.where(code == 3.0, table[2], table[3])
    return jnp.where(code <= 2.0, first, second)


def materials(code, cond_t, nu_t):
    outside = code == 0.0
    return (
        jnp.where(outside, jnp.float32(1.0), lookup(code, cond_t)),
        jnp.where(outside, jnp.float32(0.0), lookup(code, nu_t)),
    )


def pack_kernel(odd_ref, guess, source, regions, code, a1, b1, a2, b2, reg, cod, sems):
    odd = odd_ref[0]
    run_copies([(regions, reg)], sems)

    def body(i, carry):
        cod[i] = (reg[i] + 1).astype(F32)
        return carry

    lax.fori_loop(0, LX, body, 0)
    pairs = [(cod, code)]
    for one, two, top in ((a1, a2, 1 - odd), (b1, b2, odd)):
        for c in range(3):
            pairs.append((guess.at[0, c, pl.ds(top * (LX - 2), 2)], one.at[pl.ds(2 * c, 2)]))
            pairs.append((source.at[1, c, pl.ds(top * (LX - 1), 1)], one.at[pl.ds(6 + c, 1)]))
            pairs.append((source.at[0, c, pl.ds(top * (LX - 3), 3)], two.at[pl.ds(3 * c, 3)]))
        pairs.append((cod.at[pl.ds(top * (LX - 1), 1)], one.at[pl.ds(9, 1)]))
        pairs.append((cod.at[pl.ds(top * (LX - 7), 7)], two.at[pl.ds(9, 7)]))
    run_copies(pairs, sems)


def first_middle_kernel(cond_t, nu_t, guess, source, code, out, x, y, held, f, cod, cond, nu, sems):
    pairs = [(code.at[pl.ds(2, 8)], cod)]
    pairs += [(guess.at[0, c, pl.ds(2, 8)], x.at[c]) for c in range(3)]
    pairs += [(source.at[1, c, pl.ds(2, 8)], f.at[c]) for c in range(3)]
    run_copies(pairs, sems)

    def body(i, carry):
        cond[i], nu[i] = materials(cod[i], cond_t, nu_t)
        return carry

    lax.fori_loop(1, 7, body, 0)

    def into(buf):
        def store(c, i, value):
            buf[c, i] = value
        return store

    fine_sweep(x, into(y), held, cond, nu, 1, 7, f)
    fine_sweep(y, into(x), held, cond, nu, 2, 6)
    run_copies([(x.at[:, pl.ds(2, 4)], out)], sems)


def first_kernel(odd_ref, cond_t, nu_t, guess, source, code, ra, rb, out_a, out_b, x, y, held, f, cod, cond, nu, sems):
    odd = odd_ref[0]
    n = LX + 4
    pairs = [(code, cod.at[pl.ds(2, LX)])]
    for c in range(3):
        pairs.append((guess.at[0, c], x.at[c, pl.ds(2, LX)]))
        pairs.append((source.at[1, c], f.at[c, pl.ds(2, LX)]))
    for pack, high in ((ra, 1 - odd), (rb, odd)):
        for c in range(3):
            pairs.append((pack.at[pl.ds(2 * c, 2)], x.at[c, pl.ds(high * (n - 2), 2)]))
            pairs.append((pack.at[pl.ds(6 + c, 1)], f.at[c, pl.ds(1 + high * (n - 3), 1)]))
        pairs.append((pack.at[pl.ds(9, 1)], cod.at[pl.ds(1 + high * (n - 3), 1)]))
    run_copies(pairs, sems)

    def body(i, carry):
        cond[i], nu[i] = materials(cod[i], cond_t, nu_t)
        return carry

    lax.fori_loop(1, n - 1, body, 0)

    def into(buf):
        def store(c, i, value):
            buf[c, i] = value
        return store

    fine_sweep(x, into(y), held, cond, nu, 1, 7, f)
    fine_sweep(x, into(y), held, cond, nu, 9, n - 1, f)
    fine_sweep(y, into(x), held, cond, nu, 2, 6)
    fine_sweep(y, into(x), held, cond, nu, 10, 14)
    run_copies(
        [
            (x.at[:, pl.ds(2 + (1 - odd) * 8, 4)], out_a),
            (x.at[:, pl.ds(2 + odd * 8, 4)], out_b),
        ],
        sems,
    )


def material_kernel(odd_ref, cond_t, nu_t, code, ra, rb, cond_o, nu_o, keep_o, spread_o, cod, cond, nu, keep, spread, sems):
    odd = odd_ref[0]
    run_copies(
        [
            (code, cod.at[pl.ds(7, LX)]),
            (ra.at[pl.ds(9, 7)], cod.at[pl.ds((1 - odd) * (LX + 7), 7)]),
            (rb.at[pl.ds(9, 7)], cod.at[pl.ds(odd * (LX + 7), 7)]),
        ],
        sems,
    )

    def body(i, carry):
        cv, nv = materials(cod[i], cond_t, nu_t)
        cond[i] = cv
        nu[i] = nv
        half = 0.5 * cv
        scale = 1.0 / (half + 6.0 * nv)
        keep[i] = half * scale
        spread[i] = nv * scale
        return carry

    lax.fori_loop(0, LX + 14, body, 0)
    run_copies(
        [
            (cond.at[pl.ds(4, LX + 6)], cond_o),
            (nu.at[pl.ds(4, LX + 6)], nu_o),
            (keep, keep_o),
            (spread, spread_o),
        ],
        sems,
    )


def extended_pairs(odd, pieces, halos, x):
    a, b, m = pieces
    ha, hb = halos
    return [
        (a, x.at[:, pl.ds(4 + (1 - odd) * 8, 4)]),
        (b, x.at[:, pl.ds(4 + odd * 8, 4)]),
        (m, x.at[:, pl.ds(8, 4)]),
        (ha, x.at[:, pl.ds((1 - odd) * 16, 4)]),
        (hb, x.at[:, pl.ds(odd * 16, 4)]),
    ]


def force_pairs(odd, source, which, width, packs, start, f):
    pairs = []
    for c in range(3):
        pairs.append((source.at[which, c], f.at[c, pl.ds(4, LX)]))
        for pack, high in ((packs[0], 1 - odd), (packs[1], odd)):
            pairs.append(
                (
                    pack.at[pl.ds(start + width * c, width)],
                    f.at[c, pl.ds(4 - width + high * (LX + width), width)],
                )
            )
    return pairs


def second_kernel(
    odd_ref, va, vb, vm, ha, hb, source, a1, b1, a2, b2, cond_i, nu_i,
    u0_o, oa, ob, om, x, y, held, f0, f1, cond, nu, sems,
):
    odd = odd_ref[0]
    pairs = extended_pairs(odd, (va, vb, vm), (ha, hb), x)
    pairs += force_pairs(odd, source, 0, 3, (a2, b2), 0, f0)
    pairs += force_pairs(odd, source, 1, 1, (a1, b1), 6, f1)
    pairs += [(cond_i, cond.at[pl.ds(1, LX + 6)]), (nu_i, nu.at[pl.ds(1, LX + 6)])]
    run_copies(pairs, sems)

    def into(buf):
        def store(c, i, value):
            buf[c, i] = value
        return store

    fine_sweep(x, into(y), held, cond, nu, 1, 19, f0)
    fine_sweep(y, into(x), held, cond, nu, 2, 18)
    kept = copy_all([(x.at[:, pl.ds(2, LX + 4)], u0_o)], sems, 30)
    fine_sweep(x, into(y), held, cond, nu, 3, 17, f1)
    wait_all(kept)
    fine_sweep(y, into(x), held, cond, nu, 4, 16)
    run_copies(
        [
            (x.at[:, pl.ds(4 + (1 - odd) * 8, 4)], oa),
            (x.at[:, pl.ds(4 + odd * 8, 4)], ob),
            (x.at[:, pl.ds(8, 4)], om),
        ],
        sems,
    )


def residual_kernel(
    odd_ref, va, vb, vm, ha, hb, source, a2, b2, cond_i, nu_i, keep_i, spread_i, u0_i,
    res_o, l0, l1, l2, x, y, held, f0, cond, nu, keep, spread, u0, sems,
):
    odd = odd_ref[0]
    pairs = extended_pairs(odd, (va, vb, vm), (ha, hb), x)
    pairs += force_pairs(odd, source, 0, 3, (a2, b2), 0, f0)
    pairs += [(cond_i, cond.at[pl.ds(1, LX + 6)]), (nu_i, nu.at[pl.ds(1, LX + 6)])]
    pairs += [(keep_i, keep), (spread_i, spread), (u0_i, u0.at[:, pl.ds(2, LX + 4)])]
    run_copies(pairs, sems)

    def into(buf):
        def store(c, i, value):
            buf[c, i] = value
        return store

    def less(c, i, value):
        x[c, i] = value - u0[c, i]

    def put(buf):
        def store(at, value):
            buf[at] = value
        return store

    comps = [(0,), (1,), (2,)]
    fine_sweep(x, into(y), held, cond, nu, 1, 19, f0)
    fine_sweep(y, less, held, cond, nu, 2, 18)
    kept = copy_all([(x.at[:, pl.ds(4, LX)], res_o.at[0])], sems, 30)
    coarse_sweep(x, put(y), held, keep, spread, 3, 3, 17, True, comps)
    wait_all(kept)
    coarse_sweep(y, put(x), held, keep, spread, 3, 4, 16, False, comps)
    run_copies([(x.at[c, pl.ds(4, LX)], o) for c, o in enumerate((l0, l1, l2))], sems)


def add_kernel(w, odd_ref, base, moved, total_o, sa, sb, x, y, sems):
    odd = odd_ref[0]
    run_copies([(base, x), (moved, y)], sems)

    def body(i, carry):
        x[i] = x[i] + y[i]
        return carry

    lax.fori_loop(0, LX, body, 0)
    run_copies(
        [
            (x, total_o),
            (x.at[pl.ds((1 - odd) * (LX - w), w)], sa),
            (x.at[pl.ds(odd * (LX - w), w)], sb),
        ],
        sems,
    )


def power_kernel(w, odd_ref, value, ha, hb, keep_i, spread_i, out, x, y, held, keep, spread, sems):
    odd = odd_ref[0]
    run_copies(
        [
            (value, x.at[pl.ds(w, LX)]),
            (ha, x.at[pl.ds((1 - odd) * (LX + w), w)]),
            (hb, x.at[pl.ds(odd * (LX + w), w)]),
            (keep_i, keep),
            (spread_i, spread),
        ],
        sems,
    )

    def put(buf):
        def store(at, value):
            buf[at] = value
        return store

    for step in range(w // 2):
        lo = 1 + 2 * step
        coarse_sweep(x, put(y), held, keep, spread, 7 - w, lo, LX + 2 * w - lo, True, [()])
        coarse_sweep(y, put(x), held, keep, spread, 7 - w, lo + 1, LX + 2 * w - lo - 1, False, [()])
    run_copies([(x.at[pl.ds(w, LX)], out)], sems)


def last_kernel(
    odd_ref, p0, p1, p2, a_0, a_1, a_2, b_0, b_1, b_2, source, a1, b1, cond_i, nu_i,
    field, x, y, held, f1, cond, nu, sems,
):
    odd = odd_ref[0]
    pairs = force_pairs(odd, source, 1, 1, (a1, b1), 6, f1)
    pairs += [(cond_i, cond.at[pl.ds(1, LX + 6)]), (nu_i, nu.at[pl.ds(1, LX + 6)])]
    for c, (p, a, b) in enumerate(((p0, a_0, b_0), (p1, a_1, b_1), (p2, a_2, b_2))):
        pairs.append((p, x.at[c, pl.ds(4, LX)]))
        pairs.append((a, x.at[c, pl.ds(2 + (1 - odd) * (LX + 2), 2)]))
        pairs.append((b, x.at[c, pl.ds(2 + odd * (LX + 2), 2)]))
    run_copies(pairs, sems)

    def into(buf):
        def store(c, i, value):
            buf[c, i] = value
        return store

    kept = copy_all([(x.at[:, pl.ds(4, LX)], field.at[0])], sems, 30)
    fine_sweep(x, into(y), held, cond, nu, 3, 17, f1)
    wait_all(kept)
    fine_sweep(y, into(x), held, cond, nu, 4, 16)
    run_copies([(x.at[:, pl.ds(4, LX)], field.at[1])], sems)


def body(guess, source, regions, conductance, reluct):
    slices = lax.axis_size("tm")
    slabs = lax.axis_size("space")
    odd = (lax.axis_index("space") % 2).astype(jnp.int32).reshape(1)
    on_chip = [(i, i ^ 1) for i in range(slabs)]
    off_chip = [(i, i + 1) for i in range(1, slabs - 1, 2)]
    off_chip += [(j, i) for i, j in off_chip]

    def from_a(x):
        return lax.ppermute(x, "space", on_chip)

    def from_b(x):
        return lax.ppermute(x, "space", off_chip)

    def later(x, distance):
        return lax.ppermute(x, "tm", [(i, (i + distance) % slices) for i in range(slices)])

    code, sa1, sb1, sa2, sb2 = call(
        pack_kernel, "pack", (odd, guess, source, regions),
        [planes(LX), planes(10), planes(10), planes(16), planes(16)],
        [pltpu.VMEM((LX, NY, NZ), jnp.int32), vmem(LX)], 32,
    )
    b1 = from_b(sb1)
    a1 = from_a(sa1)
    um = call(
        first_middle_kernel, "first_middle", (conductance, reluct, guess, source, code),
        planes(3, 4), [vmem(3, 8)] * 4 + [vmem(8)] * 3, 32,
    )
    vm = later(um, 1)
    b2 = from_b(sb2)
    a2 = from_a(sa2)
    ua, ub = call(
        first_kernel, "first", (odd, conductance, reluct, guess, source, code, a1, b1),
        [planes(3, 4), planes(3, 4)], [vmem(3, LX + 4)] * 4 + [vmem(LX + 4)] * 3, 32,
    )
    vb = later(ub, 1)
    va = later(ua, 1)
    cond, nu, keep, spread = call(
        material_kernel, "material", (odd, conductance, reluct, code, a2, b2),
        [planes(LX + 6), planes(LX + 6), planes(LX + 14), planes(LX + 14)],
        [vmem(LX + 14)] * 5, 32,
    )
    hb = from_b(vb)
    ha = from_a(va)
    n = LX + 8
    u0, ua, ub, um = call(
        second_kernel, "second",
        (odd, va, vb, vm, ha, hb, source, a1, b1, a2, b2, cond, nu),
        [planes(3, LX + 4), planes(3, 4), planes(3, 4), planes(3, 4)],
        [vmem(3, n)] * 5 + [vmem(n)] * 2, 32,
    )
    vb = later(ub, 1)
    va = later(ua, 1)
    vm = later(um, 1)
    hb = from_b(vb)
    ha = from_a(va)
    residual, *moving = call(
        residual_kernel, "residual",
        (odd, va, vb, vm, ha, hb, source, a2, b2, cond, nu, keep, spread, u0),
        [planes(1, 3, LX)] + [planes(LX)] * 3,
        [vmem(3, n)] * 4 + [vmem(n)] * 2 + [vmem(LX + 14)] * 2 + [vmem(3, n)], 32,
    )
    u0_own = [u0[c, 2:2 + LX] for c in range(3)]
    totals = [residual[0, c] for c in range(3)]
    for distance, width in ((1, 4), (2, 8), (4, 2)):
        moved = [later(m, distance) for m in moving]
        bases = u0_own if distance == 4 else totals
        if distance == 4:
            bases = [t + u for t, u in zip(totals, u0_own)]
        totals, moving, sides = [], [], []
        for c in range(3):
            total, sa, sb = call(
                functools.partial(add_kernel, width), "add%d" % width, (odd, bases[c], moved[c]),
                [planes(LX), planes(width), planes(width)], [vmem(LX)] * 2, 8,
            )
            hb = from_b(sb)
            ha = from_a(sa)
            totals.append(total)
            sides.append((ha, hb))
            if distance < 4:
                moving.append(
                    call(
                        functools.partial(power_kernel, width), "power%d" % width,
                        (odd, total, ha, hb, keep, spread), planes(LX),
                        [vmem(LX + 2 * width)] * 3 + [vmem(LX + 14)] * 2, 8,
                    )
                )
    field = call(
        last_kernel, "last",
        (odd, *totals, *[s[0] for s in sides], *[s[1] for s in sides], source, a1, b1, cond, nu),
        planes(2, 3, LX), [vmem(3, n)] * 4 + [vmem(n)] * 2, 32,
    )
    return field, residual


def solution(mesh):
    whole = P("tm", None, "space", None, None)
    return jax.shard_map(
        body, mesh=mesh, in_specs=(whole, whole, P("space", None, None), P(), P()),
        out_specs=(whole, whole), check_vma=False,
    )
```

time: 583 us -> 290 us (0.50); the launches traced: 573 us -> 288 us
  waiting for transfers between devices: 302 us -> 99.2 us
  starting transfers between devices: 241 us -> 70 us
  Pallas kernels: 0 us -> 112 us
  other arithmetic: 25.5 us -> 0.21 us
    ppermute x62 -> x41, waiting for transfers between devices: 302 us -> 99.2 us  [the longest x15 56.8 us: later(): lax.ppermute(x, 'tm', [(i, (i + distance) % slices) for i in range(slices)])]
    ppermute x62 -> x41, starting transfers between devices: 241 us -> 70 us  [the longest x13 46.6 us: from_b(): return lax.ppermute(x, 'space', off_chip)]
    pallas_call x0 -> x22, Pallas kernels: none -> 112 us  [call(): pl.pallas_call(kernel, name=name, out_shape=outs, in_specs=in_specs, out_...]
    add x17 -> x1, other arithmetic: 8.9 us -> 0.21 us  [body(): bases = [t + u for t, u in zip(totals, u0_own)]]
    div x10 -> x0, other arithmetic: 7.43 us -> none  [the longest x8 5.64 us: body(): (cond_coarse * flat + base_nu * neighbour_sum(rim_one(coarse_state))) / (...]
    reduce_sum x11 -> x0, other arithmetic: 6.67 us -> none  [the longest x10 6.34 us: fine_update(): square = jnp.sum(centre * centre, axis=0)]
  transfers between devices with their start and end apart: 62 -> 41, of which waited for: 52 -> 16; matrix products, arithmetic and copies ran while one was open for 1% -> 1% of each run, Pallas kernels for 0% -> 26%
where the time goes in v1:
time: 290 us; the launch traced here: 288 us
  Pallas kernels  112 us (39%)
  waiting for transfers between devices  99.2 us (34%)
  starting transfers between devices  70 us (24%)
  local copies, waits for them, and re-layouts  5.68 us (2%)
    pallas_call x22, Pallas kernels, call(): pl.pallas_call(kernel, name=name, out_shape=outs, in_specs=in_specs, out_...  112 us
    ppermute x15, waiting for transfers between devices, later(): lax.ppermute(x, 'tm', [(i, (i + distance) % slices) for i in range(slices)])  56.8 us
    ppermute x13, starting transfers between devices, from_b(): return lax.ppermute(x, 'space', off_chip)  46.6 us
    ppermute x13, waiting for transfers between devices, from_b(): return lax.ppermute(x, 'space', off_chip)  42.3 us
    ppermute x15, starting transfers between devices, later(): lax.ppermute(x, 'tm', [(i, (i + distance) % slices) for i in range(slices)])  17.3 us
    ppermute x13, starting transfers between devices, from_a(): return lax.ppermute(x, 'space', on_chip)  6.16 us
  transfers between devices with their start and end apart: 41, of which 16 were waited for; matrix products, arithmetic and copies ran while one was open for 1% of the time, Pallas kernels for 26%

profile of v1, /device:TPU:17, one launch (start us, length us, event | category | flops | bytes accessed | tf_op | source)
XLA Modules:
  0.0 288.3 jit_solution(11681944247297572715)
XLA Ops:
  12.2 8.4 %collective-permute-done.1.rb.b1 = f32[10,64,128]{2,1,0:T(8,128)S(1)} collective-permute-done((f32[10,64,128]{2,1,0:T(8,128)S(1)}, f32[10,64,128]{2,1,0:T(8,128)S(1)}, u32[]{:S(2)}, u32[]{:S(2)}) %collective-permute-start.1) | collective-permute-done | bytes 327712 | tf_op jit(solution)/shard_map/ppermute | solution.py:412
  20.6 5.9 %first.1 = (f32[3,4,64,128]{3,2,1,0:T(8,128)S(1)}, f32[3,4,64,128]{3,2,1,0:T(8,128)S(1)}) custom-call(s32[1]{0:T(128)} %bitcast.odd_ref, f32[4]{0:T(128)S(1)} %copy-done.4, f32[4]{0:T(128)S(1)} %copy-done.5, f32[2,3,12,64,128]{4,3,2,1,0:T(8,128)S(1)} %copy-done.2, f32[2,3,12,64,128]{4,3,2,1,0:T(8,128)S(1)} %copy-done, ...), custom_call_target="tpu_custom_call" | custom-call | bytes 4194304 | tf_op jit(solution)/shard_map/first/pallas_call | solution.py:45
  36.4 7.7 %collective-permute-done.2.va = f32[3,4,64,128]{3,2,1,0:T(8,128)S(1)} collective-permute-done((f32[3,4,64,128]{3,2,1,0:T(8,128)S(1)}, f32[3,4,64,128]{3,2,1,0:T(8,128)S(1)}, u32[]{:S(2)}, u32[]{:S(2)}) %collective-permute-start.2) | collective-permute-done | bytes 393248 | tf_op jit(solution)/shard_map/ppermute | solution.py:415
  44.1 12.1 %collective-permute-done.3.vb = f32[3,4,64,128]{3,2,1,0:T(8,128)S(1)} collective-permute-done((f32[3,4,64,128]{3,2,1,0:T(8,128)S(1)}, f32[3,4,64,128]{3,2,1,0:T(8,128)S(1)}, u32[]{:S(2)}, u32[]{:S(2)}) %collective-permute-start.3) | collective-permute-done | bytes 393248 | tf_op jit(solution)/shard_map/ppermute | solution.py:415
  59.8 12.3 %collective-permute-done.8.rb.b2 = f32[16,64,128]{2,1,0:T(8,128)S(1)} collective-permute-done((f32[16,64,128]{2,1,0:T(8,128)S(1)}, f32[16,64,128]{2,1,0:T(8,128)S(1)}, u32[]{:S(2)}, u32[]{:S(2)}) %collective-permute-start.8) | collective-permute-done | bytes 524320 | tf_op jit(solution)/shard_map/ppermute | solution.py:412
  76.4 10.7 %second.1 = (f32[3,16,64,128]{3,2,1,0:T(8,128)S(1)}, f32[3,4,64,128]{3,2,1,0:T(8,128)S(1)}, f32[3,4,64,128]{3,2,1,0:T(8,128)S(1)}, f32[3,4,64,128]{3,2,1,0:T(8,128)S(1)}) custom-call(s32[1]{0:T(128)} %bitcast.odd_ref, f32[3,4,64,128]{3,2,1,0:T(8,128)S(1)} %collective-permute-done.2.va, f32[3,4,64,128]{3,2,1,0:T(8,128)S(1)} %collective-permute-done.3.vb, ...), custom_call_target="tpu_custom_call" | custom-call | bytes 4194304 | tf_op jit(solution)/shard_map/second/pallas_call | solution.py:45
  87.4 13.8 %collective-permute-done.9.va = f32[3,4,64,128]{3,2,1,0:T(8,128)S(1)} collective-permute-done((f32[3,4,64,128]{3,2,1,0:T(8,128)S(1)}, f32[3,4,64,128]{3,2,1,0:T(8,128)S(1)}, u32[]{:S(2)}, u32[]{:S(2)}) %collective-permute-start.9) | collective-permute-done | bytes 393248 | tf_op jit(solution)/shard_map/ppermute | solution.py:415
  115.8 10.6 %residual.1 = (f32[1,3,12,64,128]{4,3,2,1,0:T(8,128)}, f32[12,64,128]{2,1,0:T(8,128)S(1)}, f32[12,64,128]{2,1,0:T(8,128)S(1)}, f32[12,64,128]{2,1,0:T(8,128)S(1)}) custom-call(s32[1]{0:T(128)} %bitcast.odd_ref, f32[3,4,64,128]{3,2,1,0:T(8,128)S(1)} %collective-permute-done.9.va, f32[3,4,64,128]{3,2,1,0:T(8,128)S(1)} %collective-permute-done.10.vb, ...), custom_call_target="tpu_custom_call" | custom-call | bytes 4194304 | tf_op jit(solution)/shard_map/residual/pallas_call | solution.py:45
  128.0 13.3 %collective-permute-done.21.moved = f32[12,64,128]{2,1,0:T(8,128)S(1)} collective-permute-done((f32[12,64,128]{2,1,0:T(8,128)S(1)}, f32[12,64,128]{2,1,0:T(8,128)S(1)}, u32[]{:S(2)}, u32[]{:S(2)}) %collective-permute-start.21) | collective-permute-done | bytes 393248 | tf_op jit(solution)/shard_map/ppermute | solution.py:415
  142.4 5.2 %collective-permute-start.23 = (f32[4,64,128]{2,1,0:T(8,128)S(1)}, f32[4,64,128]{2,1,0:T(8,128)S(1)}, u32[]{:S(2)}, u32[]{:S(2)}) collective-permute-start(f32[4,64,128]{2,1,0:T(8,128)S(1)} %get-tuple-element.75), channel_id=1, source_target_pairs={{1,2},{3,4},{5,6},{7,8},{9,10},{11,12},{13,14},{2,1},{4,3},{6,5},{... | collective-permute-start | bytes 393224 | tf_op jit(solution)/shard_map/ppermute | solution.py:412
  147.7 9.0 %collective-permute-done.23.hb = f32[4,64,128]{2,1,0:T(8,128)S(1)} collective-permute-done((f32[4,64,128]{2,1,0:T(8,128)S(1)}, f32[4,64,128]{2,1,0:T(8,128)S(1)}, u32[]{:S(2)}, u32[]{:S(2)}) %collective-permute-start.23) | collective-permute-done | bytes 131104 | tf_op jit(solution)/shard_map/ppermute | solution.py:412
  156.7 6.4 %power4.4 = f32[12,64,128]{2,1,0:T(8,128)S(1)} custom-call(s32[1]{0:T(128)} %bitcast.odd_ref, f32[12,64,128]{2,1,0:T(8,128)S(1)} %get-tuple-element.73.value.base, f32[4,64,128]{2,1,0:T(8,128)S(1)} %collective-permute-done.22.ha, f32[4,64,128]{2,1,0:T(8,128)S(1)} %collective-permute-done.23.hb, f32[26,64,128]{2,1,0:T(8,128)S(1)} %get-tuple-element.60.keep_i, ...), custom_call_target="tpu_custom_call" | custom-call | bytes 4194304 | tf_op jit(solution)/shard_map/power4/pallas_call | solution.py:45
  164.3 4.4 %collective-permute-start.16 = (f32[4,64,128]{2,1,0:T(8,128)S(1)}, f32[4,64,128]{2,1,0:T(8,128)S(1)}, u32[]{:S(2)}, u32[]{:S(2)}) collective-permute-start(f32[4,64,128]{2,1,0:T(8,128)S(1)} %get-tuple-element.67), channel_id=1, source_target_pairs={{1,2},{3,4},{5,6},{7,8},{9,10},{11,12},{13,14},{2,1},{4,3},{6,5},{... | collective-permute-start | bytes 393224 | tf_op jit(solution)/shard_map/ppermute | solution.py:412
  172.4 4.6 %collective-permute-start.30 = (f32[4,64,128]{2,1,0:T(8,128)S(1)}, f32[4,64,128]{2,1,0:T(8,128)S(1)}, u32[]{:S(2)}, u32[]{:S(2)}) collective-permute-start(f32[4,64,128]{2,1,0:T(8,128)S(1)} %get-tuple-element.83), channel_id=1, source_target_pairs={{1,2},{3,4},{5,6},{7,8},{9,10},{11,12},{13,14},{2,1},{4,3},{6,5},{... | collective-permute-start | bytes 393224 | tf_op jit(solution)/shard_map/ppermute | solution.py:412
  177.2 6.4 %power4.3 = f32[12,64,128]{2,1,0:T(8,128)S(1)} custom-call(s32[1]{0:T(128)} %bitcast.odd_ref, f32[12,64,128]{2,1,0:T(8,128)S(1)} %get-tuple-element.65.value.base, f32[4,64,128]{2,1,0:T(8,128)S(1)} %collective-permute-done.15.ha, f32[4,64,128]{2,1,0:T(8,128)S(1)} %collective-permute-done.16.hb, f32[26,64,128]{2,1,0:T(8,128)S(1)} %get-tuple-element.60.keep_i, ...), custom_call_target="tpu_custom_call" | custom-call | bytes 4194304 | tf_op jit(solution)/shard_map/power4/pallas_call | solution.py:45
  185.6 6.4 %power4.5 = f32[12,64,128]{2,1,0:T(8,128)S(1)} custom-call(s32[1]{0:T(128)} %bitcast.odd_ref, f32[12,64,128]{2,1,0:T(8,128)S(1)} %get-tuple-element.81.value.base, f32[4,64,128]{2,1,0:T(8,128)S(1)} %collective-permute-done.29.ha, f32[4,64,128]{2,1,0:T(8,128)S(1)} %collective-permute-done.30.hb, f32[26,64,128]{2,1,0:T(8,128)S(1)} %get-tuple-element.60.keep_i, ...), custom_call_target="tpu_custom_call" | custom-call | bytes 4194304 | tf_op jit(solution)/shard_map/power4/pallas_call | solution.py:45
  192.0 8.1 %collective-permute-start.31 = (f32[12,64,128]{2,1,0:T(8,128)S(1)}, f32[12,64,128]{2,1,0:T(8,128)S(1)}, u32[]{:S(2)}, u32[]{:S(2)}) collective-permute-start(f32[12,64,128]{2,1,0:T(8,128)S(1)} %power4.5), channel_id=1, source_target_pairs={{0,32},{16,48},{32,64},{48,80},{64,96},{80,112},{96,0},{112,16},{1... | collective-permute-start | bytes 1179656 | tf_op jit(solution)/shard_map/ppermute | solution.py:415
  212.5 5.0 %collective-permute-done.26.hb = f32[8,64,128]{2,1,0:T(8,128)S(1)} collective-permute-done((f32[8,64,128]{2,1,0:T(8,128)S(1)}, f32[8,64,128]{2,1,0:T(8,128)S(1)}, u32[]{:S(2)}, u32[]{:S(2)}) %collective-permute-start.26) | collective-permute-done | bytes 262176 | tf_op jit(solution)/shard_map/ppermute | solution.py:412
  217.5 14.2 %power8.4 = f32[12,64,128]{2,1,0:T(8,128)S(1)} custom-call(s32[1]{0:T(128)} %bitcast.odd_ref, f32[12,64,128]{2,1,0:T(8,128)S(1)} %get-tuple-element.76.value, f32[8,64,128]{2,1,0:T(8,128)S(1)} %collective-permute-done.25.ha, f32[8,64,128]{2,1,0:T(8,128)S(1)} %collective-permute-done.26.hb, f32[26,64,128]{2,1,0:T(8,128)S(1)} %get-tuple-element.60.keep_i, ...), custom_call_target="tpu_custom_call" | custom-call | bytes 4194304 | tf_op jit(solution)/shard_map/power8/pallas_call | solution.py:45
  231.8 14.2 %power8.3 = f32[12,64,128]{2,1,0:T(8,128)S(1)} custom-call(s32[1]{0:T(128)} %bitcast.odd_ref, f32[12,64,128]{2,1,0:T(8,128)S(1)} %get-tuple-element.68.value, f32[8,64,128]{2,1,0:T(8,128)S(1)} %collective-permute-done.18.ha, f32[8,64,128]{2,1,0:T(8,128)S(1)} %collective-permute-done.19.hb, f32[26,64,128]{2,1,0:T(8,128)S(1)} %get-tuple-element.60.keep_i, ...), custom_call_target="tpu_custom_call" | custom-call | bytes 4194304 | tf_op jit(solution)/shard_map/power8/pallas_call | solution.py:45
  249.0 14.2 %power8.5 = f32[12,64,128]{2,1,0:T(8,128)S(1)} custom-call(s32[1]{0:T(128)} %bitcast.odd_ref, f32[12,64,128]{2,1,0:T(8,128)S(1)} %get-tuple-element.84.value, f32[8,64,128]{2,1,0:T(8,128)S(1)} %collective-permute-done.32.ha, f32[8,64,128]{2,1,0:T(8,128)S(1)} %collective-permute-done.33.hb, f32[26,64,128]{2,1,0:T(8,128)S(1)} %get-tuple-element.60.keep_i, ...), custom_call_target="tpu_custom_call" | custom-call | bytes 4194304 | tf_op jit(solution)/shard_map/power8/pallas_call | solution.py:45
  264.6 4.9 %collective-permute-start.39 = (f32[2,64,128]{2,1,0:T(8,128)S(1)}, f32[2,64,128]{2,1,0:T(8,128)S(1)}, u32[]{:S(2)}, u32[]{:S(2)}) collective-permute-start(f32[2,64,128]{2,1,0:T(8,128)S(1)} %get-tuple-element.92), channel_id=1, source_target_pairs={{1,2},{3,4},{5,6},{7,8},{9,10},{11,12},{13,14},{2,1},{4,3},{6,5},{... | collective-permute-start | bytes 196616 | tf_op jit(solution)/shard_map/ppermute | solution.py:412
  274.5 4.7 %collective-permute-start.40 = (f32[2,64,128]{2,1,0:T(8,128)S(1)}, f32[2,64,128]{2,1,0:T(8,128)S(1)}, u32[]{:S(2)}, u32[]{:S(2)}) collective-permute-start(f32[2,64,128]{2,1,0:T(8,128)S(1)} %get-tuple-element.93), channel_id=1, source_target_pairs={{1,2},{3,4},{5,6},{7,8},{9,10},{11,12},{13,14},{2,1},{4,3},{6,5},{... | collective-permute-start | bytes 196616 | tf_op jit(solution)/shard_map/ppermute | solution.py:412
  281.5 6.7 %last.1 = f32[2,3,12,64,128]{4,3,2,1,0:T(8,128)} custom-call(s32[1]{0:T(128)} %bitcast.odd_ref, f32[12,64,128]{2,1,0:T(8,128)S(1)} %get-tuple-element.71.p0, f32[12,64,128]{2,1,0:T(8,128)S(1)} %get-tuple-element.79.p1, f32[12,64,128]{2,1,0:T(8,128)S(1)} %get-tuple-element.87.p2, f32[2,64,128]{2,1,0:T(8,128)S(1)} %collective-permute-done.35.a_0, ...), custom_call_target="tpu_custom_call" | custom-call | bytes 4194304 | tf_op jit(solution)/shard_map/last/pallas_call | solution.py:45
  (94 shorter events, 77.9 us)
Async XLA Ops:
  26.5 17.6 %collective-permute-start.2 = (f32[3,4,64,128]{3,2,1,0:T(8,128)S(1)}, f32[3,4,64,128]{3,2,1,0:T(8,128)S(1)}, u32[]{:S(2)}, u32[]{:S(2)}) collective-permute-start(f32[3,4,64,128]{3,2,1,0:T(8,128)S(1)} %get-tuple-element.51), channel_id=1, source_target_pairs={{0,16},{16,32},{32,48},{48,64},{64,80},{80,96},{96,112},{112,0},{1... | collective-permute-start | bytes 1179656 | tf_op jit(solution)/shard_map/ppermute | solution.py:415
  27.8 28.4 %collective-permute-start.3 = (f32[3,4,64,128]{3,2,1,0:T(8,128)S(1)}, f32[3,4,64,128]{3,2,1,0:T(8,128)S(1)}, u32[]{:S(2)}, u32[]{:S(2)}) collective-permute-start(f32[3,4,64,128]{3,2,1,0:T(8,128)S(1)} %get-tuple-element.52), channel_id=1, source_target_pairs={{0,16},{16,32},{32,48},{48,64},{64,80},{80,96},{96,112},{112,0},{1... | collective-permute-start | bytes 1179656 | tf_op jit(solution)/shard_map/ppermute | solution.py:415
  29.0 30.8 %collective-permute-start.7 = (f32[16,64,128]{2,1,0:T(8,128)S(1)}, f32[16,64,128]{2,1,0:T(8,128)S(1)}, u32[]{:S(2)}, u32[]{:S(2)}) collective-permute-start(f32[16,64,128]{2,1,0:T(8,128)S(1)} %get-tuple-element.53), channel_id=1, source_target_pairs={{0,1},{1,0},{2,3},{3,2},{4,5},{5,4},{6,7},{7,6},{8,9},{9,8},{10,11... | collective-permute-start | bytes 1572872 | tf_op jit(solution)/shard_map/ppermute | solution.py:409
  29.0 43.2 %collective-permute-start.8 = (f32[16,64,128]{2,1,0:T(8,128)S(1)}, f32[16,64,128]{2,1,0:T(8,128)S(1)}, u32[]{:S(2)}, u32[]{:S(2)}) collective-permute-start(f32[16,64,128]{2,1,0:T(8,128)S(1)} %get-tuple-element.54), channel_id=1, source_target_pairs={{1,2},{3,4},{5,6},{7,8},{9,10},{11,12},{13,14},{2,1},{4,3},{6,5},{... | collective-permute-start | bytes 1572872 | tf_op jit(solution)/shard_map/ppermute | solution.py:412
  35.4 39.7 %collective-permute-start.4 = (f32[3,4,64,128]{3,2,1,0:T(8,128)S(1)}, f32[3,4,64,128]{3,2,1,0:T(8,128)S(1)}, u32[]{:S(2)}, u32[]{:S(2)}) collective-permute-start(f32[3,4,64,128]{3,2,1,0:T(8,128)S(1)} %first_middle.1), channel_id=1, source_target_pairs={{0,16},{16,32},{32,48},{48,64},{64,80},{80,96},{96,112},{112,0},{1... | collective-permute-start | bytes 1179656 | tf_op jit(solution)/shard_map/ppermute | solution.py:415
  44.1 31.0 %collective-permute-start.5 = (f32[3,4,64,128]{3,2,1,0:T(8,128)S(1)}, f32[3,4,64,128]{3,2,1,0:T(8,128)S(1)}, u32[]{:S(2)}, u32[]{:S(2)}) collective-permute-start(f32[3,4,64,128]{3,2,1,0:T(8,128)S(1)} %collective-permute-done.2.va), channel_id=1, source_target_pairs={{0,1},{1,0},{2,3},{3,2},{4,5},{5,4},{6,7},{7,6},{8,9},{9,8},{10,11... | collective-permute-start | bytes 1179656 | tf_op jit(solution)/shard_map/ppermute | solution.py:409
  56.2 20.2 %collective-permute-start.6 = (f32[3,4,64,128]{3,2,1,0:T(8,128)S(1)}, f32[3,4,64,128]{3,2,1,0:T(8,128)S(1)}, u32[]{:S(2)}, u32[]{:S(2)}) collective-permute-start(f32[3,4,64,128]{3,2,1,0:T(8,128)S(1)} %collective-permute-done.3.vb), channel_id=1, source_target_pairs={{1,2},{3,4},{5,6},{7,8},{9,10},{11,12},{13,14},{2,1},{4,3},{6,5},{... | collective-permute-start | bytes 1179656 | tf_op jit(solution)/shard_map/ppermute | solution.py:412
  87.2 18.1 %collective-permute-start.10 = (f32[3,4,64,128]{3,2,1,0:T(8,128)S(1)}, f32[3,4,64,128]{3,2,1,0:T(8,128)S(1)}, u32[]{:S(2)}, u32[]{:S(2)}) collective-permute-start(f32[3,4,64,128]{3,2,1,0:T(8,128)S(1)} %get-tuple-element.58), channel_id=1, source_target_pairs={{0,16},{16,32},{32,48},{48,64},{64,80},{80,96},{96,112},{112,0},{1... | collective-permute-start | bytes 1179656 | tf_op jit(solution)/shard_map/ppermute | solution.py:415
  87.3 24.6 %collective-permute-start.11 = (f32[3,4,64,128]{3,2,1,0:T(8,128)S(1)}, f32[3,4,64,128]{3,2,1,0:T(8,128)S(1)}, u32[]{:S(2)}, u32[]{:S(2)}) collective-permute-start(f32[3,4,64,128]{3,2,1,0:T(8,128)S(1)} %get-tuple-element.59), channel_id=1, source_target_pairs={{0,16},{16,32},{32,48},{48,64},{64,80},{80,96},{96,112},{112,0},{1... | collective-permute-start | bytes 1179656 | tf_op jit(solution)/shard_map/ppermute | solution.py:415
  126.4 14.9 %collective-permute-start.21 = (f32[12,64,128]{2,1,0:T(8,128)S(1)}, f32[12,64,128]{2,1,0:T(8,128)S(1)}, u32[]{:S(2)}, u32[]{:S(2)}) collective-permute-start(f32[12,64,128]{2,1,0:T(8,128)S(1)} %get-tuple-element.72), channel_id=1, source_target_pairs={{0,16},{16,32},{32,48},{48,64},{64,80},{80,96},{96,112},{112,0},{1... | collective-permute-start | bytes 1179656 | tf_op jit(solution)/shard_map/ppermute | solution.py:415
  126.5 36.6 %collective-permute-start.14 = (f32[12,64,128]{2,1,0:T(8,128)S(1)}, f32[12,64,128]{2,1,0:T(8,128)S(1)}, u32[]{:S(2)}, u32[]{:S(2)}) collective-permute-start(f32[12,64,128]{2,1,0:T(8,128)S(1)} %get-tuple-element.64), channel_id=1, source_target_pairs={{0,16},{16,32},{32,48},{48,64},{64,80},{80,96},{96,112},{112,0},{1... | collective-permute-start | bytes 1179656 | tf_op jit(solution)/shard_map/ppermute | solution.py:415
  126.6 42.1 %collective-permute-start.28 = (f32[12,64,128]{2,1,0:T(8,128)S(1)}, f32[12,64,128]{2,1,0:T(8,128)S(1)}, u32[]{:S(2)}, u32[]{:S(2)}) collective-permute-start(f32[12,64,128]{2,1,0:T(8,128)S(1)} %get-tuple-element.80), channel_id=1, source_target_pairs={{0,16},{16,32},{32,48},{48,64},{64,80},{80,96},{96,112},{112,0},{1... | collective-permute-start | bytes 1179656 | tf_op jit(solution)/shard_map/ppermute | solution.py:415
  163.0 37.0 %collective-permute-start.24 = (f32[12,64,128]{2,1,0:T(8,128)S(1)}, f32[12,64,128]{2,1,0:T(8,128)S(1)}, u32[]{:S(2)}, u32[]{:S(2)}) collective-permute-start(f32[12,64,128]{2,1,0:T(8,128)S(1)} %power4.4), channel_id=1, source_target_pairs={{0,32},{16,48},{32,64},{48,80},{64,96},{80,112},{96,0},{112,16},{1... | collective-permute-start | bytes 1179656 | tf_op jit(solution)/shard_map/ppermute | solution.py:415
  169.8 15.9 %collective-permute-start.29 = (f32[4,64,128]{2,1,0:T(8,128)S(1)}, f32[4,64,128]{2,1,0:T(8,128)S(1)}, u32[]{:S(2)}, u32[]{:S(2)}) collective-permute-start(f32[4,64,128]{2,1,0:T(8,128)S(1)} %get-tuple-element.82), channel_id=1, source_target_pairs={{0,1},{1,0},{2,3},{3,2},{4,5},{5,4},{6,7},{7,6},{8,9},{9,8},{10,11... | collective-permute-start | bytes 393224 | tf_op jit(solution)/shard_map/ppermute | solution.py:409
  183.6 19.3 %collective-permute-start.17 = (f32[12,64,128]{2,1,0:T(8,128)S(1)}, f32[12,64,128]{2,1,0:T(8,128)S(1)}, u32[]{:S(2)}, u32[]{:S(2)}) collective-permute-start(f32[12,64,128]{2,1,0:T(8,128)S(1)} %power4.3), channel_id=1, source_target_pairs={{0,32},{16,48},{32,64},{48,80},{64,96},{80,112},{96,0},{112,16},{1... | collective-permute-start | bytes 1179656 | tf_op jit(solution)/shard_map/ppermute | solution.py:415
  192.0 16.2 %collective-permute-start.31 = (f32[12,64,128]{2,1,0:T(8,128)S(1)}, f32[12,64,128]{2,1,0:T(8,128)S(1)}, u32[]{:S(2)}, u32[]{:S(2)}) collective-permute-start(f32[12,64,128]{2,1,0:T(8,128)S(1)} %power4.5), channel_id=1, source_target_pairs={{0,32},{16,48},{32,64},{48,80},{64,96},{80,112},{96,0},{112,16},{1... | collective-permute-start | bytes 1179656 | tf_op jit(solution)/shard_map/ppermute | solution.py:415
  200.9 16.6 %collective-permute-start.26 = (f32[8,64,128]{2,1,0:T(8,128)S(1)}, f32[8,64,128]{2,1,0:T(8,128)S(1)}, u32[]{:S(2)}, u32[]{:S(2)}) collective-permute-start(f32[8,64,128]{2,1,0:T(8,128)S(1)} %get-tuple-element.78), channel_id=1, source_target_pairs={{1,2},{3,4},{5,6},{7,8},{9,10},{11,12},{13,14},{2,1},{4,3},{6,5},{... | collective-permute-start | bytes 786440 | tf_op jit(solution)/shard_map/ppermute | solution.py:412
  203.6 28.2 %collective-permute-start.18 = (f32[8,64,128]{2,1,0:T(8,128)S(1)}, f32[8,64,128]{2,1,0:T(8,128)S(1)}, u32[]{:S(2)}, u32[]{:S(2)}) collective-permute-start(f32[8,64,128]{2,1,0:T(8,128)S(1)} %get-tuple-element.69), channel_id=1, source_target_pairs={{0,1},{1,0},{2,3},{3,2},{4,5},{5,4},{6,7},{7,6},{8,9},{9,8},{10,11... | collective-permute-start | bytes 786440 | tf_op jit(solution)/shard_map/ppermute | solution.py:409
  204.2 27.6 %collective-permute-start.19 = (f32[8,64,128]{2,1,0:T(8,128)S(1)}, f32[8,64,128]{2,1,0:T(8,128)S(1)}, u32[]{:S(2)}, u32[]{:S(2)}) collective-permute-start(f32[8,64,128]{2,1,0:T(8,128)S(1)} %get-tuple-element.70), channel_id=1, source_target_pairs={{1,2},{3,4},{5,6},{7,8},{9,10},{11,12},{13,14},{2,1},{4,3},{6,5},{... | collective-permute-start | bytes 786440 | tf_op jit(solution)/shard_map/ppermute | solution.py:412
  208.9 40.1 %collective-permute-start.32 = (f32[8,64,128]{2,1,0:T(8,128)S(1)}, f32[8,64,128]{2,1,0:T(8,128)S(1)}, u32[]{:S(2)}, u32[]{:S(2)}) collective-permute-start(f32[8,64,128]{2,1,0:T(8,128)S(1)} %get-tuple-element.85), channel_id=1, source_target_pairs={{0,1},{1,0},{2,3},{3,2},{4,5},{5,4},{6,7},{7,6},{8,9},{9,8},{10,11... | collective-permute-start | bytes 786440 | tf_op jit(solution)/shard_map/ppermute | solution.py:409
  210.6 38.4 %collective-permute-start.33 = (f32[8,64,128]{2,1,0:T(8,128)S(1)}, f32[8,64,128]{2,1,0:T(8,128)S(1)}, u32[]{:S(2)}, u32[]{:S(2)}) collective-permute-start(f32[8,64,128]{2,1,0:T(8,128)S(1)} %get-tuple-element.86), channel_id=1, source_target_pairs={{1,2},{3,4},{5,6},{7,8},{9,10},{11,12},{13,14},{2,1},{4,3},{6,5},{... | collective-permute-start | bytes 786440 | tf_op jit(solution)/shard_map/ppermute | solution.py:412
  231.7 31.9 %collective-permute-start.27 = (f32[12,64,128]{2,1,0:T(8,128)S(1)}, f32[12,64,128]{2,1,0:T(8,128)S(1)}, u32[]{:S(2)}, u32[]{:S(2)}) collective-permute-start(f32[12,64,128]{2,1,0:T(8,128)S(1)} %power8.4), channel_id=1, source_target_pairs={{0,64},{16,80},{32,96},{48,112},{64,0},{80,16},{96,32},{112,48},{1... | collective-permute-start | bytes 1179656 | tf_op jit(solution)/shard_map/ppermute | solution.py:415
  246.0 23.5 %collective-permute-start.20 = (f32[12,64,128]{2,1,0:T(8,128)S(1)}, f32[12,64,128]{2,1,0:T(8,128)S(1)}, u32[]{:S(2)}, u32[]{:S(2)}) collective-permute-start(f32[12,64,128]{2,1,0:T(8,128)S(1)} %power8.3), channel_id=1, source_target_pairs={{0,64},{16,80},{32,96},{48,112},{64,0},{80,16},{96,32},{112,48},{1... | collective-permute-start | bytes 1179656 | tf_op jit(solution)/shard_map/ppermute | solution.py:415
  264.6 14.7 %collective-permute-start.39 = (f32[2,64,128]{2,1,0:T(8,128)S(1)}, f32[2,64,128]{2,1,0:T(8,128)S(1)}, u32[]{:S(2)}, u32[]{:S(2)}) collective-permute-start(f32[2,64,128]{2,1,0:T(8,128)S(1)} %get-tuple-element.92), channel_id=1, source_target_pairs={{1,2},{3,4},{5,6},{7,8},{9,10},{11,12},{13,14},{2,1},{4,3},{6,5},{... | collective-permute-start | bytes 196616 | tf_op jit(solution)/shard_map/ppermute | solution.py:412
  (23 other events, 217.4 us)

commit v2 on v1

--- a/solution.py
+++ b/solution.py
@@ -10,6 +10,7 @@
 LX, NY, NZ = 12, 64, 128
 F32 = jnp.float32
 ANY = pl.BlockSpec(memory_space=pl.ANY)
+VMEM = pl.BlockSpec(memory_space=pltpu.VMEM)
 SMEM = pl.BlockSpec(memory_space=pltpu.SMEM)
 
 
@@ -39,19 +40,32 @@
     wait_all(copy_all(pairs, sems, base))
 
 
-def call(kernel, name, args, outs, scratch, n_sems, flops=0):
-    in_specs = [SMEM if a.ndim == 1 else ANY for a in args]
+def call(kernel, name, args, outs, scratch, n_sems, flops=0, place=ANY):
+    in_specs = [SMEM if a.ndim == 1 else place for a in args]
     single = not isinstance(outs, (list, tuple))
     return pl.pallas_call(
         kernel,
         name=name,
         out_shape=outs,
         in_specs=in_specs,
-        out_specs=ANY if single else [ANY] * len(outs),
-        scratch_shapes=list(scratch) + [pltpu.SemaphoreType.DMA((n_sems,))],
+        out_specs=place if single else [place] * len(outs),
+        scratch_shapes=list(scratch) + [pltpu.SemaphoreType.DMA((n_sems,))] * (n_sems > 0),
         compiler_params=pltpu.CompilerParams(vmem_limit_bytes=40 * 1024 * 1024),
         cost_estimate=pl.CostEstimate(flops=flops, bytes_accessed=4 << 20, transcendentals=0),
     )(*args)
+
+
+def over_layers(lo, hi, step, at_once):
+    rounds = (hi - lo) // at_once
+
+    def body(t, carry):
+        for k in range(at_once):
+            step(lo + t * at_once + k)
+        return carry
+
+    lax.fori_loop(0, rounds, body, 0)
+    for i in range(lo + rounds * at_once, hi):
+        step(i)
 
 
 def neighbours(src, at):
@@ -71,7 +85,7 @@
 
 
 def fine_sweep(src, store, held, cond, nu, lo, hi, force=None):
-    def body(i, carry):
+    def step(i):
         square = src[0, i] * src[0, i] + src[1, i] * src[1, i] + src[2, i] * src[2, i]
         base = nu[i]
         weight = cond[i]
@@ -87,13 +101,12 @@
             else:
                 fixed = held[c, i]
             store(c, i, fixed * keep + neighbours(src, (c, i)) * spread)
-        return carry
-
-    lax.fori_loop(lo, hi, body, 0)
+
+    over_layers(lo, hi, step, 4)
 
 
 def coarse_sweep(src, store, held, keep, spread, off, lo, hi, first, comps):
-    def body(i, carry):
+    def step(i):
         k = keep[i + off]
         s = spread[i + off]
         for lead in comps:
@@ -104,9 +117,8 @@
             else:
                 fixed = held[at]
             store(at, fixed + s * neighbours(src, at))
-        return carry
-
-    lax.fori_loop(lo, hi, body, 0)
+
+    over_layers(lo, hi, step, 8 if len(comps) == 1 else 3)
 
 
 def lookup(code, table):
@@ -165,7 +177,7 @@
     run_copies([(x.at[:, pl.ds(2, 4)], out)], sems)
 
 
-def first_kernel(odd_ref, cond_t, nu_t, guess, source, code, ra, rb, out_a, out_b, x, y, held, f, cod, cond, nu, sems):
+def first_kernel(odd_ref, cond_t, nu_t, guess, source, code, ra, rb, after, out_a, out_b, x, y, held, f, cod, cond, nu, sems):
     odd = odd_ref[0]
     n = LX + 4
     pairs = [(code, cod.at[pl.ds(2, LX)])]
@@ -328,48 +340,33 @@
     run_copies([(x.at[c, pl.ds(4, LX)], o) for c, o in enumerate((l0, l1, l2))], sems)
 
 
-def add_kernel(w, odd_ref, base, moved, total_o, sa, sb, x, y, sems):
-    odd = odd_ref[0]
-    run_copies([(base, x), (moved, y)], sems)
-
-    def body(i, carry):
-        x[i] = x[i] + y[i]
-        return carry
-
-    lax.fori_loop(0, LX, body, 0)
-    run_copies(
-        [
-            (x, total_o),
-            (x.at[pl.ds((1 - odd) * (LX - w), w)], sa),
-            (x.at[pl.ds(odd * (LX - w), w)], sb),
-        ],
-        sems,
-    )
-
-
-def power_kernel(w, odd_ref, value, ha, hb, keep_i, spread_i, out, x, y, held, keep, spread, sems):
-    odd = odd_ref[0]
-    run_copies(
-        [
-            (value, x.at[pl.ds(w, LX)]),
-            (ha, x.at[pl.ds((1 - odd) * (LX + w), w)]),
-            (hb, x.at[pl.ds(odd * (LX + w), w)]),
-            (keep_i, keep),
-            (spread_i, spread),
-        ],
-        sems,
-    )
-
-    def put(buf):
+def add_kernel(w, odd_ref, base, moved, total_o, sa, sb):
+    odd = odd_ref[0]
+    for i in range(LX):
+        total_o[i] = base[i] + moved[i]
+    for side, top in ((sa, 1 - odd), (sb, odd)):
+        for i in range(w):
+            side[i] = total_o[i + top * (LX - w)]
+
+
+def power_kernel(w, odd_ref, value, ha, hb, keep, spread, out, x, y, held):
+    odd = odd_ref[0]
+    for i in range(LX):
+        x[i + w] = value[i]
+    for side, high in ((ha, 1 - odd), (hb, odd)):
+        for i in range(w):
+            x[i + high * (LX + w)] = side[i]
+
+    def put(buf, shift=0):
         def store(at, value):
-            buf[at] = value
+            buf[at[0] - shift] = value
         return store
 
     for step in range(w // 2):
         lo = 1 + 2 * step
+        last = put(out, w) if step == w // 2 - 1 else put(x)
         coarse_sweep(x, put(y), held, keep, spread, 7 - w, lo, LX + 2 * w - lo, True, [()])
-        coarse_sweep(y, put(x), held, keep, spread, 7 - w, lo + 1, LX + 2 * w - lo - 1, False, [()])
-    run_copies([(x.at[pl.ds(w, LX)], out)], sems)
+        coarse_sweep(y, last, held, keep, spread, 7 - w, lo + 1, LX + 2 * w - lo - 1, False, [()])
 
 
 def last_kernel(
@@ -429,7 +426,7 @@
     b2 = from_b(sb2)
     a2 = from_a(sa2)
     ua, ub = call(
-        first_kernel, "first", (odd, conductance, reluct, guess, source, code, a1, b1),
+        first_kernel, "first", (odd, conductance, reluct, guess, source, code, a1, b1, um),
         [planes(3, 4), planes(3, 4)], [vmem(3, LX + 4)] * 4 + [vmem(LX + 4)] * 3, 32,
     )
     vb = later(ub, 1)
@@ -470,7 +467,7 @@
         for c in range(3):
             total, sa, sb = call(
                 functools.partial(add_kernel, width), "add%d" % width, (odd, bases[c], moved[c]),
-                [planes(LX), planes(width), planes(width)], [vmem(LX)] * 2, 8,
+                [planes(LX), planes(width), planes(width)], [], 0, place=VMEM,
             )
             hb = from_b(sb)
             ha = from_a(sa)
@@ -481,7 +478,7 @@
                     call(
                         functools.partial(power_kernel, width), "power%d" % width,
                         (odd, total, ha, hb, keep, spread), planes(LX),
-                        [vmem(LX + 2 * width)] * 3 + [vmem(LX + 14)] * 2, 8,
+                        [vmem(LX + 2 * width)] * 3, 0, place=VMEM,
                     )
                 )
     field = call(

time: 290 us -> 277 us (0.955); the launches traced: 288 us -> 272 us
  Pallas kernels: 112 us -> 51.5 us
  starting transfers between devices: 70 us -> 113 us
    pallas_call x22, Pallas kernels: 112 us -> 51.5 us  [call(): pl.pallas_call(kernel, name=name, out_shape=outs, in_specs=in_specs, out_...]
    ppermute x13, starting transfers between devices: 6.16 us -> 47.9 us  [from_a(): return lax.ppermute(x, 'space', on_chip)]
    ppermute x15, starting transfers between devices: 17.3 us -> 28.7 us  [later(): lax.ppermute(x, 'tm', [(i, (i + distance) % slices) for i in range(slices)])]
    ppermute x13, starting transfers between devices: 46.6 us -> 36.5 us  [from_b(): return lax.ppermute(x, 'space', off_chip)]
  transfers between devices with their start and end apart: 41 -> 41, of which waited for: 16 -> 13; matrix products, arithmetic and copies ran while one was open for 1% -> 1% of each run, Pallas kernels for 26% -> 8%
where the time goes in v2:
time: 277 us; the launch traced here: 272 us
  starting transfers between devices  113 us (41%)
  waiting for transfers between devices  100 us (36%)
  Pallas kernels  51.5 us (19%)
  local copies, waits for them, and re-layouts  5.68 us (2%)
    ppermute x15, waiting for transfers between devices, later(): lax.ppermute(x, 'tm', [(i, (i + distance) % slices) for i in range(slices)])  56.5 us
    pallas_call x22, Pallas kernels, call(): pl.pallas_call(kernel, name=name, out_shape=outs, in_specs=in_specs, out_...  51.5 us
    ppermute x13, starting transfers between devices, from_a(): return lax.ppermute(x, 'space', on_chip)  47.9 us
    ppermute x13, waiting for transfers between devices, from_b(): return lax.ppermute(x, 'space', off_chip)  43.9 us
    ppermute x13, starting transfers between devices, from_b(): return lax.ppermute(x, 'space', off_chip)  36.5 us
    ppermute x15, starting transfers between devices, later(): lax.ppermute(x, 'tm', [(i, (i + distance) % slices) for i in range(slices)])  28.7 us
  transfers between devices with their start and end apart: 41, of which 13 were waited for; matrix products, arithmetic and copies ran while one was open for 1% of the time, Pallas kernels for 8%

profile of v2, /device:TPU:17, one launch (start us, length us, event | category | flops | bytes accessed | tf_op | source)
XLA Modules:
  0.0 272.3 jit_solution(17194392264674258312)
XLA Ops:
  14.1 6.5 %collective-permute-done.1.rb.b1 = f32[10,64,128]{2,1,0:T(8,128)S(1)} collective-permute-done((f32[10,64,128]{2,1,0:T(8,128)S(1)}, f32[10,64,128]{2,1,0:T(8,128)S(1)}, u32[]{:S(2)}, u32[]{:S(2)}) %collective-permute-start.1) | collective-permute-done | bytes 327712 | tf_op jit(solution)/shard_map/ppermute | solution.py:409
  20.6 4.8 %first.1 = (f32[3,4,64,128]{3,2,1,0:T(8,128)S(1)}, f32[3,4,64,128]{3,2,1,0:T(8,128)S(1)}) custom-call(s32[1]{0:T(128)} %bitcast.odd_ref, f32[4]{0:T(128)S(1)} %copy-done.4, f32[4]{0:T(128)S(1)} %copy-done.5, f32[2,3,12,64,128]{4,3,2,1,0:T(8,128)S(1)} %copy-done.2, f32[2,3,12,64,128]{4,3,2,1,0:T(8,128)S(1)} %copy-done.1, ...), custom_call_target="tpu_custom_call" | custom-call | bytes 4194304 | tf_op jit(solution)/shard_map/first/pallas_call | solution.py:46
  32.9 10.1 %collective-permute-done.2.va = f32[3,4,64,128]{3,2,1,0:T(8,128)S(1)} collective-permute-done((f32[3,4,64,128]{3,2,1,0:T(8,128)S(1)}, f32[3,4,64,128]{3,2,1,0:T(8,128)S(1)}, u32[]{:S(2)}, u32[]{:S(2)}) %collective-permute-start.2) | collective-permute-done | bytes 393248 | tf_op jit(solution)/shard_map/ppermute | solution.py:412
  43.1 12.1 %collective-permute-done.3.vb = f32[3,4,64,128]{3,2,1,0:T(8,128)S(1)} collective-permute-done((f32[3,4,64,128]{3,2,1,0:T(8,128)S(1)}, f32[3,4,64,128]{3,2,1,0:T(8,128)S(1)}, u32[]{:S(2)}, u32[]{:S(2)}) %collective-permute-start.3) | collective-permute-done | bytes 393248 | tf_op jit(solution)/shard_map/ppermute | solution.py:412
  58.8 12.3 %collective-permute-done.8.rb.b2 = f32[16,64,128]{2,1,0:T(8,128)S(1)} collective-permute-done((f32[16,64,128]{2,1,0:T(8,128)S(1)}, f32[16,64,128]{2,1,0:T(8,128)S(1)}, u32[]{:S(2)}, u32[]{:S(2)}) %collective-permute-start.8) | collective-permute-done | bytes 524320 | tf_op jit(solution)/shard_map/ppermute | solution.py:409
  75.3 8.0 %second.1 = (f32[3,16,64,128]{3,2,1,0:T(8,128)S(1)}, f32[3,4,64,128]{3,2,1,0:T(8,128)S(1)}, f32[3,4,64,128]{3,2,1,0:T(8,128)S(1)}, f32[3,4,64,128]{3,2,1,0:T(8,128)S(1)}) custom-call(s32[1]{0:T(128)} %bitcast.odd_ref, f32[3,4,64,128]{3,2,1,0:T(8,128)S(1)} %collective-permute-done.2.va, f32[3,4,64,128]{3,2,1,0:T(8,128)S(1)} %collective-permute-done.3.vb, ...), custom_call_target="tpu_custom_call" | custom-call | bytes 4194304 | tf_op jit(solution)/shard_map/second/pallas_call | solution.py:46
  83.6 13.8 %collective-permute-done.9.va = f32[3,4,64,128]{3,2,1,0:T(8,128)S(1)} collective-permute-done((f32[3,4,64,128]{3,2,1,0:T(8,128)S(1)}, f32[3,4,64,128]{3,2,1,0:T(8,128)S(1)}, u32[]{:S(2)}, u32[]{:S(2)}) %collective-permute-start.9) | collective-permute-done | bytes 393248 | tf_op jit(solution)/shard_map/ppermute | solution.py:412
  97.4 4.2 %collective-permute-done.10.vb = f32[3,4,64,128]{3,2,1,0:T(8,128)S(1)} collective-permute-done((f32[3,4,64,128]{3,2,1,0:T(8,128)S(1)}, f32[3,4,64,128]{3,2,1,0:T(8,128)S(1)}, u32[]{:S(2)}, u32[]{:S(2)}) %collective-permute-start.10) | collective-permute-done | bytes 393248 | tf_op jit(solution)/shard_map/ppermute | solution.py:412
  106.7 5.3 %collective-permute-done.13.hb = f32[3,4,64,128]{3,2,1,0:T(8,128)S(1)} collective-permute-done((f32[3,4,64,128]{3,2,1,0:T(8,128)S(1)}, f32[3,4,64,128]{3,2,1,0:T(8,128)S(1)}, u32[]{:S(2)}, u32[]{:S(2)}) %collective-permute-start.13) | collective-permute-done | bytes 393248 | tf_op jit(solution)/shard_map/ppermute | solution.py:409
  112.1 7.8 %residual.1 = (f32[1,3,12,64,128]{4,3,2,1,0:T(8,128)}, f32[12,64,128]{2,1,0:T(8,128)S(1)}, f32[12,64,128]{2,1,0:T(8,128)S(1)}, f32[12,64,128]{2,1,0:T(8,128)S(1)}) custom-call(s32[1]{0:T(128)} %bitcast.odd_ref, f32[3,4,64,128]{3,2,1,0:T(8,128)S(1)} %collective-permute-done.9.va, f32[3,4,64,128]{3,2,1,0:T(8,128)S(1)} %collective-permute-done.10.vb, ...), custom_call_target="tpu_custom_call" | custom-call | bytes 4194304 | tf_op jit(solution)/shard_map/residual/pallas_call | solution.py:46
  121.6 13.3 %collective-permute-done.21.moved = f32[12,64,128]{2,1,0:T(8,128)S(1)} collective-permute-done((f32[12,64,128]{2,1,0:T(8,128)S(1)}, f32[12,64,128]{2,1,0:T(8,128)S(1)}, u32[]{:S(2)}, u32[]{:S(2)}) %collective-permute-start.21) | collective-permute-done | bytes 393248 | tf_op jit(solution)/shard_map/ppermute | solution.py:412
  135.1 5.2 %collective-permute-start.23 = (f32[4,64,128]{2,1,0:T(8,128)S(1)}, f32[4,64,128]{2,1,0:T(8,128)S(1)}, u32[]{:S(2)}, u32[]{:S(2)}) collective-permute-start(f32[4,64,128]{2,1,0:T(8,128)S(1)} %get-tuple-element.75), channel_id=1, source_target_pairs={{1,2},{3,4},{5,6},{7,8},{9,10},{11,12},{13,14},{2,1},{4,3},{6,5},{... | collective-permute-start | bytes 393224 | tf_op jit(solution)/shard_map/ppermute | solution.py:409
  140.3 9.4 %collective-permute-done.23.hb = f32[4,64,128]{2,1,0:T(8,128)S(1)} collective-permute-done((f32[4,64,128]{2,1,0:T(8,128)S(1)}, f32[4,64,128]{2,1,0:T(8,128)S(1)}, u32[]{:S(2)}, u32[]{:S(2)}) %collective-permute-start.23) | collective-permute-done | bytes 131104 | tf_op jit(solution)/shard_map/ppermute | solution.py:409
  156.8 8.5 %collective-permute-start.29 = (f32[4,64,128]{2,1,0:T(8,128)S(1)}, f32[4,64,128]{2,1,0:T(8,128)S(1)}, u32[]{:S(2)}, u32[]{:S(2)}) collective-permute-start(f32[4,64,128]{2,1,0:T(8,128)S(1)} %get-tuple-element.82), channel_id=1, source_target_pairs={{0,1},{1,0},{2,3},{3,2},{4,5},{5,4},{6,7},{7,6},{8,9},{9,8},{10,11... | collective-permute-start | bytes 393224 | tf_op jit(solution)/shard_map/ppermute | solution.py:406
  170.9 11.8 %collective-permute-start.17 = (f32[12,64,128]{2,1,0:T(8,128)S(1)}, f32[12,64,128]{2,1,0:T(8,128)S(1)}, u32[]{:S(2)}, u32[]{:S(2)}) collective-permute-start(f32[12,64,128]{2,1,0:T(8,128)S(1)} %power4.3), channel_id=1, source_target_pairs={{0,32},{16,48},{32,64},{48,80},{64,96},{80,112},{96,0},{112,16},{1... | collective-permute-start | bytes 1179656 | tf_op jit(solution)/shard_map/ppermute | solution.py:412
  187.1 11.6 %collective-permute-start.25 = (f32[8,64,128]{2,1,0:T(8,128)S(1)}, f32[8,64,128]{2,1,0:T(8,128)S(1)}, u32[]{:S(2)}, u32[]{:S(2)}) collective-permute-start(f32[8,64,128]{2,1,0:T(8,128)S(1)} %get-tuple-element.77), channel_id=1, source_target_pairs={{0,1},{1,0},{2,3},{3,2},{4,5},{5,4},{6,7},{7,6},{8,9},{9,8},{10,11... | collective-permute-start | bytes 786440 | tf_op jit(solution)/shard_map/ppermute | solution.py:406
  211.8 5.4 %collective-permute-done.26.hb = f32[8,64,128]{2,1,0:T(8,128)S(1)} collective-permute-done((f32[8,64,128]{2,1,0:T(8,128)S(1)}, f32[8,64,128]{2,1,0:T(8,128)S(1)}, u32[]{:S(2)}, u32[]{:S(2)}) %collective-permute-start.26) | collective-permute-done | bytes 262176 | tf_op jit(solution)/shard_map/ppermute | solution.py:409
  221.3 6.2 %collective-permute-start.27 = (f32[12,64,128]{2,1,0:T(8,128)S(1)}, f32[12,64,128]{2,1,0:T(8,128)S(1)}, u32[]{:S(2)}, u32[]{:S(2)}) collective-permute-start(f32[12,64,128]{2,1,0:T(8,128)S(1)} %power8.4), channel_id=1, source_target_pairs={{0,64},{16,80},{32,96},{48,112},{64,0},{80,16},{96,32},{112,48},{1... | collective-permute-start | bytes 1179656 | tf_op jit(solution)/shard_map/ppermute | solution.py:412
  227.5 4.1 %power8.3 = f32[12,64,128]{2,1,0:T(8,128)S(1)} custom-call(s32[1]{0:T(128)} %bitcast.odd_ref, f32[12,64,128]{2,1,0:T(8,128)S(1)} %get-tuple-element.68.value, f32[8,64,128]{2,1,0:T(8,128)S(1)} %collective-permute-done.18.ha, f32[8,64,128]{2,1,0:T(8,128)S(1)} %collective-permute-done.19.hb, f32[26,64,128]{2,1,0:T(8,128)S(1)} %get-tuple-element.60.keep_i.keep, ...), custom_call_target="tpu_custom_call" | custom-call | bytes 4194304 | tf_op jit(solution)/shard_map/power8/pallas_call | solution.py:46
  232.0 4.1 %power8.5 = f32[12,64,128]{2,1,0:T(8,128)S(1)} custom-call(s32[1]{0:T(128)} %bitcast.odd_ref, f32[12,64,128]{2,1,0:T(8,128)S(1)} %get-tuple-element.84.value, f32[8,64,128]{2,1,0:T(8,128)S(1)} %collective-permute-done.32.ha, f32[8,64,128]{2,1,0:T(8,128)S(1)} %collective-permute-done.33.hb, f32[26,64,128]{2,1,0:T(8,128)S(1)} %get-tuple-element.60.keep_i.keep, ...), custom_call_target="tpu_custom_call" | custom-call | bytes 4194304 | tf_op jit(solution)/shard_map/power8/pallas_call | solution.py:46
  239.9 6.8 %collective-permute-start.36 = (f32[2,64,128]{2,1,0:T(8,128)S(1)}, f32[2,64,128]{2,1,0:T(8,128)S(1)}, u32[]{:S(2)}, u32[]{:S(2)}) collective-permute-start(f32[2,64,128]{2,1,0:T(8,128)S(1)} %get-tuple-element.89), channel_id=1, source_target_pairs={{0,1},{1,0},{2,3},{3,2},{4,5},{5,4},{6,7},{7,6},{8,9},{9,8},{10,11... | collective-permute-start | bytes 196616 | tf_op jit(solution)/shard_map/ppermute | solution.py:406
  248.7 4.3 %collective-permute-start.35 = (f32[2,64,128]{2,1,0:T(8,128)S(1)}, f32[2,64,128]{2,1,0:T(8,128)S(1)}, u32[]{:S(2)}, u32[]{:S(2)}) collective-permute-start(f32[2,64,128]{2,1,0:T(8,128)S(1)} %get-tuple-element.88), channel_id=1, source_target_pairs={{0,1},{1,0},{2,3},{3,2},{4,5},{5,4},{6,7},{7,6},{8,9},{9,8},{10,11... | collective-permute-start | bytes 196616 | tf_op jit(solution)/shard_map/ppermute | solution.py:406
  255.0 6.0 %collective-permute-start.37 = (f32[2,64,128]{2,1,0:T(8,128)S(1)}, f32[2,64,128]{2,1,0:T(8,128)S(1)}, u32[]{:S(2)}, u32[]{:S(2)}) collective-permute-start(f32[2,64,128]{2,1,0:T(8,128)S(1)} %get-tuple-element.90), channel_id=1, source_target_pairs={{0,1},{1,0},{2,3},{3,2},{4,5},{5,4},{6,7},{7,6},{8,9},{9,8},{10,11... | collective-permute-start | bytes 196616 | tf_op jit(solution)/shard_map/ppermute | solution.py:406
  266.6 5.5 %last.1 = f32[2,3,12,64,128]{4,3,2,1,0:T(8,128)} custom-call(s32[1]{0:T(128)} %bitcast.odd_ref, f32[12,64,128]{2,1,0:T(8,128)S(1)} %get-tuple-element.71.p0, f32[12,64,128]{2,1,0:T(8,128)S(1)} %get-tuple-element.79.p1, f32[12,64,128]{2,1,0:T(8,128)S(1)} %get-tuple-element.87.p2, f32[2,64,128]{2,1,0:T(8,128)S(1)} %collective-permute-done.35.a_0, ...), custom_call_target="tpu_custom_call" | custom-call | bytes 4194304 | tf_op jit(solution)/shard_map/last/pallas_call | solution.py:46
  (94 shorter events, 83.6 us)
Async XLA Ops:
  26.7 28.4 %collective-permute-start.3 = (f32[3,4,64,128]{3,2,1,0:T(8,128)S(1)}, f32[3,4,64,128]{3,2,1,0:T(8,128)S(1)}, u32[]{:S(2)}, u32[]{:S(2)}) collective-permute-start(f32[3,4,64,128]{3,2,1,0:T(8,128)S(1)} %get-tuple-element.52), channel_id=1, source_target_pairs={{0,16},{16,32},{32,48},{48,64},{64,80},{80,96},{96,112},{112,0},{1... | collective-permute-start | bytes 1179656 | tf_op jit(solution)/shard_map/ppermute | solution.py:412
  27.9 30.8 %collective-permute-start.7 = (f32[16,64,128]{2,1,0:T(8,128)S(1)}, f32[16,64,128]{2,1,0:T(8,128)S(1)}, u32[]{:S(2)}, u32[]{:S(2)}) collective-permute-start(f32[16,64,128]{2,1,0:T(8,128)S(1)} %get-tuple-element.53), channel_id=1, source_target_pairs={{0,1},{1,0},{2,3},{3,2},{4,5},{5,4},{6,7},{7,6},{8,9},{9,8},{10,11... | collective-permute-start | bytes 1572872 | tf_op jit(solution)/shard_map/ppermute | solution.py:406
  27.9 43.2 %collective-permute-start.8 = (f32[16,64,128]{2,1,0:T(8,128)S(1)}, f32[16,64,128]{2,1,0:T(8,128)S(1)}, u32[]{:S(2)}, u32[]{:S(2)}) collective-permute-start(f32[16,64,128]{2,1,0:T(8,128)S(1)} %get-tuple-element.54), channel_id=1, source_target_pairs={{1,2},{3,4},{5,6},{7,8},{9,10},{11,12},{13,14},{2,1},{4,3},{6,5},{... | collective-permute-start | bytes 1572872 | tf_op jit(solution)/shard_map/ppermute | solution.py:409
  32.0 42.1 %collective-permute-start.4 = (f32[3,4,64,128]{3,2,1,0:T(8,128)S(1)}, f32[3,4,64,128]{3,2,1,0:T(8,128)S(1)}, u32[]{:S(2)}, u32[]{:S(2)}) collective-permute-start(f32[3,4,64,128]{3,2,1,0:T(8,128)S(1)} %first_middle.1.after), channel_id=1, source_target_pairs={{0,16},{16,32},{32,48},{48,64},{64,80},{80,96},{96,112},{112,0},{1... | collective-permute-start | bytes 1179656 | tf_op jit(solution)/shard_map/ppermute | solution.py:412
  43.1 31.0 %collective-permute-start.5 = (f32[3,4,64,128]{3,2,1,0:T(8,128)S(1)}, f32[3,4,64,128]{3,2,1,0:T(8,128)S(1)}, u32[]{:S(2)}, u32[]{:S(2)}) collective-permute-start(f32[3,4,64,128]{3,2,1,0:T(8,128)S(1)} %collective-permute-done.2.va), channel_id=1, source_target_pairs={{0,1},{1,0},{2,3},{3,2},{4,5},{5,4},{6,7},{7,6},{8,9},{9,8},{10,11... | collective-permute-start | bytes 1179656 | tf_op jit(solution)/shard_map/ppermute | solution.py:406
  55.1 20.2 %collective-permute-start.6 = (f32[3,4,64,128]{3,2,1,0:T(8,128)S(1)}, f32[3,4,64,128]{3,2,1,0:T(8,128)S(1)}, u32[]{:S(2)}, u32[]{:S(2)}) collective-permute-start(f32[3,4,64,128]{3,2,1,0:T(8,128)S(1)} %collective-permute-done.3.vb), channel_id=1, source_target_pairs={{1,2},{3,4},{5,6},{7,8},{9,10},{11,12},{13,14},{2,1},{4,3},{6,5},{... | collective-permute-start | bytes 1179656 | tf_op jit(solution)/shard_map/ppermute | solution.py:409
  83.4 18.1 %collective-permute-start.10 = (f32[3,4,64,128]{3,2,1,0:T(8,128)S(1)}, f32[3,4,64,128]{3,2,1,0:T(8,128)S(1)}, u32[]{:S(2)}, u32[]{:S(2)}) collective-permute-start(f32[3,4,64,128]{3,2,1,0:T(8,128)S(1)} %get-tuple-element.58), channel_id=1, source_target_pairs={{0,16},{16,32},{32,48},{48,64},{64,80},{80,96},{96,112},{112,0},{1... | collective-permute-start | bytes 1179656 | tf_op jit(solution)/shard_map/ppermute | solution.py:412
  83.5 23.2 %collective-permute-start.11 = (f32[3,4,64,128]{3,2,1,0:T(8,128)S(1)}, f32[3,4,64,128]{3,2,1,0:T(8,128)S(1)}, u32[]{:S(2)}, u32[]{:S(2)}) collective-permute-start(f32[3,4,64,128]{3,2,1,0:T(8,128)S(1)} %get-tuple-element.59), channel_id=1, source_target_pairs={{0,16},{16,32},{32,48},{48,64},{64,80},{80,96},{96,112},{112,0},{1... | collective-permute-start | bytes 1179656 | tf_op jit(solution)/shard_map/ppermute | solution.py:412
  120.1 31.3 %collective-permute-start.14 = (f32[12,64,128]{2,1,0:T(8,128)S(1)}, f32[12,64,128]{2,1,0:T(8,128)S(1)}, u32[]{:S(2)}, u32[]{:S(2)}) collective-permute-start(f32[12,64,128]{2,1,0:T(8,128)S(1)} %get-tuple-element.64), channel_id=1, source_target_pairs={{0,16},{16,32},{32,48},{48,64},{64,80},{80,96},{96,112},{112,0},{1... | collective-permute-start | bytes 1179656 | tf_op jit(solution)/shard_map/ppermute | solution.py:412
  120.2 36.5 %collective-permute-start.28 = (f32[12,64,128]{2,1,0:T(8,128)S(1)}, f32[12,64,128]{2,1,0:T(8,128)S(1)}, u32[]{:S(2)}, u32[]{:S(2)}) collective-permute-start(f32[12,64,128]{2,1,0:T(8,128)S(1)} %get-tuple-element.80), channel_id=1, source_target_pairs={{0,16},{16,32},{32,48},{48,64},{64,80},{80,96},{96,112},{112,0},{1... | collective-permute-start | bytes 1179656 | tf_op jit(solution)/shard_map/ppermute | solution.py:412
  151.3 35.7 %collective-permute-start.24 = (f32[12,64,128]{2,1,0:T(8,128)S(1)}, f32[12,64,128]{2,1,0:T(8,128)S(1)}, u32[]{:S(2)}, u32[]{:S(2)}) collective-permute-start(f32[12,64,128]{2,1,0:T(8,128)S(1)} %power4.4), channel_id=1, source_target_pairs={{0,32},{16,48},{32,64},{48,80},{64,96},{80,112},{96,0},{112,16},{1... | collective-permute-start | bytes 1179656 | tf_op jit(solution)/shard_map/ppermute | solution.py:412
  151.5 17.9 %collective-permute-start.15 = (f32[4,64,128]{2,1,0:T(8,128)S(1)}, f32[4,64,128]{2,1,0:T(8,128)S(1)}, u32[]{:S(2)}, u32[]{:S(2)}) collective-permute-start(f32[4,64,128]{2,1,0:T(8,128)S(1)} %get-tuple-element.66), channel_id=1, source_target_pairs={{0,1},{1,0},{2,3},{3,2},{4,5},{5,4},{6,7},{7,6},{8,9},{9,8},{10,11... | collective-permute-start | bytes 393224 | tf_op jit(solution)/shard_map/ppermute | solution.py:406
  156.8 26.0 %collective-permute-start.29 = (f32[4,64,128]{2,1,0:T(8,128)S(1)}, f32[4,64,128]{2,1,0:T(8,128)S(1)}, u32[]{:S(2)}, u32[]{:S(2)}) collective-permute-start(f32[4,64,128]{2,1,0:T(8,128)S(1)} %get-tuple-element.82), channel_id=1, source_target_pairs={{0,1},{1,0},{2,3},{3,2},{4,5},{5,4},{6,7},{7,6},{8,9},{9,8},{10,11... | collective-permute-start | bytes 393224 | tf_op jit(solution)/shard_map/ppermute | solution.py:406
  170.9 29.7 %collective-permute-start.17 = (f32[12,64,128]{2,1,0:T(8,128)S(1)}, f32[12,64,128]{2,1,0:T(8,128)S(1)}, u32[]{:S(2)}, u32[]{:S(2)}) collective-permute-start(f32[12,64,128]{2,1,0:T(8,128)S(1)} %power4.3), channel_id=1, source_target_pairs={{0,32},{16,48},{32,64},{48,80},{64,96},{80,112},{96,0},{112,16},{1... | collective-permute-start | bytes 1179656 | tf_op jit(solution)/shard_map/ppermute | solution.py:412
  184.3 22.0 %collective-permute-start.31 = (f32[12,64,128]{2,1,0:T(8,128)S(1)}, f32[12,64,128]{2,1,0:T(8,128)S(1)}, u32[]{:S(2)}, u32[]{:S(2)}) collective-permute-start(f32[12,64,128]{2,1,0:T(8,128)S(1)} %power4.5), channel_id=1, source_target_pairs={{0,32},{16,48},{32,64},{48,80},{64,96},{80,112},{96,0},{112,16},{1... | collective-permute-start | bytes 1179656 | tf_op jit(solution)/shard_map/ppermute | solution.py:412
  187.1 22.7 %collective-permute-start.25 = (f32[8,64,128]{2,1,0:T(8,128)S(1)}, f32[8,64,128]{2,1,0:T(8,128)S(1)}, u32[]{:S(2)}, u32[]{:S(2)}) collective-permute-start(f32[8,64,128]{2,1,0:T(8,128)S(1)} %get-tuple-element.77), channel_id=1, source_target_pairs={{0,1},{1,0},{2,3},{3,2},{4,5},{5,4},{6,7},{7,6},{8,9},{9,8},{10,11... | collective-permute-start | bytes 786440 | tf_op jit(solution)/shard_map/ppermute | solution.py:406
  198.8 18.4 %collective-permute-start.26 = (f32[8,64,128]{2,1,0:T(8,128)S(1)}, f32[8,64,128]{2,1,0:T(8,128)S(1)}, u32[]{:S(2)}, u32[]{:S(2)}) collective-permute-start(f32[8,64,128]{2,1,0:T(8,128)S(1)} %get-tuple-element.78), channel_id=1, source_target_pairs={{1,2},{3,4},{5,6},{7,8},{9,10},{11,12},{13,14},{2,1},{4,3},{6,5},{... | collective-permute-start | bytes 786440 | tf_op jit(solution)/shard_map/ppermute | solution.py:409
  200.8 26.8 %collective-permute-start.18 = (f32[8,64,128]{2,1,0:T(8,128)S(1)}, f32[8,64,128]{2,1,0:T(8,128)S(1)}, u32[]{:S(2)}, u32[]{:S(2)}) collective-permute-start(f32[8,64,128]{2,1,0:T(8,128)S(1)} %get-tuple-element.69), channel_id=1, source_target_pairs={{0,1},{1,0},{2,3},{3,2},{4,5},{5,4},{6,7},{7,6},{8,9},{9,8},{10,11... | collective-permute-start | bytes 786440 | tf_op jit(solution)/shard_map/ppermute | solution.py:406
  204.3 23.2 %collective-permute-start.19 = (f32[8,64,128]{2,1,0:T(8,128)S(1)}, f32[8,64,128]{2,1,0:T(8,128)S(1)}, u32[]{:S(2)}, u32[]{:S(2)}) collective-permute-start(f32[8,64,128]{2,1,0:T(8,128)S(1)} %get-tuple-element.70), channel_id=1, source_target_pairs={{1,2},{3,4},{5,6},{7,8},{9,10},{11,12},{13,14},{2,1},{4,3},{6,5},{... | collective-permute-start | bytes 786440 | tf_op jit(solution)/shard_map/ppermute | solution.py:409
  206.3 25.7 %collective-permute-start.32 = (f32[8,64,128]{2,1,0:T(8,128)S(1)}, f32[8,64,128]{2,1,0:T(8,128)S(1)}, u32[]{:S(2)}, u32[]{:S(2)}) collective-permute-start(f32[8,64,128]{2,1,0:T(8,128)S(1)} %get-tuple-element.85), channel_id=1, source_target_pairs={{0,1},{1,0},{2,3},{3,2},{4,5},{5,4},{6,7},{7,6},{8,9},{9,8},{10,11... | collective-permute-start | bytes 786440 | tf_op jit(solution)/shard_map/ppermute | solution.py:406
  209.9 22.2 %collective-permute-start.33 = (f32[8,64,128]{2,1,0:T(8,128)S(1)}, f32[8,64,128]{2,1,0:T(8,128)S(1)}, u32[]{:S(2)}, u32[]{:S(2)}) collective-permute-start(f32[8,64,128]{2,1,0:T(8,128)S(1)} %get-tuple-element.86), channel_id=1, source_target_pairs={{1,2},{3,4},{5,6},{7,8},{9,10},{11,12},{13,14},{2,1},{4,3},{6,5},{... | collective-permute-start | bytes 786440 | tf_op jit(solution)/shard_map/ppermute | solution.py:409
  221.3 18.5 %collective-permute-start.27 = (f32[12,64,128]{2,1,0:T(8,128)S(1)}, f32[12,64,128]{2,1,0:T(8,128)S(1)}, u32[]{:S(2)}, u32[]{:S(2)}) collective-permute-start(f32[12,64,128]{2,1,0:T(8,128)S(1)} %power8.4), channel_id=1, source_target_pairs={{0,64},{16,80},{32,96},{48,112},{64,0},{80,16},{96,32},{112,48},{1... | collective-permute-start | bytes 1179656 | tf_op jit(solution)/shard_map/ppermute | solution.py:412
  236.2 18.8 %collective-permute-start.34 = (f32[12,64,128]{2,1,0:T(8,128)S(1)}, f32[12,64,128]{2,1,0:T(8,128)S(1)}, u32[]{:S(2)}, u32[]{:S(2)}) collective-permute-start(f32[12,64,128]{2,1,0:T(8,128)S(1)} %power8.5), channel_id=1, source_target_pairs={{0,64},{16,80},{32,96},{48,112},{64,0},{80,16},{96,32},{112,48},{1... | collective-permute-start | bytes 1179656 | tf_op jit(solution)/shard_map/ppermute | solution.py:412
  239.9 21.1 %collective-permute-start.36 = (f32[2,64,128]{2,1,0:T(8,128)S(1)}, f32[2,64,128]{2,1,0:T(8,128)S(1)}, u32[]{:S(2)}, u32[]{:S(2)}) collective-permute-start(f32[2,64,128]{2,1,0:T(8,128)S(1)} %get-tuple-element.89), channel_id=1, source_target_pairs={{0,1},{1,0},{2,3},{3,2},{4,5},{5,4},{6,7},{7,6},{8,9},{9,8},{10,11... | collective-permute-start | bytes 196616 | tf_op jit(solution)/shard_map/ppermute | solution.py:406
  (23 other events, 234.1 us)

commit v3 on v2

v3 whole, which is shorter than its diff:
```python
import functools

import jax
import jax.numpy as jnp
from jax import lax
from jax.experimental import pallas as pl
from jax.experimental.pallas import tpu as pltpu
from jax.sharding import PartitionSpec as P

LX, NY, NZ = 12, 64, 128
F32 = jnp.float32
ANY = pl.BlockSpec(memory_space=pl.ANY)
HBM = pl.BlockSpec(memory_space=pltpu.HBM)
VMEM = pl.BlockSpec(memory_space=pltpu.VMEM)
SMEM = pl.BlockSpec(memory_space=pltpu.SMEM)


def planes(*lead):
    return jax.ShapeDtypeStruct(tuple(lead) + (NY, NZ), F32)


def vmem(*lead):
    return pltpu.VMEM(tuple(lead) + (NY, NZ), F32)


def copy_all(pairs, sems, base=0):
    copies = [
        pltpu.make_async_copy(src, dst, sems.at[base + n]) for n, (src, dst) in enumerate(pairs)
    ]
    for copy in copies:
        copy.start()
    return copies


def wait_all(copies):
    for copy in copies:
        copy.wait()


def run_copies(pairs, sems, base=0):
    wait_all(copy_all(pairs, sems, base))


def call(kernel, name, args, outs, scratch, n_sems=0, out_specs=None, in_place=VMEM):
    in_specs = [SMEM if a.ndim == 1 else in_place for a in args]
    single = not isinstance(outs, (list, tuple))
    return pl.pallas_call(
        kernel,
        name=name,
        out_shape=outs,
        in_specs=in_specs,
        out_specs=out_specs or (VMEM if single else [VMEM] * len(outs)),
        scratch_shapes=list(scratch) + [pltpu.SemaphoreType.DMA((n_sems,))] * (n_sems > 0),
        compiler_params=pltpu.CompilerParams(vmem_limit_bytes=40 * 1024 * 1024),
        cost_estimate=pl.CostEstimate(flops=0, bytes_accessed=4 << 20, transcendentals=0),
    )(*args)


def over_layers(lo, hi, step, at_once):
    rounds = (hi - lo) // at_once

    def body(t, carry):
        for k in range(at_once):
            step(lo + t * at_once + k)
        return carry

    lax.fori_loop(0, rounds, body, 0)
    for i in range(lo + rounds * at_once, hi):
        step(i)


def neighbours(src, at):
    row = lax.broadcasted_iota(jnp.int32, (NY, NZ), 0)
    lane = lax.broadcasted_iota(jnp.int32, (NY, NZ), 1)
    zero = jnp.float32(0.0)
    def of(*lead_i):
        *lead, i = lead_i
        a = src[(*lead, i)]
        first = src[(*lead, i + 1)] + src[(*lead, i - 1)]
        up = jnp.where(row == 0, zero, pltpu.roll(a, 1, 0))
        down = jnp.where(row == NY - 1, zero, pltpu.roll(a, NY - 1, 0))
        left = jnp.where(lane == 0, zero, pltpu.roll(a, 1, 1))
        right = jnp.where(lane == NZ - 1, zero, pltpu.roll(a, NZ - 1, 1))
        return (first + (up + down)) + (left + right)
    return of(*at)


def fine_sweep(src, store, held, cond, nu, lo, hi, force=None, off=0):
    def step(i):
        square = src[0, i] * src[0, i] + src[1, i] * src[1, i] + src[2, i] * src[2, i]
        base = nu[i - off]
        weight = cond[i - off]
        grown = 1.0 + square
        strong = base * (1.0 + 1.5 * square)
        scale = 1.0 / (weight * grown + 6.0 * strong)
        keep = grown * scale
        spread = strong * scale
        for c in range(3):
            if force is not None:
                fixed = weight * src[c, i] + force[c, i]
                held[c, i] = fixed
            else:
                fixed = held[c, i]
            store(c, i, fixed * keep + neighbours(src, (c, i)) * spread)

    over_layers(lo, hi, step, 4)


def coarse_sweep(src, store, held, keep, spread, off, lo, hi, first, comps):
    def step(i):
        k = keep[i + off]
        s = spread[i + off]
        for lead in comps:
            at = lead + (i,)
            if first:
                fixed = k * src[at]
                held[at] = fixed
            else:
                fixed = held[at]
            store(at, fixed + s * neighbours(src, at))

    over_layers(lo, hi, step, 8 if len(comps) == 1 else 3)


def lookup(code, table):
    first = jnp.where(code == 1, table[0], table[1])
    second = jnp.where(code == 3, table[2], table[3])
    return jnp.where(code <= 2, first, second)


def materials(code, cond_t, nu_t):
    outside = code == 0
    return (
        jnp.where(outside, jnp.float32(1.0), lookup(code, cond_t)),
        jnp.where(outside, jnp.float32(0.0), lookup(code, nu_t)),
    )


def into(buf):
    def store(c, i, value):
        buf[c, i] = value
    return store


def put(buf, shift=0):
    def store(at, value):
        buf[at[:-1] + (at[-1] - shift,)] = value
    return store


def edges(odd, n, width):
    return (1 - odd) * (n - width), odd * (n - width)


def first_pack_kernel(odd_ref, guess, source, regions, a1, b1, reg, sems):
    odd = odd_ref[0]
    pairs = [(regions.at[pl.ds(0, 1)], reg.at[pl.ds(0, 1)]), (regions.at[pl.ds(LX - 1, 1)], reg.at[pl.ds(1, 1)])]
    for one, two_from, one_from in zip((a1, b1), edges(odd, LX, 2), edges(odd, LX, 1)):
        for c in range(3):
            pairs.append((guess.at[0, c, pl.ds(two_from, 2)], one.at[pl.ds(2 * c, 2)]))
            pairs.append((source.at[1, c, pl.ds(one_from, 1)], one.at[pl.ds(6 + c, 1)]))
    run_copies(pairs, sems)
    a1[9] = (reg[1 - odd] + 1).astype(F32)
    b1[9] = (reg[odd] + 1).astype(F32)


def second_pack_kernel(odd_ref, source, regions, a2, b2, a3, b3, reg, sems):
    odd = odd_ref[0]
    pairs = [(regions, reg)]
    for two, start in zip((a2, b2), edges(odd, LX, 3)):
        for c in range(3):
            pairs.append((source.at[0, c, pl.ds(start, 3)], two.at[pl.ds(3 * c, 3)]))
    run_copies(pairs, sems)
    for two, start in zip((a2, b2), edges(odd, LX, 3)):
        for k in range(3):
            two[9 + k] = (reg[start + k] + 1).astype(F32)
    for three, high in ((a3, 1 - odd), (b3, odd)):
        for k in range(4):
            three[k] = (reg[high * (LX - 7) + (1 - high) * 3 + k] + 1).astype(F32)


def first_middle_kernel(cond_t, nu_t, guess, source, regions, out, y, held, cond, nu):
    def prepare(i):
        cond[i], nu[i] = materials(regions[i] + 1, cond_t, nu_t)

    over_layers(3, 9, prepare, 6)
    fine_sweep(guess.at[0], into(y), held, cond, nu, 3, 9, source.at[1])

    def store(c, i, value):
        out[c, i - 4] = value

    fine_sweep(y, store, held, cond, nu, 4, 8)


def first_kernel(odd_ref, cond_t, nu_t, guess, source, regions, ra, rb, after, out_a, out_b, x, y, held, f, cond, nu):
    odd = odd_ref[0]
    n = LX + 4
    for c in range(3):
        for i in (0, 1, 2, 3, 4, 5, 6, 7, 8, 9, 10, 11):
            x[c, i + 2] = guess[0, c, i]
            f[c, i + 2] = source[1, c, i]
    for i in range(LX):
        cond[i + 2], nu[i + 2] = materials(regions[i] + 1, cond_t, nu_t)
    for pack, high in ((ra, 1 - odd), (rb, odd)):
        for c in range(3):
            for k in range(2):
                x[c, high * (n - 2) + k] = pack[2 * c + k]
            f[c, 1 + high * (n - 3)] = pack[6 + c]
        cond[1 + high * (n - 3)], nu[1 + high * (n - 3)] = materials(pack[9], cond_t, nu_t)
    fine_sweep(x, into(y), held, cond, nu, 1, 7, f)
    fine_sweep(x, into(y), held, cond, nu, 9, n - 1, f)
    fine_sweep(y, into(x), held, cond, nu, 2, 6)
    fine_sweep(y, into(x), held, cond, nu, 10, 14)
    for c in range(3):
        for k in range(4):
            out_a[c, k] = x[c, 2 + (1 - odd) * 8 + k]
            out_b[c, k] = x[c, 2 + odd * 8 + k]


def material_kernel(odd_ref, cond_t, nu_t, regions, ra, rb, cond, nu, keep, spread):
    odd = odd_ref[0]

    def fill(at, code):
        cv, nv = materials(code, cond_t, nu_t)
        cond[at] = cv
        nu[at] = nv
        half = 0.5 * cv
        scale = 1.0 / (half + 6.0 * nv)
        keep[at] = half * scale
        spread[at] = nv * scale

    for i in range(LX):
        fill(3 + i, regions[i] + 1)
    for pack, high in ((ra, 1 - odd), (rb, odd)):
        for k in range(3):
            fill(high * (LX + 3) + k, pack[9 + k])


def wide_kernel(odd_ref, cond_t, nu_t, keep_i, spread_i, ra, rb, keep, spread):
    odd = odd_ref[0]
    for i in range(LX + 6):
        keep[i + 4] = keep_i[i]
        spread[i + 4] = spread_i[i]
    for pack, high in ((ra, 1 - odd), (rb, odd)):
        for k in range(4):
            at = high * (LX + 10) + k
            cv, nv = materials(pack[k], cond_t, nu_t)
            half = 0.5 * cv
            scale = 1.0 / (half + 6.0 * nv)
            keep[at] = half * scale
            spread[at] = nv * scale


def extend(odd, pieces, halos, x):
    a, b, m = pieces
    ha, hb = halos
    for c in range(3):
        for k in range(4):
            x[c, 8 + k] = m[c, k]
            x[c, 4 + (1 - odd) * 8 + k] = a[c, k]
            x[c, 4 + odd * 8 + k] = b[c, k]
            x[c, (1 - odd) * 16 + k] = ha[c, k]
            x[c, odd * 16 + k] = hb[c, k]


def extend_force(odd, source, which, width, packs, start, f):
    for c in range(3):
        for i in range(LX):
            f[c, 4 + i] = source[which, c, i]
        for pack, high in ((packs[0], 1 - odd), (packs[1], odd)):
            for k in range(width):
                f[c, 4 - width + high * (LX + width) + k] = pack[start + width * c + k]


def second_kernel(
    odd_ref, hb, vb, ha, va, vm, source, a1, b1, a2, b2, cond, nu,
    u0, oa, ob, om, x, y, held, f0, f1,
):
    odd = odd_ref[0]
    extend(odd, (va, vb, vm), (ha, hb), x)
    extend_force(odd, source, 0, 3, (a2, b2), 0, f0)
    extend_force(odd, source, 1, 1, (a1, b1), 6, f1)

    def keep_u0(c, i, value):
        x[c, i] = value
        u0[c, i - 2] = value

    fine_sweep(x, into(y), held, cond, nu, 1, 19, f0, 1)
    fine_sweep(y, keep_u0, held, cond, nu, 2, 18, None, 1)
    fine_sweep(x, into(y), held, cond, nu, 3, 17, f1, 1)
    fine_sweep(y, into(x), held, cond, nu, 4, 16, None, 1)
    for c in range(3):
        for k in range(4):
            om[c, k] = x[c, 8 + k]
            oa[c, k] = x[c, 4 + (1 - odd) * 8 + k]
            ob[c, k] = x[c, 4 + odd * 8 + k]


def residual_kernel(
    odd_ref, hb, vb, ha, va, vm, source, a2, b2, cond, nu, keep, spread, u0,
    res_o, l0, l1, l2, r0, r1, r2, x, y, held, f0, sems,
):
    odd = odd_ref[0]
    extend(odd, (va, vb, vm), (ha, hb), x)
    extend_force(odd, source, 0, 3, (a2, b2), 0, f0)

    def less(c, i, value):
        x[c, i] = value - u0[c, i - 2]

    fine_sweep(x, into(y), held, cond, nu, 1, 19, f0, 1)
    fine_sweep(y, less, held, cond, nu, 2, 18, None, 1)
    kept = copy_all([(x.at[:, pl.ds(4, LX)], res_o.at[0])], sems)
    comps = [(0,), (1,), (2,)]
    coarse_sweep(x, put(y), held, keep, spread, -1, 3, 17, True, comps)
    for c, out in enumerate((r0, r1, r2)):
        for i in range(LX):
            out[i] = x[c, 4 + i]

    def store(at, value):
        (l0, l1, l2)[at[0]][at[1] - 4] = value

    coarse_sweep(y, store, held, keep, spread, -1, 4, 16, False, comps)
    wait_all(kept)


def add_kernel(w, odd_ref, *refs):
    odd = odd_ref[0]
    *terms, total, sa, sb = refs
    for i in range(LX):
        value = terms[0][i]
        for term in terms[1:]:
            value = value + term[i]
        total[i] = value
    for side, top in ((sa, 1 - odd), (sb, odd)):
        for i in range(w):
            side[i] = total[i + top * (LX - w)]


def power_kernel(w, odd_ref, value, ha, hb, keep, spread, out, x, y, held):
    odd = odd_ref[0]
    for i in range(LX):
        x[i + w] = value[i]
    for side, high in ((ha, 1 - odd), (hb, odd)):
        for i in range(w):
            x[i + high * (LX + w)] = side[i]

    for step in range(w // 2):
        lo = 1 + 2 * step
        last = put(out, w) if step == w // 2 - 1 else put(x)
        coarse_sweep(x, put(y), held, keep, spread, -1, lo, LX + 2 * w - lo, True, [()])
        coarse_sweep(y, last, held, keep, spread, -1, lo + 1, LX + 2 * w - lo - 1, False, [()])


def last_kernel(
    odd_ref, p0, p1, p2, a_0, a_1, a_2, b_0, b_1, b_2, source, a1, b1, cond, nu,
    field, x, y, held, f1, sems,
):
    odd = odd_ref[0]
    kept = copy_all([(p, field.at[0, c]) for c, p in enumerate((p0, p1, p2))], sems)
    extend_force(odd, source, 1, 1, (a1, b1), 6, f1)
    for c, (p, a, b) in enumerate(((p0, a_0, b_0), (p1, a_1, b_1), (p2, a_2, b_2))):
        for i in range(LX):
            x[c, 4 + i] = p[i]
        for k in range(2):
            x[c, 2 + (1 - odd) * (LX + 2) + k] = a[k]
            x[c, 2 + odd * (LX + 2) + k] = b[k]
    fine_sweep(x, into(y), held, cond, nu, 3, 17, f1, 1)
    fine_sweep(y, into(x), held, cond, nu, 4, 10, None, 1)
    kept += copy_all([(x.at[:, pl.ds(4, 6)], field.at[1, :, pl.ds(0, 6)])], sems, 3)
    fine_sweep(y, into(x), held, cond, nu, 10, 16, None, 1)
    kept += copy_all([(x.at[:, pl.ds(10, 6)], field.at[1, :, pl.ds(6, 6)])], sems, 4)
    wait_all(kept)


def body(guess, source, regions, conductance, reluct):
    slices = lax.axis_size("tm")
    slabs = lax.axis_size("space")
    odd = (lax.axis_index("space") % 2).astype(jnp.int32).reshape(1)
    on_chip = [(i, i ^ 1) for i in range(slabs)]
    off_chip = [(i, i + 1) for i in range(1, slabs - 1, 2)]
    off_chip += [(j, i) for i, j in off_chip]
    fence = lax.optimization_barrier

    def from_a(x):
        return lax.ppermute(x, "space", on_chip)

    def from_b(x):
        return lax.ppermute(x, "space", off_chip)

    def later(x, distance):
        return lax.ppermute(x, "tm", [(i, (i + distance) % slices) for i in range(slices)])

    tables = (conductance, reluct)
    sa1, sb1 = call(
        first_pack_kernel, "first_pack", (odd, guess, source, regions),
        [planes(10), planes(10)], [pltpu.VMEM((2, NY, NZ), jnp.int32)], 16, in_place=HBM,
    )
    b1 = from_b(sb1)
    a1 = from_a(sa1)
    um = call(
        first_middle_kernel, "first_middle", (*tables, guess, source, regions),
        planes(3, 4), [vmem(3, LX)] * 2 + [vmem(LX)] * 2,
    )
    sa2, sb2, sa3, sb3 = call(
        second_pack_kernel, "second_pack", (odd, source, regions),
        [planes(12), planes(12), planes(4), planes(4)], [pltpu.VMEM((LX, NY, NZ), jnp.int32)], 8, in_place=HBM,
    )
    vm = later(um, 1)
    sb2, sa2, b1 = fence((sb2, sa2, b1))
    b2 = from_b(sb2)
    a2 = from_a(sa2)
    ua, ub = call(
        first_kernel, "first", (odd, *tables, guess, source, regions, a1, b1, um),
        [planes(3, 4), planes(3, 4)], [vmem(3, LX + 4)] * 4 + [vmem(LX + 4)] * 2,
    )
    vb = later(ub, 1)
    va = later(ua, 1)
    cond, nu, keep, spread = call(
        material_kernel, "material", (odd, *tables, regions, a2, b2), [planes(LX + 6)] * 4, [],
    )
    vb, vm, cond = fence((vb, vm, cond))
    hb = from_b(vb)
    ha = from_a(va)
    sb3, sa3, vb = fence((sb3, sa3, vb))
    b3 = from_b(sb3)
    a3 = from_a(sa3)
    n = LX + 8
    u0, ua, ub, um = call(
        second_kernel, "second",
        (odd, hb, vb, ha, va, vm, source, a1, b1, a2, b2, cond, nu),
        [planes(3, LX + 4), planes(3, 4), planes(3, 4), planes(3, 4)], [vmem(3, n)] * 5,
    )
    vb = later(ub, 1)
    va = later(ua, 1)
    vm = later(um, 1)
    hb = from_b(vb)
    ha = from_a(va)
    wide_keep, wide_spread = call(
        wide_kernel, "wide", (odd, *tables, keep, spread, a3, b3), [planes(LX + 14)] * 2, [],
    )
    residual, *rest = call(
        residual_kernel, "residual",
        (odd, hb, vb, ha, va, vm, source, a2, b2, cond, nu, keep, spread, u0),
        [planes(1, 3, LX)] + [planes(LX)] * 6, [vmem(3, n)] * 4, 1, [ANY] + [VMEM] * 6,
    )
    moving, totals = rest[:3], rest[3:]
    u0_own = [u0[c, 2:2 + LX] for c in range(3)]
    for distance, width in ((1, 4), (2, 8), (4, 2)):
        moved = [later(m, distance) for m in moving]
        bases = [(t,) for t in totals]
        if distance == 4:
            bases = [(t, u) for t, u in zip(totals, u0_own)]
        totals, moving, sides = [], [], []
        for c in range(3):
            total, sa, sb = call(
                functools.partial(add_kernel, width), "add%d" % width, (odd, *bases[c], moved[c]),
                [planes(LX), planes(width), planes(width)], [],
            )
            hb = from_b(sb)
            ha = from_a(sa)
            totals.append(total)
            sides.append((ha, hb))
            if distance < 4:
                pair = (wide_keep, wide_spread) if width == 8 else (keep, spread)
                moving.append(
                    call(
                        functools.partial(power_kernel, width), "power%d" % width,
                        (odd, total, ha, hb, *pair), planes(LX), [vmem(LX + 2 * width)] * 3,
                    )
                )
    field = call(
        last_kernel, "last",
        (odd, *totals, *[s[0] for s in sides], *[s[1] for s in sides], source, a1, b1, cond, nu),
        planes(2, 3, LX), [vmem(3, n)] * 4, 5, ANY,
    )
    return field, residual


def solution(mesh):
    whole = P("tm", None, "space", None, None)
    return jax.shard_map(
        body, mesh=mesh, in_specs=(whole, whole, P("space", None, None), P(), P()),
        out_specs=(whole, whole), check_vma=False,
    )
```

time: 277 us -> 281 us (1.014)
  waiting for transfers between devices: 100 us -> 118 us
  Pallas kernels: 51.5 us -> 38.6 us
    ppermute x13 -> x14, starting transfers between devices: 47.9 us -> 65.3 us  [from_a(): return lax.ppermute(x, 'space', on_chip)]
    ppermute x13 -> x14, waiting for transfers between devices: 43.9 us -> 60.2 us  [from_b(): return lax.ppermute(x, 'space', off_chip)]
    ppermute x15, starting transfers between devices: 28.7 us -> 14.8 us  [later(): lax.ppermute(x, 'tm', [(i, (i + distance) % slices) for i in range(slices)])]
    pallas_call x22 -> x24, Pallas kernels: 51.5 us -> 38.6 us  [call(): pl.pallas_call(kernel, name=name, out_shape=outs, in_specs=in_specs, out_...]
    ppermute x13 -> x14, starting transfers between devices: 36.5 us -> 34.9 us  [from_b(): return lax.ppermute(x, 'space', off_chip)]
  transfers between devices with their start and end apart: 41 -> 43, of which waited for: 13 -> 13; matrix products, arithmetic and copies ran while one was open for 1% -> 0% of each run, Pallas kernels for 8% -> 9%
where the time goes in v3:
time: 281 us; the launch traced here: 278 us
  waiting for transfers between devices  118 us (42%)
  starting transfers between devices  115 us (41%)
  Pallas kernels  38.6 us (14%)
  local copies, waits for them, and re-layouts  4.45 us (2%)
    ppermute x14, starting transfers between devices, from_a(): return lax.ppermute(x, 'space', on_chip)  65.3 us
    ppermute x14, waiting for transfers between devices, from_b(): return lax.ppermute(x, 'space', off_chip)  60.2 us
    ppermute x15, waiting for transfers between devices, later(): lax.ppermute(x, 'tm', [(i, (i + distance) % slices) for i in range(slices)])  57.9 us
    pallas_call x24, Pallas kernels, call(): pl.pallas_call(kernel, name=name, out_shape=outs, in_specs=in_specs, out_...  38.6 us
    ppermute x14, starting transfers between devices, from_b(): return lax.ppermute(x, 'space', off_chip)  34.9 us
    ppermute x15, starting transfers between devices, later(): lax.ppermute(x, 'tm', [(i, (i + distance) % slices) for i in range(slices)])  14.8 us
  transfers between devices with their start and end apart: 43, of which 13 were waited for; matrix products, arithmetic and copies ran while one was open for 0% of the time, Pallas kernels for 9%

profile of v3, /device:TPU:17, one launch (start us, length us, event | category | flops | bytes accessed | tf_op | source)
XLA Modules:
  0.0 277.5 jit_solution(5836254977894794306)
XLA Ops:
  14.0 4.4 %collective-permute-done.1.rb.b1 = f32[10,64,128]{2,1,0:T(8,128)S(1)} collective-permute-done((f32[10,64,128]{2,1,0:T(8,128)S(1)}, f32[10,64,128]{2,1,0:T(8,128)S(1)}, u32[]{:S(2)}, u32[]{:S(2)}) %collective-permute-start.1) | collective-permute-done | bytes 327712 | tf_op jit(solution)/shard_map/ppermute | solution.py:388
  27.0 8.6 %collective-permute-done.5.rb.b2 = f32[12,64,128]{2,1,0:T(8,128)S(1)} collective-permute-done((f32[12,64,128]{2,1,0:T(8,128)S(1)}, f32[12,64,128]{2,1,0:T(8,128)S(1)}, u32[]{:S(2)}, u32[]{:S(2)}) %collective-permute-start.5) | collective-permute-done | bytes 393248 | tf_op jit(solution)/shard_map/ppermute | solution.py:388
  36.5 4.4 %collective-permute-done.2.vb = f32[3,4,64,128]{3,2,1,0:T(8,128)S(1)} collective-permute-done((f32[3,4,64,128]{3,2,1,0:T(8,128)S(1)}, f32[3,4,64,128]{3,2,1,0:T(8,128)S(1)}, u32[]{:S(2)}, u32[]{:S(2)}) %collective-permute-start.2) | collective-permute-done | bytes 393248 | tf_op jit(solution)/shard_map/ppermute | solution.py:391
  41.0 10.9 %collective-permute-done.7.va = f32[3,4,64,128]{3,2,1,0:T(8,128)S(1)} collective-permute-done((f32[3,4,64,128]{3,2,1,0:T(8,128)S(1)}, f32[3,4,64,128]{3,2,1,0:T(8,128)S(1)}, u32[]{:S(2)}, u32[]{:S(2)}) %collective-permute-start.7) | collective-permute-done | bytes 393248 | tf_op jit(solution)/shard_map/ppermute | solution.py:391
  54.8 11.4 %collective-permute-done.6.hb = f32[3,4,64,128]{3,2,1,0:T(8,128)S(1)} collective-permute-done((f32[3,4,64,128]{3,2,1,0:T(8,128)S(1)}, f32[3,4,64,128]{3,2,1,0:T(8,128)S(1)}, u32[]{:S(2)}, u32[]{:S(2)}) %collective-permute-start.6) | collective-permute-done | bytes 393248 | tf_op jit(solution)/shard_map/ppermute | solution.py:388
  66.2 5.1 %second.1 = (f32[3,16,64,128]{3,2,1,0:T(8,128)S(1)}, f32[3,4,64,128]{3,2,1,0:T(8,128)S(1)}, f32[3,4,64,128]{3,2,1,0:T(8,128)S(1)}, f32[3,4,64,128]{3,2,1,0:T(8,128)S(1)}) custom-call(s32[1]{0:T(128)} %bitcast.odd_ref, f32[3,4,64,128]{3,2,1,0:T(8,128)S(1)} %collective-permute-done.6.hb, f32[3,4,64,128]{3,2,1,0:T(8,128)S(1)} %collective-permute-done.2.vb, ...), custom_call_target="tpu_custom_call" | custom-call | bytes 4194304 | tf_op jit(solution)/shard_map/second/pallas_call | solution.py:47
  71.5 4.3 %collective-permute-start.13 = (f32[3,4,64,128]{3,2,1,0:T(8,128)S(1)}, f32[3,4,64,128]{3,2,1,0:T(8,128)S(1)}, u32[]{:S(2)}, u32[]{:S(2)}) collective-permute-start(f32[3,4,64,128]{3,2,1,0:T(8,128)S(1)} %get-tuple-element.82), channel_id=1, source_target_pairs={{0,16},{16,32},{32,48},{48,64},{64,80},{80,96},{96,112},{112,0},{1... | collective-permute-start | bytes 1179656 | tf_op jit(solution)/shard_map/ppermute | solution.py:391
  75.8 10.3 %collective-permute-done.9.vb = f32[3,4,64,128]{3,2,1,0:T(8,128)S(1)} collective-permute-done((f32[3,4,64,128]{3,2,1,0:T(8,128)S(1)}, f32[3,4,64,128]{3,2,1,0:T(8,128)S(1)}, u32[]{:S(2)}, u32[]{:S(2)}) %collective-permute-start.9) | collective-permute-done | bytes 393248 | tf_op jit(solution)/shard_map/ppermute | solution.py:391
  88.1 7.4 %collective-permute-done.11.va = f32[3,4,64,128]{3,2,1,0:T(8,128)S(1)} collective-permute-done((f32[3,4,64,128]{3,2,1,0:T(8,128)S(1)}, f32[3,4,64,128]{3,2,1,0:T(8,128)S(1)}, u32[]{:S(2)}, u32[]{:S(2)}) %collective-permute-start.11) | collective-permute-done | bytes 393248 | tf_op jit(solution)/shard_map/ppermute | solution.py:391
  95.4 10.3 %collective-permute-done.13.vm = f32[3,4,64,128]{3,2,1,0:T(8,128)S(1)} collective-permute-done((f32[3,4,64,128]{3,2,1,0:T(8,128)S(1)}, f32[3,4,64,128]{3,2,1,0:T(8,128)S(1)}, u32[]{:S(2)}, u32[]{:S(2)}) %collective-permute-start.13) | collective-permute-done | bytes 393248 | tf_op jit(solution)/shard_map/ppermute | solution.py:391
  105.8 7.0 %collective-permute-done.10.hb = f32[3,4,64,128]{3,2,1,0:T(8,128)S(1)} collective-permute-done((f32[3,4,64,128]{3,2,1,0:T(8,128)S(1)}, f32[3,4,64,128]{3,2,1,0:T(8,128)S(1)}, u32[]{:S(2)}, u32[]{:S(2)}) %collective-permute-start.10) | collective-permute-done | bytes 393248 | tf_op jit(solution)/shard_map/ppermute | solution.py:388
  112.8 5.0 %residual.1 = (f32[1,3,12,64,128]{4,3,2,1,0:T(8,128)}, f32[12,64,128]{2,1,0:T(8,128)S(1)}, f32[12,64,128]{2,1,0:T(8,128)S(1)}, f32[12,64,128]{2,1,0:T(8,128)S(1)...) custom-call(s32[1]{0:T(128)} %bitcast.odd_ref, ...), custom_call_target="tpu_custom_call" | custom-call | bytes 4194304 | tf_op jit(solution)/shard_map/residual/pallas_call | solution.py:47
  118.2 14.5 %collective-permute-done.14.refs_1_ = f32[12,64,128]{2,1,0:T(8,128)S(1)} collective-permute-done((f32[12,64,128]{2,1,0:T(8,128)S(1)}, f32[12,64,128]{2,1,0:T(8,128)S(1)}, u32[]{:S(2)}, u32[]{:S(2)}) %collective-permute-start.14) | collective-permute-done | bytes 393248 | tf_op jit(solution)/shard_map/ppermute | solution.py:391
  132.9 4.4 %collective-permute-start.16 = (f32[4,64,128]{2,1,0:T(8,128)S(1)}, f32[4,64,128]{2,1,0:T(8,128)S(1)}, u32[]{:S(2)}, u32[]{:S(2)}) collective-permute-start(f32[4,64,128]{2,1,0:T(8,128)S(1)} %get-tuple-element.90), channel_id=1, source_target_pairs={{1,2},{3,4},{5,6},{7,8},{9,10},{11,12},{13,14},{2,1},{4,3},{6,5},{... | collective-permute-start | bytes 393224 | tf_op jit(solution)/shard_map/ppermute | solution.py:388
  137.3 8.1 %collective-permute-done.16.hb = f32[4,64,128]{2,1,0:T(8,128)S(1)} collective-permute-done((f32[4,64,128]{2,1,0:T(8,128)S(1)}, f32[4,64,128]{2,1,0:T(8,128)S(1)}, u32[]{:S(2)}, u32[]{:S(2)}) %collective-permute-start.16) | collective-permute-done | bytes 131104 | tf_op jit(solution)/shard_map/ppermute | solution.py:388
  147.2 12.2 %collective-permute-start.24 = (f32[4,64,128]{2,1,0:T(8,128)S(1)}, f32[4,64,128]{2,1,0:T(8,128)S(1)}, u32[]{:S(2)}, u32[]{:S(2)}) collective-permute-start(f32[4,64,128]{2,1,0:T(8,128)S(1)} %get-tuple-element.102), channel_id=1, source_target_pairs={{0,1},{1,0},{2,3},{3,2},{4,5},{5,4},{6,7},{7,6},{8,9},{9,8},{10,11... | collective-permute-start | bytes 393224 | tf_op jit(solution)/shard_map/ppermute | solution.py:385
  161.4 19.2 %collective-permute-start.31 = (f32[4,64,128]{2,1,0:T(8,128)S(1)}, f32[4,64,128]{2,1,0:T(8,128)S(1)}, u32[]{:S(2)}, u32[]{:S(2)}) collective-permute-start(f32[4,64,128]{2,1,0:T(8,128)S(1)} %get-tuple-element.111), channel_id=1, source_target_pairs={{0,1},{1,0},{2,3},{3,2},{4,5},{5,4},{6,7},{7,6},{8,9},{9,8},{10,11... | collective-permute-start | bytes 393224 | tf_op jit(solution)/shard_map/ppermute | solution.py:385
  185.2 17.2 %collective-permute-done.32.hb = f32[4,64,128]{2,1,0:T(8,128)S(1)} collective-permute-done((f32[4,64,128]{2,1,0:T(8,128)S(1)}, f32[4,64,128]{2,1,0:T(8,128)S(1)}, u32[]{:S(2)}, u32[]{:S(2)}) %collective-permute-start.32) | collective-permute-done | bytes 131104 | tf_op jit(solution)/shard_map/ppermute | solution.py:388
  210.4 6.4 %collective-permute-start.27 = (f32[8,64,128]{2,1,0:T(8,128)S(1)}, f32[8,64,128]{2,1,0:T(8,128)S(1)}, u32[]{:S(2)}, u32[]{:S(2)}) collective-permute-start(f32[8,64,128]{2,1,0:T(8,128)S(1)} %get-tuple-element.105), channel_id=1, source_target_pairs={{0,1},{1,0},{2,3},{3,2},{4,5},{5,4},{6,7},{7,6},{8,9},{9,8},{10,11... | collective-permute-start | bytes 786440 | tf_op jit(solution)/shard_map/ppermute | solution.py:385
  218.8 8.2 %collective-permute-start.34 = (f32[8,64,128]{2,1,0:T(8,128)S(1)}, f32[8,64,128]{2,1,0:T(8,128)S(1)}, u32[]{:S(2)}, u32[]{:S(2)}) collective-permute-start(f32[8,64,128]{2,1,0:T(8,128)S(1)} %get-tuple-element.114), channel_id=1, source_target_pairs={{0,1},{1,0},{2,3},{3,2},{4,5},{5,4},{6,7},{7,6},{8,9},{9,8},{10,11... | collective-permute-start | bytes 786440 | tf_op jit(solution)/shard_map/ppermute | solution.py:385
  229.7 4.2 %power8.3 = f32[12,64,128]{2,1,0:T(8,128)S(1)} custom-call(s32[1]{0:T(128)} %bitcast.odd_ref, f32[12,64,128]{2,1,0:T(8,128)S(1)} %get-tuple-element.91.value.refs_0_, f32[8,64,128]{2,1,0:T(8,128)S(1)} %collective-permute-done.18.ha, f32[8,64,128]{2,1,0:T(8,128)S(1)} %collective-permute-done.19.hb, f32[26,64,128]{2,1,0:T(8,128)S(1)} %get-tuple-element.96.keep, ...), custom_call_target="tpu_custom_call" | custom-call | bytes 4194304 | tf_op jit(solution)/shard_map/power8/pallas_call | solution.py:47
  247.3 7.4 %collective-permute-start.37 = (f32[2,64,128]{2,1,0:T(8,128)S(1)}, f32[2,64,128]{2,1,0:T(8,128)S(1)}, u32[]{:S(2)}, u32[]{:S(2)}) collective-permute-start(f32[2,64,128]{2,1,0:T(8,128)S(1)} %get-tuple-element.117), channel_id=1, source_target_pairs={{0,1},{1,0},{2,3},{3,2},{4,5},{5,4},{6,7},{7,6},{8,9},{9,8},{10,11... | collective-permute-start | bytes 196616 | tf_op jit(solution)/shard_map/ppermute | solution.py:385
  256.8 4.6 %collective-permute-start.38 = (f32[2,64,128]{2,1,0:T(8,128)S(1)}, f32[2,64,128]{2,1,0:T(8,128)S(1)}, u32[]{:S(2)}, u32[]{:S(2)}) collective-permute-start(f32[2,64,128]{2,1,0:T(8,128)S(1)} %get-tuple-element.118), channel_id=1, source_target_pairs={{0,1},{1,0},{2,3},{3,2},{4,5},{5,4},{6,7},{7,6},{8,9},{9,8},{10,11... | collective-permute-start | bytes 196616 | tf_op jit(solution)/shard_map/ppermute | solution.py:385
  263.3 5.5 %collective-permute-start.39 = (f32[2,64,128]{2,1,0:T(8,128)S(1)}, f32[2,64,128]{2,1,0:T(8,128)S(1)}, u32[]{:S(2)}, u32[]{:S(2)}) collective-permute-start(f32[2,64,128]{2,1,0:T(8,128)S(1)} %get-tuple-element.119), channel_id=1, source_target_pairs={{0,1},{1,0},{2,3},{3,2},{4,5},{5,4},{6,7},{7,6},{8,9},{9,8},{10,11... | collective-permute-start | bytes 196616 | tf_op jit(solution)/shard_map/ppermute | solution.py:385
  (101 shorter events, 75.1 us)
Async XLA Ops:
  11.7 24.8 %collective-permute-start.3 = (f32[3,4,64,128]{3,2,1,0:T(8,128)S(1)}, f32[3,4,64,128]{3,2,1,0:T(8,128)S(1)}, u32[]{:S(2)}, u32[]{:S(2)}) collective-permute-start(f32[3,4,64,128]{3,2,1,0:T(8,128)S(1)} %first_middle.1.after), channel_id=1, source_target_pairs={{0,16},{16,32},{32,48},{48,64},{64,80},{80,96},{96,112},{112,0},{1... | collective-permute-start | bytes 1179656 | tf_op jit(solution)/shard_map/ppermute | solution.py:391
  18.4 17.1 %collective-permute-start.5 = (f32[12,64,128]{2,1,0:T(8,128)S(1)}, f32[12,64,128]{2,1,0:T(8,128)S(1)}, u32[]{:S(2)}, u32[]{:S(2)}) collective-permute-start(f32[12,64,128]{2,1,0:T(8,128)S(1)} %get-tuple-element.70), channel_id=1, source_target_pairs={{1,2},{3,4},{5,6},{7,8},{9,10},{11,12},{13,14},{2,1},{4,3},{6,5},{... | collective-permute-start | bytes 1179656 | tf_op jit(solution)/shard_map/ppermute | solution.py:388
  24.5 16.5 %collective-permute-start.2 = (f32[3,4,64,128]{3,2,1,0:T(8,128)S(1)}, f32[3,4,64,128]{3,2,1,0:T(8,128)S(1)}, u32[]{:S(2)}, u32[]{:S(2)}) collective-permute-start(f32[3,4,64,128]{3,2,1,0:T(8,128)S(1)} %get-tuple-element.68), channel_id=1, source_target_pairs={{0,16},{16,32},{32,48},{48,64},{64,80},{80,96},{96,112},{112,0},{1... | collective-permute-start | bytes 1179656 | tf_op jit(solution)/shard_map/ppermute | solution.py:391
  25.8 26.1 %collective-permute-start.7 = (f32[3,4,64,128]{3,2,1,0:T(8,128)S(1)}, f32[3,4,64,128]{3,2,1,0:T(8,128)S(1)}, u32[]{:S(2)}, u32[]{:S(2)}) collective-permute-start(f32[3,4,64,128]{3,2,1,0:T(8,128)S(1)} %get-tuple-element.76), channel_id=1, source_target_pairs={{0,16},{16,32},{32,48},{48,64},{64,80},{80,96},{96,112},{112,0},{1... | collective-permute-start | bytes 1179656 | tf_op jit(solution)/shard_map/ppermute | solution.py:391
  71.4 24.0 %collective-permute-start.11 = (f32[3,4,64,128]{3,2,1,0:T(8,128)S(1)}, f32[3,4,64,128]{3,2,1,0:T(8,128)S(1)}, u32[]{:S(2)}, u32[]{:S(2)}) collective-permute-start(f32[3,4,64,128]{3,2,1,0:T(8,128)S(1)} %get-tuple-element.81), channel_id=1, source_target_pairs={{0,16},{16,32},{32,48},{48,64},{64,80},{80,96},{96,112},{112,0},{1... | collective-permute-start | bytes 1179656 | tf_op jit(solution)/shard_map/ppermute | solution.py:391
  71.5 34.3 %collective-permute-start.13 = (f32[3,4,64,128]{3,2,1,0:T(8,128)S(1)}, f32[3,4,64,128]{3,2,1,0:T(8,128)S(1)}, u32[]{:S(2)}, u32[]{:S(2)}) collective-permute-start(f32[3,4,64,128]{3,2,1,0:T(8,128)S(1)} %get-tuple-element.82), channel_id=1, source_target_pairs={{0,16},{16,32},{32,48},{48,64},{64,80},{80,96},{96,112},{112,0},{1... | collective-permute-start | bytes 1179656 | tf_op jit(solution)/shard_map/ppermute | solution.py:391
  86.1 26.6 %collective-permute-start.10 = (f32[3,4,64,128]{3,2,1,0:T(8,128)S(1)}, f32[3,4,64,128]{3,2,1,0:T(8,128)S(1)}, u32[]{:S(2)}, u32[]{:S(2)}) collective-permute-start(f32[3,4,64,128]{3,2,1,0:T(8,128)S(1)} %collective-permute-done.9.vb), channel_id=1, source_target_pairs={{1,2},{3,4},{5,6},{7,8},{9,10},{11,12},{13,14},{2,1},{4,3},{6,5},{... | collective-permute-start | bytes 1179656 | tf_op jit(solution)/shard_map/ppermute | solution.py:388
  95.4 17.4 %collective-permute-start.12 = (f32[3,4,64,128]{3,2,1,0:T(8,128)S(1)}, f32[3,4,64,128]{3,2,1,0:T(8,128)S(1)}, u32[]{:S(2)}, u32[]{:S(2)}) collective-permute-start(f32[3,4,64,128]{3,2,1,0:T(8,128)S(1)} %collective-permute-done.11.va), channel_id=1, source_target_pairs={{0,1},{1,0},{2,3},{3,2},{4,5},{5,4},{6,7},{7,6},{8,9},{9,8},{10,11... | collective-permute-start | bytes 1179656 | tf_op jit(solution)/shard_map/ppermute | solution.py:385
  117.9 29.2 %collective-permute-start.23 = (f32[12,64,128]{2,1,0:T(8,128)S(1)}, f32[12,64,128]{2,1,0:T(8,128)S(1)}, u32[]{:S(2)}, u32[]{:S(2)}) collective-permute-start(f32[12,64,128]{2,1,0:T(8,128)S(1)} %get-tuple-element.100), channel_id=1, source_target_pairs={{0,16},{16,32},{32,48},{48,64},{64,80},{80,96},{96,112},{112,0},{1... | collective-permute-start | bytes 1179656 | tf_op jit(solution)/shard_map/ppermute | solution.py:391
  118.2 43.1 %collective-permute-start.30 = (f32[12,64,128]{2,1,0:T(8,128)S(1)}, f32[12,64,128]{2,1,0:T(8,128)S(1)}, u32[]{:S(2)}, u32[]{:S(2)}) collective-permute-start(f32[12,64,128]{2,1,0:T(8,128)S(1)} %get-tuple-element.109), channel_id=1, source_target_pairs={{0,16},{16,32},{32,48},{48,64},{64,80},{80,96},{96,112},{112,0},{1... | collective-permute-start | bytes 1179656 | tf_op jit(solution)/shard_map/ppermute | solution.py:391
  147.0 57.0 %collective-permute-start.17 = (f32[12,64,128]{2,1,0:T(8,128)S(1)}, f32[12,64,128]{2,1,0:T(8,128)S(1)}, u32[]{:S(2)}, u32[]{:S(2)}) collective-permute-start(f32[12,64,128]{2,1,0:T(8,128)S(1)} %power4.3), channel_id=1, source_target_pairs={{0,32},{16,48},{32,64},{48,80},{64,96},{80,112},{96,0},{112,16},{1... | collective-permute-start | bytes 1179656 | tf_op jit(solution)/shard_map/ppermute | solution.py:391
  147.2 35.4 %collective-permute-start.24 = (f32[4,64,128]{2,1,0:T(8,128)S(1)}, f32[4,64,128]{2,1,0:T(8,128)S(1)}, u32[]{:S(2)}, u32[]{:S(2)}) collective-permute-start(f32[4,64,128]{2,1,0:T(8,128)S(1)} %get-tuple-element.102), channel_id=1, source_target_pairs={{0,1},{1,0},{2,3},{3,2},{4,5},{5,4},{6,7},{7,6},{8,9},{9,8},{10,11... | collective-permute-start | bytes 393224 | tf_op jit(solution)/shard_map/ppermute | solution.py:385
  159.4 23.2 %collective-permute-start.25 = (f32[4,64,128]{2,1,0:T(8,128)S(1)}, f32[4,64,128]{2,1,0:T(8,128)S(1)}, u32[]{:S(2)}, u32[]{:S(2)}) collective-permute-start(f32[4,64,128]{2,1,0:T(8,128)S(1)} %get-tuple-element.103), channel_id=1, source_target_pairs={{1,2},{3,4},{5,6},{7,8},{9,10},{11,12},{13,14},{2,1},{4,3},{6,5},{... | collective-permute-start | bytes 393224 | tf_op jit(solution)/shard_map/ppermute | solution.py:388
  161.4 23.8 %collective-permute-start.31 = (f32[4,64,128]{2,1,0:T(8,128)S(1)}, f32[4,64,128]{2,1,0:T(8,128)S(1)}, u32[]{:S(2)}, u32[]{:S(2)}) collective-permute-start(f32[4,64,128]{2,1,0:T(8,128)S(1)} %get-tuple-element.111), channel_id=1, source_target_pairs={{0,1},{1,0},{2,3},{3,2},{4,5},{5,4},{6,7},{7,6},{8,9},{9,8},{10,11... | collective-permute-start | bytes 393224 | tf_op jit(solution)/shard_map/ppermute | solution.py:385
  180.6 21.7 %collective-permute-start.32 = (f32[4,64,128]{2,1,0:T(8,128)S(1)}, f32[4,64,128]{2,1,0:T(8,128)S(1)}, u32[]{:S(2)}, u32[]{:S(2)}) collective-permute-start(f32[4,64,128]{2,1,0:T(8,128)S(1)} %get-tuple-element.112), channel_id=1, source_target_pairs={{1,2},{3,4},{5,6},{7,8},{9,10},{11,12},{13,14},{2,1},{4,3},{6,5},{... | collective-permute-start | bytes 393224 | tf_op jit(solution)/shard_map/ppermute | solution.py:388
  184.1 22.5 %collective-permute-start.26 = (f32[12,64,128]{2,1,0:T(8,128)S(1)}, f32[12,64,128]{2,1,0:T(8,128)S(1)}, u32[]{:S(2)}, u32[]{:S(2)}) collective-permute-start(f32[12,64,128]{2,1,0:T(8,128)S(1)} %power4.4), channel_id=1, source_target_pairs={{0,32},{16,48},{32,64},{48,80},{64,96},{80,112},{96,0},{112,16},{1... | collective-permute-start | bytes 1179656 | tf_op jit(solution)/shard_map/ppermute | solution.py:391
  204.1 22.9 %collective-permute-start.18 = (f32[8,64,128]{2,1,0:T(8,128)S(1)}, f32[8,64,128]{2,1,0:T(8,128)S(1)}, u32[]{:S(2)}, u32[]{:S(2)}) collective-permute-start(f32[8,64,128]{2,1,0:T(8,128)S(1)} %get-tuple-element.92), channel_id=1, source_target_pairs={{0,1},{1,0},{2,3},{3,2},{4,5},{5,4},{6,7},{7,6},{8,9},{9,8},{10,11... | collective-permute-start | bytes 786440 | tf_op jit(solution)/shard_map/ppermute | solution.py:385
  206.6 23.1 %collective-permute-start.19 = (f32[8,64,128]{2,1,0:T(8,128)S(1)}, f32[8,64,128]{2,1,0:T(8,128)S(1)}, u32[]{:S(2)}, u32[]{:S(2)}) collective-permute-start(f32[8,64,128]{2,1,0:T(8,128)S(1)} %get-tuple-element.93), channel_id=1, source_target_pairs={{1,2},{3,4},{5,6},{7,8},{9,10},{11,12},{13,14},{2,1},{4,3},{6,5},{... | collective-permute-start | bytes 786440 | tf_op jit(solution)/shard_map/ppermute | solution.py:388
  210.4 24.9 %collective-permute-start.27 = (f32[8,64,128]{2,1,0:T(8,128)S(1)}, f32[8,64,128]{2,1,0:T(8,128)S(1)}, u32[]{:S(2)}, u32[]{:S(2)}) collective-permute-start(f32[8,64,128]{2,1,0:T(8,128)S(1)} %get-tuple-element.105), channel_id=1, source_target_pairs={{0,1},{1,0},{2,3},{3,2},{4,5},{5,4},{6,7},{7,6},{8,9},{9,8},{10,11... | collective-permute-start | bytes 786440 | tf_op jit(solution)/shard_map/ppermute | solution.py:385
  216.8 18.5 %collective-permute-start.28 = (f32[8,64,128]{2,1,0:T(8,128)S(1)}, f32[8,64,128]{2,1,0:T(8,128)S(1)}, u32[]{:S(2)}, u32[]{:S(2)}) collective-permute-start(f32[8,64,128]{2,1,0:T(8,128)S(1)} %get-tuple-element.106), channel_id=1, source_target_pairs={{1,2},{3,4},{5,6},{7,8},{9,10},{11,12},{13,14},{2,1},{4,3},{6,5},{... | collective-permute-start | bytes 786440 | tf_op jit(solution)/shard_map/ppermute | solution.py:388
  218.8 22.6 %collective-permute-start.34 = (f32[8,64,128]{2,1,0:T(8,128)S(1)}, f32[8,64,128]{2,1,0:T(8,128)S(1)}, u32[]{:S(2)}, u32[]{:S(2)}) collective-permute-start(f32[8,64,128]{2,1,0:T(8,128)S(1)} %get-tuple-element.114), channel_id=1, source_target_pairs={{0,1},{1,0},{2,3},{3,2},{4,5},{5,4},{6,7},{7,6},{8,9},{9,8},{10,11... | collective-permute-start | bytes 786440 | tf_op jit(solution)/shard_map/ppermute | solution.py:385
  239.4 17.3 %collective-permute-start.29 = (f32[12,64,128]{2,1,0:T(8,128)S(1)}, f32[12,64,128]{2,1,0:T(8,128)S(1)}, u32[]{:S(2)}, u32[]{:S(2)}) collective-permute-start(f32[12,64,128]{2,1,0:T(8,128)S(1)} %power8.4), channel_id=1, source_target_pairs={{0,64},{16,80},{32,96},{48,112},{64,0},{80,16},{96,32},{112,48},{1... | collective-permute-start | bytes 1179656 | tf_op jit(solution)/shard_map/ppermute | solution.py:391
  245.5 17.7 %collective-permute-start.36 = (f32[12,64,128]{2,1,0:T(8,128)S(1)}, f32[12,64,128]{2,1,0:T(8,128)S(1)}, u32[]{:S(2)}, u32[]{:S(2)}) collective-permute-start(f32[12,64,128]{2,1,0:T(8,128)S(1)} %power8.5), channel_id=1, source_target_pairs={{0,64},{16,80},{32,96},{48,112},{64,0},{80,16},{96,32},{112,48},{1... | collective-permute-start | bytes 1179656 | tf_op jit(solution)/shard_map/ppermute | solution.py:391
  247.3 21.5 %collective-permute-start.37 = (f32[2,64,128]{2,1,0:T(8,128)S(1)}, f32[2,64,128]{2,1,0:T(8,128)S(1)}, u32[]{:S(2)}, u32[]{:S(2)}) collective-permute-start(f32[2,64,128]{2,1,0:T(8,128)S(1)} %get-tuple-element.117), channel_id=1, source_target_pairs={{0,1},{1,0},{2,3},{3,2},{4,5},{5,4},{6,7},{7,6},{8,9},{9,8},{10,11... | collective-permute-start | bytes 196616 | tf_op jit(solution)/shard_map/ppermute | solution.py:385
  (26 other events, 234.5 us)

commit v4 on v3

--- a/solution.py
+++ b/solution.py
@@ -387,8 +387,23 @@
     def from_b(x):
         return lax.ppermute(x, "space", off_chip)
 
-    def later(x, distance):
-        return lax.ppermute(x, "tm", [(i, (i + distance) % slices) for i in range(slices)])
+    half = slices // 2
+    column = lax.axis_index("tm") % half
+
+    def later(x, distance, route="direct"):
+        def send(value, pairs):
+            return lax.ppermute(value, "tm", pairs)
+
+        if route == "direct" or distance == half:
+            return send(x, [(i, (i + distance) % slices) for i in range(slices)])
+        wrapping = [i for i in range(slices) if i % half + distance >= half]
+        if route == "first":
+            stops = [(i + half) % slices for i in wrapping]
+        else:
+            stops = [(i - 1 + half) % slices for i in wrapping]
+        around = send(send(x, list(zip(wrapping, stops))), [(j, (i + distance) % slices) for i, j in zip(wrapping, stops)])
+        plain = send(x, [(i, i + distance) for i in range(slices) if i not in wrapping])
+        return jnp.where(column < distance, around, plain)
 
     tables = (conductance, reluct)
     sa1, sb1 = call(
@@ -405,7 +420,7 @@
         second_pack_kernel, "second_pack", (odd, source, regions),
         [planes(12), planes(12), planes(4), planes(4)], [pltpu.VMEM((LX, NY, NZ), jnp.int32)], 8, in_place=HBM,
     )
-    vm = later(um, 1)
+    vm = later(um, 1, "first")
     sb2, sa2, b1 = fence((sb2, sa2, b1))
     b2 = from_b(sb2)
     a2 = from_a(sa2)
@@ -414,11 +429,11 @@
         [planes(3, 4), planes(3, 4)], [vmem(3, LX + 4)] * 4 + [vmem(LX + 4)] * 2,
     )
     vb = later(ub, 1)
-    va = later(ua, 1)
+    va = later(ua, 1, "middle")
     cond, nu, keep, spread = call(
         material_kernel, "material", (odd, *tables, regions, a2, b2), [planes(LX + 6)] * 4, [],
     )
-    vb, vm, cond = fence((vb, vm, cond))
+    va, cond = fence((va, cond))
     hb = from_b(vb)
     ha = from_a(va)
     sb3, sa3, vb = fence((sb3, sa3, vb))
@@ -431,8 +446,8 @@
         [planes(3, LX + 4), planes(3, 4), planes(3, 4), planes(3, 4)], [vmem(3, n)] * 5,
     )
     vb = later(ub, 1)
-    va = later(ua, 1)
-    vm = later(um, 1)
+    va = later(ua, 1, "middle")
+    vm = later(um, 1, "first")
     hb = from_b(vb)
     ha = from_a(va)
     wide_keep, wide_spread = call(
@@ -445,8 +460,12 @@
     )
     moving, totals = rest[:3], rest[3:]
     u0_own = [u0[c, 2:2 + LX] for c in range(3)]
-    for distance, width in ((1, 4), (2, 8), (4, 2)):
-        moved = [later(m, distance) for m in moving]
+    for distance, width, routes in (
+        (1, 4, ("direct", "first", "middle")),
+        (2, 8, ("first", "direct", "first")),
+        (4, 2, ("direct",) * 3),
+    ):
+        moved = [later(m, distance, r) for m, r in zip(moving, routes)]
         bases = [(t,) for t in totals]
         if distance == 4:
             bases = [(t, u) for t, u in zip(totals, u0_own)]

time: 281 us -> 271 us (0.964)
  waiting for transfers between devices: 118 us -> 97.9 us
  local copies, waits for them, and re-layouts: 4.45 us -> 13.8 us
  starting transfers between devices: 115 us -> 106 us
  Pallas kernels: 38.6 us -> 46 us
  other arithmetic: 0 us -> 3.46 us
    ppermute x14, starting transfers between devices: 65.3 us -> 9.42 us  [from_a(): return lax.ppermute(x, 'space', on_chip)]
    ppermute x15 -> x31, starting transfers between devices: 14.8 us -> 58 us  [send(): return lax.ppermute(value, 'tm', pairs)]
    ppermute x14, waiting for transfers between devices: 60.2 us -> 22.7 us  [from_b(): return lax.ppermute(x, 'space', off_chip)]
    ppermute x15 -> x31, waiting for transfers between devices: 57.9 us -> 74.2 us  [send(): return lax.ppermute(value, 'tm', pairs)]
    unnamed x14 -> x64, local copies, waits for them, and re-layouts: 4.33 us -> 13.7 us
    pallas_call x24, Pallas kernels: 38.6 us -> 46 us  [call(): pl.pallas_call(kernel, name=name, out_shape=outs, in_specs=in_specs, out_...]
    select_n x0 -> x7, other arithmetic: none -> 3.46 us  [later(): return jnp.where(column < distance, around, plain)]
    ppermute x14, starting transfers between devices: 34.9 us -> 38.2 us  [from_b(): return lax.ppermute(x, 'space', off_chip)]
  transfers between devices with their start and end apart: 43 -> 59, of which waited for: 13 -> 20; matrix products, arithmetic and copies ran while one was open for 0% -> 1% of each run, Pallas kernels for 9% -> 11%
where the time goes in v4:
time: 271 us; the launch traced here: 269 us
  starting transfers between devices  106 us (39%)
  waiting for transfers between devices  97.9 us (36%)
  Pallas kernels  46 us (17%)
  local copies, waits for them, and re-layouts  13.8 us (5%)
  other arithmetic  3.46 us (1%)
    ppermute x31, waiting for transfers between devices, send(): return lax.ppermute(value, 'tm', pairs)  74.2 us
    ppermute x31, starting transfers between devices, send(): return lax.ppermute(value, 'tm', pairs)  58 us
    pallas_call x24, Pallas kernels, call(): pl.pallas_call(kernel, name=name, out_shape=outs, in_specs=in_specs, out_...  46 us
    ppermute x14, starting transfers between devices, from_b(): return lax.ppermute(x, 'space', off_chip)  38.2 us
    ppermute x14, waiting for transfers between devices, from_b(): return lax.ppermute(x, 'space', off_chip)  22.7 us
    unnamed x64, local copies, waits for them, and re-layouts  13.7 us
    ppermute x14, starting transfers between devices, from_a(): return lax.ppermute(x, 'space', on_chip)  9.42 us
  transfers between devices with their start and end apart: 59, of which 20 were waited for; matrix products, arithmetic and copies ran while one was open for 1% of the time, Pallas kernels for 11%

profile of v4, /device:TPU:17, one launch (start us, length us, event | category | flops | bytes accessed | tf_op | source)
XLA Modules:
  0.0 268.6 jit_solution(14951204337138983897)
XLA Ops:
  6.0 4.1 %collective-permute-start.1 = (f32[10,64,128]{2,1,0:T(8,128)S(1)}, f32[10,64,128]{2,1,0:T(8,128)S(1)}, u32[]{:S(2)}, u32[]{:S(2)}) collective-permute-start(f32[10,64,128]{2,1,0:T(8,128)S(1)} %get-tuple-element.65), channel_id=1, source_target_pairs={{1,2},{3,4},{5,6},{7,8},{9,10},{11,12},{13,14},{2,1},{4,3},{6,5},{... | collective-permute-start | bytes 983048 | tf_op jit(solution)/shard_map/ppermute | solution.py:388
  18.4 4.0 %first.1 = (f32[3,4,64,128]{3,2,1,0:T(8,128)}, f32[3,4,64,128]{3,2,1,0:T(8,128)}) custom-call(s32[1]{0:T(128)} %bitcast.odd_ref, f32[4]{0:T(128)S(1)} %copy-done.28, f32[4]{0:T(128)S(1)} %copy-done.29, f32[2,3,12,64,128]{4,3,2,1,0:T(8,128)S(1)} %copy-done.2, f32[2,3,12,64,128]{4,3,2,1,0:T(8,128)S(1)} %copy-done.1, s32[12,64,128]{2,1,0:T(8,128)S(1)} %copy-done.4, ...), custom_call_target="tpu_custom_call" | custom-call | bytes 4194304 | tf_op jit(solution)/shard_map/first/pallas_call | solution.py:47
  25.0 3.9 %collective-permute-start.8 = (f32[12,64,128]{2,1,0:T(8,128)S(1)}, f32[12,64,128]{2,1,0:T(8,128)S(1)}, u32[]{:S(2)}, u32[]{:S(2)}) collective-permute-start(f32[12,64,128]{2,1,0:T(8,128)S(1)} %get-tuple-element.73), channel_id=1, source_target_pairs={{1,2},{3,4},{5,6},{7,8},{9,10},{11,12},{13,14},{2,1},{4,3},{6,5},{... | collective-permute-start | bytes 1179656 | tf_op jit(solution)/shard_map/ppermute | solution.py:388
  34.1 9.1 %collective-permute-done.2.vb = f32[3,4,64,128]{3,2,1,0:T(8,128)} collective-permute-done((f32[3,4,64,128]{3,2,1,0:T(8,128)}, f32[3,4,64,128]{3,2,1,0:T(8,128)}, u32[]{:S(2)}, u32[]{:S(2)}) %collective-permute-start.2) | collective-permute-done | bytes 393248 | tf_op jit(solution)/shard_map/ppermute | solution.py:395
  60.3 5.2 %collective-permute-done.11 = f32[3,4,64,128]{3,2,1,0:T(8,128)S(1)} collective-permute-done((f32[3,4,64,128]{3,2,1,0:T(8,128)}, f32[3,4,64,128]{3,2,1,0:T(8,128)S(1)}, u32[]{:S(2)}, u32[]{:S(2)}) %collective-permute-start.11) | collective-permute-done | bytes 393248 | tf_op jit(solution)/shard_map/ppermute | solution.py:395
  65.7 6.5 %second.1 = (f32[3,16,64,128]{3,2,1,0:T(8,128)S(1)}, f32[3,4,64,128]{3,2,1,0:T(8,128)S(1)}, f32[3,4,64,128]{3,2,1,0:T(8,128)S(1)}, f32[3,4,64,128]{3,2,1,0:T(8,128)S(1)}) custom-call(s32[1]{0:T(128)} %bitcast.odd_ref, f32[3,4,64,128]{3,2,1,0:T(8,128)S(1)} %collective-permute-done.3.hb, f32[3,4,64,128]{3,2,1,0:T(8,128)} %collective-permute-done.2.vb, ...), custom_call_target="tpu_custom_call" | custom-call | bytes 4194304 | tf_op jit(solution)/shard_map/second/pallas_call | solution.py:47
  81.5 5.7 %collective-permute-done.13.vb = f32[3,4,64,128]{3,2,1,0:T(8,128)S(1)} collective-permute-done((f32[3,4,64,128]{3,2,1,0:T(8,128)S(1)}, f32[3,4,64,128]{3,2,1,0:T(8,128)S(1)}, u32[]{:S(2)}, u32[]{:S(2)}) %collective-permute-start.13) | collective-permute-done | bytes 393248 | tf_op jit(solution)/shard_map/ppermute | solution.py:395
  90.4 11.9 %collective-permute-done.16 = f32[3,4,64,128]{3,2,1,0:T(8,128)S(1)} collective-permute-done((f32[3,4,64,128]{3,2,1,0:T(8,128)S(1)}, f32[3,4,64,128]{3,2,1,0:T(8,128)S(1)}, u32[]{:S(2)}, u32[]{:S(2)}) %collective-permute-start.16) | collective-permute-done | bytes 393248 | tf_op jit(solution)/shard_map/ppermute | solution.py:395
  104.5 6.3 %collective-permute-done.20 = f32[3,4,64,128]{3,2,1,0:T(8,128)S(1)} collective-permute-done((f32[3,4,64,128]{3,2,1,0:T(8,128)S(1)}, f32[3,4,64,128]{3,2,1,0:T(8,128)S(1)}, u32[]{:S(2)}, u32[]{:S(2)}) %collective-permute-start.20) | collective-permute-done | bytes 393248 | tf_op jit(solution)/shard_map/ppermute | solution.py:395
  110.9 5.2 %residual.1 = (f32[1,3,12,64,128]{4,3,2,1,0:T(8,128)}, f32[12,64,128]{2,1,0:T(8,128)S(1)}, f32[12,64,128]{2,1,0:T(8,128)S(1)}, f32[12,64,128]{2,1,0:T(8,128)S(1)...) custom-call(s32[1]{0:T(128)} %bitcast.odd_ref, ...), custom_call_target="tpu_custom_call" | custom-call | bytes 4194304 | tf_op jit(solution)/shard_map/residual/pallas_call | solution.py:47
  119.1 8.1 %collective-permute-start.44 = (f32[12,64,128]{2,1,0:T(8,128)S(1)}, f32[12,64,128]{2,1,0:T(8,128)S(1)}, u32[]{:S(2)}, u32[]{:S(2)}) collective-permute-start(f32[12,64,128]{2,1,0:T(8,128)S(1)} %get-tuple-element.107), channel_id=1, source_target_pairs={{0,16},{16,32},{32,48},{64,80},{80,96},{96,112},{1,17},{17,33},{33... | collective-permute-start | bytes 1179656 | tf_op jit(solution)/shard_map/ppermute | solution.py:395
  135.9 5.7 %collective-permute-done.24.hb = f32[4,64,128]{2,1,0:T(8,128)S(1)} collective-permute-done((f32[4,64,128]{2,1,0:T(8,128)S(1)}, f32[4,64,128]{2,1,0:T(8,128)S(1)}, u32[]{:S(2)}, u32[]{:S(2)}) %collective-permute-start.24) | collective-permute-done | bytes 131104 | tf_op jit(solution)/shard_map/ppermute | solution.py:388
  145.4 11.2 %collective-permute-done.43 = f32[12,64,128]{2,1,0:T(8,128)S(1)} collective-permute-done((f32[12,64,128]{2,1,0:T(8,128)S(1)}, f32[12,64,128]{2,1,0:T(8,128)S(1)}, u32[]{:S(2)}, u32[]{:S(2)}) %collective-permute-start.43) | collective-permute-done | bytes 393248 | tf_op jit(solution)/shard_map/ppermute | solution.py:395
  161.3 5.8 %collective-permute-done.46.hb = f32[4,64,128]{2,1,0:T(8,128)S(1)} collective-permute-done((f32[4,64,128]{2,1,0:T(8,128)S(1)}, f32[4,64,128]{2,1,0:T(8,128)S(1)}, u32[]{:S(2)}, u32[]{:S(2)}) %collective-permute-start.46) | collective-permute-done | bytes 131104 | tf_op jit(solution)/shard_map/ppermute | solution.py:388
  177.9 6.0 %collective-permute-done.37.hb = f32[4,64,128]{2,1,0:T(8,128)S(1)} collective-permute-done((f32[4,64,128]{2,1,0:T(8,128)S(1)}, f32[4,64,128]{2,1,0:T(8,128)S(1)}, u32[]{:S(2)}, u32[]{:S(2)}) %collective-permute-start.37) | collective-permute-done | bytes 131104 | tf_op jit(solution)/shard_map/ppermute | solution.py:388
  186.9 4.2 %collective-permute-start.38 = (f32[12,64,128]{2,1,0:T(8,128)}, f32[12,64,128]{2,1,0:T(8,128)}, u32[]{:S(2)}, u32[]{:S(2)}) collective-permute-start(f32[12,64,128]{2,1,0:T(8,128)} %power4.4), channel_id=1, source_target_pairs={{0,32},{16,48},{32,64},{48,80},{64,96},{80,112},{96,0},{112,16},{1... | collective-permute-start | bytes 1179656 | tf_op jit(solution)/shard_map/ppermute | solution.py:395
  191.1 3.9 %collective-permute-start.49 = (f32[12,64,128]{2,1,0:T(8,128)}, f32[12,64,128]{2,1,0:T(8,128)}, u32[]{:S(2)}, u32[]{:S(2)}) collective-permute-start(f32[12,64,128]{2,1,0:T(8,128)} %power4.5), channel_id=1, source_target_pairs={{0,32},{16,48},{64,96},{80,112},{1,33},{17,49},{65,97},{81,113},{2... | collective-permute-start | bytes 1179656 | tf_op jit(solution)/shard_map/ppermute | solution.py:395
  199.1 4.2 %collective-permute-done.38.refs_1_ = f32[12,64,128]{2,1,0:T(8,128)} collective-permute-done((f32[12,64,128]{2,1,0:T(8,128)}, f32[12,64,128]{2,1,0:T(8,128)}, u32[]{:S(2)}, u32[]{:S(2)}) %collective-permute-start.38) | collective-permute-done | bytes 393248 | tf_op jit(solution)/shard_map/ppermute | solution.py:395
  213.3 4.1 %collective-permute-start.40 = (f32[8,64,128]{2,1,0:T(8,128)S(1)}, f32[8,64,128]{2,1,0:T(8,128)S(1)}, u32[]{:S(2)}, u32[]{:S(2)}) collective-permute-start(f32[8,64,128]{2,1,0:T(8,128)S(1)} %get-tuple-element.104), channel_id=1, source_target_pairs={{1,2},{3,4},{5,6},{7,8},{9,10},{11,12},{13,14},{2,1},{4,3},{6,5},{... | collective-permute-start | bytes 786440 | tf_op jit(solution)/shard_map/ppermute | solution.py:388
  222.3 4.0 %power8.3 = f32[12,64,128]{2,1,0:T(8,128)S(1)} custom-call(s32[1]{0:T(128)} %bitcast.odd_ref, f32[12,64,128]{2,1,0:T(8,128)S(1)} %get-tuple-element.89.value.refs_0_, f32[8,64,128]{2,1,0:T(8,128)S(1)} %collective-permute-done.28.ha, f32[8,64,128]{2,1,0:T(8,128)S(1)} %collective-permute-done.29.hb, f32[26,64,128]{2,1,0:T(8,128)S(1)} %get-tuple-element.94.keep, ...), custom_call_target="tpu_custom_call" | custom-call | bytes 4194304 | tf_op jit(solution)/shard_map/power8/pallas_call | solution.py:47
  229.1 4.0 %power8.4 = f32[12,64,128]{2,1,0:T(8,128)S(1)} custom-call(s32[1]{0:T(128)} %bitcast.odd_ref, f32[12,64,128]{2,1,0:T(8,128)S(1)} %get-tuple-element.102.value.refs_0_, f32[8,64,128]{2,1,0:T(8,128)S(1)} %collective-permute-done.39.ha, f32[8,64,128]{2,1,0:T(8,128)S(1)} %collective-permute-done.40.hb, f32[26,64,128]{2,1,0:T(8,128)S(1)} %get-tuple-element.94.keep, ...), custom_call_target="tpu_custom_call" | custom-call | bytes 4194304 | tf_op jit(solution)/shard_map/power8/pallas_call | solution.py:47
  234.5 4.0 %power8.5 = f32[12,64,128]{2,1,0:T(8,128)S(1)} custom-call(s32[1]{0:T(128)} %bitcast.odd_ref, f32[12,64,128]{2,1,0:T(8,128)S(1)} %get-tuple-element.111.value.refs_0_, f32[8,64,128]{2,1,0:T(8,128)S(1)} %collective-permute-done.50.ha, f32[8,64,128]{2,1,0:T(8,128)S(1)} %collective-permute-done.51.hb, f32[26,64,128]{2,1,0:T(8,128)S(1)} %get-tuple-element.94.keep, ...), custom_call_target="tpu_custom_call" | custom-call | bytes 4194304 | tf_op jit(solution)/shard_map/power8/pallas_call | solution.py:47
  246.3 7.0 %collective-permute-done.41.refs_2_ = f32[12,64,128]{2,1,0:T(8,128)S(1)} collective-permute-done((f32[12,64,128]{2,1,0:T(8,128)S(1)}, f32[12,64,128]{2,1,0:T(8,128)S(1)}, u32[]{:S(2)}, u32[]{:S(2)}) %collective-permute-start.41) | collective-permute-done | bytes 393248 | tf_op jit(solution)/shard_map/ppermute | solution.py:395
  255.5 3.8 %collective-permute-done.52.refs_2_ = f32[12,64,128]{2,1,0:T(8,128)S(1)} collective-permute-done((f32[12,64,128]{2,1,0:T(8,128)S(1)}, f32[12,64,128]{2,1,0:T(8,128)S(1)}, u32[]{:S(2)}, u32[]{:S(2)}) %collective-permute-start.52) | collective-permute-done | bytes 393248 | tf_op jit(solution)/shard_map/ppermute | solution.py:395
  (190 shorter events, 128.8 us)
Async XLA Ops:
  23.8 19.4 %collective-permute-start.2 = (f32[3,4,64,128]{3,2,1,0:T(8,128)}, f32[3,4,64,128]{3,2,1,0:T(8,128)}, u32[]{:S(2)}, u32[]{:S(2)}) collective-permute-start(f32[3,4,64,128]{3,2,1,0:T(8,128)} %get-tuple-element.67), channel_id=1, source_target_pairs={{0,16},{16,32},{32,48},{48,64},{64,80},{80,96},{96,112},{112,0},{1... | collective-permute-start | bytes 1179656 | tf_op jit(solution)/shard_map/ppermute | solution.py:395
  25.0 19.5 %collective-permute-start.7 = (f32[12,64,128]{2,1,0:T(8,128)}, f32[12,64,128]{2,1,0:T(8,128)S(1)}, u32[]{:S(2)}, u32[]{:S(2)}) collective-permute-start(f32[12,64,128]{2,1,0:T(8,128)} %get-tuple-element.72), channel_id=1, source_target_pairs={{0,1},{1,0},{2,3},{3,2},{4,5},{5,4},{6,7},{7,6},{8,9},{9,8},{10,11... | collective-permute-start | bytes 1179656 | tf_op jit(solution)/shard_map/ppermute | solution.py:385
  25.0 22.0 %collective-permute-start.8 = (f32[12,64,128]{2,1,0:T(8,128)S(1)}, f32[12,64,128]{2,1,0:T(8,128)S(1)}, u32[]{:S(2)}, u32[]{:S(2)}) collective-permute-start(f32[12,64,128]{2,1,0:T(8,128)S(1)} %get-tuple-element.73), channel_id=1, source_target_pairs={{1,2},{3,4},{5,6},{7,8},{9,10},{11,12},{13,14},{2,1},{4,3},{6,5},{... | collective-permute-start | bytes 1179656 | tf_op jit(solution)/shard_map/ppermute | solution.py:388
  28.9 26.5 %collective-permute-start.6 = (f32[3,4,64,128]{3,2,1,0:T(8,128)}, f32[3,4,64,128]{3,2,1,0:T(8,128)}, u32[]{:S(2)}, u32[]{:S(2)}) collective-permute-start(f32[3,4,64,128]{3,2,1,0:T(8,128)} %get-tuple-element.71), channel_id=1, source_target_pairs={{0,16},{16,32},{32,48},{64,80},{80,96},{96,112},{1,17},{17,33},{33... | collective-permute-start | bytes 1179656 | tf_op jit(solution)/shard_map/ppermute | solution.py:395
  32.7 26.1 %collective-permute-start.5 = (f32[3,4,64,128]{3,2,1,0:T(8,128)}, f32[3,4,64,128]{3,2,1,0:T(8,128)}, u32[]{:S(2)}, u32[]{:S(2)}) collective-permute-start(f32[3,4,64,128]{3,2,1,0:T(8,128)} %collective-permute-done.4), channel_id=1, source_target_pairs={{96,64},{32,0},{97,65},{33,1},{98,66},{34,2},{99,67},{35,3},{100,6... | collective-permute-start | bytes 1179656 | tf_op jit(solution)/shard_map/ppermute | solution.py:395
  45.3 20.3 %collective-permute-start.11 = (f32[3,4,64,128]{3,2,1,0:T(8,128)}, f32[3,4,64,128]{3,2,1,0:T(8,128)S(1)}, u32[]{:S(2)}, u32[]{:S(2)}) collective-permute-start(f32[3,4,64,128]{3,2,1,0:T(8,128)} %collective-permute-done.10), channel_id=1, source_target_pairs={{112,64},{48,0},{113,65},{49,1},{114,66},{50,2},{115,67},{51,3},{1... | collective-permute-start | bytes 1179656 | tf_op jit(solution)/shard_map/ppermute | solution.py:395
  47.8 17.9 %collective-permute-start.3 = (f32[3,4,64,128]{3,2,1,0:T(8,128)}, f32[3,4,64,128]{3,2,1,0:T(8,128)S(1)}, u32[]{:S(2)}, u32[]{:S(2)}) collective-permute-start(f32[3,4,64,128]{3,2,1,0:T(8,128)} %collective-permute-done.2.vb), channel_id=1, source_target_pairs={{1,2},{3,4},{5,6},{7,8},{9,10},{11,12},{13,14},{2,1},{4,3},{6,5},{... | collective-permute-start | bytes 1179656 | tf_op jit(solution)/shard_map/ppermute | solution.py:388
  76.9 25.3 %collective-permute-start.16 = (f32[3,4,64,128]{3,2,1,0:T(8,128)S(1)}, f32[3,4,64,128]{3,2,1,0:T(8,128)S(1)}, u32[]{:S(2)}, u32[]{:S(2)}) collective-permute-start(f32[3,4,64,128]{3,2,1,0:T(8,128)S(1)} %collective-permute-done.15), channel_id=1, source_target_pairs={{96,64},{32,0},{97,65},{33,1},{98,66},{34,2},{99,67},{35,3},{100,6... | collective-permute-start | bytes 1179656 | tf_op jit(solution)/shard_map/ppermute | solution.py:395
  78.2 26.2 %collective-permute-start.21 = (f32[3,4,64,128]{3,2,1,0:T(8,128)S(1)}, f32[3,4,64,128]{3,2,1,0:T(8,128)S(1)}, u32[]{:S(2)}, u32[]{:S(2)}) collective-permute-start(f32[3,4,64,128]{3,2,1,0:T(8,128)S(1)} %get-tuple-element.80), channel_id=1, source_target_pairs={{0,16},{16,32},{32,48},{64,80},{80,96},{96,112},{1,17},{17,33},{33... | collective-permute-start | bytes 1179656 | tf_op jit(solution)/shard_map/ppermute | solution.py:395
  87.2 23.7 %collective-permute-start.14 = (f32[3,4,64,128]{3,2,1,0:T(8,128)S(1)}, f32[3,4,64,128]{3,2,1,0:T(8,128)S(1)}, u32[]{:S(2)}, u32[]{:S(2)}) collective-permute-start(f32[3,4,64,128]{3,2,1,0:T(8,128)S(1)} %collective-permute-done.13.vb), channel_id=1, source_target_pairs={{1,2},{3,4},{5,6},{7,8},{9,10},{11,12},{13,14},{2,1},{4,3},{6,5},{... | collective-permute-start | bytes 1179656 | tf_op jit(solution)/shard_map/ppermute | solution.py:388
  89.1 21.7 %collective-permute-start.20 = (f32[3,4,64,128]{3,2,1,0:T(8,128)S(1)}, f32[3,4,64,128]{3,2,1,0:T(8,128)S(1)}, u32[]{:S(2)}, u32[]{:S(2)}) collective-permute-start(f32[3,4,64,128]{3,2,1,0:T(8,128)S(1)} %collective-permute-done.19), channel_id=1, source_target_pairs={{112,64},{48,0},{113,65},{49,1},{114,66},{50,2},{115,67},{51,3},{1... | collective-permute-start | bytes 1179656 | tf_op jit(solution)/shard_map/ppermute | solution.py:395
  117.7 27.7 %collective-permute-start.35 = (f32[12,64,128]{2,1,0:T(8,128)S(1)}, f32[12,64,128]{2,1,0:T(8,128)S(1)}, u32[]{:S(2)}, u32[]{:S(2)}) collective-permute-start(f32[12,64,128]{2,1,0:T(8,128)S(1)} %get-tuple-element.98), channel_id=1, source_target_pairs={{0,16},{16,32},{32,48},{64,80},{80,96},{96,112},{1,17},{17,33},{33... | collective-permute-start | bytes 1179656 | tf_op jit(solution)/shard_map/ppermute | solution.py:395
  119.1 26.2 %collective-permute-start.44 = (f32[12,64,128]{2,1,0:T(8,128)S(1)}, f32[12,64,128]{2,1,0:T(8,128)S(1)}, u32[]{:S(2)}, u32[]{:S(2)}) collective-permute-start(f32[12,64,128]{2,1,0:T(8,128)S(1)} %get-tuple-element.107), channel_id=1, source_target_pairs={{0,16},{16,32},{32,48},{64,80},{80,96},{96,112},{1,17},{17,33},{33... | collective-permute-start | bytes 1179656 | tf_op jit(solution)/shard_map/ppermute | solution.py:395
  127.3 18.1 %collective-permute-start.34 = (f32[12,64,128]{2,1,0:T(8,128)S(1)}, f32[12,64,128]{2,1,0:T(8,128)S(1)}, u32[]{:S(2)}, u32[]{:S(2)}) collective-permute-start(f32[12,64,128]{2,1,0:T(8,128)S(1)} %collective-permute-done.33), channel_id=1, source_target_pairs={{112,64},{48,0},{113,65},{49,1},{114,66},{50,2},{115,67},{51,3},{1... | collective-permute-start | bytes 1179656 | tf_op jit(solution)/shard_map/ppermute | solution.py:395
  128.6 28.0 %collective-permute-start.43 = (f32[12,64,128]{2,1,0:T(8,128)S(1)}, f32[12,64,128]{2,1,0:T(8,128)S(1)}, u32[]{:S(2)}, u32[]{:S(2)}) collective-permute-start(f32[12,64,128]{2,1,0:T(8,128)S(1)} %collective-permute-done.42), channel_id=1, source_target_pairs={{96,64},{32,0},{97,65},{33,1},{98,66},{34,2},{99,67},{35,3},{100,6... | collective-permute-start | bytes 1179656 | tf_op jit(solution)/shard_map/ppermute | solution.py:395
  143.9 30.2 %collective-permute-start.25 = (f32[12,64,128]{2,1,0:T(8,128)}, f32[12,64,128]{2,1,0:T(8,128)}, u32[]{:S(2)}, u32[]{:S(2)}) collective-permute-start(f32[12,64,128]{2,1,0:T(8,128)} %power4.3), channel_id=1, source_target_pairs={{32,96},{48,112},{96,32},{112,48},{33,97},{49,113},{97,33},{113,49... | collective-permute-start | bytes 1179656 | tf_op jit(solution)/shard_map/ppermute | solution.py:395
  170.1 24.9 %collective-permute-start.47 = (f32[12,64,128]{2,1,0:T(8,128)}, f32[12,64,128]{2,1,0:T(8,128)}, u32[]{:S(2)}, u32[]{:S(2)}) collective-permute-start(f32[12,64,128]{2,1,0:T(8,128)} %power4.5), channel_id=1, source_target_pairs={{32,96},{48,112},{96,32},{112,48},{33,97},{49,113},{97,33},{113,49... | collective-permute-start | bytes 1179656 | tf_op jit(solution)/shard_map/ppermute | solution.py:395
  171.5 24.8 %collective-permute-start.27 = (f32[12,64,128]{2,1,0:T(8,128)}, f32[12,64,128]{2,1,0:T(8,128)}, u32[]{:S(2)}, u32[]{:S(2)}) collective-permute-start(f32[12,64,128]{2,1,0:T(8,128)} %power4.3), channel_id=1, source_target_pairs={{0,32},{16,48},{64,96},{80,112},{1,33},{17,49},{65,97},{81,113},{2... | collective-permute-start | bytes 1179656 | tf_op jit(solution)/shard_map/ppermute | solution.py:395
  174.1 22.2 %collective-permute-start.26 = (f32[12,64,128]{2,1,0:T(8,128)}, f32[12,64,128]{2,1,0:T(8,128)}, u32[]{:S(2)}, u32[]{:S(2)}) collective-permute-start(f32[12,64,128]{2,1,0:T(8,128)} %collective-permute-done.25), channel_id=1, source_target_pairs={{96,64},{112,80},{32,0},{48,16},{97,65},{113,81},{33,1},{49,17},{9... | collective-permute-start | bytes 1179656 | tf_op jit(solution)/shard_map/ppermute | solution.py:395
  198.5 19.2 %collective-permute-start.28 = (f32[8,64,128]{2,1,0:T(8,128)S(1)}, f32[8,64,128]{2,1,0:T(8,128)S(1)}, u32[]{:S(2)}, u32[]{:S(2)}) collective-permute-start(f32[8,64,128]{2,1,0:T(8,128)S(1)} %get-tuple-element.90), channel_id=1, source_target_pairs={{0,1},{1,0},{2,3},{3,2},{4,5},{5,4},{6,7},{7,6},{8,9},{9,8},{10,11... | collective-permute-start | bytes 786440 | tf_op jit(solution)/shard_map/ppermute | solution.py:385
  211.2 17.8 %collective-permute-start.39 = (f32[8,64,128]{2,1,0:T(8,128)S(1)}, f32[8,64,128]{2,1,0:T(8,128)S(1)}, u32[]{:S(2)}, u32[]{:S(2)}) collective-permute-start(f32[8,64,128]{2,1,0:T(8,128)S(1)} %get-tuple-element.103), channel_id=1, source_target_pairs={{0,1},{1,0},{2,3},{3,2},{4,5},{5,4},{6,7},{7,6},{8,9},{9,8},{10,11... | collective-permute-start | bytes 786440 | tf_op jit(solution)/shard_map/ppermute | solution.py:385
  226.3 17.9 %collective-permute-start.32 = (f32[12,64,128]{2,1,0:T(8,128)S(1)}, f32[12,64,128]{2,1,0:T(8,128)S(1)}, u32[]{:S(2)}, u32[]{:S(2)}) collective-permute-start(f32[12,64,128]{2,1,0:T(8,128)S(1)} %power8.3), channel_id=1, source_target_pairs={{0,64},{16,80},{32,96},{48,112},{64,0},{80,16},{96,32},{112,48},{1... | collective-permute-start | bytes 1179656 | tf_op jit(solution)/shard_map/ppermute | solution.py:395
  233.1 20.2 %collective-permute-start.41 = (f32[12,64,128]{2,1,0:T(8,128)S(1)}, f32[12,64,128]{2,1,0:T(8,128)S(1)}, u32[]{:S(2)}, u32[]{:S(2)}) collective-permute-start(f32[12,64,128]{2,1,0:T(8,128)S(1)} %power8.4), channel_id=1, source_target_pairs={{0,64},{16,80},{32,96},{48,112},{64,0},{80,16},{96,32},{112,48},{1... | collective-permute-start | bytes 1179656 | tf_op jit(solution)/shard_map/ppermute | solution.py:395
  238.5 20.8 %collective-permute-start.52 = (f32[12,64,128]{2,1,0:T(8,128)S(1)}, f32[12,64,128]{2,1,0:T(8,128)S(1)}, u32[]{:S(2)}, u32[]{:S(2)}) collective-permute-start(f32[12,64,128]{2,1,0:T(8,128)S(1)} %power8.5), channel_id=1, source_target_pairs={{0,64},{16,80},{32,96},{48,112},{64,0},{80,16},{96,32},{112,48},{1... | collective-permute-start | bytes 1179656 | tf_op jit(solution)/shard_map/ppermute | solution.py:395
  (67 other events, 778.5 us)

commit v5 on v3

--- a/solution.py
+++ b/solution.py
@@ -1,5 +1,3 @@
-import functools
-
 import jax
 import jax.numpy as jnp
 from jax import lax
@@ -12,6 +10,7 @@
 ANY = pl.BlockSpec(memory_space=pl.ANY)
 HBM = pl.BlockSpec(memory_space=pltpu.HBM)
 VMEM = pl.BlockSpec(memory_space=pltpu.VMEM)
+COMPS = [(0,), (1,), (2,)]
 SMEM = pl.BlockSpec(memory_space=pltpu.SMEM)
 
 
@@ -51,7 +50,7 @@
         in_specs=in_specs,
         out_specs=out_specs or (VMEM if single else [VMEM] * len(outs)),
         scratch_shapes=list(scratch) + [pltpu.SemaphoreType.DMA((n_sems,))] * (n_sems > 0),
-        compiler_params=pltpu.CompilerParams(vmem_limit_bytes=40 * 1024 * 1024),
+        compiler_params=pltpu.CompilerParams(vmem_limit_bytes=16 * 1024 * 1024),
         cost_estimate=pl.CostEstimate(flops=0, bytes_accessed=4 << 20, transcendentals=0),
     )(*args)
 
@@ -252,11 +251,14 @@
 
 
 def extend(odd, pieces, halos, x):
-    a, b, m = pieces
+    a, b, *m = pieces
     ha, hb = halos
     for c in range(3):
         for k in range(4):
-            x[c, 8 + k] = m[c, k]
+            middle = m[0][c, k]
+            for other in m[1:]:
+                middle = middle + other[c, k]
+            x[c, 8 + k] = middle
             x[c, 4 + (1 - odd) * 8 + k] = a[c, k]
             x[c, 4 + odd * 8 + k] = b[c, k]
             x[c, (1 - odd) * 16 + k] = ha[c, k]
@@ -273,11 +275,11 @@
 
 
 def second_kernel(
-    odd_ref, hb, vb, ha, va, vm, source, a1, b1, a2, b2, cond, nu,
+    odd_ref, hb, vb, ha, va, vm, vn, source, a1, b1, a2, b2, cond, nu,
     u0, oa, ob, om, x, y, held, f0, f1,
 ):
     odd = odd_ref[0]
-    extend(odd, (va, vb, vm), (ha, hb), x)
+    extend(odd, (va, vb, vm, vn), (ha, hb), x)
     extend_force(odd, source, 0, 3, (a2, b2), 0, f0)
     extend_force(odd, source, 1, 1, (a1, b1), 6, f1)
 
@@ -296,12 +298,20 @@
             ob[c, k] = x[c, 4 + odd * 8 + k]
 
 
+def split(odd, x, start, b, a, m):
+    for c in range(3):
+        for k in range(4):
+            b[c, k] = x[c, start + odd * 8 + k]
+            a[c, k] = x[c, start + (1 - odd) * 8 + k]
+            m[c, k] = x[c, start + 4 + k]
+
+
 def residual_kernel(
-    odd_ref, hb, vb, ha, va, vm, source, a2, b2, cond, nu, keep, spread, u0,
-    res_o, l0, l1, l2, r0, r1, r2, x, y, held, f0, sems,
+    odd_ref, hb, vb, ha, va, vm, vn, source, a2, b2, cond, nu, keep, spread, u0,
+    res_o, lb, la, lm, rb, ra, rm, x, y, held, f0, sems,
 ):
     odd = odd_ref[0]
-    extend(odd, (va, vb, vm), (ha, hb), x)
+    extend(odd, (va, vb, vm, vn), (ha, hb), x)
     extend_force(odd, source, 0, 3, (a2, b2), 0, f0)
 
     def less(c, i, value):
@@ -310,60 +320,77 @@
     fine_sweep(x, into(y), held, cond, nu, 1, 19, f0, 1)
     fine_sweep(y, less, held, cond, nu, 2, 18, None, 1)
     kept = copy_all([(x.at[:, pl.ds(4, LX)], res_o.at[0])], sems)
-    comps = [(0,), (1,), (2,)]
-    coarse_sweep(x, put(y), held, keep, spread, -1, 3, 17, True, comps)
-    for c, out in enumerate((r0, r1, r2)):
-        for i in range(LX):
-            out[i] = x[c, 4 + i]
-
-    def store(at, value):
-        (l0, l1, l2)[at[0]][at[1] - 4] = value
-
-    coarse_sweep(y, store, held, keep, spread, -1, 4, 16, False, comps)
+    split(odd, x, 4, rb, ra, rm)
+    coarse_sweep(x, put(y), held, keep, spread, -1, 3, 17, True, COMPS)
     wait_all(kept)
-
-
-def add_kernel(w, odd_ref, *refs):
-    odd = odd_ref[0]
-    *terms, total, sa, sb = refs
-    for i in range(LX):
-        value = terms[0][i]
-        for term in terms[1:]:
-            value = value + term[i]
-        total[i] = value
-    for side, top in ((sa, 1 - odd), (sb, odd)):
-        for i in range(w):
-            side[i] = total[i + top * (LX - w)]
-
-
-def power_kernel(w, odd_ref, value, ha, hb, keep, spread, out, x, y, held):
-    odd = odd_ref[0]
-    for i in range(LX):
-        x[i + w] = value[i]
-    for side, high in ((ha, 1 - odd), (hb, odd)):
-        for i in range(w):
-            x[i + high * (LX + w)] = side[i]
-
-    for step in range(w // 2):
-        lo = 1 + 2 * step
-        last = put(out, w) if step == w // 2 - 1 else put(x)
-        coarse_sweep(x, put(y), held, keep, spread, -1, lo, LX + 2 * w - lo, True, [()])
-        coarse_sweep(y, last, held, keep, spread, -1, lo + 1, LX + 2 * w - lo - 1, False, [()])
+    coarse_sweep(y, put(x), held, keep, spread, -1, 4, 16, False, COMPS)
+    split(odd, x, 4, lb, la, lm)
+
+
+def square_kernel(odd_ref, hb, sb, ha, sa, sm, keep, spread, ob, oa, om, x, y, held):
+    odd = odd_ref[0]
+    extend(odd, (sa, sb, sm), (ha, hb), x)
+    for lo in (1, 3):
+        coarse_sweep(x, put(y), held, keep, spread, -1, lo, 20 - lo, True, COMPS)
+        coarse_sweep(y, put(x), held, keep, spread, -1, lo + 1, 19 - lo, False, COMPS)
+    split(odd, x, 4, ob, oa, om)
+
+
+def fourth_kernel(
+    odd_ref, near_b, tb, far_b, tm, far_a, near_a, ta, u0, keep, spread,
+    ob, oa, om, bb, ba, bm, x, y, held,
+):
+    odd = odd_ref[0]
+    for c in range(3):
+        for k in range(4):
+            x[c, 8 + odd * 8 + k] = tb[c, k]
+            x[c, 8 + (1 - odd) * 8 + k] = ta[c, k]
+            x[c, 12 + k] = tm[c, k]
+            x[c, 4 + odd * 16 + k] = near_b[c, k]
+            x[c, 4 + (1 - odd) * 16 + k] = near_a[c, k]
+            x[c, odd * 24 + k] = far_b[c, k]
+            x[c, (1 - odd) * 24 + k] = far_a[c, k]
+    for c in range(3):
+        for k in range(4):
+            bb[c, k] = tb[c, k] + u0[c, 2 + odd * 8 + k]
+            ba[c, k] = ta[c, k] + u0[c, 2 + (1 - odd) * 8 + k]
+            bm[c, k] = tm[c, k] + u0[c, 6 + k]
+    for lo in (1, 3, 5, 7):
+        coarse_sweep(x, put(y), held, keep, spread, -1, lo, 28 - lo, True, COMPS)
+        coarse_sweep(y, put(x), held, keep, spread, -1, lo + 1, 27 - lo, False, COMPS)
+    split(odd, x, 8, ob, oa, om)
+
+
+def edge_kernel(odd_ref, base, moved, total, edge):
+    odd = odd_ref[0]
+    for c in range(3):
+        for k in range(4):
+            total[c, k] = base[c, k] + moved[c, k]
+        for k in range(2):
+            edge[c, k] = total[c, odd * 2 + k]
 
 
 def last_kernel(
-    odd_ref, p0, p1, p2, a_0, a_1, a_2, b_0, b_1, b_2, source, a1, b1, cond, nu,
-    field, x, y, held, f1, sems,
+    odd_ref, hb, eb, ha, ea, em, source, a1, b1, cond, nu, field, x, y, held, f1, sems,
 ):
     odd = odd_ref[0]
-    kept = copy_all([(p, field.at[0, c]) for c, p in enumerate((p0, p1, p2))], sems)
+    kept = copy_all(
+        [
+            (eb, field.at[0, :, pl.ds(odd * 8, 4)]),
+            (ea, field.at[0, :, pl.ds((1 - odd) * 8, 4)]),
+            (em, field.at[0, :, pl.ds(4, 4)]),
+        ],
+        sems,
+    )
     extend_force(odd, source, 1, 1, (a1, b1), 6, f1)
-    for c, (p, a, b) in enumerate(((p0, a_0, b_0), (p1, a_1, b_1), (p2, a_2, b_2))):
-        for i in range(LX):
-            x[c, 4 + i] = p[i]
+    for c in range(3):
+        for k in range(4):
+            x[c, 4 + odd * 8 + k] = eb[c, k]
+            x[c, 4 + (1 - odd) * 8 + k] = ea[c, k]
+            x[c, 8 + k] = em[c, k]
         for k in range(2):
-            x[c, 2 + (1 - odd) * (LX + 2) + k] = a[k]
-            x[c, 2 + odd * (LX + 2) + k] = b[k]
+            x[c, 2 + odd * 14 + k] = hb[c, k]
+            x[c, 2 + (1 - odd) * 14 + k] = ha[c, odd * 2 + k]
     fine_sweep(x, into(y), held, cond, nu, 3, 17, f1, 1)
     fine_sweep(y, into(x), held, cond, nu, 4, 10, None, 1)
     kept += copy_all([(x.at[:, pl.ds(4, 6)], field.at[1, :, pl.ds(0, 6)])], sems, 3)
@@ -387,8 +414,20 @@
     def from_b(x):
         return lax.ppermute(x, "space", off_chip)
 
+    half = slices // 2
+
+    def along(x, pairs):
+        return lax.ppermute(x, "tm", pairs)
+
     def later(x, distance):
-        return lax.ppermute(x, "tm", [(i, (i + distance) % slices) for i in range(slices)])
+        return along(x, [(i, (i + distance) % slices) for i in range(slices)])
+
+    def later_parts(x, distance):
+        wrapping = [i for i in range(slices) if i % half + distance >= half]
+        across = along(x, [(i, (i + half) % slices) for i in wrapping])
+        around = along(across, [((i + half) % slices, (i + distance) % slices) for i in wrapping])
+        plain = along(x, [(i, i + distance) for i in range(slices) if i not in wrapping])
+        return around, plain
 
     tables = (conductance, reluct)
     sa1, sb1 = call(
@@ -405,7 +444,7 @@
         second_pack_kernel, "second_pack", (odd, source, regions),
         [planes(12), planes(12), planes(4), planes(4)], [pltpu.VMEM((LX, NY, NZ), jnp.int32)], 8, in_place=HBM,
     )
-    vm = later(um, 1)
+    vm = later_parts(um, 1)
     sb2, sa2, b1 = fence((sb2, sa2, b1))
     b2 = from_b(sb2)
     a2 = from_a(sa2)
@@ -418,7 +457,7 @@
     cond, nu, keep, spread = call(
         material_kernel, "material", (odd, *tables, regions, a2, b2), [planes(LX + 6)] * 4, [],
     )
-    vb, vm, cond = fence((vb, vm, cond))
+    va, cond = fence((va, cond))
     hb = from_b(vb)
     ha = from_a(va)
     sb3, sa3, vb = fence((sb3, sa3, vb))
@@ -427,50 +466,54 @@
     n = LX + 8
     u0, ua, ub, um = call(
         second_kernel, "second",
-        (odd, hb, vb, ha, va, vm, source, a1, b1, a2, b2, cond, nu),
+        (odd, hb, vb, ha, va, *vm, source, a1, b1, a2, b2, cond, nu),
         [planes(3, LX + 4), planes(3, 4), planes(3, 4), planes(3, 4)], [vmem(3, n)] * 5,
     )
     vb = later(ub, 1)
     va = later(ua, 1)
-    vm = later(um, 1)
+    vm = later_parts(um, 1)
     hb = from_b(vb)
     ha = from_a(va)
     wide_keep, wide_spread = call(
         wide_kernel, "wide", (odd, *tables, keep, spread, a3, b3), [planes(LX + 14)] * 2, [],
     )
-    residual, *rest = call(
+    residual, lb, la, lm, rb, ra, rm = call(
         residual_kernel, "residual",
-        (odd, hb, vb, ha, va, vm, source, a2, b2, cond, nu, keep, spread, u0),
-        [planes(1, 3, LX)] + [planes(LX)] * 6, [vmem(3, n)] * 4, 1, [ANY] + [VMEM] * 6,
-    )
-    moving, totals = rest[:3], rest[3:]
-    u0_own = [u0[c, 2:2 + LX] for c in range(3)]
-    for distance, width in ((1, 4), (2, 8), (4, 2)):
-        moved = [later(m, distance) for m in moving]
-        bases = [(t,) for t in totals]
-        if distance == 4:
-            bases = [(t, u) for t, u in zip(totals, u0_own)]
-        totals, moving, sides = [], [], []
-        for c in range(3):
-            total, sa, sb = call(
-                functools.partial(add_kernel, width), "add%d" % width, (odd, *bases[c], moved[c]),
-                [planes(LX), planes(width), planes(width)], [],
-            )
-            hb = from_b(sb)
-            ha = from_a(sa)
-            totals.append(total)
-            sides.append((ha, hb))
-            if distance < 4:
-                pair = (wide_keep, wide_spread) if width == 8 else (keep, spread)
-                moving.append(
-                    call(
-                        functools.partial(power_kernel, width), "power%d" % width,
-                        (odd, total, ha, hb, *pair), planes(LX), [vmem(LX + 2 * width)] * 3,
-                    )
-                )
+        (odd, hb, vb, ha, va, *vm, source, a2, b2, cond, nu, keep, spread, u0),
+        [planes(1, 3, LX)] + [planes(3, 4)] * 6, [vmem(3, n)] * 4, 1, [ANY] + [VMEM] * 6,
+    )
+    sb = rb + later(lb, 1)
+    hb = from_b(sb)
+    sa = ra + later(la, 1)
+    ha = from_a(sa)
+    around, plain = later_parts(lm, 1)
+    sm = rm + (around + plain)
+    lb, la, lm = call(
+        square_kernel, "square", (odd, hb, sb, ha, sa, sm, keep, spread),
+        [planes(3, 4)] * 3, [vmem(3, n)] * 3,
+    )
+    tb = sb + later(lb, 2)
+    near_b = from_b(tb)
+    tm = sm + later(lm, 2)
+    far_b = from_b(tm)
+    around, plain = later_parts(la, 2)
+    ta = sa + (around + plain)
+    near_a = from_a(ta)
+    far_a = from_a(tm)
+    lb, la, lm, bb, ba, bm = call(
+        fourth_kernel, "fourth",
+        (odd, near_b, tb, far_b, tm, far_a, near_a, ta, u0, wide_keep, wide_spread),
+        [planes(3, 4)] * 6, [vmem(3, LX + 16)] * 3,
+    )
+    eb, edge = call(
+        edge_kernel, "edge", (odd, bb, later(lb, half)), [planes(3, 4), planes(3, 2)], [],
+    )
+    hb = from_b(edge)
+    ea, edge = lax.optimization_barrier((ba + later(la, half), edge))
+    ha = from_a(ea)
+    em = bm + later(lm, half)
     field = call(
-        last_kernel, "last",
-        (odd, *totals, *[s[0] for s in sides], *[s[1] for s in sides], source, a1, b1, cond, nu),
+        last_kernel, "last", (odd, hb, eb, ha, ea, em, source, a1, b1, cond, nu),
         planes(2, 3, LX), [vmem(3, n)] * 4, 5, ANY,
     )
     return field, residual

time: 281 us -> 239 us (0.85)
  starting transfers between devices: 115 us -> 71.9 us
  waiting for transfers between devices: 118 us -> 123 us
    ppermute x14 -> x9, starting transfers between devices: 65.3 us -> 9.89 us  [from_a(): return lax.ppermute(x, 'space', on_chip)]
    ppermute x15 -> x23, waiting for transfers between devices: 57.9 us -> 83.1 us  [along(): return lax.ppermute(x, 'tm', pairs)]
    ppermute x14 -> x9, waiting for transfers between devices: 60.2 us -> 36.6 us  [from_b(): return lax.ppermute(x, 'space', off_chip)]
    ppermute x15 -> x23, starting transfers between devices: 14.8 us -> 31.2 us  [along(): return lax.ppermute(x, 'tm', pairs)]
    ppermute x14 -> x9, starting transfers between devices: 34.9 us -> 30.7 us  [from_b(): return lax.ppermute(x, 'space', off_chip)]
    ppermute x14 -> x9, waiting for transfers between devices: 0.04 us -> 2.91 us  [from_a(): return lax.ppermute(x, 'space', on_chip)]
    pallas_call x24 -> x12, Pallas kernels: 38.6 us -> 37.8 us  [call(): pl.pallas_call(kernel, name=name, out_shape=outs, in_specs=in_specs, out_...]
  transfers between devices with their start and end apart: 43 -> 41, of which waited for: 13 -> 21; matrix products, arithmetic and copies ran while one was open for 0% -> 0% of each run, Pallas kernels for 9% -> 3%
where the time goes in v5:
time: 239 us; the launch traced here: 238 us
  waiting for transfers between devices  123 us (51%)
  starting transfers between devices  71.9 us (30%)
  Pallas kernels  37.8 us (16%)
  local copies, waits for them, and re-layouts  4.33 us (2%)
    ppermute x23, waiting for transfers between devices, along(): return lax.ppermute(x, 'tm', pairs)  83.1 us
    pallas_call x12, Pallas kernels, call(): pl.pallas_call(kernel, name=name, out_shape=outs, in_specs=in_specs, out_...  37.8 us
    ppermute x9, waiting for transfers between devices, from_b(): return lax.ppermute(x, 'space', off_chip)  36.6 us
    ppermute x23, starting transfers between devices, along(): return lax.ppermute(x, 'tm', pairs)  31.2 us
    ppermute x9, starting transfers between devices, from_b(): return lax.ppermute(x, 'space', off_chip)  30.7 us
    ppermute x9, starting transfers between devices, from_a(): return lax.ppermute(x, 'space', on_chip)  9.89 us
  transfers between devices with their start and end apart: 41, of which 21 were waited for; matrix products, arithmetic and copies ran while one was open for 0% of the time, Pallas kernels for 3%

profile of v5, /device:TPU:17, one launch (start us, length us, event | category | flops | bytes accessed | tf_op | source)
XLA Modules:
  0.0 238.3 jit_solution(17282153073913382416)
XLA Ops:
  6.0 4.1 %collective-permute-start.1 = (f32[10,64,128]{2,1,0:T(8,128)S(1)}, f32[10,64,128]{2,1,0:T(8,128)S(1)}, u32[]{:S(2)}, u32[]{:S(2)}) collective-permute-start(f32[10,64,128]{2,1,0:T(8,128)S(1)} %get-tuple-element.50), channel_id=1, source_target_pairs={{1,2},{3,4},{5,6},{7,8},{9,10},{11,12},{13,14},{2,1},{4,3},{6,5},{... | collective-permute-start | bytes 983048 | tf_op jit(solution)/shard_map/ppermute | solution.py:415
  13.5 4.9 %collective-permute-done.1.rb.b1 = f32[10,64,128]{2,1,0:T(8,128)S(1)} collective-permute-done((f32[10,64,128]{2,1,0:T(8,128)S(1)}, f32[10,64,128]{2,1,0:T(8,128)S(1)}, u32[]{:S(2)}, u32[]{:S(2)}) %collective-permute-start.1) | collective-permute-done | bytes 327712 | tf_op jit(solution)/shard_map/ppermute | solution.py:415
  31.1 17.7 %collective-permute-done.6.rb.b2 = f32[12,64,128]{2,1,0:T(8,128)S(1)} collective-permute-done((f32[12,64,128]{2,1,0:T(8,128)S(1)}, f32[12,64,128]{2,1,0:T(8,128)S(1)}, u32[]{:S(2)}, u32[]{:S(2)}) %collective-permute-start.6) | collective-permute-done | bytes 393248 | tf_op jit(solution)/shard_map/ppermute | solution.py:415
  56.0 7.4 %collective-permute-done.3.hb = f32[3,4,64,128]{3,2,1,0:T(8,128)S(1)} collective-permute-done((f32[3,4,64,128]{3,2,1,0:T(8,128)S(1)}, f32[3,4,64,128]{3,2,1,0:T(8,128)S(1)}, u32[]{:S(2)}, u32[]{:S(2)}) %collective-permute-start.3) | collective-permute-done | bytes 393248 | tf_op jit(solution)/shard_map/ppermute | solution.py:415
  63.4 5.1 %second.1 = (f32[3,16,64,128]{3,2,1,0:T(8,128)S(1)}, f32[3,4,64,128]{3,2,1,0:T(8,128)S(1)}, f32[3,4,64,128]{3,2,1,0:T(8,128)S(1)}, f32[3,4,64,128]{3,2,1,0:T(8,128)S(1)}) custom-call(s32[1]{0:T(128)} %bitcast.odd_ref, f32[3,4,64,128]{3,2,1,0:T(8,128)S(1)} %collective-permute-done.3.hb, f32[3,4,64,128]{3,2,1,0:T(8,128)S(1)} %collective-permute-done.2.vb, ...), custom_call_target="tpu_custom_call" | custom-call | bytes 4194304 | tf_op jit(solution)/shard_map/second/pallas_call | solution.py:46
  70.7 12.7 %collective-permute-done.11.vb = f32[3,4,64,128]{3,2,1,0:T(8,128)S(1)} collective-permute-done((f32[3,4,64,128]{3,2,1,0:T(8,128)S(1)}, f32[3,4,64,128]{3,2,1,0:T(8,128)S(1)}, u32[]{:S(2)}, u32[]{:S(2)}) %collective-permute-start.11) | collective-permute-done | bytes 393248 | tf_op jit(solution)/shard_map/ppermute | solution.py:420
  87.0 7.4 %collective-permute-done.13.va = f32[3,4,64,128]{3,2,1,0:T(8,128)S(1)} collective-permute-done((f32[3,4,64,128]{3,2,1,0:T(8,128)S(1)}, f32[3,4,64,128]{3,2,1,0:T(8,128)S(1)}, u32[]{:S(2)}, u32[]{:S(2)}) %collective-permute-start.13) | collective-permute-done | bytes 393248 | tf_op jit(solution)/shard_map/ppermute | solution.py:420
  96.2 11.5 %collective-permute-done.16.vm = f32[3,4,64,128]{3,2,1,0:T(8,128)S(1)} collective-permute-done((f32[3,4,64,128]{3,2,1,0:T(8,128)S(1)}, f32[3,4,64,128]{3,2,1,0:T(8,128)S(1)}, u32[]{:S(2)}, u32[]{:S(2)}) %collective-permute-start.16) | collective-permute-done | bytes 393248 | tf_op jit(solution)/shard_map/ppermute | solution.py:420
  107.7 5.2 %residual.1 = (f32[1,3,12,64,128]{4,3,2,1,0:T(8,128)}, f32[3,4,64,128]{3,2,1,0:T(8,128)S(1)}, f32[3,4,64,128]{3,2,1,0:T(8,128)S(1)}, f32[3,4,64,128]{3,2,1,0:T(8...) custom-call(s32[1]{0:T(128)} %bitcast.odd_ref, ...), custom_call_target="tpu_custom_call" | custom-call | bytes 4194304 | tf_op jit(solution)/shard_map/residual/pallas_call | solution.py:46
  118.2 8.3 %collective-permute-done.18 = f32[3,4,64,128]{3,2,1,0:T(8,128)S(1)} collective-permute-done((f32[3,4,64,128]{3,2,1,0:T(8,128)S(1)}, f32[3,4,64,128]{3,2,1,0:T(8,128)S(1)}, u32[]{:S(2)}, u32[]{:S(2)}) %collective-permute-start.18) | collective-permute-done | bytes 393248 | tf_op jit(solution)/shard_map/ppermute | solution.py:420
  126.5 5.3 %collective-permute-start.19 = (f32[3,4,64,128]{3,2,1,0:T(8,128)S(1)}, f32[3,4,64,128]{3,2,1,0:T(8,128)S(1)}, u32[]{:S(2)}, u32[]{:S(2)}) collective-permute-start(f32[3,4,64,128]{3,2,1,0:T(8,128)S(1)} %add.35.sb), channel_id=1, source_target_pairs={{1,2},{3,4},{5,6},{7,8},{9,10},{11,12},{13,14},{2,1},{4,3},{6,5},{... | collective-permute-start | bytes 1179656 | tf_op jit(solution)/shard_map/ppermute | solution.py:415
  131.8 5.3 %collective-permute-done.20 = f32[3,4,64,128]{3,2,1,0:T(8,128)S(1)} collective-permute-done((f32[3,4,64,128]{3,2,1,0:T(8,128)S(1)}, f32[3,4,64,128]{3,2,1,0:T(8,128)S(1)}, u32[]{:S(2)}, u32[]{:S(2)}) %collective-permute-start.20) | collective-permute-done | bytes 393248 | tf_op jit(solution)/shard_map/ppermute | solution.py:420
  137.1 4.3 %collective-permute-start.21 = (f32[3,4,64,128]{3,2,1,0:T(8,128)S(1)}, f32[3,4,64,128]{3,2,1,0:T(8,128)S(1)}, u32[]{:S(2)}, u32[]{:S(2)}) collective-permute-start(f32[3,4,64,128]{3,2,1,0:T(8,128)S(1)} %add.36.sa), channel_id=1, source_target_pairs={{0,1},{1,0},{2,3},{3,2},{4,5},{5,4},{6,7},{7,6},{8,9},{9,8},{10,11... | collective-permute-start | bytes 1179656 | tf_op jit(solution)/shard_map/ppermute | solution.py:412
  142.8 4.8 %square.1 = (f32[3,4,64,128]{3,2,1,0:T(8,128)S(1)}, f32[3,4,64,128]{3,2,1,0:T(8,128)S(1)}, f32[3,4,64,128]{3,2,1,0:T(8,128)S(1)}) custom-call(s32[1]{0:T(128)} %bitcast.odd_ref, f32[3,4,64,128]{3,2,1,0:T(8,128)S(1)} %collective-permute-done.19.hb, f32[3,4,64,128]{3,2,1,0:T(8,128)S(1)} %add.35.sb, f32[3,4,64,128]{3,2,1,0:T(8,128)S(1)} %collective-permute-done.21.ha, ...), custom_call_target="tpu_custom_call" | custom-call | bytes 4194304 | tf_op jit(solution)/shard_map/square/pallas_call | solution.py:46
  148.8 5.2 %collective-permute-start.25 = (f32[3,4,64,128]{3,2,1,0:T(8,128)S(1)}, f32[3,4,64,128]{3,2,1,0:T(8,128)S(1)}, u32[]{:S(2)}, u32[]{:S(2)}) collective-permute-start(f32[3,4,64,128]{3,2,1,0:T(8,128)S(1)} %get-tuple-element.75), channel_id=1, source_target_pairs={{0,32},{16,48},{32,64},{48,80},{64,96},{80,112},{96,0},{112,16},{1... | collective-permute-start | bytes 1179656 | tf_op jit(solution)/shard_map/ppermute | solution.py:420
  157.3 5.2 %collective-permute-done.27 = f32[3,4,64,128]{3,2,1,0:T(8,128)S(1)} collective-permute-done((f32[3,4,64,128]{3,2,1,0:T(8,128)S(1)}, f32[3,4,64,128]{3,2,1,0:T(8,128)S(1)}, u32[]{:S(2)}, u32[]{:S(2)}) %collective-permute-start.27) | collective-permute-done | bytes 393248 | tf_op jit(solution)/shard_map/ppermute | solution.py:420
  166.6 4.4 %collective-permute-done.25 = f32[3,4,64,128]{3,2,1,0:T(8,128)S(1)} collective-permute-done((f32[3,4,64,128]{3,2,1,0:T(8,128)S(1)}, f32[3,4,64,128]{3,2,1,0:T(8,128)S(1)}, u32[]{:S(2)}, u32[]{:S(2)}) %collective-permute-start.25) | collective-permute-done | bytes 393248 | tf_op jit(solution)/shard_map/ppermute | solution.py:420
  171.0 3.8 %collective-permute-start.26 = (f32[3,4,64,128]{3,2,1,0:T(8,128)S(1)}, f32[3,4,64,128]{3,2,1,0:T(8,128)S(1)}, u32[]{:S(2)}, u32[]{:S(2)}) collective-permute-start(f32[3,4,64,128]{3,2,1,0:T(8,128)S(1)} %add.39.tb), channel_id=1, source_target_pairs={{1,2},{3,4},{5,6},{7,8},{9,10},{11,12},{13,14},{2,1},{4,3},{6,5},{... | collective-permute-start | bytes 1179656 | tf_op jit(solution)/shard_map/ppermute | solution.py:415
  184.5 6.3 %collective-permute-done.35.rb = f32[4,64,128]{2,1,0:T(8,128)S(1)} collective-permute-done((f32[4,64,128]{2,1,0:T(8,128)S(1)}, f32[4,64,128]{2,1,0:T(8,128)S(1)}, u32[]{:S(2)}, u32[]{:S(2)}) %collective-permute-start.35) | collective-permute-done | bytes 131104 | tf_op jit(solution)/shard_map/ppermute | solution.py:415
  191.6 12.0 %fourth.1 = (f32[3,4,64,128]{3,2,1,0:T(8,128)S(1)}, f32[3,4,64,128]{3,2,1,0:T(8,128)S(1)}, f32[3,4,64,128]{3,2,1,0:T(8,128)S(1)}, f32[3,4,64,128]{3,2,1,0:T(8,12...) custom-call(s32[1]{0:T(128)} %bitcast.odd_ref, ...), custom_call_target="tpu_custom_call" | custom-call | bytes 4194304 | tf_op jit(solution)/shard_map/fourth/pallas_call | solution.py:46
  209.1 7.3 %collective-permute-done.36.moved = f32[3,4,64,128]{3,2,1,0:T(8,128)S(1)} collective-permute-done((f32[3,4,64,128]{3,2,1,0:T(8,128)S(1)}, f32[3,4,64,128]{3,2,1,0:T(8,128)S(1)}, u32[]{:S(2)}, u32[]{:S(2)}) %collective-permute-start.36) | collective-permute-done | bytes 393248 | tf_op jit(solution)/shard_map/ppermute | solution.py:420
  216.4 8.4 %collective-permute-done.38 = f32[3,4,64,128]{3,2,1,0:T(8,128)S(1)} collective-permute-done((f32[3,4,64,128]{3,2,1,0:T(8,128)S(1)}, f32[3,4,64,128]{3,2,1,0:T(8,128)S(1)}, u32[]{:S(2)}, u32[]{:S(2)}) %collective-permute-start.38) | collective-permute-done | bytes 393248 | tf_op jit(solution)/shard_map/ppermute | solution.py:420
  225.1 3.8 %collective-permute-start.37 = (f32[3,2,64,128]{3,2,1,0:T(8,128)S(1)}, f32[3,2,64,128]{3,2,1,0:T(8,128)S(1)}, u32[]{:S(2)}, u32[]{:S(2)}) collective-permute-start(f32[3,2,64,128]{3,2,1,0:T(8,128)S(1)} %get-tuple-element.84), channel_id=1, source_target_pairs={{1,2},{3,4},{5,6},{7,8},{9,10},{11,12},{13,14},{2,1},{4,3},{6,5},{... | collective-permute-start | bytes 589832 | tf_op jit(solution)/shard_map/ppermute | solution.py:415
  228.9 6.2 %collective-permute-done.40 = f32[3,4,64,128]{3,2,1,0:T(8,128)S(1)} collective-permute-done((f32[3,4,64,128]{3,2,1,0:T(8,128)S(1)}, f32[3,4,64,128]{3,2,1,0:T(8,128)S(1)}, u32[]{:S(2)}, u32[]{:S(2)}) %collective-permute-start.40) | collective-permute-done | bytes 393248 | tf_op jit(solution)/shard_map/ppermute | solution.py:420
  (92 shorter events, 70.4 us)
Async XLA Ops:
  11.7 15.3 %collective-permute-start.8 = (f32[3,4,64,128]{3,2,1,0:T(8,128)S(1)}, f32[3,4,64,128]{3,2,1,0:T(8,128)S(1)}, u32[]{:S(2)}, u32[]{:S(2)}) collective-permute-start(f32[3,4,64,128]{3,2,1,0:T(8,128)S(1)} %first_middle.1.after), channel_id=1, source_target_pairs={{48,112},{112,48},{49,113},{113,49},{50,114},{114,50},{51,115},{11... | collective-permute-start | bytes 1179656 | tf_op jit(solution)/shard_map/ppermute | solution.py:420
  18.4 30.4 %collective-permute-start.6 = (f32[12,64,128]{2,1,0:T(8,128)S(1)}, f32[12,64,128]{2,1,0:T(8,128)S(1)}, u32[]{:S(2)}, u32[]{:S(2)}) collective-permute-start(f32[12,64,128]{2,1,0:T(8,128)S(1)} %get-tuple-element.58), channel_id=1, source_target_pairs={{1,2},{3,4},{5,6},{7,8},{9,10},{11,12},{13,14},{2,1},{4,3},{6,5},{... | collective-permute-start | bytes 1179656 | tf_op jit(solution)/shard_map/ppermute | solution.py:415
  24.5 25.4 %collective-permute-start.4 = (f32[3,4,64,128]{3,2,1,0:T(8,128)S(1)}, f32[3,4,64,128]{3,2,1,0:T(8,128)S(1)}, u32[]{:S(2)}, u32[]{:S(2)}) collective-permute-start(f32[3,4,64,128]{3,2,1,0:T(8,128)S(1)} %get-tuple-element.56), channel_id=1, source_target_pairs={{0,16},{16,32},{32,48},{48,64},{64,80},{80,96},{96,112},{112,0},{1... | collective-permute-start | bytes 1179656 | tf_op jit(solution)/shard_map/ppermute | solution.py:420
  25.8 24.3 %collective-permute-start.2 = (f32[3,4,64,128]{3,2,1,0:T(8,128)S(1)}, f32[3,4,64,128]{3,2,1,0:T(8,128)S(1)}, u32[]{:S(2)}, u32[]{:S(2)}) collective-permute-start(f32[3,4,64,128]{3,2,1,0:T(8,128)S(1)} %get-tuple-element.52), channel_id=1, source_target_pairs={{0,16},{16,32},{32,48},{48,64},{64,80},{80,96},{96,112},{112,0},{1... | collective-permute-start | bytes 1179656 | tf_op jit(solution)/shard_map/ppermute | solution.py:420
  27.0 26.6 %collective-permute-start.10 = (f32[3,4,64,128]{3,2,1,0:T(8,128)S(1)}, f32[3,4,64,128]{3,2,1,0:T(8,128)S(1)}, u32[]{:S(2)}, u32[]{:S(2)}) collective-permute-start(f32[3,4,64,128]{3,2,1,0:T(8,128)S(1)} %first_middle.1.after), channel_id=1, source_target_pairs={{0,16},{16,32},{32,48},{64,80},{80,96},{96,112},{1,17},{17,33},{33... | collective-permute-start | bytes 1179656 | tf_op jit(solution)/shard_map/ppermute | solution.py:420
  29.8 26.1 %collective-permute-start.9 = (f32[3,4,64,128]{3,2,1,0:T(8,128)S(1)}, f32[3,4,64,128]{3,2,1,0:T(8,128)S(1)}, u32[]{:S(2)}, u32[]{:S(2)}) collective-permute-start(f32[3,4,64,128]{3,2,1,0:T(8,128)S(1)} %collective-permute-done.8), channel_id=1, source_target_pairs={{112,64},{48,0},{113,65},{49,1},{114,66},{50,2},{115,67},{51,3},{1... | collective-permute-start | bytes 1179656 | tf_op jit(solution)/shard_map/ppermute | solution.py:420
  50.1 13.3 %collective-permute-start.3 = (f32[3,4,64,128]{3,2,1,0:T(8,128)S(1)}, f32[3,4,64,128]{3,2,1,0:T(8,128)S(1)}, u32[]{:S(2)}, u32[]{:S(2)}) collective-permute-start(f32[3,4,64,128]{3,2,1,0:T(8,128)S(1)} %collective-permute-done.2.vb), channel_id=1, source_target_pairs={{1,2},{3,4},{5,6},{7,8},{9,10},{11,12},{13,14},{2,1},{4,3},{6,5},{... | collective-permute-start | bytes 1179656 | tf_op jit(solution)/shard_map/ppermute | solution.py:415
  68.6 14.9 %collective-permute-start.11 = (f32[3,4,64,128]{3,2,1,0:T(8,128)S(1)}, f32[3,4,64,128]{3,2,1,0:T(8,128)S(1)}, u32[]{:S(2)}, u32[]{:S(2)}) collective-permute-start(f32[3,4,64,128]{3,2,1,0:T(8,128)S(1)} %get-tuple-element.63), channel_id=1, source_target_pairs={{0,16},{16,32},{32,48},{48,64},{64,80},{80,96},{96,112},{112,0},{1... | collective-permute-start | bytes 1179656 | tf_op jit(solution)/shard_map/ppermute | solution.py:420
  68.6 25.8 %collective-permute-start.13 = (f32[3,4,64,128]{3,2,1,0:T(8,128)S(1)}, f32[3,4,64,128]{3,2,1,0:T(8,128)S(1)}, u32[]{:S(2)}, u32[]{:S(2)}) collective-permute-start(f32[3,4,64,128]{3,2,1,0:T(8,128)S(1)} %get-tuple-element.64), channel_id=1, source_target_pairs={{0,16},{16,32},{32,48},{48,64},{64,80},{80,96},{96,112},{112,0},{1... | collective-permute-start | bytes 1179656 | tf_op jit(solution)/shard_map/ppermute | solution.py:420
  68.7 25.7 %collective-permute-start.15 = (f32[3,4,64,128]{3,2,1,0:T(8,128)S(1)}, f32[3,4,64,128]{3,2,1,0:T(8,128)S(1)}, u32[]{:S(2)}, u32[]{:S(2)}) collective-permute-start(f32[3,4,64,128]{3,2,1,0:T(8,128)S(1)} %get-tuple-element.65), channel_id=1, source_target_pairs={{48,112},{112,48},{49,113},{113,49},{50,114},{114,50},{51,115},{11... | collective-permute-start | bytes 1179656 | tf_op jit(solution)/shard_map/ppermute | solution.py:420
  69.4 26.3 %collective-permute-start.17 = (f32[3,4,64,128]{3,2,1,0:T(8,128)S(1)}, f32[3,4,64,128]{3,2,1,0:T(8,128)S(1)}, u32[]{:S(2)}, u32[]{:S(2)}) collective-permute-start(f32[3,4,64,128]{3,2,1,0:T(8,128)S(1)} %get-tuple-element.65), channel_id=1, source_target_pairs={{0,16},{16,32},{32,48},{64,80},{80,96},{96,112},{1,17},{17,33},{33... | collective-permute-start | bytes 1179656 | tf_op jit(solution)/shard_map/ppermute | solution.py:420
  113.6 23.4 %collective-permute-start.20 = (f32[3,4,64,128]{3,2,1,0:T(8,128)S(1)}, f32[3,4,64,128]{3,2,1,0:T(8,128)S(1)}, u32[]{:S(2)}, u32[]{:S(2)}) collective-permute-start(f32[3,4,64,128]{3,2,1,0:T(8,128)S(1)} %get-tuple-element.72), channel_id=1, source_target_pairs={{0,16},{16,32},{32,48},{48,64},{64,80},{80,96},{96,112},{112,0},{1... | collective-permute-start | bytes 1179656 | tf_op jit(solution)/shard_map/ppermute | solution.py:420
  113.9 27.5 %collective-permute-start.24 = (f32[3,4,64,128]{3,2,1,0:T(8,128)S(1)}, f32[3,4,64,128]{3,2,1,0:T(8,128)S(1)}, u32[]{:S(2)}, u32[]{:S(2)}) collective-permute-start(f32[3,4,64,128]{3,2,1,0:T(8,128)S(1)} %get-tuple-element.74), channel_id=1, source_target_pairs={{0,16},{16,32},{32,48},{64,80},{80,96},{96,112},{1,17},{17,33},{33... | collective-permute-start | bytes 1179656 | tf_op jit(solution)/shard_map/ppermute | solution.py:420
  116.9 24.5 %collective-permute-start.23 = (f32[3,4,64,128]{3,2,1,0:T(8,128)S(1)}, f32[3,4,64,128]{3,2,1,0:T(8,128)S(1)}, u32[]{:S(2)}, u32[]{:S(2)}) collective-permute-start(f32[3,4,64,128]{3,2,1,0:T(8,128)S(1)} %collective-permute-done.22), channel_id=1, source_target_pairs={{112,64},{48,0},{113,65},{49,1},{114,66},{50,2},{115,67},{51,3},{1... | collective-permute-start | bytes 1179656 | tf_op jit(solution)/shard_map/ppermute | solution.py:420
  126.5 14.9 %collective-permute-start.19 = (f32[3,4,64,128]{3,2,1,0:T(8,128)S(1)}, f32[3,4,64,128]{3,2,1,0:T(8,128)S(1)}, u32[]{:S(2)}, u32[]{:S(2)}) collective-permute-start(f32[3,4,64,128]{3,2,1,0:T(8,128)S(1)} %add.35.sb), channel_id=1, source_target_pairs={{1,2},{3,4},{5,6},{7,8},{9,10},{11,12},{13,14},{2,1},{4,3},{6,5},{... | collective-permute-start | bytes 1179656 | tf_op jit(solution)/shard_map/ppermute | solution.py:415
  148.2 14.3 %collective-permute-start.27 = (f32[3,4,64,128]{3,2,1,0:T(8,128)S(1)}, f32[3,4,64,128]{3,2,1,0:T(8,128)S(1)}, u32[]{:S(2)}, u32[]{:S(2)}) collective-permute-start(f32[3,4,64,128]{3,2,1,0:T(8,128)S(1)} %get-tuple-element.76), channel_id=1, source_target_pairs={{0,32},{16,48},{32,64},{48,80},{64,96},{80,112},{96,0},{112,16},{1... | collective-permute-start | bytes 1179656 | tf_op jit(solution)/shard_map/ppermute | solution.py:420
  148.8 22.2 %collective-permute-start.25 = (f32[3,4,64,128]{3,2,1,0:T(8,128)S(1)}, f32[3,4,64,128]{3,2,1,0:T(8,128)S(1)}, u32[]{:S(2)}, u32[]{:S(2)}) collective-permute-start(f32[3,4,64,128]{3,2,1,0:T(8,128)S(1)} %get-tuple-element.75), channel_id=1, source_target_pairs={{0,32},{16,48},{32,64},{48,80},{64,96},{80,112},{96,0},{112,16},{1... | collective-permute-start | bytes 1179656 | tf_op jit(solution)/shard_map/ppermute | solution.py:420
  154.0 20.9 %collective-permute-start.32 = (f32[3,4,64,128]{3,2,1,0:T(8,128)S(1)}, f32[3,4,64,128]{3,2,1,0:T(8,128)S(1)}, u32[]{:S(2)}, u32[]{:S(2)}) collective-permute-start(f32[3,4,64,128]{3,2,1,0:T(8,128)S(1)} %get-tuple-element.77), channel_id=1, source_target_pairs={{0,32},{16,48},{64,96},{80,112},{1,33},{17,49},{65,97},{81,113},{2... | collective-permute-start | bytes 1179656 | tf_op jit(solution)/shard_map/ppermute | solution.py:420
  156.0 22.7 %collective-permute-start.31 = (f32[3,4,64,128]{3,2,1,0:T(8,128)S(1)}, f32[3,4,64,128]{3,2,1,0:T(8,128)S(1)}, u32[]{:S(2)}, u32[]{:S(2)}) collective-permute-start(f32[3,4,64,128]{3,2,1,0:T(8,128)S(1)} %collective-permute-done.30), channel_id=1, source_target_pairs={{96,64},{112,80},{32,0},{48,16},{97,65},{113,81},{33,1},{49,17},{9... | collective-permute-start | bytes 1179656 | tf_op jit(solution)/shard_map/ppermute | solution.py:420
  162.6 29.0 %collective-permute-start.29 = (f32[3,4,64,128]{3,2,1,0:T(8,128)S(1)}, f32[3,4,64,128]{3,2,1,0:T(8,128)S(1)}, u32[]{:S(2)}, u32[]{:S(2)}) collective-permute-start(f32[3,4,64,128]{3,2,1,0:T(8,128)S(1)} %add.40.tm), channel_id=1, source_target_pairs={{0,1},{1,0},{2,3},{3,2},{4,5},{5,4},{6,7},{7,6},{8,9},{9,8},{10,11... | collective-permute-start | bytes 1179656 | tf_op jit(solution)/shard_map/ppermute | solution.py:412
  164.7 27.0 %collective-permute-start.28 = (f32[3,4,64,128]{3,2,1,0:T(8,128)S(1)}, f32[3,4,64,128]{3,2,1,0:T(8,128)S(1)}, u32[]{:S(2)}, u32[]{:S(2)}) collective-permute-start(f32[3,4,64,128]{3,2,1,0:T(8,128)S(1)} %add.40.tm), channel_id=1, source_target_pairs={{1,2},{3,4},{5,6},{7,8},{9,10},{11,12},{13,14},{2,1},{4,3},{6,5},{... | collective-permute-start | bytes 1179656 | tf_op jit(solution)/shard_map/ppermute | solution.py:415
  171.0 20.6 %collective-permute-start.26 = (f32[3,4,64,128]{3,2,1,0:T(8,128)S(1)}, f32[3,4,64,128]{3,2,1,0:T(8,128)S(1)}, u32[]{:S(2)}, u32[]{:S(2)}) collective-permute-start(f32[3,4,64,128]{3,2,1,0:T(8,128)S(1)} %add.39.tb), channel_id=1, source_target_pairs={{1,2},{3,4},{5,6},{7,8},{9,10},{11,12},{13,14},{2,1},{4,3},{6,5},{... | collective-permute-start | bytes 1179656 | tf_op jit(solution)/shard_map/ppermute | solution.py:415
  206.1 18.7 %collective-permute-start.38 = (f32[3,4,64,128]{3,2,1,0:T(8,128)S(1)}, f32[3,4,64,128]{3,2,1,0:T(8,128)S(1)}, u32[]{:S(2)}, u32[]{:S(2)}) collective-permute-start(f32[3,4,64,128]{3,2,1,0:T(8,128)S(1)} %get-tuple-element.87), channel_id=1, source_target_pairs={{0,64},{16,80},{32,96},{48,112},{64,0},{80,16},{96,32},{112,48},{1... | collective-permute-start | bytes 1179656 | tf_op jit(solution)/shard_map/ppermute | solution.py:420
  206.7 28.4 %collective-permute-start.40 = (f32[3,4,64,128]{3,2,1,0:T(8,128)S(1)}, f32[3,4,64,128]{3,2,1,0:T(8,128)S(1)}, u32[]{:S(2)}, u32[]{:S(2)}) collective-permute-start(f32[3,4,64,128]{3,2,1,0:T(8,128)S(1)} %get-tuple-element.90), channel_id=1, source_target_pairs={{0,64},{16,80},{32,96},{48,112},{64,0},{80,16},{96,32},{112,48},{1... | collective-permute-start | bytes 1179656 | tf_op jit(solution)/shard_map/ppermute | solution.py:420
  (24 other events, 186.1 us)

commit v6 on v5

--- a/solution.py
+++ b/solution.py
@@ -151,16 +151,26 @@
     return (1 - odd) * (n - width), odd * (n - width)
 
 
-def first_pack_kernel(odd_ref, guess, source, regions, a1, b1, reg, sems):
-    odd = odd_ref[0]
-    pairs = [(regions.at[pl.ds(0, 1)], reg.at[pl.ds(0, 1)]), (regions.at[pl.ds(LX - 1, 1)], reg.at[pl.ds(1, 1)])]
-    for one, two_from, one_from in zip((a1, b1), edges(odd, LX, 2), edges(odd, LX, 1)):
+def first_pack_kernel(odd_ref, g_low, g_high, s_low, s_high, r_low, r_high, a1, b1):
+    odd = odd_ref[0]
+
+    def fill(low, high):
         for c in range(3):
-            pairs.append((guess.at[0, c, pl.ds(two_from, 2)], one.at[pl.ds(2 * c, 2)]))
-            pairs.append((source.at[1, c, pl.ds(one_from, 1)], one.at[pl.ds(6 + c, 1)]))
-    run_copies(pairs, sems)
-    a1[9] = (reg[1 - odd] + 1).astype(F32)
-    b1[9] = (reg[odd] + 1).astype(F32)
+            for k in range(2):
+                low[2 * c + k] = g_low[0, c, k]
+                high[2 * c + k] = g_high[0, c, k]
+            low[6 + c] = s_low[0, c, 0]
+            high[6 + c] = s_high[0, c, 0]
+        low[9] = (r_low[0] + 1).astype(F32)
+        high[9] = (r_high[0] + 1).astype(F32)
+
+    @pl.when(odd == 0)
+    def even_slab():
+        fill(b1, a1)
+
+    @pl.when(odd == 1)
+    def odd_slab():
+        fill(a1, b1)
 
 
 def second_pack_kernel(odd_ref, source, regions, a2, b2, a3, b3, reg, sems):
@@ -321,9 +331,9 @@
     fine_sweep(y, less, held, cond, nu, 2, 18, None, 1)
     kept = copy_all([(x.at[:, pl.ds(4, LX)], res_o.at[0])], sems)
     split(odd, x, 4, rb, ra, rm)
-    coarse_sweep(x, put(y), held, keep, spread, -1, 3, 17, True, COMPS)
+    coarse_sweep(x, put(y), held, keep, spread, 3, 3, 17, True, COMPS)
     wait_all(kept)
-    coarse_sweep(y, put(x), held, keep, spread, -1, 4, 16, False, COMPS)
+    coarse_sweep(y, put(x), held, keep, spread, 3, 4, 16, False, COMPS)
     split(odd, x, 4, lb, la, lm)
 
 
@@ -431,8 +441,9 @@
 
     tables = (conductance, reluct)
     sa1, sb1 = call(
-        first_pack_kernel, "first_pack", (odd, guess, source, regions),
-        [planes(10), planes(10)], [pltpu.VMEM((2, NY, NZ), jnp.int32)], 16, in_place=HBM,
+        first_pack_kernel, "first_pack",
+        (odd, guess[:1, :, :2], guess[:1, :, LX - 2:], source[1:, :, :1], source[1:, :, LX - 1:], regions[:1], regions[LX - 1:]),
+        [planes(10), planes(10)], [],
     )
     b1 = from_b(sb1)
     a1 = from_a(sa1)
@@ -457,36 +468,39 @@
     cond, nu, keep, spread = call(
         material_kernel, "material", (odd, *tables, regions, a2, b2), [planes(LX + 6)] * 4, [],
     )
-    va, cond = fence((va, cond))
+    vb, cond = fence((vb, cond))
     hb = from_b(vb)
+    va, *vm = fence((va, *vm))
     ha = from_a(va)
-    sb3, sa3, vb = fence((sb3, sa3, vb))
-    b3 = from_b(sb3)
-    a3 = from_a(sa3)
     n = LX + 8
     u0, ua, ub, um = call(
         second_kernel, "second",
         (odd, hb, vb, ha, va, *vm, source, a1, b1, a2, b2, cond, nu),
         [planes(3, LX + 4), planes(3, 4), planes(3, 4), planes(3, 4)], [vmem(3, n)] * 5,
     )
+    sb3, sa3, ub = fence((sb3, sa3, ub))
     vb = later(ub, 1)
     va = later(ua, 1)
-    vm = later_parts(um, 1)
+    around, plain = later_parts(um, 1)
     hb = from_b(vb)
-    ha = from_a(va)
+    b3 = from_b(sb3)
+    a3 = from_a(sa3)
     wide_keep, wide_spread = call(
         wide_kernel, "wide", (odd, *tables, keep, spread, a3, b3), [planes(LX + 14)] * 2, [],
     )
+    va, around, wide_keep = fence((va, around, wide_keep))
+    ha = from_a(va)
     residual, lb, la, lm, rb, ra, rm = call(
         residual_kernel, "residual",
-        (odd, hb, vb, ha, va, *vm, source, a2, b2, cond, nu, keep, spread, u0),
+        (odd, hb, vb, ha, va, around, plain, source, a2, b2, cond, nu, wide_keep, wide_spread, u0),
         [planes(1, 3, LX)] + [planes(3, 4)] * 6, [vmem(3, n)] * 4, 1, [ANY] + [VMEM] * 6,
     )
     sb = rb + later(lb, 1)
     hb = from_b(sb)
-    sa = ra + later(la, 1)
+    around, plain = later_parts(lm, 1)
+    moved, around = fence((later(la, 1), around))
+    sa = ra + moved
     ha = from_a(sa)
-    around, plain = later_parts(lm, 1)
     sm = rm + (around + plain)
     lb, la, lm = call(
         square_kernel, "square", (odd, hb, sb, ha, sa, sm, keep, spread),
@@ -509,7 +523,8 @@
         edge_kernel, "edge", (odd, bb, later(lb, half)), [planes(3, 4), planes(3, 2)], [],
     )
     hb = from_b(edge)
-    ea, edge = lax.optimization_barrier((ba + later(la, half), edge))
+    moved, hb = fence((later(la, half), hb))
+    ea = ba + moved
     ha = from_a(ea)
     em = bm + later(lm, half)
     field = call(

time: 239 us -> 232 us (0.971)
  waiting for transfers between devices: 123 us -> 108 us
  local copies, waits for them, and re-layouts: 4.33 us -> 8.44 us
  starting transfers between devices: 71.9 us -> 74.5 us
    ppermute x23, waiting for transfers between devices: 83.1 us -> 71.1 us  [along(): return lax.ppermute(x, 'tm', pairs)]
    ppermute x23, starting transfers between devices: 31.2 us -> 36.7 us  [along(): return lax.ppermute(x, 'tm', pairs)]
    ppermute x9, starting transfers between devices: 9.89 us -> 5.82 us  [from_a(): return lax.ppermute(x, 'space', on_chip)]
    slice x0 -> x3, local copies, waits for them, and re-layouts: none -> 2.8 us  [the longest x1 1.06 us: body(): guess[:1, :, LX - 2:]]
    unnamed x14 -> x16, local copies, waits for them, and re-layouts: 4.33 us -> 5.65 us
  transfers between devices with their start and end apart: 41 -> 41, of which waited for: 21 -> 20; matrix products, arithmetic and copies ran while one was open for 0% -> 0% of each run, Pallas kernels for 3% -> 3%
where the time goes in v6:
time: 232 us; the launch traced here: 230 us
  waiting for transfers between devices  108 us (47%)
  starting transfers between devices  74.5 us (32%)
  Pallas kernels  36.8 us (16%)
  local copies, waits for them, and re-layouts  8.44 us (4%)
    ppermute x23, waiting for transfers between devices, along(): return lax.ppermute(x, 'tm', pairs)  71.1 us
    pallas_call x12, Pallas kernels, call(): pl.pallas_call(kernel, name=name, out_shape=outs, in_specs=in_specs, out_...  36.8 us
    ppermute x23, starting transfers between devices, along(): return lax.ppermute(x, 'tm', pairs)  36.7 us
    ppermute x9, waiting for transfers between devices, from_b(): return lax.ppermute(x, 'space', off_chip)  35.1 us
    ppermute x9, starting transfers between devices, from_b(): return lax.ppermute(x, 'space', off_chip)  32 us
    ppermute x9, starting transfers between devices, from_a(): return lax.ppermute(x, 'space', on_chip)  5.82 us
    unnamed x16, local copies, waits for them, and re-layouts  5.65 us
  transfers between devices with their start and end apart: 41, of which 20 were waited for; matrix products, arithmetic and copies ran while one was open for 0% of the time, Pallas kernels for 3%

profile of v6, /device:TPU:17, one launch (start us, length us, event | category | flops | bytes accessed | tf_op | source)
XLA Modules:
  0.0 229.6 jit_solution(16320436722264236016)
XLA Ops:
  26.9 4.8 %collective-permute-start.6 = (f32[3,4,64,128]{3,2,1,0:T(8,128)S(1)}, f32[3,4,64,128]{3,2,1,0:T(8,128)S(1)}, u32[]{:S(2)}, u32[]{:S(2)}) collective-permute-start(f32[3,4,64,128]{3,2,1,0:T(8,128)S(1)} %get-tuple-element.68), channel_id=1, source_target_pairs={{0,16},{16,32},{32,48},{48,64},{64,80},{80,96},{96,112},{112,0},{1... | collective-permute-start | bytes 1179656 | tf_op jit(solution)/shard_map/ppermute | solution.py:430
  34.0 4.1 %collective-permute-done.2.vb = f32[3,4,64,128]{3,2,1,0:T(8,128)S(1)} collective-permute-done((f32[3,4,64,128]{3,2,1,0:T(8,128)S(1)}, f32[3,4,64,128]{3,2,1,0:T(8,128)S(1)}, u32[]{:S(2)}, u32[]{:S(2)}) %collective-permute-start.2) | collective-permute-done | bytes 393248 | tf_op jit(solution)/shard_map/ppermute | solution.py:430
  41.7 7.2 %collective-permute-done.6.va = f32[3,4,64,128]{3,2,1,0:T(8,128)S(1)} collective-permute-done((f32[3,4,64,128]{3,2,1,0:T(8,128)S(1)}, f32[3,4,64,128]{3,2,1,0:T(8,128)S(1)}, u32[]{:S(2)}, u32[]{:S(2)}) %collective-permute-start.6) | collective-permute-done | bytes 393248 | tf_op jit(solution)/shard_map/ppermute | solution.py:430
  48.9 5.8 %collective-permute-done.8.vm = f32[3,4,64,128]{3,2,1,0:T(8,128)S(1)} collective-permute-done((f32[3,4,64,128]{3,2,1,0:T(8,128)S(1)}, f32[3,4,64,128]{3,2,1,0:T(8,128)S(1)}, u32[]{:S(2)}, u32[]{:S(2)}) %collective-permute-start.8) | collective-permute-done | bytes 393248 | tf_op jit(solution)/shard_map/ppermute | solution.py:430
  57.2 5.1 %second.1 = (f32[3,16,64,128]{3,2,1,0:T(8,128)S(1)}, f32[3,4,64,128]{3,2,1,0:T(8,128)S(1)}, f32[3,4,64,128]{3,2,1,0:T(8,128)S(1)}, f32[3,4,64,128]{3,2,1,0:T(8,128)S(1)}) custom-call(s32[1]{0:T(128)} %bitcast.odd_ref, f32[3,4,64,128]{3,2,1,0:T(8,128)S(1)} %collective-permute-done.5.hb, f32[3,4,64,128]{3,2,1,0:T(8,128)S(1)} %collective-permute-done.2.vb, ...), custom_call_target="tpu_custom_call" | custom-call | bytes 4194304 | tf_op jit(solution)/shard_map/second/pallas_call | solution.py:46
  69.5 4.6 %collective-permute-start.19 = (f32[3,4,64,128]{3,2,1,0:T(8,128)S(1)}, f32[3,4,64,128]{3,2,1,0:T(8,128)S(1)}, u32[]{:S(2)}, u32[]{:S(2)}) collective-permute-start(f32[3,4,64,128]{3,2,1,0:T(8,128)S(1)} %get-tuple-element.77), channel_id=1, source_target_pairs={{0,16},{16,32},{32,48},{64,80},{80,96},{96,112},{1,17},{17,33},{33... | collective-permute-start | bytes 1179656 | tf_op jit(solution)/shard_map/ppermute | solution.py:430
  74.2 19.5 %collective-permute-done.17.rb = f32[4,64,128]{2,1,0:T(8,128)S(1)} collective-permute-done((f32[4,64,128]{2,1,0:T(8,128)S(1)}, f32[4,64,128]{2,1,0:T(8,128)S(1)}, u32[]{:S(2)}, u32[]{:S(2)}) %collective-permute-start.17) | collective-permute-done | bytes 131104 | tf_op jit(solution)/shard_map/ppermute | solution.py:425
  94.5 4.3 %collective-permute-start.12 = (f32[3,4,64,128]{3,2,1,0:T(8,128)S(1)}, f32[3,4,64,128]{3,2,1,0:T(8,128)S(1)}, u32[]{:S(2)}, u32[]{:S(2)}) collective-permute-start(f32[3,4,64,128]{3,2,1,0:T(8,128)S(1)} %collective-permute-done.11.vb), channel_id=1, source_target_pairs={{1,2},{3,4},{5,6},{7,8},{9,10},{11,12},{13,14},{2,1},{4,3},{6,5},{... | collective-permute-start | bytes 1179656 | tf_op jit(solution)/shard_map/ppermute | solution.py:425
  99.0 5.1 %collective-permute-done.12.hb = f32[3,4,64,128]{3,2,1,0:T(8,128)S(1)} collective-permute-done((f32[3,4,64,128]{3,2,1,0:T(8,128)S(1)}, f32[3,4,64,128]{3,2,1,0:T(8,128)S(1)}, u32[]{:S(2)}, u32[]{:S(2)}) %collective-permute-start.12) | collective-permute-done | bytes 393248 | tf_op jit(solution)/shard_map/ppermute | solution.py:425
  104.2 5.2 %residual.1 = (f32[1,3,12,64,128]{4,3,2,1,0:T(8,128)}, f32[3,4,64,128]{3,2,1,0:T(8,128)S(1)}, f32[3,4,64,128]{3,2,1,0:T(8,128)S(1)}, f32[3,4,64,128]{3,2,1,0:T(8...) custom-call(s32[1]{0:T(128)} %bitcast.odd_ref, ...), custom_call_target="tpu_custom_call" | custom-call | bytes 4194304 | tf_op jit(solution)/shard_map/residual/pallas_call | solution.py:46
  113.0 12.9 %collective-permute-done.20 = f32[3,4,64,128]{3,2,1,0:T(8,128)S(1)} collective-permute-done((f32[3,4,64,128]{3,2,1,0:T(8,128)S(1)}, f32[3,4,64,128]{3,2,1,0:T(8,128)S(1)}, u32[]{:S(2)}, u32[]{:S(2)}) %collective-permute-start.20) | collective-permute-done | bytes 393248 | tf_op jit(solution)/shard_map/ppermute | solution.py:430
  125.9 4.5 %collective-permute-start.21 = (f32[3,4,64,128]{3,2,1,0:T(8,128)S(1)}, f32[3,4,64,128]{3,2,1,0:T(8,128)S(1)}, u32[]{:S(2)}, u32[]{:S(2)}) collective-permute-start(f32[3,4,64,128]{3,2,1,0:T(8,128)S(1)} %add.35.sb), channel_id=1, source_target_pairs={{1,2},{3,4},{5,6},{7,8},{9,10},{11,12},{13,14},{2,1},{4,3},{6,5},{... | collective-permute-start | bytes 1179656 | tf_op jit(solution)/shard_map/ppermute | solution.py:425
  130.3 4.1 %collective-permute-done.22 = f32[3,4,64,128]{3,2,1,0:T(8,128)S(1)} collective-permute-done((f32[3,4,64,128]{3,2,1,0:T(8,128)S(1)}, f32[3,4,64,128]{3,2,1,0:T(8,128)S(1)}, u32[]{:S(2)}, u32[]{:S(2)}) %collective-permute-start.22) | collective-permute-done | bytes 393248 | tf_op jit(solution)/shard_map/ppermute | solution.py:430
  138.3 4.8 %square.1 = (f32[3,4,64,128]{3,2,1,0:T(8,128)S(1)}, f32[3,4,64,128]{3,2,1,0:T(8,128)S(1)}, f32[3,4,64,128]{3,2,1,0:T(8,128)S(1)}) custom-call(s32[1]{0:T(128)} %bitcast.odd_ref, f32[3,4,64,128]{3,2,1,0:T(8,128)S(1)} %collective-permute-done.21.hb, f32[3,4,64,128]{3,2,1,0:T(8,128)S(1)} %add.35.sb, f32[3,4,64,128]{3,2,1,0:T(8,128)S(1)} %collective-permute-done.25.ha, ...), custom_call_target="tpu_custom_call" | custom-call | bytes 4194304 | tf_op jit(solution)/shard_map/square/pallas_call | solution.py:46
  143.8 6.5 %collective-permute-start.27 = (f32[3,4,64,128]{3,2,1,0:T(8,128)S(1)}, f32[3,4,64,128]{3,2,1,0:T(8,128)S(1)}, u32[]{:S(2)}, u32[]{:S(2)}) collective-permute-start(f32[3,4,64,128]{3,2,1,0:T(8,128)S(1)} %get-tuple-element.96), channel_id=1, source_target_pairs={{0,32},{16,48},{32,64},{48,80},{64,96},{80,112},{96,0},{112,16},{1... | collective-permute-start | bytes 1179656 | tf_op jit(solution)/shard_map/ppermute | solution.py:430
  153.6 4.7 %collective-permute-done.29 = f32[3,4,64,128]{3,2,1,0:T(8,128)S(1)} collective-permute-done((f32[3,4,64,128]{3,2,1,0:T(8,128)S(1)}, f32[3,4,64,128]{3,2,1,0:T(8,128)S(1)}, u32[]{:S(2)}, u32[]{:S(2)}) %collective-permute-start.29) | collective-permute-done | bytes 393248 | tf_op jit(solution)/shard_map/ppermute | solution.py:430
  162.6 4.1 %collective-permute-done.27 = f32[3,4,64,128]{3,2,1,0:T(8,128)S(1)} collective-permute-done((f32[3,4,64,128]{3,2,1,0:T(8,128)S(1)}, f32[3,4,64,128]{3,2,1,0:T(8,128)S(1)}, u32[]{:S(2)}, u32[]{:S(2)}) %collective-permute-start.27) | collective-permute-done | bytes 393248 | tf_op jit(solution)/shard_map/ppermute | solution.py:430
  166.8 4.3 %collective-permute-start.28 = (f32[3,4,64,128]{3,2,1,0:T(8,128)S(1)}, f32[3,4,64,128]{3,2,1,0:T(8,128)S(1)}, u32[]{:S(2)}, u32[]{:S(2)}) collective-permute-start(f32[3,4,64,128]{3,2,1,0:T(8,128)S(1)} %add.39.tb), channel_id=1, source_target_pairs={{1,2},{3,4},{5,6},{7,8},{9,10},{11,12},{13,14},{2,1},{4,3},{6,5},{... | collective-permute-start | bytes 1179656 | tf_op jit(solution)/shard_map/ppermute | solution.py:425
  171.1 5.2 %collective-permute-done.33 = f32[3,4,64,128]{3,2,1,0:T(8,128)S(1)} collective-permute-done((f32[3,4,64,128]{3,2,1,0:T(8,128)S(1)}, f32[3,4,64,128]{3,2,1,0:T(8,128)S(1)}, u32[]{:S(2)}, u32[]{:S(2)}) %collective-permute-start.33) | collective-permute-done | bytes 393248 | tf_op jit(solution)/shard_map/ppermute | solution.py:430
  177.4 6.8 %collective-permute-done.28.near_b = f32[3,4,64,128]{3,2,1,0:T(8,128)S(1)} collective-permute-done((f32[3,4,64,128]{3,2,1,0:T(8,128)S(1)}, f32[3,4,64,128]{3,2,1,0:T(8,128)S(1)}, u32[]{:S(2)}, u32[]{:S(2)}) %collective-permute-start.28) | collective-permute-done | bytes 393248 | tf_op jit(solution)/shard_map/ppermute | solution.py:425
  184.2 11.9 %fourth.1 = (f32[3,4,64,128]{3,2,1,0:T(8,128)S(1)}, f32[3,4,64,128]{3,2,1,0:T(8,128)S(1)}, f32[3,4,64,128]{3,2,1,0:T(8,128)S(1)}, f32[3,4,64,128]{3,2,1,0:T(8,12...) custom-call(s32[1]{0:T(128)} %bitcast.odd_ref, ...), custom_call_target="tpu_custom_call" | custom-call | bytes 4194304 | tf_op jit(solution)/shard_map/fourth/pallas_call | solution.py:46
  199.2 11.8 %collective-permute-done.37.moved = f32[3,4,64,128]{3,2,1,0:T(8,128)S(1)} collective-permute-done((f32[3,4,64,128]{3,2,1,0:T(8,128)S(1)}, f32[3,4,64,128]{3,2,1,0:T(8,128)S(1)}, u32[]{:S(2)}, u32[]{:S(2)}) %collective-permute-start.37) | collective-permute-done | bytes 393248 | tf_op jit(solution)/shard_map/ppermute | solution.py:430
  214.5 4.3 %collective-permute-done.36 = f32[3,4,64,128]{3,2,1,0:T(8,128)S(1)} collective-permute-done((f32[3,4,64,128]{3,2,1,0:T(8,128)S(1)}, f32[3,4,64,128]{3,2,1,0:T(8,128)S(1)}, u32[]{:S(2)}, u32[]{:S(2)}) %collective-permute-start.36) | collective-permute-done | bytes 393248 | tf_op jit(solution)/shard_map/ppermute | solution.py:430
  221.6 4.9 %collective-permute-done.40 = f32[3,4,64,128]{3,2,1,0:T(8,128)S(1)} collective-permute-done((f32[3,4,64,128]{3,2,1,0:T(8,128)S(1)}, f32[3,4,64,128]{3,2,1,0:T(8,128)S(1)}, u32[]{:S(2)}, u32[]{:S(2)}) %collective-permute-start.40) | collective-permute-done | bytes 393248 | tf_op jit(solution)/shard_map/ppermute | solution.py:430
  (97 shorter events, 71.7 us)
Async XLA Ops:
  16.6 15.1 %collective-permute-start.3 = (f32[12,64,128]{2,1,0:T(8,128)S(1)}, f32[12,64,128]{2,1,0:T(8,128)S(1)}, u32[]{:S(2)}, u32[]{:S(2)}) collective-permute-start(f32[12,64,128]{2,1,0:T(8,128)S(1)} %get-tuple-element.64), channel_id=1, source_target_pairs={{0,1},{1,0},{2,3},{3,2},{4,5},{5,4},{6,7},{7,6},{8,9},{9,8},{10,11... | collective-permute-start | bytes 1179656 | tf_op jit(solution)/shard_map/ppermute | solution.py:422
  17.2 15.8 %collective-permute-start.4 = (f32[12,64,128]{2,1,0:T(8,128)S(1)}, f32[12,64,128]{2,1,0:T(8,128)S(1)}, u32[]{:S(2)}, u32[]{:S(2)}) collective-permute-start(f32[12,64,128]{2,1,0:T(8,128)S(1)} %get-tuple-element.65), channel_id=1, source_target_pairs={{1,2},{3,4},{5,6},{7,8},{9,10},{11,12},{13,14},{2,1},{4,3},{6,5},{... | collective-permute-start | bytes 1179656 | tf_op jit(solution)/shard_map/ppermute | solution.py:425
  22.5 15.7 %collective-permute-start.2 = (f32[3,4,64,128]{3,2,1,0:T(8,128)S(1)}, f32[3,4,64,128]{3,2,1,0:T(8,128)S(1)}, u32[]{:S(2)}, u32[]{:S(2)}) collective-permute-start(f32[3,4,64,128]{3,2,1,0:T(8,128)S(1)} %get-tuple-element.63), channel_id=1, source_target_pairs={{0,16},{16,32},{32,48},{48,64},{64,80},{80,96},{96,112},{112,0},{1... | collective-permute-start | bytes 1179656 | tf_op jit(solution)/shard_map/ppermute | solution.py:430
  23.8 17.9 %collective-permute-start.9 = (f32[3,4,64,128]{3,2,1,0:T(8,128)S(1)}, f32[3,4,64,128]{3,2,1,0:T(8,128)S(1)}, u32[]{:S(2)}, u32[]{:S(2)}) collective-permute-start(f32[3,4,64,128]{3,2,1,0:T(8,128)S(1)} %first_middle.1.after), channel_id=1, source_target_pairs={{0,16},{16,32},{32,48},{64,80},{80,96},{96,112},{1,17},{17,33},{33... | collective-permute-start | bytes 1179656 | tf_op jit(solution)/shard_map/ppermute | solution.py:430
  26.9 22.0 %collective-permute-start.6 = (f32[3,4,64,128]{3,2,1,0:T(8,128)S(1)}, f32[3,4,64,128]{3,2,1,0:T(8,128)S(1)}, u32[]{:S(2)}, u32[]{:S(2)}) collective-permute-start(f32[3,4,64,128]{3,2,1,0:T(8,128)S(1)} %get-tuple-element.68), channel_id=1, source_target_pairs={{0,16},{16,32},{32,48},{48,64},{64,80},{80,96},{96,112},{112,0},{1... | collective-permute-start | bytes 1179656 | tf_op jit(solution)/shard_map/ppermute | solution.py:430
  31.7 23.0 %collective-permute-start.8 = (f32[3,4,64,128]{3,2,1,0:T(8,128)S(1)}, f32[3,4,64,128]{3,2,1,0:T(8,128)S(1)}, u32[]{:S(2)}, u32[]{:S(2)}) collective-permute-start(f32[3,4,64,128]{3,2,1,0:T(8,128)S(1)} %collective-permute-done.7), channel_id=1, source_target_pairs={{112,64},{48,0},{113,65},{49,1},{114,66},{50,2},{115,67},{51,3},{1... | collective-permute-start | bytes 1179656 | tf_op jit(solution)/shard_map/ppermute | solution.py:430
  38.1 18.5 %collective-permute-start.5 = (f32[3,4,64,128]{3,2,1,0:T(8,128)S(1)}, f32[3,4,64,128]{3,2,1,0:T(8,128)S(1)}, u32[]{:S(2)}, u32[]{:S(2)}) collective-permute-start(f32[3,4,64,128]{3,2,1,0:T(8,128)S(1)} %collective-permute-done.2.vb), channel_id=1, source_target_pairs={{1,2},{3,4},{5,6},{7,8},{9,10},{11,12},{13,14},{2,1},{4,3},{6,5},{... | collective-permute-start | bytes 1179656 | tf_op jit(solution)/shard_map/ppermute | solution.py:425
  63.0 31.4 %collective-permute-start.11 = (f32[3,4,64,128]{3,2,1,0:T(8,128)S(1)}, f32[3,4,64,128]{3,2,1,0:T(8,128)S(1)}, u32[]{:S(2)}, u32[]{:S(2)}) collective-permute-start(f32[3,4,64,128]{3,2,1,0:T(8,128)S(1)} %get-tuple-element.75), channel_id=1, source_target_pairs={{0,16},{16,32},{32,48},{48,64},{64,80},{80,96},{96,112},{112,0},{1... | collective-permute-start | bytes 1179656 | tf_op jit(solution)/shard_map/ppermute | solution.py:430
  63.1 35.6 %collective-permute-start.13 = (f32[3,4,64,128]{3,2,1,0:T(8,128)S(1)}, f32[3,4,64,128]{3,2,1,0:T(8,128)S(1)}, u32[]{:S(2)}, u32[]{:S(2)}) collective-permute-start(f32[3,4,64,128]{3,2,1,0:T(8,128)S(1)} %get-tuple-element.76), channel_id=1, source_target_pairs={{0,16},{16,32},{32,48},{48,64},{64,80},{80,96},{96,112},{112,0},{1... | collective-permute-start | bytes 1179656 | tf_op jit(solution)/shard_map/ppermute | solution.py:430
  63.2 35.5 %collective-permute-start.15 = (f32[3,4,64,128]{3,2,1,0:T(8,128)S(1)}, f32[3,4,64,128]{3,2,1,0:T(8,128)S(1)}, u32[]{:S(2)}, u32[]{:S(2)}) collective-permute-start(f32[3,4,64,128]{3,2,1,0:T(8,128)S(1)} %collective-permute-done.14), channel_id=1, source_target_pairs={{112,64},{48,0},{113,65},{49,1},{114,66},{50,2},{115,67},{51,3},{1... | collective-permute-start | bytes 1179656 | tf_op jit(solution)/shard_map/ppermute | solution.py:430
  65.5 28.2 %collective-permute-start.17 = (f32[4,64,128]{2,1,0:T(8,128)S(1)}, f32[4,64,128]{2,1,0:T(8,128)S(1)}, u32[]{:S(2)}, u32[]{:S(2)}) collective-permute-start(f32[4,64,128]{2,1,0:T(8,128)S(1)} %get-tuple-element.81), channel_id=1, source_target_pairs={{1,2},{3,4},{5,6},{7,8},{9,10},{11,12},{13,14},{2,1},{4,3},{6,5},{... | collective-permute-start | bytes 393224 | tf_op jit(solution)/shard_map/ppermute | solution.py:425
  69.5 29.5 %collective-permute-start.19 = (f32[3,4,64,128]{3,2,1,0:T(8,128)S(1)}, f32[3,4,64,128]{3,2,1,0:T(8,128)S(1)}, u32[]{:S(2)}, u32[]{:S(2)}) collective-permute-start(f32[3,4,64,128]{3,2,1,0:T(8,128)S(1)} %get-tuple-element.77), channel_id=1, source_target_pairs={{0,16},{16,32},{32,48},{64,80},{80,96},{96,112},{1,17},{17,33},{33... | collective-permute-start | bytes 1179656 | tf_op jit(solution)/shard_map/ppermute | solution.py:430
  110.1 15.8 %collective-permute-start.20 = (f32[3,4,64,128]{3,2,1,0:T(8,128)S(1)}, f32[3,4,64,128]{3,2,1,0:T(8,128)S(1)}, u32[]{:S(2)}, u32[]{:S(2)}) collective-permute-start(f32[3,4,64,128]{3,2,1,0:T(8,128)S(1)} %get-tuple-element.89), channel_id=1, source_target_pairs={{0,16},{16,32},{32,48},{48,64},{64,80},{80,96},{96,112},{112,0},{1... | collective-permute-start | bytes 1179656 | tf_op jit(solution)/shard_map/ppermute | solution.py:430
  110.1 24.3 %collective-permute-start.22 = (f32[3,4,64,128]{3,2,1,0:T(8,128)S(1)}, f32[3,4,64,128]{3,2,1,0:T(8,128)S(1)}, u32[]{:S(2)}, u32[]{:S(2)}) collective-permute-start(f32[3,4,64,128]{3,2,1,0:T(8,128)S(1)} %get-tuple-element.91), channel_id=1, source_target_pairs={{0,16},{16,32},{32,48},{48,64},{64,80},{80,96},{96,112},{112,0},{1... | collective-permute-start | bytes 1179656 | tf_op jit(solution)/shard_map/ppermute | solution.py:430
  110.2 26.2 %collective-permute-start.24 = (f32[3,4,64,128]{3,2,1,0:T(8,128)S(1)}, f32[3,4,64,128]{3,2,1,0:T(8,128)S(1)}, u32[]{:S(2)}, u32[]{:S(2)}) collective-permute-start(f32[3,4,64,128]{3,2,1,0:T(8,128)S(1)} %collective-permute-done.23), channel_id=1, source_target_pairs={{112,64},{48,0},{113,65},{49,1},{114,66},{50,2},{115,67},{51,3},{1... | collective-permute-start | bytes 1179656 | tf_op jit(solution)/shard_map/ppermute | solution.py:430
  111.5 25.0 %collective-permute-start.26 = (f32[3,4,64,128]{3,2,1,0:T(8,128)S(1)}, f32[3,4,64,128]{3,2,1,0:T(8,128)S(1)}, u32[]{:S(2)}, u32[]{:S(2)}) collective-permute-start(f32[3,4,64,128]{3,2,1,0:T(8,128)S(1)} %get-tuple-element.92), channel_id=1, source_target_pairs={{0,16},{16,32},{32,48},{64,80},{80,96},{96,112},{1,17},{17,33},{33... | collective-permute-start | bytes 1179656 | tf_op jit(solution)/shard_map/ppermute | solution.py:430
  143.8 22.9 %collective-permute-start.27 = (f32[3,4,64,128]{3,2,1,0:T(8,128)S(1)}, f32[3,4,64,128]{3,2,1,0:T(8,128)S(1)}, u32[]{:S(2)}, u32[]{:S(2)}) collective-permute-start(f32[3,4,64,128]{3,2,1,0:T(8,128)S(1)} %get-tuple-element.96), channel_id=1, source_target_pairs={{0,32},{16,48},{32,64},{48,80},{64,96},{80,112},{96,0},{112,16},{1... | collective-permute-start | bytes 1179656 | tf_op jit(solution)/shard_map/ppermute | solution.py:430
  150.3 20.8 %collective-permute-start.34 = (f32[3,4,64,128]{3,2,1,0:T(8,128)S(1)}, f32[3,4,64,128]{3,2,1,0:T(8,128)S(1)}, u32[]{:S(2)}, u32[]{:S(2)}) collective-permute-start(f32[3,4,64,128]{3,2,1,0:T(8,128)S(1)} %get-tuple-element.98), channel_id=1, source_target_pairs={{0,32},{16,48},{64,96},{80,112},{1,33},{17,49},{65,97},{81,113},{2... | collective-permute-start | bytes 1179656 | tf_op jit(solution)/shard_map/ppermute | solution.py:430
  152.3 24.0 %collective-permute-start.33 = (f32[3,4,64,128]{3,2,1,0:T(8,128)S(1)}, f32[3,4,64,128]{3,2,1,0:T(8,128)S(1)}, u32[]{:S(2)}, u32[]{:S(2)}) collective-permute-start(f32[3,4,64,128]{3,2,1,0:T(8,128)S(1)} %collective-permute-done.32), channel_id=1, source_target_pairs={{96,64},{112,80},{32,0},{48,16},{97,65},{113,81},{33,1},{49,17},{9... | collective-permute-start | bytes 1179656 | tf_op jit(solution)/shard_map/ppermute | solution.py:430
  158.3 25.9 %collective-permute-start.31 = (f32[3,4,64,128]{3,2,1,0:T(8,128)S(1)}, f32[3,4,64,128]{3,2,1,0:T(8,128)S(1)}, u32[]{:S(2)}, u32[]{:S(2)}) collective-permute-start(f32[3,4,64,128]{3,2,1,0:T(8,128)S(1)} %add.40.tm), channel_id=1, source_target_pairs={{0,1},{1,0},{2,3},{3,2},{4,5},{5,4},{6,7},{7,6},{8,9},{9,8},{10,11... | collective-permute-start | bytes 1179656 | tf_op jit(solution)/shard_map/ppermute | solution.py:422
  159.9 24.3 %collective-permute-start.30 = (f32[3,4,64,128]{3,2,1,0:T(8,128)S(1)}, f32[3,4,64,128]{3,2,1,0:T(8,128)S(1)}, u32[]{:S(2)}, u32[]{:S(2)}) collective-permute-start(f32[3,4,64,128]{3,2,1,0:T(8,128)S(1)} %add.40.tm), channel_id=1, source_target_pairs={{1,2},{3,4},{5,6},{7,8},{9,10},{11,12},{13,14},{2,1},{4,3},{6,5},{... | collective-permute-start | bytes 1179656 | tf_op jit(solution)/shard_map/ppermute | solution.py:425
  166.8 17.5 %collective-permute-start.28 = (f32[3,4,64,128]{3,2,1,0:T(8,128)S(1)}, f32[3,4,64,128]{3,2,1,0:T(8,128)S(1)}, u32[]{:S(2)}, u32[]{:S(2)}) collective-permute-start(f32[3,4,64,128]{3,2,1,0:T(8,128)S(1)} %add.39.tb), channel_id=1, source_target_pairs={{1,2},{3,4},{5,6},{7,8},{9,10},{11,12},{13,14},{2,1},{4,3},{6,5},{... | collective-permute-start | bytes 1179656 | tf_op jit(solution)/shard_map/ppermute | solution.py:425
  196.2 14.9 %collective-permute-start.37 = (f32[3,4,64,128]{3,2,1,0:T(8,128)S(1)}, f32[3,4,64,128]{3,2,1,0:T(8,128)S(1)}, u32[]{:S(2)}, u32[]{:S(2)}) collective-permute-start(f32[3,4,64,128]{3,2,1,0:T(8,128)S(1)} %get-tuple-element.101), channel_id=1, source_target_pairs={{0,64},{16,80},{32,96},{48,112},{64,0},{80,16},{96,32},{112,48},{1... | collective-permute-start | bytes 1179656 | tf_op jit(solution)/shard_map/ppermute | solution.py:430
  197.7 21.2 %collective-permute-start.36 = (f32[3,4,64,128]{3,2,1,0:T(8,128)S(1)}, f32[3,4,64,128]{3,2,1,0:T(8,128)S(1)}, u32[]{:S(2)}, u32[]{:S(2)}) collective-permute-start(f32[3,4,64,128]{3,2,1,0:T(8,128)S(1)} %get-tuple-element.99), channel_id=1, source_target_pairs={{0,64},{16,80},{32,96},{48,112},{64,0},{80,16},{96,32},{112,48},{1... | collective-permute-start | bytes 1179656 | tf_op jit(solution)/shard_map/ppermute | solution.py:430
  (25 other events, 144.8 us)

commit v7 on v6

v7 whole, which is shorter than its diff:
```python
import jax
import jax.numpy as jnp
from jax import lax
from jax.experimental import pallas as pl
from jax.experimental.pallas import tpu as pltpu
from jax.sharding import PartitionSpec as P

LX, NY, NZ = 12, 64, 128
ROWS = pl.ds(8, NY)
F32 = jnp.float32
ANY = pl.BlockSpec(memory_space=pl.ANY)
HBM = pl.BlockSpec(memory_space=pltpu.HBM)
VMEM = pl.BlockSpec(memory_space=pltpu.VMEM)
SMEM = pl.BlockSpec(memory_space=pltpu.SMEM)


def planes(*lead):
    return jax.ShapeDtypeStruct(tuple(lead) + (NY, NZ), F32)


def vmem(*lead):
    return pltpu.VMEM(tuple(lead) + (NY, NZ), F32)


def padded(*lead):
    return pltpu.VMEM(tuple(lead) + (NY + 16, NZ), F32)


def clear(*bufs):
    zero = jnp.zeros((8, NZ), F32)

    def body(i, carry):
        for buf in bufs:
            for c in range(3):
                buf[c, i, pl.ds(0, 8)] = zero
                buf[c, i, pl.ds(NY + 8, 8)] = zero
        return carry

    lax.fori_loop(0, bufs[0].shape[1], body, 0)


def copy_all(pairs, sems, base=0):
    copies = [
        pltpu.make_async_copy(src, dst, sems.at[base + n]) for n, (src, dst) in enumerate(pairs)
    ]
    for copy in copies:
        copy.start()
    return copies


def wait_all(copies):
    for copy in copies:
        copy.wait()


def run_copies(pairs, sems, base=0):
    wait_all(copy_all(pairs, sems, base))


def call(kernel, name, args, outs, scratch, n_sems=0, out_specs=None, in_place=VMEM):
    in_specs = [SMEM if a.ndim == 1 else in_place for a in args]
    single = not isinstance(outs, (list, tuple))
    return pl.pallas_call(
        kernel,
        name=name,
        out_shape=outs,
        in_specs=in_specs,
        out_specs=out_specs or (VMEM if single else [VMEM] * len(outs)),
        scratch_shapes=list(scratch) + [pltpu.SemaphoreType.DMA((n_sems,))] * (n_sems > 0),
        compiler_params=pltpu.CompilerParams(vmem_limit_bytes=20 * 1024 * 1024),
        cost_estimate=pl.CostEstimate(flops=0, bytes_accessed=4 << 20, transcendentals=0),
    )(*args)


def over_layers(lo, hi, step, at_once):
    rounds = (hi - lo) // at_once

    def body(t, carry):
        for k in range(at_once):
            step(lo + t * at_once + k)
        return carry

    lax.fori_loop(0, rounds, body, 0)
    for i in range(lo + rounds * at_once, hi):
        step(i)


def neighbours(src, c, i):
    lane = lax.broadcasted_iota(jnp.int32, (NY, NZ), 1)
    zero = jnp.float32(0.0)
    if src.shape[-2] == NY:
        row = lax.broadcasted_iota(jnp.int32, (NY, NZ), 0)
        a = src[c, i]
        first = src[c, i + 1] + src[c, i - 1]
        up = jnp.where(row == 0, zero, pltpu.roll(a, 1, 0))
        down = jnp.where(row == NY - 1, zero, pltpu.roll(a, NY - 1, 0))
    else:
        a = src[c, i, ROWS]
        first = src[c, i + 1, ROWS] + src[c, i - 1, ROWS]
        up = src[c, i, pl.ds(7, NY)]
        down = src[c, i, pl.ds(9, NY)]
    left = jnp.where(lane == 0, zero, pltpu.roll(a, 1, 1))
    right = jnp.where(lane == NZ - 1, zero, pltpu.roll(a, NZ - 1, 1))
    return (first + (up + down)) + (left + right)


def layer(src, c, i):
    return src[c, i] if src.shape[-2] == NY else src[c, i, ROWS]


def fine_sweep(src, store, held, cond, nu, lo, hi, force=None, off=0):
    def step(i):
        state = [layer(src, c, i) for c in range(3)]
        square = state[0] * state[0] + state[1] * state[1] + state[2] * state[2]
        base = nu[i - off]
        weight = cond[i - off]
        grown = 1.0 + square
        strong = base * (1.0 + 1.5 * square)
        scale = 1.0 / (weight * grown + 6.0 * strong)
        keep = grown * scale
        spread = strong * scale
        for c in range(3):
            if force is not None:
                fixed = weight * state[c] + force[c, i]
                held[c, i] = fixed
            else:
                fixed = held[c, i]
            store(c, i, fixed * keep + neighbours(src, c, i) * spread)

    over_layers(lo, hi, step, 6)


def coarse_sweep(src, dst, held, keep, spread, off, lo, hi, first):
    def step(i):
        k = keep[i + off]
        s = spread[i + off]
        for c in range(3):
            if first:
                fixed = k * src[c, i, ROWS]
                held[c, i] = fixed
            else:
                fixed = held[c, i]
            dst[c, i, ROWS] = fixed + s * neighbours(src, c, i)

    over_layers(lo, hi, step, 6)


def lookup(code, table):
    first = jnp.where(code == 1, table[0], table[1])
    second = jnp.where(code == 3, table[2], table[3])
    return jnp.where(code <= 2, first, second)


def materials(code, cond_t, nu_t):
    outside = code == 0
    return (
        jnp.where(outside, jnp.float32(1.0), lookup(code, cond_t)),
        jnp.where(outside, jnp.float32(0.0), lookup(code, nu_t)),
    )


def into(buf):
    def store(c, i, value):
        buf[c, i, ROWS] = value
    return store


def edges(odd, n, width):
    return (1 - odd) * (n - width), odd * (n - width)


def first_pack_kernel(odd_ref, g_low, g_high, s_low, s_high, r_low, r_high, a1, b1):
    odd = odd_ref[0]

    def fill(low, high):
        for c in range(3):
            for k in range(2):
                low[2 * c + k] = g_low[0, c, k]
                high[2 * c + k] = g_high[0, c, k]
            low[6 + c] = s_low[0, c, 0]
            high[6 + c] = s_high[0, c, 0]
        low[9] = (r_low[0] + 1).astype(F32)
        high[9] = (r_high[0] + 1).astype(F32)

    @pl.when(odd == 0)
    def even_slab():
        fill(b1, a1)

    @pl.when(odd == 1)
    def odd_slab():
        fill(a1, b1)


def second_pack_kernel(odd_ref, source, regions, a2, b2):
    odd = odd_ref[0]
    for two, start in zip((a2, b2), edges(odd, LX, 3)):
        for c in range(3):
            for k in range(3):
                two[3 * c + k] = source[0, c, start + k]
    for two, start in zip((a2, b2), edges(odd, LX, 7)):
        for k in range(7):
            two[9 + k] = (regions[start + k] + 1).astype(F32)


def first_middle_kernel(cond_t, nu_t, guess, source, regions, after, out, y, held, cond, nu):
    def prepare(i):
        cond[i], nu[i] = materials(regions[i] + 1, cond_t, nu_t)

    over_layers(3, 9, prepare, 6)
    clear(y)
    fine_sweep(guess.at[0], into(y), held, cond, nu, 3, 9, source.at[1])

    def store(c, i, value):
        out[c, i - 4] = value

    fine_sweep(y, store, held, cond, nu, 4, 8)


def first_kernel(odd_ref, cond_t, nu_t, guess, source, regions, ra, rb, after, out_a, out_b, x, y, held, f, cond, nu):
    odd = odd_ref[0]
    clear(x, y)
    n = LX + 4
    for c in range(3):
        for i in (0, 1, 2, 3, 4, 5, 6, 7, 8, 9, 10, 11):
            x[c, i + 2, ROWS] = guess[0, c, i]
            f[c, i + 2] = source[1, c, i]
    for i in range(LX):
        cond[i + 2], nu[i + 2] = materials(regions[i] + 1, cond_t, nu_t)
    for pack, high in ((ra, 1 - odd), (rb, odd)):
        for c in range(3):
            for k in range(2):
                x[c, high * (n - 2) + k, ROWS] = pack[2 * c + k]
            f[c, 1 + high * (n - 3)] = pack[6 + c]
        cond[1 + high * (n - 3)], nu[1 + high * (n - 3)] = materials(pack[9], cond_t, nu_t)
    fine_sweep(x, into(y), held, cond, nu, 1, 7, f)
    fine_sweep(x, into(y), held, cond, nu, 9, n - 1, f)
    fine_sweep(y, into(x), held, cond, nu, 2, 6)
    fine_sweep(y, into(x), held, cond, nu, 10, 14)
    for c in range(3):
        for k in range(4):
            out_a[c, k] = x[c, 2 + (1 - odd) * 8 + k, ROWS]
            out_b[c, k] = x[c, 2 + odd * 8 + k, ROWS]


def material_kernel(odd_ref, cond_t, nu_t, regions, ra, rb, cond, nu, keep, spread):
    odd = odd_ref[0]

    def fill(at, code, near=True):
        cv, nv = materials(code, cond_t, nu_t)
        if near:
            cond[at - 4] = cv
            nu[at - 4] = nv
        half = 0.5 * cv
        scale = 1.0 / (half + 6.0 * nv)
        keep[at] = half * scale
        spread[at] = nv * scale

    for i in range(LX):
        fill(7 + i, regions[i] + 1)
    for k in range(7):
        from_on, from_off = ra[9 + k], rb[9 + k]
        fill(k, jnp.where(odd == 1, from_on, from_off), k >= 4)
        fill(LX + 7 + k, jnp.where(odd == 1, from_off, from_on), k < 3)


def extend(odd, pieces, halos, x):
    a, b, *m = pieces
    ha, hb = halos
    for c in range(3):
        for k in range(4):
            middle = m[0][c, k]
            for other in m[1:]:
                middle = middle + other[c, k]
            x[c, 8 + k, ROWS] = middle
            x[c, 4 + (1 - odd) * 8 + k, ROWS] = a[c, k]
            x[c, 4 + odd * 8 + k, ROWS] = b[c, k]
            x[c, (1 - odd) * 16 + k, ROWS] = ha[c, k]
            x[c, odd * 16 + k, ROWS] = hb[c, k]


def extend_force(odd, source, which, width, packs, start, f):
    for c in range(3):
        for i in range(LX):
            f[c, 4 + i] = source[which, c, i]
        for pack, high in ((packs[0], 1 - odd), (packs[1], odd)):
            for k in range(width):
                f[c, 4 - width + high * (LX + width) + k] = pack[start + width * c + k]


def second_kernel(
    odd_ref, hb, vb, ha, va, vm, source, a1, b1, a2, b2, cond, nu,
    u0, oa, ob, om, x, y, held, f0, f1,
):
    odd = odd_ref[0]
    clear(x, y)
    extend(odd, (va, vb, vm), (ha, hb), x)
    extend_force(odd, source, 0, 3, (a2, b2), 0, f0)
    extend_force(odd, source, 1, 1, (a1, b1), 6, f1)

    def keep_u0(c, i, value):
        x[c, i, ROWS] = value
        u0[c, i - 2] = value

    fine_sweep(x, into(y), held, cond, nu, 1, 19, f0, 1)
    fine_sweep(y, keep_u0, held, cond, nu, 2, 18, None, 1)
    fine_sweep(x, into(y), held, cond, nu, 3, 17, f1, 1)
    fine_sweep(y, into(x), held, cond, nu, 4, 16, None, 1)
    for c in range(3):
        for k in range(4):
            om[c, k] = x[c, 8 + k, ROWS]
            oa[c, k] = x[c, 4 + (1 - odd) * 8 + k, ROWS]
            ob[c, k] = x[c, 4 + odd * 8 + k, ROWS]


def split(odd, x, start, b, a, m):
    for c in range(3):
        for k in range(4):
            b[c, k] = x[c, start + odd * 8 + k, ROWS]
            a[c, k] = x[c, start + (1 - odd) * 8 + k, ROWS]
            m[c, k] = x[c, start + 4 + k, ROWS]


def residual_kernel(
    odd_ref, hb, vb, ha, va, vm, vn, source, a2, b2, cond, nu, keep, spread, u0,
    res_o, lb, la, lm, rb, ra, rm, x, y, held, f0, sems,
):
    odd = odd_ref[0]
    clear(x, y)
    extend(odd, (va, vb, vm, vn), (ha, hb), x)
    extend_force(odd, source, 0, 3, (a2, b2), 0, f0)

    def less(c, i, value):
        x[c, i, ROWS] = value - u0[c, i - 2]

    fine_sweep(x, into(y), held, cond, nu, 1, 19, f0, 1)
    fine_sweep(y, less, held, cond, nu, 2, 18, None, 1)
    kept = copy_all([(x.at[:, pl.ds(4, LX), ROWS], res_o.at[0])], sems)
    split(odd, x, 4, rb, ra, rm)
    coarse_sweep(x, y, held, keep, spread, 3, 3, 17, True)
    wait_all(kept)
    coarse_sweep(y, x, held, keep, spread, 3, 4, 16, False)
    split(odd, x, 4, lb, la, lm)


def square_kernel(odd_ref, hb, sb, ha, sa, sm, keep, spread, ob, oa, om, x, y, held):
    odd = odd_ref[0]
    clear(x, y)
    extend(odd, (sa, sb, sm), (ha, hb), x)
    for lo in (1, 3):
        coarse_sweep(x, y, held, keep, spread, 3, lo, 20 - lo, True)
        coarse_sweep(y, x, held, keep, spread, 3, lo + 1, 19 - lo, False)
    split(odd, x, 4, ob, oa, om)


def fourth_kernel(
    odd_ref, near_b, tb, far_b, tm, far_a, near_a, ta, u0, keep, spread,
    ob, oa, om, bb, ba, bm, x, y, held,
):
    odd = odd_ref[0]
    clear(x, y)
    for c in range(3):
        for k in range(4):
            x[c, 8 + odd * 8 + k, ROWS] = tb[c, k]
            x[c, 8 + (1 - odd) * 8 + k, ROWS] = ta[c, k]
            x[c, 12 + k, ROWS] = tm[c, k]
            x[c, 4 + odd * 16 + k, ROWS] = near_b[c, k]
            x[c, 4 + (1 - odd) * 16 + k, ROWS] = near_a[c, k]
            x[c, odd * 24 + k, ROWS] = far_b[c, k]
            x[c, (1 - odd) * 24 + k, ROWS] = far_a[c, k]
    for c in range(3):
        for k in range(4):
            bb[c, k] = tb[c, k] + u0[c, 2 + odd * 8 + k]
            ba[c, k] = ta[c, k] + u0[c, 2 + (1 - odd) * 8 + k]
            bm[c, k] = tm[c, k] + u0[c, 6 + k]
    for lo in (1, 3, 5, 7):
        coarse_sweep(x, y, held, keep, spread, -1, lo, 28 - lo, True)
        coarse_sweep(y, x, held, keep, spread, -1, lo + 1, 27 - lo, False)
    split(odd, x, 8, ob, oa, om)


def edge_kernel(odd_ref, base, moved, total, edge):
    odd = odd_ref[0]
    for c in range(3):
        for k in range(4):
            total[c, k] = base[c, k] + moved[c, k]
        for k in range(2):
            edge[c, k] = total[c, odd * 2 + k]


def last_kernel(
    odd_ref, hb, eb, ha, ea, em, source, a1, b1, cond, nu, field, x, y, held, f1, sems,
):
    odd = odd_ref[0]
    clear(x, y)
    kept = copy_all(
        [
            (eb, field.at[0, :, pl.ds(odd * 8, 4)]),
            (ea, field.at[0, :, pl.ds((1 - odd) * 8, 4)]),
            (em, field.at[0, :, pl.ds(4, 4)]),
        ],
        sems,
    )
    extend_force(odd, source, 1, 1, (a1, b1), 6, f1)
    for c in range(3):
        for k in range(4):
            x[c, 4 + odd * 8 + k, ROWS] = eb[c, k]
            x[c, 4 + (1 - odd) * 8 + k, ROWS] = ea[c, k]
            x[c, 8 + k, ROWS] = em[c, k]
        for k in range(2):
            x[c, 2 + odd * 14 + k, ROWS] = hb[c, k]
            x[c, 2 + (1 - odd) * 14 + k, ROWS] = ha[c, odd * 2 + k]
    fine_sweep(x, into(y), held, cond, nu, 3, 17, f1, 1)
    fine_sweep(y, into(x), held, cond, nu, 4, 10, None, 1)
    kept += copy_all([(x.at[:, pl.ds(4, 6), ROWS], field.at[1, :, pl.ds(0, 6)])], sems, 3)
    fine_sweep(y, into(x), held, cond, nu, 10, 16, None, 1)
    kept += copy_all([(x.at[:, pl.ds(10, 6), ROWS], field.at[1, :, pl.ds(6, 6)])], sems, 4)
    wait_all(kept)


def body(guess, source, regions, conductance, reluct):
    slices = lax.axis_size("tm")
    slabs = lax.axis_size("space")
    odd = (lax.axis_index("space") % 2).astype(jnp.int32).reshape(1)
    on_chip = [(i, i ^ 1) for i in range(slabs)]
    off_chip = [(i, i + 1) for i in range(1, slabs - 1, 2)]
    off_chip += [(j, i) for i, j in off_chip]
    fence = lax.optimization_barrier

    def from_a(x):
        return lax.ppermute(x, "space", on_chip)

    def from_b(x):
        return lax.ppermute(x, "space", off_chip)

    half = slices // 2

    def along(x, pairs):
        return lax.ppermute(x, "tm", pairs)

    def later(x, distance):
        return along(x, [(i, (i + distance) % slices) for i in range(slices)])

    def later_parts(x, distance):
        wrapping = [i for i in range(slices) if i % half + distance >= half]
        across = along(x, [(i, (i + half) % slices) for i in wrapping])
        around = along(across, [((i + half) % slices, (i + distance) % slices) for i in wrapping])
        plain = along(x, [(i, i + distance) for i in range(slices) if i not in wrapping])
        return around, plain

    tables = (conductance, reluct)
    sa1, sb1 = call(
        first_pack_kernel, "first_pack",
        (odd, guess[:1, :, :2], guess[:1, :, LX - 2:], source[1:, :, :1], source[1:, :, LX - 1:], regions[:1], regions[LX - 1:]),
        [planes(10), planes(10)], [],
    )
    b1 = from_b(sb1)
    a1 = from_a(sa1)
    um = call(
        first_middle_kernel, "first_middle", (*tables, guess, source, regions, sb1),
        planes(3, 4), [padded(3, LX), vmem(3, LX)] + [vmem(LX)] * 2,
    )
    sa2, sb2 = call(
        second_pack_kernel, "second_pack", (odd, source, regions), [planes(16), planes(16)], [],
    )
    vm = later(um, 1)
    sb2, sa2, b1 = fence((sb2, sa2, b1))
    b2 = from_b(sb2)
    a2 = from_a(sa2)
    ua, ub = call(
        first_kernel, "first", (odd, *tables, guess, source, regions, a1, b1, um),
        [planes(3, 4), planes(3, 4)], [padded(3, LX + 4)] * 2 + [vmem(3, LX + 4)] * 2 + [vmem(LX + 4)] * 2,
    )
    ub, vm = fence((ub, vm))
    vb = later(ub, 1)
    around, plain = later_parts(ua, 1)
    va = around + plain
    cond, nu, keep, spread = call(
        material_kernel, "material", (odd, *tables, regions, a2, b2),
        [planes(LX + 6)] * 2 + [planes(LX + 14)] * 2, [],
    )
    vb, cond = fence((vb, cond))
    hb = from_b(vb)
    ha = from_a(va)
    n = LX + 8
    u0, ua, ub, um = call(
        second_kernel, "second",
        (odd, hb, vb, ha, va, vm, source, a1, b1, a2, b2, cond, nu),
        [planes(3, LX + 4), planes(3, 4), planes(3, 4), planes(3, 4)], [padded(3, n)] * 2 + [vmem(3, n)] * 3,
    )
    vb = later(ub, 1)
    va = later(ua, 1)
    around, plain = later_parts(um, 1)
    hb = from_b(vb)
    va, around = fence((va, around))
    ha = from_a(va)
    residual, lb, la, lm, rb, ra, rm = call(
        residual_kernel, "residual",
        (odd, hb, vb, ha, va, around, plain, source, a2, b2, cond, nu, keep, spread, u0),
        [planes(1, 3, LX)] + [planes(3, 4)] * 6, [padded(3, n)] * 2 + [vmem(3, n)] * 2, 1, [ANY] + [VMEM] * 6,
    )
    sb = rb + later(lb, 1)
    hb = from_b(sb)
    around, plain = later_parts(lm, 1)
    moved, around = fence((later(la, 1), around))
    sa = ra + moved
    ha = from_a(sa)
    sm = rm + (around + plain)
    lb, la, lm = call(
        square_kernel, "square", (odd, hb, sb, ha, sa, sm, keep, spread),
        [planes(3, 4)] * 3, [padded(3, n)] * 2 + [vmem(3, n)],
    )
    tb = sb + later(lb, 2)
    near_b = from_b(tb)
    tm = sm + later(lm, 2)
    far_b = from_b(tm)
    around, plain = later_parts(la, 2)
    ta = sa + (around + plain)
    near_a = from_a(ta)
    far_a = from_a(tm)
    lb, la, lm, bb, ba, bm = call(
        fourth_kernel, "fourth",
        (odd, near_b, tb, far_b, tm, far_a, near_a, ta, u0, keep, spread),
        [planes(3, 4)] * 6, [padded(3, LX + 16)] * 2 + [vmem(3, LX + 16)],
    )
    eb, edge = call(
        edge_kernel, "edge", (odd, bb, later(lb, half)), [planes(3, 4), planes(3, 2)], [],
    )
    hb = from_b(edge)
    moved, hb = fence((later(la, half), hb))
    ea = ba + moved
    ha = from_a(ea)
    em = bm + later(lm, half)
    field = call(
        last_kernel, "last", (odd, hb, eb, ha, ea, em, source, a1, b1, cond, nu),
        planes(2, 3, LX), [padded(3, n)] * 2 + [vmem(3, n)] * 2, 5, ANY,
    )
    return field, residual


def solution(mesh):
    whole = P("tm", None, "space", None, None)
    return jax.shard_map(
        body, mesh=mesh, in_specs=(whole, whole, P("space", None, None), P(), P()),
        out_specs=(whole, whole), check_vma=False,
    )
```

time: 232 us -> 236 us (1.017)
  waiting for transfers between devices: 108 us -> 127 us
  starting transfers between devices: 74.5 us -> 65.2 us
  Pallas kernels: 36.8 us -> 32.3 us
    ppermute x23, waiting for transfers between devices: 71.1 us -> 95.1 us  [along(): return lax.ppermute(x, 'tm', pairs)]
    ppermute x9 -> x8, starting transfers between devices: 32 us -> 21.3 us  [from_b(): return lax.ppermute(x, 'space', off_chip)]
    ppermute x9 -> x8, waiting for transfers between devices: 35.1 us -> 28.7 us  [from_b(): return lax.ppermute(x, 'space', off_chip)]
    pallas_call x12 -> x11, Pallas kernels: 36.8 us -> 32.3 us  [call(): pl.pallas_call(kernel, name=name, out_shape=outs, in_specs=in_specs, out_...]
    ppermute x9 -> x8, starting transfers between devices: 5.82 us -> 5.95 us  [from_a(): return lax.ppermute(x, 'space', on_chip)]
  transfers between devices with their start and end apart: 41 -> 39, of which waited for: 20 -> 20; matrix products, arithmetic and copies ran while one was open for 0% -> 0% of each run, Pallas kernels for 3% -> 2%
where the time goes in v7:
time: 236 us; the launch traced here: 235 us
  waiting for transfers between devices  127 us (54%)
  starting transfers between devices  65.2 us (28%)
  Pallas kernels  32.3 us (14%)
  local copies, waits for them, and re-layouts  8.79 us (4%)
    ppermute x23, waiting for transfers between devices, along(): return lax.ppermute(x, 'tm', pairs)  95.1 us
    ppermute x23, starting transfers between devices, along(): return lax.ppermute(x, 'tm', pairs)  37.9 us
    pallas_call x11, Pallas kernels, call(): pl.pallas_call(kernel, name=name, out_shape=outs, in_specs=in_specs, out_...  32.3 us
    ppermute x8, waiting for transfers between devices, from_b(): return lax.ppermute(x, 'space', off_chip)  28.7 us
    ppermute x8, starting transfers between devices, from_b(): return lax.ppermute(x, 'space', off_chip)  21.3 us
    unnamed x16, local copies, waits for them, and re-layouts  5.99 us
    ppermute x8, starting transfers between devices, from_a(): return lax.ppermute(x, 'space', on_chip)  5.95 us
  transfers between devices with their start and end apart: 39, of which 20 were waited for; matrix products, arithmetic and copies ran while one was open for 0% of the time, Pallas kernels for 2%

profile of v7, /device:TPU:17, one launch (start us, length us, event | category | flops | bytes accessed | tf_op | source)
XLA Modules:
  0.0 234.7 jit_solution(16249551443950460466)
XLA Ops:
  3.5 4.1 %collective-permute-start.1 = (f32[10,64,128]{2,1,0:T(8,128)S(1)}, f32[10,64,128]{2,1,0:T(8,128)S(1)}, u32[]{:S(2)}, u32[]{:S(2)}) collective-permute-start(f32[10,64,128]{2,1,0:T(8,128)S(1)} %get-tuple-element.50.after), channel_id=1, source_target_pairs={{1,2},{3,4},{5,6},{7,8},{9,10},{11,12},{13,14},{2,1},{4,3},{6,5},{... | collective-permute-start | bytes 983048 | tf_op jit(solution)/shard_map/ppermute | solution.py:433
  22.5 7.4 %collective-permute-done.2.vm = f32[3,4,64,128]{3,2,1,0:T(8,128)S(1)} collective-permute-done((f32[3,4,64,128]{3,2,1,0:T(8,128)S(1)}, f32[3,4,64,128]{3,2,1,0:T(8,128)S(1)}, u32[]{:S(2)}, u32[]{:S(2)}) %collective-permute-start.2) | collective-permute-done | bytes 393248 | tf_op jit(solution)/shard_map/ppermute | solution.py:438
  32.6 17.3 %collective-permute-done.5.rb.b2 = f32[16,64,128]{2,1,0:T(8,128)S(1)} collective-permute-done((f32[16,64,128]{2,1,0:T(8,128)S(1)}, f32[16,64,128]{2,1,0:T(8,128)S(1)}, u32[]{:S(2)}, u32[]{:S(2)}) %collective-permute-start.5) | collective-permute-done | bytes 524320 | tf_op jit(solution)/shard_map/ppermute | solution.py:433
  51.1 3.4 %collective-permute-start.6 = (f32[3,4,64,128]{3,2,1,0:T(8,128)S(1)}, f32[3,4,64,128]{3,2,1,0:T(8,128)S(1)}, u32[]{:S(2)}, u32[]{:S(2)}) collective-permute-start(f32[3,4,64,128]{3,2,1,0:T(8,128)S(1)} %collective-permute-done.3.vb), channel_id=1, source_target_pairs={{1,2},{3,4},{5,6},{7,8},{9,10},{11,12},{13,14},{2,1},{4,3},{6,5},{... | collective-permute-start | bytes 1179656 | tf_op jit(solution)/shard_map/ppermute | solution.py:433
  55.6 4.6 %collective-permute-done.6.hb = f32[3,4,64,128]{3,2,1,0:T(8,128)S(1)} collective-permute-done((f32[3,4,64,128]{3,2,1,0:T(8,128)S(1)}, f32[3,4,64,128]{3,2,1,0:T(8,128)S(1)}, u32[]{:S(2)}, u32[]{:S(2)}) %collective-permute-start.6) | collective-permute-done | bytes 393248 | tf_op jit(solution)/shard_map/ppermute | solution.py:433
  60.2 4.7 %second.1 = (f32[3,16,64,128]{3,2,1,0:T(8,128)S(1)}, f32[3,4,64,128]{3,2,1,0:T(8,128)S(1)}, f32[3,4,64,128]{3,2,1,0:T(8,128)S(1)}, f32[3,4,64,128]{3,2,1,0:T(8,128)S(1)}) custom-call(s32[1]{0:T(128)} %bitcast.odd_ref, f32[3,4,64,128]{3,2,1,0:T(8,128)S(1)} %collective-permute-done.6.hb, f32[3,4,64,128]{3,2,1,0:T(8,128)S(1)} %collective-permute-done.3.vb, ...), custom_call_target="tpu_custom_call" | custom-call | bytes 4194304 | tf_op jit(solution)/shard_map/second/pallas_call | solution.py:63
  67.1 5.2 %collective-permute-start.17 = (f32[3,4,64,128]{3,2,1,0:T(8,128)S(1)}, f32[3,4,64,128]{3,2,1,0:T(8,128)S(1)}, u32[]{:S(2)}, u32[]{:S(2)}) collective-permute-start(f32[3,4,64,128]{3,2,1,0:T(8,128)S(1)} %get-tuple-element.64), channel_id=1, source_target_pairs={{0,16},{16,32},{32,48},{64,80},{80,96},{96,112},{1,17},{17,33},{33... | collective-permute-start | bytes 1179656 | tf_op jit(solution)/shard_map/ppermute | solution.py:438
  72.3 8.8 %collective-permute-done.11.vb = f32[3,4,64,128]{3,2,1,0:T(8,128)S(1)} collective-permute-done((f32[3,4,64,128]{3,2,1,0:T(8,128)S(1)}, f32[3,4,64,128]{3,2,1,0:T(8,128)S(1)}, u32[]{:S(2)}, u32[]{:S(2)}) %collective-permute-start.11) | collective-permute-done | bytes 393248 | tf_op jit(solution)/shard_map/ppermute | solution.py:438
  81.1 3.6 %collective-permute-start.12 = (f32[3,4,64,128]{3,2,1,0:T(8,128)S(1)}, f32[3,4,64,128]{3,2,1,0:T(8,128)S(1)}, u32[]{:S(2)}, u32[]{:S(2)}) collective-permute-start(f32[3,4,64,128]{3,2,1,0:T(8,128)S(1)} %collective-permute-done.11.vb), channel_id=1, source_target_pairs={{1,2},{3,4},{5,6},{7,8},{9,10},{11,12},{13,14},{2,1},{4,3},{6,5},{... | collective-permute-start | bytes 1179656 | tf_op jit(solution)/shard_map/ppermute | solution.py:433
  84.8 5.6 %collective-permute-done.13.va = f32[3,4,64,128]{3,2,1,0:T(8,128)S(1)} collective-permute-done((f32[3,4,64,128]{3,2,1,0:T(8,128)S(1)}, f32[3,4,64,128]{3,2,1,0:T(8,128)S(1)}, u32[]{:S(2)}, u32[]{:S(2)}) %collective-permute-start.13) | collective-permute-done | bytes 393248 | tf_op jit(solution)/shard_map/ppermute | solution.py:438
  90.4 9.7 %collective-permute-done.15.vm = f32[3,4,64,128]{3,2,1,0:T(8,128)S(1)} collective-permute-done((f32[3,4,64,128]{3,2,1,0:T(8,128)S(1)}, f32[3,4,64,128]{3,2,1,0:T(8,128)S(1)}, u32[]{:S(2)}, u32[]{:S(2)}) %collective-permute-start.15) | collective-permute-done | bytes 393248 | tf_op jit(solution)/shard_map/ppermute | solution.py:438
  101.8 4.7 %residual.1 = (f32[1,3,12,64,128]{4,3,2,1,0:T(8,128)}, f32[3,4,64,128]{3,2,1,0:T(8,128)S(1)}, f32[3,4,64,128]{3,2,1,0:T(8,128)S(1)}, f32[3,4,64,128]{3,2,1,0:T(8...) custom-call(s32[1]{0:T(128)} %bitcast.odd_ref, ...), custom_call_target="tpu_custom_call" | custom-call | bytes 4194304 | tf_op jit(solution)/shard_map/residual/pallas_call | solution.py:63
  111.6 10.1 %collective-permute-done.18 = f32[3,4,64,128]{3,2,1,0:T(8,128)S(1)} collective-permute-done((f32[3,4,64,128]{3,2,1,0:T(8,128)S(1)}, f32[3,4,64,128]{3,2,1,0:T(8,128)S(1)}, u32[]{:S(2)}, u32[]{:S(2)}) %collective-permute-start.18) | collective-permute-done | bytes 393248 | tf_op jit(solution)/shard_map/ppermute | solution.py:438
  123.7 10.5 %collective-permute-done.20 = f32[3,4,64,128]{3,2,1,0:T(8,128)S(1)} collective-permute-done((f32[3,4,64,128]{3,2,1,0:T(8,128)S(1)}, f32[3,4,64,128]{3,2,1,0:T(8,128)S(1)}, u32[]{:S(2)}, u32[]{:S(2)}) %collective-permute-start.20) | collective-permute-done | bytes 393248 | tf_op jit(solution)/shard_map/ppermute | solution.py:438
  138.5 4.3 %square.1 = (f32[3,4,64,128]{3,2,1,0:T(8,128)S(1)}, f32[3,4,64,128]{3,2,1,0:T(8,128)S(1)}, f32[3,4,64,128]{3,2,1,0:T(8,128)S(1)}) custom-call(s32[1]{0:T(128)} %bitcast.odd_ref, f32[3,4,64,128]{3,2,1,0:T(8,128)S(1)} %collective-permute-done.19.hb, f32[3,4,64,128]{3,2,1,0:T(8,128)S(1)} %add.39.sb, f32[3,4,64,128]{3,2,1,0:T(8,128)S(1)} %collective-permute-done.23.ha, ...), custom_call_target="tpu_custom_call" | custom-call | bytes 4194304 | tf_op jit(solution)/shard_map/square/pallas_call | solution.py:63
  144.5 8.5 %collective-permute-start.25 = (f32[3,4,64,128]{3,2,1,0:T(8,128)S(1)}, f32[3,4,64,128]{3,2,1,0:T(8,128)S(1)}, u32[]{:S(2)}, u32[]{:S(2)}) collective-permute-start(f32[3,4,64,128]{3,2,1,0:T(8,128)S(1)} %get-tuple-element.78), channel_id=1, source_target_pairs={{0,32},{16,48},{32,64},{48,80},{64,96},{80,112},{96,0},{112,16},{1... | collective-permute-start | bytes 1179656 | tf_op jit(solution)/shard_map/ppermute | solution.py:438
  161.8 4.4 %collective-permute-done.25 = f32[3,4,64,128]{3,2,1,0:T(8,128)S(1)} collective-permute-done((f32[3,4,64,128]{3,2,1,0:T(8,128)S(1)}, f32[3,4,64,128]{3,2,1,0:T(8,128)S(1)}, u32[]{:S(2)}, u32[]{:S(2)}) %collective-permute-start.25) | collective-permute-done | bytes 393248 | tf_op jit(solution)/shard_map/ppermute | solution.py:438
  169.3 13.0 %collective-permute-done.31 = f32[3,4,64,128]{3,2,1,0:T(8,128)S(1)} collective-permute-done((f32[3,4,64,128]{3,2,1,0:T(8,128)S(1)}, f32[3,4,64,128]{3,2,1,0:T(8,128)S(1)}, u32[]{:S(2)}, u32[]{:S(2)}) %collective-permute-start.31) | collective-permute-done | bytes 393248 | tf_op jit(solution)/shard_map/ppermute | solution.py:438
  187.0 10.6 %fourth.1 = (f32[3,4,64,128]{3,2,1,0:T(8,128)S(1)}, f32[3,4,64,128]{3,2,1,0:T(8,128)S(1)}, f32[3,4,64,128]{3,2,1,0:T(8,128)S(1)}, f32[3,4,64,128]{3,2,1,0:T(8,12...) custom-call(s32[1]{0:T(128)} %bitcast.odd_ref, ...), custom_call_target="tpu_custom_call" | custom-call | bytes 4194304 | tf_op jit(solution)/shard_map/fourth/pallas_call | solution.py:63
  197.6 4.3 %collective-permute-start.35 = (f32[3,4,64,128]{3,2,1,0:T(8,128)S(1)}, f32[3,4,64,128]{3,2,1,0:T(8,128)S(1)}, u32[]{:S(2)}, u32[]{:S(2)}) collective-permute-start(f32[3,4,64,128]{3,2,1,0:T(8,128)S(1)} %get-tuple-element.83), channel_id=1, source_target_pairs={{0,64},{16,80},{32,96},{48,112},{64,0},{80,16},{96,32},{112,48},{1... | collective-permute-start | bytes 1179656 | tf_op jit(solution)/shard_map/ppermute | solution.py:438
  202.0 11.7 %collective-permute-done.35.moved = f32[3,4,64,128]{3,2,1,0:T(8,128)S(1)} collective-permute-done((f32[3,4,64,128]{3,2,1,0:T(8,128)S(1)}, f32[3,4,64,128]{3,2,1,0:T(8,128)S(1)}, u32[]{:S(2)}, u32[]{:S(2)}) %collective-permute-start.35) | collective-permute-done | bytes 393248 | tf_op jit(solution)/shard_map/ppermute | solution.py:438
  218.7 3.4 %collective-permute-done.34 = f32[3,4,64,128]{3,2,1,0:T(8,128)S(1)} collective-permute-done((f32[3,4,64,128]{3,2,1,0:T(8,128)S(1)}, f32[3,4,64,128]{3,2,1,0:T(8,128)S(1)}, u32[]{:S(2)}, u32[]{:S(2)}) %collective-permute-start.34) | collective-permute-done | bytes 393248 | tf_op jit(solution)/shard_map/ppermute | solution.py:438
  222.1 3.4 %collective-permute-done.36.hb = f32[3,2,64,128]{3,2,1,0:T(8,128)S(1)} collective-permute-done((f32[3,2,64,128]{3,2,1,0:T(8,128)S(1)}, f32[3,2,64,128]{3,2,1,0:T(8,128)S(1)}, u32[]{:S(2)}, u32[]{:S(2)}) %collective-permute-start.36) | collective-permute-done | bytes 196640 | tf_op jit(solution)/shard_map/ppermute | solution.py:433
  225.7 5.9 %collective-permute-done.38 = f32[3,4,64,128]{3,2,1,0:T(8,128)S(1)} collective-permute-done((f32[3,4,64,128]{3,2,1,0:T(8,128)S(1)}, f32[3,4,64,128]{3,2,1,0:T(8,128)S(1)}, u32[]{:S(2)}, u32[]{:S(2)}) %collective-permute-start.38) | collective-permute-done | bytes 393248 | tf_op jit(solution)/shard_map/ppermute | solution.py:438
  (93 shorter events, 64.0 us)
Async XLA Ops:
  14.9 15.1 %collective-permute-start.2 = (f32[3,4,64,128]{3,2,1,0:T(8,128)S(1)}, f32[3,4,64,128]{3,2,1,0:T(8,128)S(1)}, u32[]{:S(2)}, u32[]{:S(2)}) collective-permute-start(f32[3,4,64,128]{3,2,1,0:T(8,128)S(1)} %first_middle.1.after), channel_id=1, source_target_pairs={{0,16},{16,32},{32,48},{48,64},{64,80},{80,96},{96,112},{112,0},{1... | collective-permute-start | bytes 1179656 | tf_op jit(solution)/shard_map/ppermute | solution.py:438
  20.1 29.8 %collective-permute-start.5 = (f32[16,64,128]{2,1,0:T(8,128)S(1)}, f32[16,64,128]{2,1,0:T(8,128)S(1)}, u32[]{:S(2)}, u32[]{:S(2)}) collective-permute-start(f32[16,64,128]{2,1,0:T(8,128)S(1)} %get-tuple-element.55), channel_id=1, source_target_pairs={{1,2},{3,4},{5,6},{7,8},{9,10},{11,12},{13,14},{2,1},{4,3},{6,5},{... | collective-permute-start | bytes 1572872 | tf_op jit(solution)/shard_map/ppermute | solution.py:433
  29.9 21.1 %collective-permute-start.3 = (f32[3,4,64,128]{3,2,1,0:T(8,128)S(1)}, f32[3,4,64,128]{3,2,1,0:T(8,128)S(1)}, u32[]{:S(2)}, u32[]{:S(2)}) collective-permute-start(f32[3,4,64,128]{3,2,1,0:T(8,128)S(1)} %get-tuple-element.53), channel_id=1, source_target_pairs={{0,16},{16,32},{32,48},{48,64},{64,80},{80,96},{96,112},{112,0},{1... | collective-permute-start | bytes 1179656 | tf_op jit(solution)/shard_map/ppermute | solution.py:438
  29.9 24.6 %collective-permute-start.9 = (f32[3,4,64,128]{3,2,1,0:T(8,128)S(1)}, f32[3,4,64,128]{3,2,1,0:T(8,128)S(1)}, u32[]{:S(2)}, u32[]{:S(2)}) collective-permute-start(f32[3,4,64,128]{3,2,1,0:T(8,128)S(1)} %get-tuple-element.58), channel_id=1, source_target_pairs={{0,16},{16,32},{32,48},{64,80},{80,96},{96,112},{1,17},{17,33},{33... | collective-permute-start | bytes 1179656 | tf_op jit(solution)/shard_map/ppermute | solution.py:438
  31.3 23.3 %collective-permute-start.8 = (f32[3,4,64,128]{3,2,1,0:T(8,128)S(1)}, f32[3,4,64,128]{3,2,1,0:T(8,128)S(1)}, u32[]{:S(2)}, u32[]{:S(2)}) collective-permute-start(f32[3,4,64,128]{3,2,1,0:T(8,128)S(1)} %collective-permute-done.7), channel_id=1, source_target_pairs={{112,64},{48,0},{113,65},{49,1},{114,66},{50,2},{115,67},{51,3},{1... | collective-permute-start | bytes 1179656 | tf_op jit(solution)/shard_map/ppermute | solution.py:438
  65.6 15.5 %collective-permute-start.11 = (f32[3,4,64,128]{3,2,1,0:T(8,128)S(1)}, f32[3,4,64,128]{3,2,1,0:T(8,128)S(1)}, u32[]{:S(2)}, u32[]{:S(2)}) collective-permute-start(f32[3,4,64,128]{3,2,1,0:T(8,128)S(1)} %get-tuple-element.62), channel_id=1, source_target_pairs={{0,16},{16,32},{32,48},{48,64},{64,80},{80,96},{96,112},{112,0},{1... | collective-permute-start | bytes 1179656 | tf_op jit(solution)/shard_map/ppermute | solution.py:438
  65.7 24.7 %collective-permute-start.13 = (f32[3,4,64,128]{3,2,1,0:T(8,128)S(1)}, f32[3,4,64,128]{3,2,1,0:T(8,128)S(1)}, u32[]{:S(2)}, u32[]{:S(2)}) collective-permute-start(f32[3,4,64,128]{3,2,1,0:T(8,128)S(1)} %get-tuple-element.63), channel_id=1, source_target_pairs={{0,16},{16,32},{32,48},{48,64},{64,80},{80,96},{96,112},{112,0},{1... | collective-permute-start | bytes 1179656 | tf_op jit(solution)/shard_map/ppermute | solution.py:438
  65.8 34.3 %collective-permute-start.15 = (f32[3,4,64,128]{3,2,1,0:T(8,128)S(1)}, f32[3,4,64,128]{3,2,1,0:T(8,128)S(1)}, u32[]{:S(2)}, u32[]{:S(2)}) collective-permute-start(f32[3,4,64,128]{3,2,1,0:T(8,128)S(1)} %collective-permute-done.14), channel_id=1, source_target_pairs={{112,64},{48,0},{113,65},{49,1},{114,66},{50,2},{115,67},{51,3},{1... | collective-permute-start | bytes 1179656 | tf_op jit(solution)/shard_map/ppermute | solution.py:438
  67.1 33.0 %collective-permute-start.17 = (f32[3,4,64,128]{3,2,1,0:T(8,128)S(1)}, f32[3,4,64,128]{3,2,1,0:T(8,128)S(1)}, u32[]{:S(2)}, u32[]{:S(2)}) collective-permute-start(f32[3,4,64,128]{3,2,1,0:T(8,128)S(1)} %get-tuple-element.64), channel_id=1, source_target_pairs={{0,16},{16,32},{32,48},{64,80},{80,96},{96,112},{1,17},{17,33},{33... | collective-permute-start | bytes 1179656 | tf_op jit(solution)/shard_map/ppermute | solution.py:438
  81.1 19.0 %collective-permute-start.12 = (f32[3,4,64,128]{3,2,1,0:T(8,128)S(1)}, f32[3,4,64,128]{3,2,1,0:T(8,128)S(1)}, u32[]{:S(2)}, u32[]{:S(2)}) collective-permute-start(f32[3,4,64,128]{3,2,1,0:T(8,128)S(1)} %collective-permute-done.11.vb), channel_id=1, source_target_pairs={{1,2},{3,4},{5,6},{7,8},{9,10},{11,12},{13,14},{2,1},{4,3},{6,5},{... | collective-permute-start | bytes 1179656 | tf_op jit(solution)/shard_map/ppermute | solution.py:433
  107.2 14.5 %collective-permute-start.18 = (f32[3,4,64,128]{3,2,1,0:T(8,128)S(1)}, f32[3,4,64,128]{3,2,1,0:T(8,128)S(1)}, u32[]{:S(2)}, u32[]{:S(2)}) collective-permute-start(f32[3,4,64,128]{3,2,1,0:T(8,128)S(1)} %get-tuple-element.71), channel_id=1, source_target_pairs={{0,16},{16,32},{32,48},{48,64},{64,80},{80,96},{96,112},{112,0},{1... | collective-permute-start | bytes 1179656 | tf_op jit(solution)/shard_map/ppermute | solution.py:438
  107.3 26.9 %collective-permute-start.20 = (f32[3,4,64,128]{3,2,1,0:T(8,128)S(1)}, f32[3,4,64,128]{3,2,1,0:T(8,128)S(1)}, u32[]{:S(2)}, u32[]{:S(2)}) collective-permute-start(f32[3,4,64,128]{3,2,1,0:T(8,128)S(1)} %get-tuple-element.73), channel_id=1, source_target_pairs={{0,16},{16,32},{32,48},{48,64},{64,80},{80,96},{96,112},{112,0},{1... | collective-permute-start | bytes 1179656 | tf_op jit(solution)/shard_map/ppermute | solution.py:438
  107.4 28.9 %collective-permute-start.22 = (f32[3,4,64,128]{3,2,1,0:T(8,128)S(1)}, f32[3,4,64,128]{3,2,1,0:T(8,128)S(1)}, u32[]{:S(2)}, u32[]{:S(2)}) collective-permute-start(f32[3,4,64,128]{3,2,1,0:T(8,128)S(1)} %collective-permute-done.21), channel_id=1, source_target_pairs={{112,64},{48,0},{113,65},{49,1},{114,66},{50,2},{115,67},{51,3},{1... | collective-permute-start | bytes 1179656 | tf_op jit(solution)/shard_map/ppermute | solution.py:438
  108.7 28.4 %collective-permute-start.24 = (f32[3,4,64,128]{3,2,1,0:T(8,128)S(1)}, f32[3,4,64,128]{3,2,1,0:T(8,128)S(1)}, u32[]{:S(2)}, u32[]{:S(2)}) collective-permute-start(f32[3,4,64,128]{3,2,1,0:T(8,128)S(1)} %get-tuple-element.74), channel_id=1, source_target_pairs={{0,16},{16,32},{32,48},{64,80},{80,96},{96,112},{1,17},{17,33},{33... | collective-permute-start | bytes 1179656 | tf_op jit(solution)/shard_map/ppermute | solution.py:438
  121.7 15.5 %collective-permute-start.19 = (f32[3,4,64,128]{3,2,1,0:T(8,128)S(1)}, f32[3,4,64,128]{3,2,1,0:T(8,128)S(1)}, u32[]{:S(2)}, u32[]{:S(2)}) collective-permute-start(f32[3,4,64,128]{3,2,1,0:T(8,128)S(1)} %add.39.sb), channel_id=1, source_target_pairs={{1,2},{3,4},{5,6},{7,8},{9,10},{11,12},{13,14},{2,1},{4,3},{6,5},{... | collective-permute-start | bytes 1179656 | tf_op jit(solution)/shard_map/ppermute | solution.py:433
  144.5 21.7 %collective-permute-start.25 = (f32[3,4,64,128]{3,2,1,0:T(8,128)S(1)}, f32[3,4,64,128]{3,2,1,0:T(8,128)S(1)}, u32[]{:S(2)}, u32[]{:S(2)}) collective-permute-start(f32[3,4,64,128]{3,2,1,0:T(8,128)S(1)} %get-tuple-element.78), channel_id=1, source_target_pairs={{0,32},{16,48},{32,64},{48,80},{64,96},{80,112},{96,0},{112,16},{1... | collective-permute-start | bytes 1179656 | tf_op jit(solution)/shard_map/ppermute | solution.py:438
  153.0 16.2 %collective-permute-start.32 = (f32[3,4,64,128]{3,2,1,0:T(8,128)S(1)}, f32[3,4,64,128]{3,2,1,0:T(8,128)S(1)}, u32[]{:S(2)}, u32[]{:S(2)}) collective-permute-start(f32[3,4,64,128]{3,2,1,0:T(8,128)S(1)} %get-tuple-element.80), channel_id=1, source_target_pairs={{0,32},{16,48},{64,96},{80,112},{1,33},{17,49},{65,97},{81,113},{2... | collective-permute-start | bytes 1179656 | tf_op jit(solution)/shard_map/ppermute | solution.py:438
  155.1 27.2 %collective-permute-start.31 = (f32[3,4,64,128]{3,2,1,0:T(8,128)S(1)}, f32[3,4,64,128]{3,2,1,0:T(8,128)S(1)}, u32[]{:S(2)}, u32[]{:S(2)}) collective-permute-start(f32[3,4,64,128]{3,2,1,0:T(8,128)S(1)} %collective-permute-done.30), channel_id=1, source_target_pairs={{96,64},{112,80},{32,0},{48,16},{97,65},{113,81},{33,1},{49,17},{9... | collective-permute-start | bytes 1179656 | tf_op jit(solution)/shard_map/ppermute | solution.py:438
  157.8 29.2 %collective-permute-start.29 = (f32[3,4,64,128]{3,2,1,0:T(8,128)S(1)}, f32[3,4,64,128]{3,2,1,0:T(8,128)S(1)}, u32[]{:S(2)}, u32[]{:S(2)}) collective-permute-start(f32[3,4,64,128]{3,2,1,0:T(8,128)S(1)} %add.44.tm), channel_id=1, source_target_pairs={{0,1},{1,0},{2,3},{3,2},{4,5},{5,4},{6,7},{7,6},{8,9},{9,8},{10,11... | collective-permute-start | bytes 1179656 | tf_op jit(solution)/shard_map/ppermute | solution.py:430
  159.9 27.1 %collective-permute-start.28 = (f32[3,4,64,128]{3,2,1,0:T(8,128)S(1)}, f32[3,4,64,128]{3,2,1,0:T(8,128)S(1)}, u32[]{:S(2)}, u32[]{:S(2)}) collective-permute-start(f32[3,4,64,128]{3,2,1,0:T(8,128)S(1)} %add.44.tm), channel_id=1, source_target_pairs={{1,2},{3,4},{5,6},{7,8},{9,10},{11,12},{13,14},{2,1},{4,3},{6,5},{... | collective-permute-start | bytes 1179656 | tf_op jit(solution)/shard_map/ppermute | solution.py:433
  166.2 20.8 %collective-permute-start.26 = (f32[3,4,64,128]{3,2,1,0:T(8,128)S(1)}, f32[3,4,64,128]{3,2,1,0:T(8,128)S(1)}, u32[]{:S(2)}, u32[]{:S(2)}) collective-permute-start(f32[3,4,64,128]{3,2,1,0:T(8,128)S(1)} %add.43.tb), channel_id=1, source_target_pairs={{1,2},{3,4},{5,6},{7,8},{9,10},{11,12},{13,14},{2,1},{4,3},{6,5},{... | collective-permute-start | bytes 1179656 | tf_op jit(solution)/shard_map/ppermute | solution.py:433
  197.6 16.1 %collective-permute-start.35 = (f32[3,4,64,128]{3,2,1,0:T(8,128)S(1)}, f32[3,4,64,128]{3,2,1,0:T(8,128)S(1)}, u32[]{:S(2)}, u32[]{:S(2)}) collective-permute-start(f32[3,4,64,128]{3,2,1,0:T(8,128)S(1)} %get-tuple-element.83), channel_id=1, source_target_pairs={{0,64},{16,80},{32,96},{48,112},{64,0},{80,16},{96,32},{112,48},{1... | collective-permute-start | bytes 1179656 | tf_op jit(solution)/shard_map/ppermute | solution.py:438
  201.9 20.2 %collective-permute-start.34 = (f32[3,4,64,128]{3,2,1,0:T(8,128)S(1)}, f32[3,4,64,128]{3,2,1,0:T(8,128)S(1)}, u32[]{:S(2)}, u32[]{:S(2)}) collective-permute-start(f32[3,4,64,128]{3,2,1,0:T(8,128)S(1)} %get-tuple-element.81), channel_id=1, source_target_pairs={{0,64},{16,80},{32,96},{48,112},{64,0},{80,16},{96,32},{112,48},{1... | collective-permute-start | bytes 1179656 | tf_op jit(solution)/shard_map/ppermute | solution.py:438
  215.7 15.9 %collective-permute-start.38 = (f32[3,4,64,128]{3,2,1,0:T(8,128)S(1)}, f32[3,4,64,128]{3,2,1,0:T(8,128)S(1)}, u32[]{:S(2)}, u32[]{:S(2)}) collective-permute-start(f32[3,4,64,128]{3,2,1,0:T(8,128)S(1)} %get-tuple-element.90), channel_id=1, source_target_pairs={{0,64},{16,80},{32,96},{48,112},{64,0},{80,16},{96,32},{112,48},{1... | collective-permute-start | bytes 1179656 | tf_op jit(solution)/shard_map/ppermute | solution.py:438
  (23 other events, 128.1 us)

commit v8 on v7

--- a/solution.py
+++ b/solution.py
@@ -169,18 +169,19 @@
     return (1 - odd) * (n - width), odd * (n - width)
 
 
-def first_pack_kernel(odd_ref, g_low, g_high, s_low, s_high, r_low, r_high, a1, b1):
+def pack_kernel(odd_ref, g_low, g_high, s_low, s_high, t_low, t_high, r_low, r_high, a1, b1):
     odd = odd_ref[0]
 
     def fill(low, high):
-        for c in range(3):
-            for k in range(2):
-                low[2 * c + k] = g_low[0, c, k]
-                high[2 * c + k] = g_high[0, c, k]
-            low[6 + c] = s_low[0, c, 0]
-            high[6 + c] = s_high[0, c, 0]
-        low[9] = (r_low[0] + 1).astype(F32)
-        high[9] = (r_high[0] + 1).astype(F32)
+        for out, g, s, t, r in ((low, g_low, s_low, t_low, r_low), (high, g_high, s_high, t_high, r_high)):
+            for c in range(3):
+                for k in range(2):
+                    out[2 * c + k] = g[0, c, k]
+                out[6 + c] = s[0, c, 0]
+                for k in range(3):
+                    out[9 + 3 * c + k] = t[0, c, k]
+            for k in range(7):
+                out[18 + k] = (r[k] + 1).astype(F32)
 
     @pl.when(odd == 0)
     def even_slab():
@@ -189,17 +190,6 @@
     @pl.when(odd == 1)
     def odd_slab():
         fill(a1, b1)
-
-
-def second_pack_kernel(odd_ref, source, regions, a2, b2):
-    odd = odd_ref[0]
-    for two, start in zip((a2, b2), edges(odd, LX, 3)):
-        for c in range(3):
-            for k in range(3):
-                two[3 * c + k] = source[0, c, start + k]
-    for two, start in zip((a2, b2), edges(odd, LX, 7)):
-        for k in range(7):
-            two[9 + k] = (regions[start + k] + 1).astype(F32)
 
 
 def first_middle_kernel(cond_t, nu_t, guess, source, regions, after, out, y, held, cond, nu):
@@ -231,7 +221,7 @@
             for k in range(2):
                 x[c, high * (n - 2) + k, ROWS] = pack[2 * c + k]
             f[c, 1 + high * (n - 3)] = pack[6 + c]
-        cond[1 + high * (n - 3)], nu[1 + high * (n - 3)] = materials(pack[9], cond_t, nu_t)
+        cond[1 + high * (n - 3)], nu[1 + high * (n - 3)] = materials(pack[24 - 6 * high], cond_t, nu_t)
     fine_sweep(x, into(y), held, cond, nu, 1, 7, f)
     fine_sweep(x, into(y), held, cond, nu, 9, n - 1, f)
     fine_sweep(y, into(x), held, cond, nu, 2, 6)
@@ -258,7 +248,7 @@
     for i in range(LX):
         fill(7 + i, regions[i] + 1)
     for k in range(7):
-        from_on, from_off = ra[9 + k], rb[9 + k]
+        from_on, from_off = ra[18 + k], rb[18 + k]
         fill(k, jnp.where(odd == 1, from_on, from_off), k >= 4)
         fill(LX + 7 + k, jnp.where(odd == 1, from_off, from_on), k < 3)
 
@@ -288,13 +278,13 @@
 
 
 def second_kernel(
-    odd_ref, hb, vb, ha, va, vm, source, a1, b1, a2, b2, cond, nu,
+    odd_ref, hb, vb, ha, va, vm, vn, source, a1, b1, cond, nu,
     u0, oa, ob, om, x, y, held, f0, f1,
 ):
     odd = odd_ref[0]
     clear(x, y)
-    extend(odd, (va, vb, vm), (ha, hb), x)
-    extend_force(odd, source, 0, 3, (a2, b2), 0, f0)
+    extend(odd, (va, vb, vm, vn), (ha, hb), x)
+    extend_force(odd, source, 0, 3, (a1, b1), 9, f0)
     extend_force(odd, source, 1, 1, (a1, b1), 6, f1)
 
     def keep_u0(c, i, value):
@@ -321,13 +311,13 @@
 
 
 def residual_kernel(
-    odd_ref, hb, vb, ha, va, vm, vn, source, a2, b2, cond, nu, keep, spread, u0,
+    odd_ref, hb, vb, ha, va, vm, vn, source, a1, b1, cond, nu, keep, spread, u0,
     res_o, lb, la, lm, rb, ra, rm, x, y, held, f0, sems,
 ):
     odd = odd_ref[0]
     clear(x, y)
     extend(odd, (va, vb, vm, vn), (ha, hb), x)
-    extend_force(odd, source, 0, 3, (a2, b2), 0, f0)
+    extend_force(odd, source, 0, 3, (a1, b1), 9, f0)
 
     def less(c, i, value):
         x[c, i, ROWS] = value - u0[c, i - 2]
@@ -447,11 +437,19 @@
         plain = along(x, [(i, i + distance) for i in range(slices) if i not in wrapping])
         return around, plain
 
+    def later_wrapped(x, distance):
+        return later_parts(x, distance)[0]
+
+    inside = [(i, i + 1) for i in range(slices - 1) if i % half < half - 1]
+
     tables = (conductance, reluct)
     sa1, sb1 = call(
-        first_pack_kernel, "first_pack",
-        (odd, guess[:1, :, :2], guess[:1, :, LX - 2:], source[1:, :, :1], source[1:, :, LX - 1:], regions[:1], regions[LX - 1:]),
-        [planes(10), planes(10)], [],
+        pack_kernel, "pack",
+        (
+            odd, guess[:1, :, :2], guess[:1, :, LX - 2:], source[1:, :, :1], source[1:, :, LX - 1:],
+            source[:1, :, :3], source[:1, :, LX - 3:], regions[:7], regions[LX - 7:],
+        ),
+        [planes(25), planes(25)], [],
     )
     b1 = from_b(sb1)
     a1 = from_a(sa1)
@@ -459,32 +457,25 @@
         first_middle_kernel, "first_middle", (*tables, guess, source, regions, sb1),
         planes(3, 4), [padded(3, LX), vmem(3, LX)] + [vmem(LX)] * 2,
     )
-    sa2, sb2 = call(
-        second_pack_kernel, "second_pack", (odd, source, regions), [planes(16), planes(16)], [],
-    )
-    vm = later(um, 1)
-    sb2, sa2, b1 = fence((sb2, sa2, b1))
-    b2 = from_b(sb2)
-    a2 = from_a(sa2)
+    plain = along(um, inside)
     ua, ub = call(
         first_kernel, "first", (odd, *tables, guess, source, regions, a1, b1, um),
         [planes(3, 4), planes(3, 4)], [padded(3, LX + 4)] * 2 + [vmem(3, LX + 4)] * 2 + [vmem(LX + 4)] * 2,
     )
-    ub, vm = fence((ub, vm))
+    ub, plain, um = fence((ub, plain, um))
     vb = later(ub, 1)
-    around, plain = later_parts(ua, 1)
-    va = around + plain
+    va = later(ua, 1)
+    around = later_wrapped(um, 1)
     cond, nu, keep, spread = call(
-        material_kernel, "material", (odd, *tables, regions, a2, b2),
+        material_kernel, "material", (odd, *tables, regions, a1, b1),
         [planes(LX + 6)] * 2 + [planes(LX + 14)] * 2, [],
     )
-    vb, cond = fence((vb, cond))
     hb = from_b(vb)
     ha = from_a(va)
     n = LX + 8
     u0, ua, ub, um = call(
         second_kernel, "second",
-        (odd, hb, vb, ha, va, vm, source, a1, b1, a2, b2, cond, nu),
+        (odd, hb, vb, ha, va, around, plain, source, a1, b1, cond, nu),
         [planes(3, LX + 4), planes(3, 4), planes(3, 4), planes(3, 4)], [padded(3, n)] * 2 + [vmem(3, n)] * 3,
     )
     vb = later(ub, 1)
@@ -495,7 +486,7 @@
     ha = from_a(va)
     residual, lb, la, lm, rb, ra, rm = call(
         residual_kernel, "residual",
-        (odd, hb, vb, ha, va, around, plain, source, a2, b2, cond, nu, keep, spread, u0),
+        (odd, hb, vb, ha, va, around, plain, source, a1, b1, cond, nu, keep, spread, u0),
         [planes(1, 3, LX)] + [planes(3, 4)] * 6, [padded(3, n)] * 2 + [vmem(3, n)] * 2, 1, [ANY] + [VMEM] * 6,
     )
     sb = rb + later(lb, 1)

time: 236 us -> 244 us (1.034)
  the two profiles are of different devices: /device:TPU:17 before, /device:TPU:1 now
where the time goes in v8:
time: 244 us; the launch traced here: 243 us
  waiting for transfers between devices  128 us (52%)
  starting transfers between devices  69.5 us (28%)
  Pallas kernels  32.3 us (13%)
  local copies, waits for them, and re-layouts  11.7 us (5%)
    ppermute x23, waiting for transfers between devices, along(): return lax.ppermute(x, 'tm', pairs)  107 us
    ppermute x23, starting transfers between devices, along(): return lax.ppermute(x, 'tm', pairs)  41.7 us
    pallas_call x10, Pallas kernels, call(): pl.pallas_call(kernel, name=name, out_shape=outs, in_specs=in_specs, out_...  32.3 us
    ppermute x7, starting transfers between devices, from_b(): return lax.ppermute(x, 'space', off_chip)  22 us
    ppermute x7, waiting for transfers between devices, from_b(): return lax.ppermute(x, 'space', off_chip)  18 us
    unnamed x20, local copies, waits for them, and re-layouts  6.26 us
    ppermute x7, starting transfers between devices, from_a(): return lax.ppermute(x, 'space', on_chip)  5.82 us
  transfers between devices with their start and end apart: 37, of which 22 were waited for; matrix products, arithmetic and copies ran while one was open for 0% of the time, Pallas kernels for 2%

profile of v8, /device:TPU:1, one launch (start us, length us, event | category | flops | bytes accessed | tf_op | source)
XLA Modules:
  0.0 243.2 jit_solution(9295535874875208877)
XLA Ops:
  12.3 3.5 %collective-permute-start.1 = (f32[25,64,128]{2,1,0:T(8,128)S(1)}, f32[25,64,128]{2,1,0:T(8,128)S(1)}, u32[]{:S(2)}, u32[]{:S(2)}) collective-permute-start(f32[25,64,128]{2,1,0:T(8,128)S(1)} %get-tuple-element.42.after), channel_id=1, source_target_pairs={{1,2},{3,4},{5,6},{7,8},{9,10},{11,12},{13,14},{2,1},{4,3},{6,5},{... | collective-permute-start | bytes 2457608 | tf_op jit(solution)/shard_map/ppermute | solution.py:423
  19.0 3.1 %collective-permute-start.2 = (f32[3,4,64,128]{3,2,1,0:T(8,128)S(1)}, f32[3,4,64,128]{3,2,1,0:T(8,128)S(1)}, u32[]{:S(2)}, u32[]{:S(2)}) collective-permute-start(f32[3,4,64,128]{3,2,1,0:T(8,128)S(1)} %first_middle.1.after), channel_id=1, source_target_pairs={{0,16},{16,32},{32,48},{64,80},{80,96},{96,112},{1,17},{17,33},{33... | collective-permute-start | bytes 1179656 | tf_op jit(solution)/shard_map/ppermute | solution.py:428
  22.2 11.7 %collective-permute-done.1.rb.b1 = f32[25,64,128]{2,1,0:T(8,128)S(1)} collective-permute-done((f32[25,64,128]{2,1,0:T(8,128)S(1)}, f32[25,64,128]{2,1,0:T(8,128)S(1)}, u32[]{:S(2)}, u32[]{:S(2)}) %collective-permute-start.1) | collective-permute-done | bytes 819232 | tf_op jit(solution)/shard_map/ppermute | solution.py:423
  39.4 8.6 %collective-permute-done.3.vb = f32[3,4,64,128]{3,2,1,0:T(8,128)S(1)} collective-permute-done((f32[3,4,64,128]{3,2,1,0:T(8,128)S(1)}, f32[3,4,64,128]{3,2,1,0:T(8,128)S(1)}, u32[]{:S(2)}, u32[]{:S(2)}) %collective-permute-start.3) | collective-permute-done | bytes 393248 | tf_op jit(solution)/shard_map/ppermute | solution.py:428
  48.0 6.1 %collective-permute-start.4 = (f32[3,4,64,128]{3,2,1,0:T(8,128)S(1)}, f32[3,4,64,128]{3,2,1,0:T(8,128)S(1)}, u32[]{:S(2)}, u32[]{:S(2)}) collective-permute-start(f32[3,4,64,128]{3,2,1,0:T(8,128)S(1)} %collective-permute-done.3.vb), channel_id=1, source_target_pairs={{1,2},{3,4},{5,6},{7,8},{9,10},{11,12},{13,14},{2,1},{4,3},{6,5},{... | collective-permute-start | bytes 1179656 | tf_op jit(solution)/shard_map/ppermute | solution.py:423
  55.4 9.0 %collective-permute-done.5.va = f32[3,4,64,128]{3,2,1,0:T(8,128)S(1)} collective-permute-done((f32[3,4,64,128]{3,2,1,0:T(8,128)S(1)}, f32[3,4,64,128]{3,2,1,0:T(8,128)S(1)}, u32[]{:S(2)}, u32[]{:S(2)}) %collective-permute-start.5) | collective-permute-done | bytes 393248 | tf_op jit(solution)/shard_map/ppermute | solution.py:428
  71.0 4.7 %second.1 = (f32[3,16,64,128]{3,2,1,0:T(8,128)S(1)}, f32[3,4,64,128]{3,2,1,0:T(8,128)S(1)}, f32[3,4,64,128]{3,2,1,0:T(8,128)S(1)}, f32[3,4,64,128]{3,2,1,0:T(8,128)S(1)}) custom-call(s32[1]{0:T(128)} %bitcast.odd_ref, f32[3,4,64,128]{3,2,1,0:T(8,128)S(1)} %collective-permute-done.4.hb, f32[3,4,64,128]{3,2,1,0:T(8,128)S(1)} %collective-permute-done.3.vb, ...), custom_call_target="tpu_custom_call" | custom-call | bytes 4194304 | tf_op jit(solution)/shard_map/second/pallas_call | solution.py:63
  77.9 9.7 %collective-permute-start.15 = (f32[3,4,64,128]{3,2,1,0:T(8,128)S(1)}, f32[3,4,64,128]{3,2,1,0:T(8,128)S(1)}, u32[]{:S(2)}, u32[]{:S(2)}) collective-permute-start(f32[3,4,64,128]{3,2,1,0:T(8,128)S(1)} %get-tuple-element.52), channel_id=1, source_target_pairs={{0,16},{16,32},{32,48},{64,80},{80,96},{96,112},{1,17},{17,33},{33... | collective-permute-start | bytes 1179656 | tf_op jit(solution)/shard_map/ppermute | solution.py:428
  87.6 6.0 %collective-permute-done.9.vb = f32[3,4,64,128]{3,2,1,0:T(8,128)S(1)} collective-permute-done((f32[3,4,64,128]{3,2,1,0:T(8,128)S(1)}, f32[3,4,64,128]{3,2,1,0:T(8,128)S(1)}, u32[]{:S(2)}, u32[]{:S(2)}) %collective-permute-start.9) | collective-permute-done | bytes 393248 | tf_op jit(solution)/shard_map/ppermute | solution.py:428
  93.6 4.7 %collective-permute-start.10 = (f32[3,4,64,128]{3,2,1,0:T(8,128)S(1)}, f32[3,4,64,128]{3,2,1,0:T(8,128)S(1)}, u32[]{:S(2)}, u32[]{:S(2)}) collective-permute-start(f32[3,4,64,128]{3,2,1,0:T(8,128)S(1)} %collective-permute-done.9.vb), channel_id=1, source_target_pairs={{1,2},{3,4},{5,6},{7,8},{9,10},{11,12},{13,14},{2,1},{4,3},{6,5},{... | collective-permute-start | bytes 1179656 | tf_op jit(solution)/shard_map/ppermute | solution.py:423
  98.3 5.1 %collective-permute-done.11.va = f32[3,4,64,128]{3,2,1,0:T(8,128)S(1)} collective-permute-done((f32[3,4,64,128]{3,2,1,0:T(8,128)S(1)}, f32[3,4,64,128]{3,2,1,0:T(8,128)S(1)}, u32[]{:S(2)}, u32[]{:S(2)}) %collective-permute-start.11) | collective-permute-done | bytes 393248 | tf_op jit(solution)/shard_map/ppermute | solution.py:428
  103.3 7.2 %collective-permute-done.13.vm = f32[3,4,64,128]{3,2,1,0:T(8,128)S(1)} collective-permute-done((f32[3,4,64,128]{3,2,1,0:T(8,128)S(1)}, f32[3,4,64,128]{3,2,1,0:T(8,128)S(1)}, u32[]{:S(2)}, u32[]{:S(2)}) %collective-permute-start.13) | collective-permute-done | bytes 393248 | tf_op jit(solution)/shard_map/ppermute | solution.py:428
  112.2 4.7 %residual.1 = (f32[1,3,12,64,128]{4,3,2,1,0:T(8,128)}, f32[3,4,64,128]{3,2,1,0:T(8,128)S(1)}, f32[3,4,64,128]{3,2,1,0:T(8,128)S(1)}, f32[3,4,64,128]{3,2,1,0:T(8...) custom-call(s32[1]{0:T(128)} %bitcast.odd_ref, ...), custom_call_target="tpu_custom_call" | custom-call | bytes 4194304 | tf_op jit(solution)/shard_map/residual/pallas_call | solution.py:63
  122.0 9.9 %collective-permute-done.16 = f32[3,4,64,128]{3,2,1,0:T(8,128)S(1)} collective-permute-done((f32[3,4,64,128]{3,2,1,0:T(8,128)S(1)}, f32[3,4,64,128]{3,2,1,0:T(8,128)S(1)}, u32[]{:S(2)}, u32[]{:S(2)}) %collective-permute-start.16) | collective-permute-done | bytes 393248 | tf_op jit(solution)/shard_map/ppermute | solution.py:428
  133.9 10.5 %collective-permute-done.18 = f32[3,4,64,128]{3,2,1,0:T(8,128)S(1)} collective-permute-done((f32[3,4,64,128]{3,2,1,0:T(8,128)S(1)}, f32[3,4,64,128]{3,2,1,0:T(8,128)S(1)}, u32[]{:S(2)}, u32[]{:S(2)}) %collective-permute-start.18) | collective-permute-done | bytes 393248 | tf_op jit(solution)/shard_map/ppermute | solution.py:428
  148.1 4.3 %square.1 = (f32[3,4,64,128]{3,2,1,0:T(8,128)S(1)}, f32[3,4,64,128]{3,2,1,0:T(8,128)S(1)}, f32[3,4,64,128]{3,2,1,0:T(8,128)S(1)}) custom-call(s32[1]{0:T(128)} %bitcast.odd_ref, f32[3,4,64,128]{3,2,1,0:T(8,128)S(1)} %collective-permute-done.17.hb, f32[3,4,64,128]{3,2,1,0:T(8,128)S(1)} %add.35.sb, f32[3,4,64,128]{3,2,1,0:T(8,128)S(1)} %collective-permute-done.21.ha, ...), custom_call_target="tpu_custom_call" | custom-call | bytes 4194304 | tf_op jit(solution)/shard_map/square/pallas_call | solution.py:63
  153.9 9.0 %collective-permute-start.23 = (f32[3,4,64,128]{3,2,1,0:T(8,128)S(1)}, f32[3,4,64,128]{3,2,1,0:T(8,128)S(1)}, u32[]{:S(2)}, u32[]{:S(2)}) collective-permute-start(f32[3,4,64,128]{3,2,1,0:T(8,128)S(1)} %get-tuple-element.66), channel_id=1, source_target_pairs={{0,32},{16,48},{32,64},{48,80},{64,96},{80,112},{96,0},{112,16},{1... | collective-permute-start | bytes 1179656 | tf_op jit(solution)/shard_map/ppermute | solution.py:428
  171.4 4.4 %collective-permute-done.23 = f32[3,4,64,128]{3,2,1,0:T(8,128)S(1)} collective-permute-done((f32[3,4,64,128]{3,2,1,0:T(8,128)S(1)}, f32[3,4,64,128]{3,2,1,0:T(8,128)S(1)}, u32[]{:S(2)}, u32[]{:S(2)}) %collective-permute-start.23) | collective-permute-done | bytes 393248 | tf_op jit(solution)/shard_map/ppermute | solution.py:428
  179.2 13.0 %collective-permute-done.29 = f32[3,4,64,128]{3,2,1,0:T(8,128)S(1)} collective-permute-done((f32[3,4,64,128]{3,2,1,0:T(8,128)S(1)}, f32[3,4,64,128]{3,2,1,0:T(8,128)S(1)}, u32[]{:S(2)}, u32[]{:S(2)}) %collective-permute-start.29) | collective-permute-done | bytes 393248 | tf_op jit(solution)/shard_map/ppermute | solution.py:428
  193.6 3.3 %collective-permute-done.24.near_b = f32[3,4,64,128]{3,2,1,0:T(8,128)S(1)} collective-permute-done((f32[3,4,64,128]{3,2,1,0:T(8,128)S(1)}, f32[3,4,64,128]{3,2,1,0:T(8,128)S(1)}, u32[]{:S(2)}, u32[]{:S(2)}) %collective-permute-start.24) | collective-permute-done | bytes 393248 | tf_op jit(solution)/shard_map/ppermute | solution.py:423
  196.9 10.6 %fourth.1 = (f32[3,4,64,128]{3,2,1,0:T(8,128)S(1)}, f32[3,4,64,128]{3,2,1,0:T(8,128)S(1)}, f32[3,4,64,128]{3,2,1,0:T(8,128)S(1)}, f32[3,4,64,128]{3,2,1,0:T(8,12...) custom-call(s32[1]{0:T(128)} %bitcast.odd_ref, ...), custom_call_target="tpu_custom_call" | custom-call | bytes 4194304 | tf_op jit(solution)/shard_map/fourth/pallas_call | solution.py:63
  210.8 11.8 %collective-permute-done.33.moved = f32[3,4,64,128]{3,2,1,0:T(8,128)S(1)} collective-permute-done((f32[3,4,64,128]{3,2,1,0:T(8,128)S(1)}, f32[3,4,64,128]{3,2,1,0:T(8,128)S(1)}, u32[]{:S(2)}, u32[]{:S(2)}) %collective-permute-start.33) | collective-permute-done | bytes 393248 | tf_op jit(solution)/shard_map/ppermute | solution.py:428
  224.6 6.3 %collective-permute-done.32 = f32[3,4,64,128]{3,2,1,0:T(8,128)S(1)} collective-permute-done((f32[3,4,64,128]{3,2,1,0:T(8,128)S(1)}, f32[3,4,64,128]{3,2,1,0:T(8,128)S(1)}, u32[]{:S(2)}, u32[]{:S(2)}) %collective-permute-start.32) | collective-permute-done | bytes 393248 | tf_op jit(solution)/shard_map/ppermute | solution.py:428
  231.7 8.4 %collective-permute-done.36 = f32[3,4,64,128]{3,2,1,0:T(8,128)S(1)} collective-permute-done((f32[3,4,64,128]{3,2,1,0:T(8,128)S(1)}, f32[3,4,64,128]{3,2,1,0:T(8,128)S(1)}, u32[]{:S(2)}, u32[]{:S(2)}) %collective-permute-start.36) | collective-permute-done | bytes 393248 | tf_op jit(solution)/shard_map/ppermute | solution.py:428
  (92 shorter events, 66.5 us)
Async XLA Ops:
  12.3 21.6 %collective-permute-start.1 = (f32[25,64,128]{2,1,0:T(8,128)S(1)}, f32[25,64,128]{2,1,0:T(8,128)S(1)}, u32[]{:S(2)}, u32[]{:S(2)}) collective-permute-start(f32[25,64,128]{2,1,0:T(8,128)S(1)} %get-tuple-element.42.after), channel_id=1, source_target_pairs={{1,2},{3,4},{5,6},{7,8},{9,10},{11,12},{13,14},{2,1},{4,3},{6,5},{... | collective-permute-start | bytes 2457608 | tf_op jit(solution)/shard_map/ppermute | solution.py:423
  19.0 17.1 %collective-permute-start.2 = (f32[3,4,64,128]{3,2,1,0:T(8,128)S(1)}, f32[3,4,64,128]{3,2,1,0:T(8,128)S(1)}, u32[]{:S(2)}, u32[]{:S(2)}) collective-permute-start(f32[3,4,64,128]{3,2,1,0:T(8,128)S(1)} %first_middle.1.after), channel_id=1, source_target_pairs={{0,16},{16,32},{32,48},{64,80},{80,96},{96,112},{1,17},{17,33},{33... | collective-permute-start | bytes 1179656 | tf_op jit(solution)/shard_map/ppermute | solution.py:428
  37.4 16.7 %collective-permute-start.7 = (f32[3,4,64,128]{3,2,1,0:T(8,128)S(1)}, f32[3,4,64,128]{3,2,1,0:T(8,128)S(1)}, u32[]{:S(2)}, u32[]{:S(2)}) collective-permute-start(f32[3,4,64,128]{3,2,1,0:T(8,128)S(1)} %first_middle.1.after), channel_id=1, source_target_pairs={{48,112},{112,48},{49,113},{113,49},{50,114},{114,50},{51,115},{11... | collective-permute-start | bytes 1179656 | tf_op jit(solution)/shard_map/ppermute | solution.py:428
  38.1 26.3 %collective-permute-start.5 = (f32[3,4,64,128]{3,2,1,0:T(8,128)S(1)}, f32[3,4,64,128]{3,2,1,0:T(8,128)S(1)}, u32[]{:S(2)}, u32[]{:S(2)}) collective-permute-start(f32[3,4,64,128]{3,2,1,0:T(8,128)S(1)} %get-tuple-element.45), channel_id=1, source_target_pairs={{0,16},{16,32},{32,48},{48,64},{64,80},{80,96},{96,112},{112,0},{1... | collective-permute-start | bytes 1179656 | tf_op jit(solution)/shard_map/ppermute | solution.py:428
  48.0 20.0 %collective-permute-start.4 = (f32[3,4,64,128]{3,2,1,0:T(8,128)S(1)}, f32[3,4,64,128]{3,2,1,0:T(8,128)S(1)}, u32[]{:S(2)}, u32[]{:S(2)}) collective-permute-start(f32[3,4,64,128]{3,2,1,0:T(8,128)S(1)} %collective-permute-done.3.vb), channel_id=1, source_target_pairs={{1,2},{3,4},{5,6},{7,8},{9,10},{11,12},{13,14},{2,1},{4,3},{6,5},{... | collective-permute-start | bytes 1179656 | tf_op jit(solution)/shard_map/ppermute | solution.py:423
  54.1 16.9 %collective-permute-start.8 = (f32[3,4,64,128]{3,2,1,0:T(8,128)S(1)}, f32[3,4,64,128]{3,2,1,0:T(8,128)S(1)}, u32[]{:S(2)}, u32[]{:S(2)}) collective-permute-start(f32[3,4,64,128]{3,2,1,0:T(8,128)S(1)} %collective-permute-done.7), channel_id=1, source_target_pairs={{112,64},{48,0},{113,65},{49,1},{114,66},{50,2},{115,67},{51,3},{1... | collective-permute-start | bytes 1179656 | tf_op jit(solution)/shard_map/ppermute | solution.py:428
  76.4 17.2 %collective-permute-start.9 = (f32[3,4,64,128]{3,2,1,0:T(8,128)S(1)}, f32[3,4,64,128]{3,2,1,0:T(8,128)S(1)}, u32[]{:S(2)}, u32[]{:S(2)}) collective-permute-start(f32[3,4,64,128]{3,2,1,0:T(8,128)S(1)} %get-tuple-element.50), channel_id=1, source_target_pairs={{0,16},{16,32},{32,48},{48,64},{64,80},{80,96},{96,112},{112,0},{1... | collective-permute-start | bytes 1179656 | tf_op jit(solution)/shard_map/ppermute | solution.py:428
  76.5 26.8 %collective-permute-start.11 = (f32[3,4,64,128]{3,2,1,0:T(8,128)S(1)}, f32[3,4,64,128]{3,2,1,0:T(8,128)S(1)}, u32[]{:S(2)}, u32[]{:S(2)}) collective-permute-start(f32[3,4,64,128]{3,2,1,0:T(8,128)S(1)} %get-tuple-element.51), channel_id=1, source_target_pairs={{0,16},{16,32},{32,48},{48,64},{64,80},{80,96},{96,112},{112,0},{1... | collective-permute-start | bytes 1179656 | tf_op jit(solution)/shard_map/ppermute | solution.py:428
  76.6 33.9 %collective-permute-start.13 = (f32[3,4,64,128]{3,2,1,0:T(8,128)S(1)}, f32[3,4,64,128]{3,2,1,0:T(8,128)S(1)}, u32[]{:S(2)}, u32[]{:S(2)}) collective-permute-start(f32[3,4,64,128]{3,2,1,0:T(8,128)S(1)} %collective-permute-done.12), channel_id=1, source_target_pairs={{112,64},{48,0},{113,65},{49,1},{114,66},{50,2},{115,67},{51,3},{1... | collective-permute-start | bytes 1179656 | tf_op jit(solution)/shard_map/ppermute | solution.py:428
  77.9 32.6 %collective-permute-start.15 = (f32[3,4,64,128]{3,2,1,0:T(8,128)S(1)}, f32[3,4,64,128]{3,2,1,0:T(8,128)S(1)}, u32[]{:S(2)}, u32[]{:S(2)}) collective-permute-start(f32[3,4,64,128]{3,2,1,0:T(8,128)S(1)} %get-tuple-element.52), channel_id=1, source_target_pairs={{0,16},{16,32},{32,48},{64,80},{80,96},{96,112},{1,17},{17,33},{33... | collective-permute-start | bytes 1179656 | tf_op jit(solution)/shard_map/ppermute | solution.py:428
  93.6 16.9 %collective-permute-start.10 = (f32[3,4,64,128]{3,2,1,0:T(8,128)S(1)}, f32[3,4,64,128]{3,2,1,0:T(8,128)S(1)}, u32[]{:S(2)}, u32[]{:S(2)}) collective-permute-start(f32[3,4,64,128]{3,2,1,0:T(8,128)S(1)} %collective-permute-done.9.vb), channel_id=1, source_target_pairs={{1,2},{3,4},{5,6},{7,8},{9,10},{11,12},{13,14},{2,1},{4,3},{6,5},{... | collective-permute-start | bytes 1179656 | tf_op jit(solution)/shard_map/ppermute | solution.py:423
  117.7 26.6 %collective-permute-start.18 = (f32[3,4,64,128]{3,2,1,0:T(8,128)S(1)}, f32[3,4,64,128]{3,2,1,0:T(8,128)S(1)}, u32[]{:S(2)}, u32[]{:S(2)}) collective-permute-start(f32[3,4,64,128]{3,2,1,0:T(8,128)S(1)} %get-tuple-element.61), channel_id=1, source_target_pairs={{0,16},{16,32},{32,48},{48,64},{64,80},{80,96},{96,112},{112,0},{1... | collective-permute-start | bytes 1179656 | tf_op jit(solution)/shard_map/ppermute | solution.py:428
  117.8 28.1 %collective-permute-start.20 = (f32[3,4,64,128]{3,2,1,0:T(8,128)S(1)}, f32[3,4,64,128]{3,2,1,0:T(8,128)S(1)}, u32[]{:S(2)}, u32[]{:S(2)}) collective-permute-start(f32[3,4,64,128]{3,2,1,0:T(8,128)S(1)} %collective-permute-done.19), channel_id=1, source_target_pairs={{112,64},{48,0},{113,65},{49,1},{114,66},{50,2},{115,67},{51,3},{1... | collective-permute-start | bytes 1179656 | tf_op jit(solution)/shard_map/ppermute | solution.py:428
  119.1 27.7 %collective-permute-start.22 = (f32[3,4,64,128]{3,2,1,0:T(8,128)S(1)}, f32[3,4,64,128]{3,2,1,0:T(8,128)S(1)}, u32[]{:S(2)}, u32[]{:S(2)}) collective-permute-start(f32[3,4,64,128]{3,2,1,0:T(8,128)S(1)} %get-tuple-element.62), channel_id=1, source_target_pairs={{0,16},{16,32},{32,48},{64,80},{80,96},{96,112},{1,17},{17,33},{33... | collective-permute-start | bytes 1179656 | tf_op jit(solution)/shard_map/ppermute | solution.py:428
  131.9 14.9 %collective-permute-start.17 = (f32[3,4,64,128]{3,2,1,0:T(8,128)S(1)}, f32[3,4,64,128]{3,2,1,0:T(8,128)S(1)}, u32[]{:S(2)}, u32[]{:S(2)}) collective-permute-start(f32[3,4,64,128]{3,2,1,0:T(8,128)S(1)} %add.35.sb), channel_id=1, source_target_pairs={{1,2},{3,4},{5,6},{7,8},{9,10},{11,12},{13,14},{2,1},{4,3},{6,5},{... | collective-permute-start | bytes 1179656 | tf_op jit(solution)/shard_map/ppermute | solution.py:423
  153.9 21.9 %collective-permute-start.23 = (f32[3,4,64,128]{3,2,1,0:T(8,128)S(1)}, f32[3,4,64,128]{3,2,1,0:T(8,128)S(1)}, u32[]{:S(2)}, u32[]{:S(2)}) collective-permute-start(f32[3,4,64,128]{3,2,1,0:T(8,128)S(1)} %get-tuple-element.66), channel_id=1, source_target_pairs={{0,32},{16,48},{32,64},{48,80},{64,96},{80,112},{96,0},{112,16},{1... | collective-permute-start | bytes 1179656 | tf_op jit(solution)/shard_map/ppermute | solution.py:428
  163.0 16.2 %collective-permute-start.30 = (f32[3,4,64,128]{3,2,1,0:T(8,128)S(1)}, f32[3,4,64,128]{3,2,1,0:T(8,128)S(1)}, u32[]{:S(2)}, u32[]{:S(2)}) collective-permute-start(f32[3,4,64,128]{3,2,1,0:T(8,128)S(1)} %get-tuple-element.68), channel_id=1, source_target_pairs={{0,32},{16,48},{64,96},{80,112},{1,33},{17,49},{65,97},{81,113},{2... | collective-permute-start | bytes 1179656 | tf_op jit(solution)/shard_map/ppermute | solution.py:428
  165.0 27.2 %collective-permute-start.29 = (f32[3,4,64,128]{3,2,1,0:T(8,128)S(1)}, f32[3,4,64,128]{3,2,1,0:T(8,128)S(1)}, u32[]{:S(2)}, u32[]{:S(2)}) collective-permute-start(f32[3,4,64,128]{3,2,1,0:T(8,128)S(1)} %collective-permute-done.28), channel_id=1, source_target_pairs={{96,64},{112,80},{32,0},{48,16},{97,65},{113,81},{33,1},{49,17},{9... | collective-permute-start | bytes 1179656 | tf_op jit(solution)/shard_map/ppermute | solution.py:428
  167.4 29.5 %collective-permute-start.27 = (f32[3,4,64,128]{3,2,1,0:T(8,128)S(1)}, f32[3,4,64,128]{3,2,1,0:T(8,128)S(1)}, u32[]{:S(2)}, u32[]{:S(2)}) collective-permute-start(f32[3,4,64,128]{3,2,1,0:T(8,128)S(1)} %add.40.tm), channel_id=1, source_target_pairs={{0,1},{1,0},{2,3},{3,2},{4,5},{5,4},{6,7},{7,6},{8,9},{9,8},{10,11... | collective-permute-start | bytes 1179656 | tf_op jit(solution)/shard_map/ppermute | solution.py:420
  169.5 27.4 %collective-permute-start.26 = (f32[3,4,64,128]{3,2,1,0:T(8,128)S(1)}, f32[3,4,64,128]{3,2,1,0:T(8,128)S(1)}, u32[]{:S(2)}, u32[]{:S(2)}) collective-permute-start(f32[3,4,64,128]{3,2,1,0:T(8,128)S(1)} %add.40.tm), channel_id=1, source_target_pairs={{1,2},{3,4},{5,6},{7,8},{9,10},{11,12},{13,14},{2,1},{4,3},{6,5},{... | collective-permute-start | bytes 1179656 | tf_op jit(solution)/shard_map/ppermute | solution.py:423
  175.9 21.0 %collective-permute-start.24 = (f32[3,4,64,128]{3,2,1,0:T(8,128)S(1)}, f32[3,4,64,128]{3,2,1,0:T(8,128)S(1)}, u32[]{:S(2)}, u32[]{:S(2)}) collective-permute-start(f32[3,4,64,128]{3,2,1,0:T(8,128)S(1)} %add.39.tb), channel_id=1, source_target_pairs={{1,2},{3,4},{5,6},{7,8},{9,10},{11,12},{13,14},{2,1},{4,3},{6,5},{... | collective-permute-start | bytes 1179656 | tf_op jit(solution)/shard_map/ppermute | solution.py:423
  207.5 15.1 %collective-permute-start.33 = (f32[3,4,64,128]{3,2,1,0:T(8,128)S(1)}, f32[3,4,64,128]{3,2,1,0:T(8,128)S(1)}, u32[]{:S(2)}, u32[]{:S(2)}) collective-permute-start(f32[3,4,64,128]{3,2,1,0:T(8,128)S(1)} %get-tuple-element.71), channel_id=1, source_target_pairs={{0,64},{16,80},{32,96},{48,112},{64,0},{80,16},{96,32},{112,48},{1... | collective-permute-start | bytes 1179656 | tf_op jit(solution)/shard_map/ppermute | solution.py:428
  207.8 23.2 %collective-permute-start.32 = (f32[3,4,64,128]{3,2,1,0:T(8,128)S(1)}, f32[3,4,64,128]{3,2,1,0:T(8,128)S(1)}, u32[]{:S(2)}, u32[]{:S(2)}) collective-permute-start(f32[3,4,64,128]{3,2,1,0:T(8,128)S(1)} %get-tuple-element.69), channel_id=1, source_target_pairs={{0,64},{16,80},{32,96},{48,112},{64,0},{80,16},{96,32},{112,48},{1... | collective-permute-start | bytes 1179656 | tf_op jit(solution)/shard_map/ppermute | solution.py:428
  224.5 15.5 %collective-permute-start.36 = (f32[3,4,64,128]{3,2,1,0:T(8,128)S(1)}, f32[3,4,64,128]{3,2,1,0:T(8,128)S(1)}, u32[]{:S(2)}, u32[]{:S(2)}) collective-permute-start(f32[3,4,64,128]{3,2,1,0:T(8,128)S(1)} %get-tuple-element.78), channel_id=1, source_target_pairs={{0,64},{16,80},{32,96},{48,112},{64,0},{80,16},{96,32},{112,48},{1... | collective-permute-start | bytes 1179656 | tf_op jit(solution)/shard_map/ppermute | solution.py:428
  (23 other events, 150.3 us)

commit v9 on v7

--- a/solution.py
+++ b/solution.py
@@ -202,7 +202,7 @@
             two[9 + k] = (regions[start + k] + 1).astype(F32)
 
 
-def first_middle_kernel(cond_t, nu_t, guess, source, regions, after, out, y, held, cond, nu):
+def first_middle_kernel(cond_t, nu_t, guess, source, regions, out, y, held, cond, nu):
     def prepare(i):
         cond[i], nu[i] = materials(regions[i] + 1, cond_t, nu_t)
 
@@ -288,12 +288,12 @@
 
 
 def second_kernel(
-    odd_ref, hb, vb, ha, va, vm, source, a1, b1, a2, b2, cond, nu,
+    odd_ref, hb, vb, ha, va, vm, vn, source, a1, b1, a2, b2, cond, nu,
     u0, oa, ob, om, x, y, held, f0, f1,
 ):
     odd = odd_ref[0]
     clear(x, y)
-    extend(odd, (va, vb, vm), (ha, hb), x)
+    extend(odd, (va, vb, vm, vn), (ha, hb), x)
     extend_force(odd, source, 0, 3, (a2, b2), 0, f0)
     extend_force(odd, source, 1, 1, (a1, b1), 6, f1)
 
@@ -456,13 +456,13 @@
     b1 = from_b(sb1)
     a1 = from_a(sa1)
     um = call(
-        first_middle_kernel, "first_middle", (*tables, guess, source, regions, sb1),
+        first_middle_kernel, "first_middle", (*tables, guess, source, regions),
         planes(3, 4), [padded(3, LX), vmem(3, LX)] + [vmem(LX)] * 2,
     )
     sa2, sb2 = call(
         second_pack_kernel, "second_pack", (odd, source, regions), [planes(16), planes(16)], [],
     )
-    vm = later(um, 1)
+    vm = later_parts(um, 1)
     sb2, sa2, b1 = fence((sb2, sa2, b1))
     b2 = from_b(sb2)
     a2 = from_a(sa2)
@@ -470,21 +470,20 @@
         first_kernel, "first", (odd, *tables, guess, source, regions, a1, b1, um),
         [planes(3, 4), planes(3, 4)], [padded(3, LX + 4)] * 2 + [vmem(3, LX + 4)] * 2 + [vmem(LX + 4)] * 2,
     )
-    ub, vm = fence((ub, vm))
     vb = later(ub, 1)
-    around, plain = later_parts(ua, 1)
-    va = around + plain
+    va = later(ua, 1)
     cond, nu, keep, spread = call(
         material_kernel, "material", (odd, *tables, regions, a2, b2),
         [planes(LX + 6)] * 2 + [planes(LX + 14)] * 2, [],
     )
     vb, cond = fence((vb, cond))
     hb = from_b(vb)
+    va, *vm = fence((va, *vm))
     ha = from_a(va)
     n = LX + 8
     u0, ua, ub, um = call(
         second_kernel, "second",
-        (odd, hb, vb, ha, va, vm, source, a1, b1, a2, b2, cond, nu),
+        (odd, hb, vb, ha, va, *vm, source, a1, b1, a2, b2, cond, nu),
         [planes(3, LX + 4), planes(3, 4), planes(3, 4), planes(3, 4)], [padded(3, n)] * 2 + [vmem(3, n)] * 3,
     )
     vb = later(ub, 1)

time: 236 us -> 241 us (1.021)
  waiting for transfers between devices: 127 us -> 133 us
    ppermute x23, waiting for transfers between devices: 95.1 us -> 109 us  [along(): return lax.ppermute(x, 'tm', pairs)]
    ppermute x8, waiting for transfers between devices: 28.7 us -> 20.6 us  [from_b(): return lax.ppermute(x, 'space', off_chip)]
    ppermute x23, starting transfers between devices: 37.9 us -> 35.4 us  [along(): return lax.ppermute(x, 'tm', pairs)]
where the time goes in v9:
time: 241 us; the launch traced here: 240 us
  waiting for transfers between devices  133 us (55%)
  starting transfers between devices  64.7 us (27%)
  Pallas kernels  32.3 us (13%)
  local copies, waits for them, and re-layouts  8.44 us (4%)
    ppermute x23, waiting for transfers between devices, along(): return lax.ppermute(x, 'tm', pairs)  109 us
    ppermute x23, starting transfers between devices, along(): return lax.ppermute(x, 'tm', pairs)  35.4 us
    pallas_call x11, Pallas kernels, call(): pl.pallas_call(kernel, name=name, out_shape=outs, in_specs=in_specs, out_...  32.3 us
    ppermute x8, starting transfers between devices, from_b(): return lax.ppermute(x, 'space', off_chip)  21.8 us
    ppermute x8, waiting for transfers between devices, from_b(): return lax.ppermute(x, 'space', off_chip)  20.6 us
    ppermute x8, starting transfers between devices, from_a(): return lax.ppermute(x, 'space', on_chip)  7.52 us
    unnamed x16, local copies, waits for them, and re-layouts  5.65 us
  transfers between devices with their start and end apart: 39, of which 20 were waited for; matrix products, arithmetic and copies ran while one was open for 0% of the time, Pallas kernels for 2%

profile of v9, /device:TPU:17, one launch (start us, length us, event | category | flops | bytes accessed | tf_op | source)
XLA Modules:
  0.0 239.8 jit_solution(15359794229457783029)
XLA Ops:
  3.5 4.1 %collective-permute-start.1 = (f32[10,64,128]{2,1,0:T(8,128)S(1)}, f32[10,64,128]{2,1,0:T(8,128)S(1)}, u32[]{:S(2)}, u32[]{:S(2)}) collective-permute-start(f32[10,64,128]{2,1,0:T(8,128)S(1)} %get-tuple-element.51), channel_id=1, source_target_pairs={{1,2},{3,4},{5,6},{7,8},{9,10},{11,12},{13,14},{2,1},{4,3},{6,5},{... | collective-permute-start | bytes 983048 | tf_op jit(solution)/shard_map/ppermute | solution.py:433
  27.4 3.8 %collective-permute-start.2 = (f32[3,4,64,128]{3,2,1,0:T(8,128)S(1)}, f32[3,4,64,128]{3,2,1,0:T(8,128)S(1)}, u32[]{:S(2)}, u32[]{:S(2)}) collective-permute-start(f32[3,4,64,128]{3,2,1,0:T(8,128)S(1)} %get-tuple-element.53), channel_id=1, source_target_pairs={{0,16},{16,32},{32,48},{48,64},{64,80},{80,96},{96,112},{112,0},{1... | collective-permute-start | bytes 1179656 | tf_op jit(solution)/shard_map/ppermute | solution.py:438
  31.3 10.0 %collective-permute-done.6.va = f32[3,4,64,128]{3,2,1,0:T(8,128)S(1)} collective-permute-done((f32[3,4,64,128]{3,2,1,0:T(8,128)S(1)}, f32[3,4,64,128]{3,2,1,0:T(8,128)S(1)}, u32[]{:S(2)}, u32[]{:S(2)}) %collective-permute-start.6) | collective-permute-done | bytes 393248 | tf_op jit(solution)/shard_map/ppermute | solution.py:438
  41.3 6.8 %collective-permute-done.8.vm = f32[3,4,64,128]{3,2,1,0:T(8,128)S(1)} collective-permute-done((f32[3,4,64,128]{3,2,1,0:T(8,128)S(1)}, f32[3,4,64,128]{3,2,1,0:T(8,128)S(1)}, u32[]{:S(2)}, u32[]{:S(2)}) %collective-permute-start.8) | collective-permute-done | bytes 393248 | tf_op jit(solution)/shard_map/ppermute | solution.py:438
  50.7 8.1 %collective-permute-done.2.vb = f32[3,4,64,128]{3,2,1,0:T(8,128)S(1)} collective-permute-done((f32[3,4,64,128]{3,2,1,0:T(8,128)S(1)}, f32[3,4,64,128]{3,2,1,0:T(8,128)S(1)}, u32[]{:S(2)}, u32[]{:S(2)}) %collective-permute-start.2) | collective-permute-done | bytes 393248 | tf_op jit(solution)/shard_map/ppermute | solution.py:438
  62.0 10.1 %collective-permute-done.5.hb = f32[3,4,64,128]{3,2,1,0:T(8,128)S(1)} collective-permute-done((f32[3,4,64,128]{3,2,1,0:T(8,128)S(1)}, f32[3,4,64,128]{3,2,1,0:T(8,128)S(1)}, u32[]{:S(2)}, u32[]{:S(2)}) %collective-permute-start.5) | collective-permute-done | bytes 393248 | tf_op jit(solution)/shard_map/ppermute | solution.py:433
  72.1 4.7 %second.1 = (f32[3,16,64,128]{3,2,1,0:T(8,128)S(1)}, f32[3,4,64,128]{3,2,1,0:T(8,128)S(1)}, f32[3,4,64,128]{3,2,1,0:T(8,128)S(1)}, f32[3,4,64,128]{3,2,1,0:T(8,128)S(1)}) custom-call(s32[1]{0:T(128)} %bitcast.odd_ref, f32[3,4,64,128]{3,2,1,0:T(8,128)S(1)} %collective-permute-done.5.hb, f32[3,4,64,128]{3,2,1,0:T(8,128)S(1)} %collective-permute-done.2.vb, ...), custom_call_target="tpu_custom_call" | custom-call | bytes 4194304 | tf_op jit(solution)/shard_map/second/pallas_call | solution.py:63
  82.1 10.4 %collective-permute-done.11.vb = f32[3,4,64,128]{3,2,1,0:T(8,128)S(1)} collective-permute-done((f32[3,4,64,128]{3,2,1,0:T(8,128)S(1)}, f32[3,4,64,128]{3,2,1,0:T(8,128)S(1)}, u32[]{:S(2)}, u32[]{:S(2)}) %collective-permute-start.11) | collective-permute-done | bytes 393248 | tf_op jit(solution)/shard_map/ppermute | solution.py:438
  92.4 4.4 %collective-permute-start.12 = (f32[3,4,64,128]{3,2,1,0:T(8,128)S(1)}, f32[3,4,64,128]{3,2,1,0:T(8,128)S(1)}, u32[]{:S(2)}, u32[]{:S(2)}) collective-permute-start(f32[3,4,64,128]{3,2,1,0:T(8,128)S(1)} %collective-permute-done.11.vb), channel_id=1, source_target_pairs={{1,2},{3,4},{5,6},{7,8},{9,10},{11,12},{13,14},{2,1},{4,3},{6,5},{... | collective-permute-start | bytes 1179656 | tf_op jit(solution)/shard_map/ppermute | solution.py:433
  96.8 6.6 %collective-permute-done.13.va = f32[3,4,64,128]{3,2,1,0:T(8,128)S(1)} collective-permute-done((f32[3,4,64,128]{3,2,1,0:T(8,128)S(1)}, f32[3,4,64,128]{3,2,1,0:T(8,128)S(1)}, u32[]{:S(2)}, u32[]{:S(2)}) %collective-permute-start.13) | collective-permute-done | bytes 393248 | tf_op jit(solution)/shard_map/ppermute | solution.py:438
  107.9 4.7 %residual.1 = (f32[1,3,12,64,128]{4,3,2,1,0:T(8,128)}, f32[3,4,64,128]{3,2,1,0:T(8,128)S(1)}, f32[3,4,64,128]{3,2,1,0:T(8,128)S(1)}, f32[3,4,64,128]{3,2,1,0:T(8...) custom-call(s32[1]{0:T(128)} %bitcast.odd_ref, ...), custom_call_target="tpu_custom_call" | custom-call | bytes 4194304 | tf_op jit(solution)/shard_map/residual/pallas_call | solution.py:63
  114.8 6.7 %collective-permute-start.24 = (f32[3,4,64,128]{3,2,1,0:T(8,128)S(1)}, f32[3,4,64,128]{3,2,1,0:T(8,128)S(1)}, u32[]{:S(2)}, u32[]{:S(2)}) collective-permute-start(f32[3,4,64,128]{3,2,1,0:T(8,128)S(1)} %get-tuple-element.76), channel_id=1, source_target_pairs={{0,16},{16,32},{32,48},{64,80},{80,96},{96,112},{1,17},{17,33},{33... | collective-permute-start | bytes 1179656 | tf_op jit(solution)/shard_map/ppermute | solution.py:438
  121.5 6.1 %collective-permute-done.18 = f32[3,4,64,128]{3,2,1,0:T(8,128)S(1)} collective-permute-done((f32[3,4,64,128]{3,2,1,0:T(8,128)S(1)}, f32[3,4,64,128]{3,2,1,0:T(8,128)S(1)}, u32[]{:S(2)}, u32[]{:S(2)}) %collective-permute-start.18) | collective-permute-done | bytes 393248 | tf_op jit(solution)/shard_map/ppermute | solution.py:438
  129.6 7.8 %collective-permute-done.20 = f32[3,4,64,128]{3,2,1,0:T(8,128)S(1)} collective-permute-done((f32[3,4,64,128]{3,2,1,0:T(8,128)S(1)}, f32[3,4,64,128]{3,2,1,0:T(8,128)S(1)}, u32[]{:S(2)}, u32[]{:S(2)}) %collective-permute-start.20) | collective-permute-done | bytes 393248 | tf_op jit(solution)/shard_map/ppermute | solution.py:438
  137.3 9.4 %collective-permute-done.22 = f32[3,4,64,128]{3,2,1,0:T(8,128)S(1)} collective-permute-done((f32[3,4,64,128]{3,2,1,0:T(8,128)S(1)}, f32[3,4,64,128]{3,2,1,0:T(8,128)S(1)}, u32[]{:S(2)}, u32[]{:S(2)}) %collective-permute-start.22) | collective-permute-done | bytes 393248 | tf_op jit(solution)/shard_map/ppermute | solution.py:438
  149.2 4.3 %square.1 = (f32[3,4,64,128]{3,2,1,0:T(8,128)S(1)}, f32[3,4,64,128]{3,2,1,0:T(8,128)S(1)}, f32[3,4,64,128]{3,2,1,0:T(8,128)S(1)}) custom-call(s32[1]{0:T(128)} %bitcast.odd_ref, f32[3,4,64,128]{3,2,1,0:T(8,128)S(1)} %collective-permute-done.19.hb, f32[3,4,64,128]{3,2,1,0:T(8,128)S(1)} %add.35.sb, f32[3,4,64,128]{3,2,1,0:T(8,128)S(1)} %collective-permute-done.23.ha, ...), custom_call_target="tpu_custom_call" | custom-call | bytes 4194304 | tf_op jit(solution)/shard_map/square/pallas_call | solution.py:63
  154.8 4.0 %collective-permute-start.32 = (f32[3,4,64,128]{3,2,1,0:T(8,128)S(1)}, f32[3,4,64,128]{3,2,1,0:T(8,128)S(1)}, u32[]{:S(2)}, u32[]{:S(2)}) collective-permute-start(f32[3,4,64,128]{3,2,1,0:T(8,128)S(1)} %get-tuple-element.82), channel_id=1, source_target_pairs={{0,32},{16,48},{64,96},{80,112},{1,33},{17,49},{65,97},{81,113},{2... | collective-permute-start | bytes 1179656 | tf_op jit(solution)/shard_map/ppermute | solution.py:438
  160.2 8.3 %collective-permute-done.27 = f32[3,4,64,128]{3,2,1,0:T(8,128)S(1)} collective-permute-done((f32[3,4,64,128]{3,2,1,0:T(8,128)S(1)}, f32[3,4,64,128]{3,2,1,0:T(8,128)S(1)}, u32[]{:S(2)}, u32[]{:S(2)}) %collective-permute-start.27) | collective-permute-done | bytes 393248 | tf_op jit(solution)/shard_map/ppermute | solution.py:438
  172.5 7.0 %collective-permute-done.25 = f32[3,4,64,128]{3,2,1,0:T(8,128)S(1)} collective-permute-done((f32[3,4,64,128]{3,2,1,0:T(8,128)S(1)}, f32[3,4,64,128]{3,2,1,0:T(8,128)S(1)}, u32[]{:S(2)}, u32[]{:S(2)}) %collective-permute-start.25) | collective-permute-done | bytes 393248 | tf_op jit(solution)/shard_map/ppermute | solution.py:438
  183.8 9.0 %collective-permute-done.26.near_b = f32[3,4,64,128]{3,2,1,0:T(8,128)S(1)} collective-permute-done((f32[3,4,64,128]{3,2,1,0:T(8,128)S(1)}, f32[3,4,64,128]{3,2,1,0:T(8,128)S(1)}, u32[]{:S(2)}, u32[]{:S(2)}) %collective-permute-start.26) | collective-permute-done | bytes 393248 | tf_op jit(solution)/shard_map/ppermute | solution.py:433
  192.9 10.6 %fourth.1 = (f32[3,4,64,128]{3,2,1,0:T(8,128)S(1)}, f32[3,4,64,128]{3,2,1,0:T(8,128)S(1)}, f32[3,4,64,128]{3,2,1,0:T(8,128)S(1)}, f32[3,4,64,128]{3,2,1,0:T(8,12...) custom-call(s32[1]{0:T(128)} %bitcast.odd_ref, ...), custom_call_target="tpu_custom_call" | custom-call | bytes 4194304 | tf_op jit(solution)/shard_map/fourth/pallas_call | solution.py:63
  206.7 11.7 %collective-permute-done.35.moved = f32[3,4,64,128]{3,2,1,0:T(8,128)S(1)} collective-permute-done((f32[3,4,64,128]{3,2,1,0:T(8,128)S(1)}, f32[3,4,64,128]{3,2,1,0:T(8,128)S(1)}, u32[]{:S(2)}, u32[]{:S(2)}) %collective-permute-start.35) | collective-permute-done | bytes 393248 | tf_op jit(solution)/shard_map/ppermute | solution.py:438
  221.6 5.2 %collective-permute-done.34 = f32[3,4,64,128]{3,2,1,0:T(8,128)S(1)} collective-permute-done((f32[3,4,64,128]{3,2,1,0:T(8,128)S(1)}, f32[3,4,64,128]{3,2,1,0:T(8,128)S(1)}, u32[]{:S(2)}, u32[]{:S(2)}) %collective-permute-start.34) | collective-permute-done | bytes 393248 | tf_op jit(solution)/shard_map/ppermute | solution.py:438
  228.5 8.1 %collective-permute-done.38 = f32[3,4,64,128]{3,2,1,0:T(8,128)S(1)} collective-permute-done((f32[3,4,64,128]{3,2,1,0:T(8,128)S(1)}, f32[3,4,64,128]{3,2,1,0:T(8,128)S(1)}, u32[]{:S(2)}, u32[]{:S(2)}) %collective-permute-start.38) | collective-permute-done | bytes 393248 | tf_op jit(solution)/shard_map/ppermute | solution.py:438
  (92 shorter events, 66.6 us)
Async XLA Ops:
  3.5 15.4 %collective-permute-start.1 = (f32[10,64,128]{2,1,0:T(8,128)S(1)}, f32[10,64,128]{2,1,0:T(8,128)S(1)}, u32[]{:S(2)}, u32[]{:S(2)}) collective-permute-start(f32[10,64,128]{2,1,0:T(8,128)S(1)} %get-tuple-element.51), channel_id=1, source_target_pairs={{1,2},{3,4},{5,6},{7,8},{9,10},{11,12},{13,14},{2,1},{4,3},{6,5},{... | collective-permute-start | bytes 983048 | tf_op jit(solution)/shard_map/ppermute | solution.py:433
  18.9 30.6 %collective-permute-start.3 = (f32[16,64,128]{2,1,0:T(8,128)S(1)}, f32[16,64,128]{2,1,0:T(8,128)S(1)}, u32[]{:S(2)}, u32[]{:S(2)}) collective-permute-start(f32[16,64,128]{2,1,0:T(8,128)S(1)} %get-tuple-element.54), channel_id=1, source_target_pairs={{0,1},{1,0},{2,3},{3,2},{4,5},{5,4},{6,7},{7,6},{8,9},{9,8},{10,11... | collective-permute-start | bytes 1572872 | tf_op jit(solution)/shard_map/ppermute | solution.py:430
  19.5 30.0 %collective-permute-start.4 = (f32[16,64,128]{2,1,0:T(8,128)S(1)}, f32[16,64,128]{2,1,0:T(8,128)S(1)}, u32[]{:S(2)}, u32[]{:S(2)}) collective-permute-start(f32[16,64,128]{2,1,0:T(8,128)S(1)} %get-tuple-element.55), channel_id=1, source_target_pairs={{1,2},{3,4},{5,6},{7,8},{9,10},{11,12},{13,14},{2,1},{4,3},{6,5},{... | collective-permute-start | bytes 1572872 | tf_op jit(solution)/shard_map/ppermute | solution.py:433
  24.1 17.2 %collective-permute-start.6 = (f32[3,4,64,128]{3,2,1,0:T(8,128)S(1)}, f32[3,4,64,128]{3,2,1,0:T(8,128)S(1)}, u32[]{:S(2)}, u32[]{:S(2)}) collective-permute-start(f32[3,4,64,128]{3,2,1,0:T(8,128)S(1)} %get-tuple-element.58), channel_id=1, source_target_pairs={{0,16},{16,32},{32,48},{48,64},{64,80},{80,96},{96,112},{112,0},{1... | collective-permute-start | bytes 1179656 | tf_op jit(solution)/shard_map/ppermute | solution.py:438
  25.4 22.7 %collective-permute-start.8 = (f32[3,4,64,128]{3,2,1,0:T(8,128)S(1)}, f32[3,4,64,128]{3,2,1,0:T(8,128)S(1)}, u32[]{:S(2)}, u32[]{:S(2)}) collective-permute-start(f32[3,4,64,128]{3,2,1,0:T(8,128)S(1)} %collective-permute-done.7), channel_id=1, source_target_pairs={{112,64},{48,0},{113,65},{49,1},{114,66},{50,2},{115,67},{51,3},{1... | collective-permute-start | bytes 1179656 | tf_op jit(solution)/shard_map/ppermute | solution.py:438
  27.4 31.4 %collective-permute-start.2 = (f32[3,4,64,128]{3,2,1,0:T(8,128)S(1)}, f32[3,4,64,128]{3,2,1,0:T(8,128)S(1)}, u32[]{:S(2)}, u32[]{:S(2)}) collective-permute-start(f32[3,4,64,128]{3,2,1,0:T(8,128)S(1)} %get-tuple-element.53), channel_id=1, source_target_pairs={{0,16},{16,32},{32,48},{48,64},{64,80},{80,96},{96,112},{112,0},{1... | collective-permute-start | bytes 1179656 | tf_op jit(solution)/shard_map/ppermute | solution.py:438
  77.5 14.9 %collective-permute-start.11 = (f32[3,4,64,128]{3,2,1,0:T(8,128)S(1)}, f32[3,4,64,128]{3,2,1,0:T(8,128)S(1)}, u32[]{:S(2)}, u32[]{:S(2)}) collective-permute-start(f32[3,4,64,128]{3,2,1,0:T(8,128)S(1)} %get-tuple-element.64), channel_id=1, source_target_pairs={{0,16},{16,32},{32,48},{48,64},{64,80},{80,96},{96,112},{112,0},{1... | collective-permute-start | bytes 1179656 | tf_op jit(solution)/shard_map/ppermute | solution.py:438
  77.6 25.8 %collective-permute-start.13 = (f32[3,4,64,128]{3,2,1,0:T(8,128)S(1)}, f32[3,4,64,128]{3,2,1,0:T(8,128)S(1)}, u32[]{:S(2)}, u32[]{:S(2)}) collective-permute-start(f32[3,4,64,128]{3,2,1,0:T(8,128)S(1)} %get-tuple-element.65), channel_id=1, source_target_pairs={{0,16},{16,32},{32,48},{48,64},{64,80},{80,96},{96,112},{112,0},{1... | collective-permute-start | bytes 1179656 | tf_op jit(solution)/shard_map/ppermute | solution.py:438
  77.7 28.4 %collective-permute-start.15 = (f32[3,4,64,128]{3,2,1,0:T(8,128)S(1)}, f32[3,4,64,128]{3,2,1,0:T(8,128)S(1)}, u32[]{:S(2)}, u32[]{:S(2)}) collective-permute-start(f32[3,4,64,128]{3,2,1,0:T(8,128)S(1)} %collective-permute-done.14), channel_id=1, source_target_pairs={{112,64},{48,0},{113,65},{49,1},{114,66},{50,2},{115,67},{51,3},{1... | collective-permute-start | bytes 1179656 | tf_op jit(solution)/shard_map/ppermute | solution.py:438
  79.0 27.1 %collective-permute-start.17 = (f32[3,4,64,128]{3,2,1,0:T(8,128)S(1)}, f32[3,4,64,128]{3,2,1,0:T(8,128)S(1)}, u32[]{:S(2)}, u32[]{:S(2)}) collective-permute-start(f32[3,4,64,128]{3,2,1,0:T(8,128)S(1)} %get-tuple-element.66), channel_id=1, source_target_pairs={{0,16},{16,32},{32,48},{64,80},{80,96},{96,112},{1,17},{17,33},{33... | collective-permute-start | bytes 1179656 | tf_op jit(solution)/shard_map/ppermute | solution.py:438
  113.3 14.3 %collective-permute-start.18 = (f32[3,4,64,128]{3,2,1,0:T(8,128)S(1)}, f32[3,4,64,128]{3,2,1,0:T(8,128)S(1)}, u32[]{:S(2)}, u32[]{:S(2)}) collective-permute-start(f32[3,4,64,128]{3,2,1,0:T(8,128)S(1)} %get-tuple-element.73), channel_id=1, source_target_pairs={{0,16},{16,32},{32,48},{48,64},{64,80},{80,96},{96,112},{112,0},{1... | collective-permute-start | bytes 1179656 | tf_op jit(solution)/shard_map/ppermute | solution.py:438
  113.4 24.0 %collective-permute-start.20 = (f32[3,4,64,128]{3,2,1,0:T(8,128)S(1)}, f32[3,4,64,128]{3,2,1,0:T(8,128)S(1)}, u32[]{:S(2)}, u32[]{:S(2)}) collective-permute-start(f32[3,4,64,128]{3,2,1,0:T(8,128)S(1)} %get-tuple-element.75), channel_id=1, source_target_pairs={{0,16},{16,32},{32,48},{48,64},{64,80},{80,96},{96,112},{112,0},{1... | collective-permute-start | bytes 1179656 | tf_op jit(solution)/shard_map/ppermute | solution.py:438
  113.5 33.3 %collective-permute-start.22 = (f32[3,4,64,128]{3,2,1,0:T(8,128)S(1)}, f32[3,4,64,128]{3,2,1,0:T(8,128)S(1)}, u32[]{:S(2)}, u32[]{:S(2)}) collective-permute-start(f32[3,4,64,128]{3,2,1,0:T(8,128)S(1)} %collective-permute-done.21), channel_id=1, source_target_pairs={{112,64},{48,0},{113,65},{49,1},{114,66},{50,2},{115,67},{51,3},{1... | collective-permute-start | bytes 1179656 | tf_op jit(solution)/shard_map/ppermute | solution.py:438
  114.8 33.1 %collective-permute-start.24 = (f32[3,4,64,128]{3,2,1,0:T(8,128)S(1)}, f32[3,4,64,128]{3,2,1,0:T(8,128)S(1)}, u32[]{:S(2)}, u32[]{:S(2)}) collective-permute-start(f32[3,4,64,128]{3,2,1,0:T(8,128)S(1)} %get-tuple-element.76), channel_id=1, source_target_pairs={{0,16},{16,32},{32,48},{64,80},{80,96},{96,112},{1,17},{17,33},{33... | collective-permute-start | bytes 1179656 | tf_op jit(solution)/shard_map/ppermute | solution.py:438
  127.6 20.3 %collective-permute-start.19 = (f32[3,4,64,128]{3,2,1,0:T(8,128)S(1)}, f32[3,4,64,128]{3,2,1,0:T(8,128)S(1)}, u32[]{:S(2)}, u32[]{:S(2)}) collective-permute-start(f32[3,4,64,128]{3,2,1,0:T(8,128)S(1)} %add.35.sb), channel_id=1, source_target_pairs={{1,2},{3,4},{5,6},{7,8},{9,10},{11,12},{13,14},{2,1},{4,3},{6,5},{... | collective-permute-start | bytes 1179656 | tf_op jit(solution)/shard_map/ppermute | solution.py:433
  154.2 14.3 %collective-permute-start.27 = (f32[3,4,64,128]{3,2,1,0:T(8,128)S(1)}, f32[3,4,64,128]{3,2,1,0:T(8,128)S(1)}, u32[]{:S(2)}, u32[]{:S(2)}) collective-permute-start(f32[3,4,64,128]{3,2,1,0:T(8,128)S(1)} %get-tuple-element.81), channel_id=1, source_target_pairs={{0,32},{16,48},{32,64},{48,80},{64,96},{80,112},{96,0},{112,16},{1... | collective-permute-start | bytes 1179656 | tf_op jit(solution)/shard_map/ppermute | solution.py:438
  154.2 25.2 %collective-permute-start.25 = (f32[3,4,64,128]{3,2,1,0:T(8,128)S(1)}, f32[3,4,64,128]{3,2,1,0:T(8,128)S(1)}, u32[]{:S(2)}, u32[]{:S(2)}) collective-permute-start(f32[3,4,64,128]{3,2,1,0:T(8,128)S(1)} %get-tuple-element.80), channel_id=1, source_target_pairs={{0,32},{16,48},{32,64},{48,80},{64,96},{80,112},{96,0},{112,16},{1... | collective-permute-start | bytes 1179656 | tf_op jit(solution)/shard_map/ppermute | solution.py:438
  154.8 26.6 %collective-permute-start.32 = (f32[3,4,64,128]{3,2,1,0:T(8,128)S(1)}, f32[3,4,64,128]{3,2,1,0:T(8,128)S(1)}, u32[]{:S(2)}, u32[]{:S(2)}) collective-permute-start(f32[3,4,64,128]{3,2,1,0:T(8,128)S(1)} %get-tuple-element.82), channel_id=1, source_target_pairs={{0,32},{16,48},{64,96},{80,112},{1,33},{17,49},{65,97},{81,113},{2... | collective-permute-start | bytes 1179656 | tf_op jit(solution)/shard_map/ppermute | solution.py:438
  158.9 22.6 %collective-permute-start.31 = (f32[3,4,64,128]{3,2,1,0:T(8,128)S(1)}, f32[3,4,64,128]{3,2,1,0:T(8,128)S(1)}, u32[]{:S(2)}, u32[]{:S(2)}) collective-permute-start(f32[3,4,64,128]{3,2,1,0:T(8,128)S(1)} %collective-permute-done.30), channel_id=1, source_target_pairs={{96,64},{112,80},{32,0},{48,16},{97,65},{113,81},{33,1},{49,17},{9... | collective-permute-start | bytes 1179656 | tf_op jit(solution)/shard_map/ppermute | solution.py:438
  168.5 24.3 %collective-permute-start.29 = (f32[3,4,64,128]{3,2,1,0:T(8,128)S(1)}, f32[3,4,64,128]{3,2,1,0:T(8,128)S(1)}, u32[]{:S(2)}, u32[]{:S(2)}) collective-permute-start(f32[3,4,64,128]{3,2,1,0:T(8,128)S(1)} %add.40.tm), channel_id=1, source_target_pairs={{0,1},{1,0},{2,3},{3,2},{4,5},{5,4},{6,7},{7,6},{8,9},{9,8},{10,11... | collective-permute-start | bytes 1179656 | tf_op jit(solution)/shard_map/ppermute | solution.py:430
  170.6 22.2 %collective-permute-start.28 = (f32[3,4,64,128]{3,2,1,0:T(8,128)S(1)}, f32[3,4,64,128]{3,2,1,0:T(8,128)S(1)}, u32[]{:S(2)}, u32[]{:S(2)}) collective-permute-start(f32[3,4,64,128]{3,2,1,0:T(8,128)S(1)} %add.40.tm), channel_id=1, source_target_pairs={{1,2},{3,4},{5,6},{7,8},{9,10},{11,12},{13,14},{2,1},{4,3},{6,5},{... | collective-permute-start | bytes 1179656 | tf_op jit(solution)/shard_map/ppermute | solution.py:433
  203.5 15.0 %collective-permute-start.35 = (f32[3,4,64,128]{3,2,1,0:T(8,128)S(1)}, f32[3,4,64,128]{3,2,1,0:T(8,128)S(1)}, u32[]{:S(2)}, u32[]{:S(2)}) collective-permute-start(f32[3,4,64,128]{3,2,1,0:T(8,128)S(1)} %get-tuple-element.85), channel_id=1, source_target_pairs={{0,64},{16,80},{32,96},{48,112},{64,0},{80,16},{96,32},{112,48},{1... | collective-permute-start | bytes 1179656 | tf_op jit(solution)/shard_map/ppermute | solution.py:438
  204.7 22.1 %collective-permute-start.34 = (f32[3,4,64,128]{3,2,1,0:T(8,128)S(1)}, f32[3,4,64,128]{3,2,1,0:T(8,128)S(1)}, u32[]{:S(2)}, u32[]{:S(2)}) collective-permute-start(f32[3,4,64,128]{3,2,1,0:T(8,128)S(1)} %get-tuple-element.83), channel_id=1, source_target_pairs={{0,64},{16,80},{32,96},{48,112},{64,0},{80,16},{96,32},{112,48},{1... | collective-permute-start | bytes 1179656 | tf_op jit(solution)/shard_map/ppermute | solution.py:438
  220.4 16.2 %collective-permute-start.38 = (f32[3,4,64,128]{3,2,1,0:T(8,128)S(1)}, f32[3,4,64,128]{3,2,1,0:T(8,128)S(1)}, u32[]{:S(2)}, u32[]{:S(2)}) collective-permute-start(f32[3,4,64,128]{3,2,1,0:T(8,128)S(1)} %get-tuple-element.92), channel_id=1, source_target_pairs={{0,64},{16,80},{32,96},{48,112},{64,0},{80,16},{96,32},{112,48},{1... | collective-permute-start | bytes 1179656 | tf_op jit(solution)/shard_map/ppermute | solution.py:438
  (23 other events, 146.0 us)

commit v10 on v9

--- a/solution.py
+++ b/solution.py
@@ -191,15 +191,19 @@
         fill(a1, b1)
 
 
-def second_pack_kernel(odd_ref, source, regions, a2, b2):
-    odd = odd_ref[0]
+def second_pack_kernel(odd_ref, source, regions, a2, b2, a3, b3, reg, sems):
+    odd = odd_ref[0]
+    pairs = [(regions, reg)]
     for two, start in zip((a2, b2), edges(odd, LX, 3)):
         for c in range(3):
-            for k in range(3):
-                two[3 * c + k] = source[0, c, start + k]
-    for two, start in zip((a2, b2), edges(odd, LX, 7)):
-        for k in range(7):
-            two[9 + k] = (regions[start + k] + 1).astype(F32)
+            pairs.append((source.at[0, c, pl.ds(start, 3)], two.at[pl.ds(3 * c, 3)]))
+    run_copies(pairs, sems)
+    for two, start in zip((a2, b2), edges(odd, LX, 3)):
+        for k in range(3):
+            two[9 + k] = (reg[start + k] + 1).astype(F32)
+    for three, high in ((a3, 1 - odd), (b3, odd)):
+        for k in range(4):
+            three[k] = (reg[high * (LX - 7) + (1 - high) * 3 + k] + 1).astype(F32)
 
 
 def first_middle_kernel(cond_t, nu_t, guess, source, regions, out, y, held, cond, nu):
@@ -245,22 +249,35 @@
 def material_kernel(odd_ref, cond_t, nu_t, regions, ra, rb, cond, nu, keep, spread):
     odd = odd_ref[0]
 
-    def fill(at, code, near=True):
+    def fill(at, code):
         cv, nv = materials(code, cond_t, nu_t)
-        if near:
-            cond[at - 4] = cv
-            nu[at - 4] = nv
+        cond[at] = cv
+        nu[at] = nv
         half = 0.5 * cv
         scale = 1.0 / (half + 6.0 * nv)
         keep[at] = half * scale
         spread[at] = nv * scale
 
     for i in range(LX):
-        fill(7 + i, regions[i] + 1)
-    for k in range(7):
-        from_on, from_off = ra[9 + k], rb[9 + k]
-        fill(k, jnp.where(odd == 1, from_on, from_off), k >= 4)
-        fill(LX + 7 + k, jnp.where(odd == 1, from_off, from_on), k < 3)
+        fill(3 + i, regions[i] + 1)
+    for pack, high in ((ra, 1 - odd), (rb, odd)):
+        for k in range(3):
+            fill(high * (LX + 3) + k, pack[9 + k])
+
+
+def wide_kernel(odd_ref, cond_t, nu_t, keep_i, spread_i, ra, rb, keep, spread):
+    odd = odd_ref[0]
+    for i in range(LX + 6):
+        keep[i + 4] = keep_i[i]
+        spread[i + 4] = spread_i[i]
+    for pack, high in ((ra, 1 - odd), (rb, odd)):
+        for k in range(4):
+            at = high * (LX + 10) + k
+            cv, nv = materials(pack[k], cond_t, nu_t)
+            half = 0.5 * cv
+            scale = 1.0 / (half + 6.0 * nv)
+            keep[at] = half * scale
+            spread[at] = nv * scale
 
 
 def extend(odd, pieces, halos, x):
@@ -347,8 +364,8 @@
     clear(x, y)
     extend(odd, (sa, sb, sm), (ha, hb), x)
     for lo in (1, 3):
-        coarse_sweep(x, y, held, keep, spread, 3, lo, 20 - lo, True)
-        coarse_sweep(y, x, held, keep, spread, 3, lo + 1, 19 - lo, False)
+        coarse_sweep(x, y, held, keep, spread, -1, lo, 20 - lo, True)
+        coarse_sweep(y, x, held, keep, spread, -1, lo + 1, 19 - lo, False)
     split(odd, x, 4, ob, oa, om)
 
 
@@ -459,8 +476,9 @@
         first_middle_kernel, "first_middle", (*tables, guess, source, regions),
         planes(3, 4), [padded(3, LX), vmem(3, LX)] + [vmem(LX)] * 2,
     )
-    sa2, sb2 = call(
-        second_pack_kernel, "second_pack", (odd, source, regions), [planes(16), planes(16)], [],
+    sa2, sb2, sa3, sb3 = call(
+        second_pack_kernel, "second_pack", (odd, source, regions),
+        [planes(12), planes(12), planes(4), planes(4)], [pltpu.VMEM((LX, NY, NZ), jnp.int32)], 8, in_place=HBM,
     )
     vm = later_parts(um, 1)
     sb2, sa2, b1 = fence((sb2, sa2, b1))
@@ -473,8 +491,7 @@
     vb = later(ub, 1)
     va = later(ua, 1)
     cond, nu, keep, spread = call(
-        material_kernel, "material", (odd, *tables, regions, a2, b2),
-        [planes(LX + 6)] * 2 + [planes(LX + 14)] * 2, [],
+        material_kernel, "material", (odd, *tables, regions, a2, b2), [planes(LX + 6)] * 4, [],
     )
     vb, cond = fence((vb, cond))
     hb = from_b(vb)
@@ -486,15 +503,21 @@
         (odd, hb, vb, ha, va, *vm, source, a1, b1, a2, b2, cond, nu),
         [planes(3, LX + 4), planes(3, 4), planes(3, 4), planes(3, 4)], [padded(3, n)] * 2 + [vmem(3, n)] * 3,
     )
+    sb3, sa3, ub = fence((sb3, sa3, ub))
     vb = later(ub, 1)
     va = later(ua, 1)
     around, plain = later_parts(um, 1)
     hb = from_b(vb)
+    b3 = from_b(sb3)
+    a3 = from_a(sa3)
+    wide_keep, wide_spread = call(
+        wide_kernel, "wide", (odd, *tables, keep, spread, a3, b3), [planes(LX + 14)] * 2, [],
+    )
     va, around = fence((va, around))
     ha = from_a(va)
     residual, lb, la, lm, rb, ra, rm = call(
         residual_kernel, "residual",
-        (odd, hb, vb, ha, va, around, plain, source, a2, b2, cond, nu, keep, spread, u0),
+        (odd, hb, vb, ha, va, around, plain, source, a2, b2, cond, nu, wide_keep, wide_spread, u0),
         [planes(1, 3, LX)] + [planes(3, 4)] * 6, [padded(3, n)] * 2 + [vmem(3, n)] * 2, 1, [ANY] + [VMEM] * 6,
     )
     sb = rb + later(lb, 1)
@@ -518,7 +541,7 @@
     far_a = from_a(tm)
     lb, la, lm, bb, ba, bm = call(
         fourth_kernel, "fourth",
-        (odd, near_b, tb, far_b, tm, far_a, near_a, ta, u0, keep, spread),
+        (odd, near_b, tb, far_b, tm, far_a, near_a, ta, u0, wide_keep, wide_spread),
         [planes(3, 4)] * 6, [padded(3, LX + 16)] * 2 + [vmem(3, LX + 16)],
     )
     eb, edge = call(

time: 241 us -> 231 us (0.959)
  waiting for transfers between devices: 133 us -> 102 us
  starting transfers between devices: 64.7 us -> 84 us
    ppermute x23, waiting for transfers between devices: 109 us -> 86.2 us  [along(): return lax.ppermute(x, 'tm', pairs)]
    ppermute x8 -> x9, starting transfers between devices: 21.8 us -> 37.3 us  [from_b(): return lax.ppermute(x, 'space', off_chip)]
    ppermute x8 -> x9, waiting for transfers between devices: 20.6 us -> 14.6 us  [from_b(): return lax.ppermute(x, 'space', off_chip)]
    ppermute x23, starting transfers between devices: 35.4 us -> 41.2 us  [along(): return lax.ppermute(x, 'tm', pairs)]
    ppermute x8 -> x9, starting transfers between devices: 7.52 us -> 5.41 us  [from_a(): return lax.ppermute(x, 'space', on_chip)]
    pallas_call x11 -> x12, Pallas kernels: 32.3 us -> 33.9 us  [call(): pl.pallas_call(kernel, name=name, out_shape=outs, in_specs=in_specs, out_...]
  transfers between devices with their start and end apart: 39 -> 41, of which waited for: 20 -> 21; matrix products, arithmetic and copies ran while one was open for 0% -> 0% of each run, Pallas kernels for 2% -> 3%
where the time goes in v10:
time: 231 us; the launch traced here: 230 us
  waiting for transfers between devices  102 us (44%)
  starting transfers between devices  84 us (36%)
  Pallas kernels  33.9 us (15%)
  local copies, waits for them, and re-layouts  8.44 us (4%)
    ppermute x23, waiting for transfers between devices, along(): return lax.ppermute(x, 'tm', pairs)  86.2 us
    ppermute x23, starting transfers between devices, along(): return lax.ppermute(x, 'tm', pairs)  41.2 us
    ppermute x9, starting transfers between devices, from_b(): return lax.ppermute(x, 'space', off_chip)  37.3 us
    pallas_call x12, Pallas kernels, call(): pl.pallas_call(kernel, name=name, out_shape=outs, in_specs=in_specs, out_...  33.9 us
    ppermute x9, waiting for transfers between devices, from_b(): return lax.ppermute(x, 'space', off_chip)  14.6 us
    unnamed x16, local copies, waits for them, and re-layouts  5.65 us
    ppermute x9, starting transfers between devices, from_a(): return lax.ppermute(x, 'space', on_chip)  5.41 us
  transfers between devices with their start and end apart: 41, of which 21 were waited for; matrix products, arithmetic and copies ran while one was open for 0% of the time, Pallas kernels for 3%

profile of v10, /device:TPU:17, one launch (start us, length us, event | category | flops | bytes accessed | tf_op | source)
XLA Modules:
  0.0 229.6 jit_solution(13124872013080243356)
XLA Ops:
  26.7 4.9 %collective-permute-start.6 = (f32[3,4,64,128]{3,2,1,0:T(8,128)S(1)}, f32[3,4,64,128]{3,2,1,0:T(8,128)S(1)}, u32[]{:S(2)}, u32[]{:S(2)}) collective-permute-start(f32[3,4,64,128]{3,2,1,0:T(8,128)S(1)} %get-tuple-element.67), channel_id=1, source_target_pairs={{0,16},{16,32},{32,48},{48,64},{64,80},{80,96},{96,112},{112,0},{1... | collective-permute-start | bytes 1179656 | tf_op jit(solution)/shard_map/ppermute | solution.py:455
  41.5 7.1 %collective-permute-done.6.va = f32[3,4,64,128]{3,2,1,0:T(8,128)S(1)} collective-permute-done((f32[3,4,64,128]{3,2,1,0:T(8,128)S(1)}, f32[3,4,64,128]{3,2,1,0:T(8,128)S(1)}, u32[]{:S(2)}, u32[]{:S(2)}) %collective-permute-start.6) | collective-permute-done | bytes 393248 | tf_op jit(solution)/shard_map/ppermute | solution.py:455
  48.6 5.9 %collective-permute-done.8.vm = f32[3,4,64,128]{3,2,1,0:T(8,128)S(1)} collective-permute-done((f32[3,4,64,128]{3,2,1,0:T(8,128)S(1)}, f32[3,4,64,128]{3,2,1,0:T(8,128)S(1)}, u32[]{:S(2)}, u32[]{:S(2)}) %collective-permute-start.8) | collective-permute-done | bytes 393248 | tf_op jit(solution)/shard_map/ppermute | solution.py:455
  57.0 4.7 %second.1 = (f32[3,16,64,128]{3,2,1,0:T(8,128)S(1)}, f32[3,4,64,128]{3,2,1,0:T(8,128)S(1)}, f32[3,4,64,128]{3,2,1,0:T(8,128)S(1)}, f32[3,4,64,128]{3,2,1,0:T(8,128)S(1)}) custom-call(s32[1]{0:T(128)} %bitcast.odd_ref, f32[3,4,64,128]{3,2,1,0:T(8,128)S(1)} %collective-permute-done.5.hb, f32[3,4,64,128]{3,2,1,0:T(8,128)S(1)} %collective-permute-done.2.vb, ...), custom_call_target="tpu_custom_call" | custom-call | bytes 4194304 | tf_op jit(solution)/shard_map/second/pallas_call | solution.py:63
  63.9 5.3 %collective-permute-start.17 = (f32[3,4,64,128]{3,2,1,0:T(8,128)S(1)}, f32[3,4,64,128]{3,2,1,0:T(8,128)S(1)}, u32[]{:S(2)}, u32[]{:S(2)}) collective-permute-start(f32[3,4,64,128]{3,2,1,0:T(8,128)S(1)} %get-tuple-element.76), channel_id=1, source_target_pairs={{0,16},{16,32},{32,48},{64,80},{80,96},{96,112},{1,17},{17,33},{33... | collective-permute-start | bytes 1179656 | tf_op jit(solution)/shard_map/ppermute | solution.py:455
  69.3 7.4 %collective-permute-done.11.vb = f32[3,4,64,128]{3,2,1,0:T(8,128)S(1)} collective-permute-done((f32[3,4,64,128]{3,2,1,0:T(8,128)S(1)}, f32[3,4,64,128]{3,2,1,0:T(8,128)S(1)}, u32[]{:S(2)}, u32[]{:S(2)}) %collective-permute-start.11) | collective-permute-done | bytes 393248 | tf_op jit(solution)/shard_map/ppermute | solution.py:455
  76.7 6.1 %collective-permute-start.12 = (f32[3,4,64,128]{3,2,1,0:T(8,128)S(1)}, f32[3,4,64,128]{3,2,1,0:T(8,128)S(1)}, u32[]{:S(2)}, u32[]{:S(2)}) collective-permute-start(f32[3,4,64,128]{3,2,1,0:T(8,128)S(1)} %collective-permute-done.11.vb), channel_id=1, source_target_pairs={{1,2},{3,4},{5,6},{7,8},{9,10},{11,12},{13,14},{2,1},{4,3},{6,5},{... | collective-permute-start | bytes 1179656 | tf_op jit(solution)/shard_map/ppermute | solution.py:450
  82.9 4.4 %collective-permute-done.13.va = f32[3,4,64,128]{3,2,1,0:T(8,128)S(1)} collective-permute-done((f32[3,4,64,128]{3,2,1,0:T(8,128)S(1)}, f32[3,4,64,128]{3,2,1,0:T(8,128)S(1)}, u32[]{:S(2)}, u32[]{:S(2)}) %collective-permute-start.13) | collective-permute-done | bytes 393248 | tf_op jit(solution)/shard_map/ppermute | solution.py:455
  87.3 8.0 %collective-permute-done.15.vm = f32[3,4,64,128]{3,2,1,0:T(8,128)S(1)} collective-permute-done((f32[3,4,64,128]{3,2,1,0:T(8,128)S(1)}, f32[3,4,64,128]{3,2,1,0:T(8,128)S(1)}, u32[]{:S(2)}, u32[]{:S(2)}) %collective-permute-start.15) | collective-permute-done | bytes 393248 | tf_op jit(solution)/shard_map/ppermute | solution.py:455
  98.2 5.3 %collective-permute-done.19.rb = f32[4,64,128]{2,1,0:T(8,128)S(1)} collective-permute-done((f32[4,64,128]{2,1,0:T(8,128)S(1)}, f32[4,64,128]{2,1,0:T(8,128)S(1)}, u32[]{:S(2)}, u32[]{:S(2)}) %collective-permute-start.19) | collective-permute-done | bytes 131104 | tf_op jit(solution)/shard_map/ppermute | solution.py:450
  104.3 4.7 %residual.1 = (f32[1,3,12,64,128]{4,3,2,1,0:T(8,128)}, f32[3,4,64,128]{3,2,1,0:T(8,128)S(1)}, f32[3,4,64,128]{3,2,1,0:T(8,128)S(1)}, f32[3,4,64,128]{3,2,1,0:T(8...) custom-call(s32[1]{0:T(128)} %bitcast.odd_ref, ...), custom_call_target="tpu_custom_call" | custom-call | bytes 4194304 | tf_op jit(solution)/shard_map/residual/pallas_call | solution.py:63
  111.2 4.9 %collective-permute-start.26 = (f32[3,4,64,128]{3,2,1,0:T(8,128)S(1)}, f32[3,4,64,128]{3,2,1,0:T(8,128)S(1)}, u32[]{:S(2)}, u32[]{:S(2)}) collective-permute-start(f32[3,4,64,128]{3,2,1,0:T(8,128)S(1)} %get-tuple-element.90), channel_id=1, source_target_pairs={{0,16},{16,32},{32,48},{64,80},{80,96},{96,112},{1,17},{17,33},{33... | collective-permute-start | bytes 1179656 | tf_op jit(solution)/shard_map/ppermute | solution.py:455
  116.1 8.3 %collective-permute-done.20 = f32[3,4,64,128]{3,2,1,0:T(8,128)S(1)} collective-permute-done((f32[3,4,64,128]{3,2,1,0:T(8,128)S(1)}, f32[3,4,64,128]{3,2,1,0:T(8,128)S(1)}, u32[]{:S(2)}, u32[]{:S(2)}) %collective-permute-start.20) | collective-permute-done | bytes 393248 | tf_op jit(solution)/shard_map/ppermute | solution.py:455
  127.7 6.0 %collective-permute-done.22 = f32[3,4,64,128]{3,2,1,0:T(8,128)S(1)} collective-permute-done((f32[3,4,64,128]{3,2,1,0:T(8,128)S(1)}, f32[3,4,64,128]{3,2,1,0:T(8,128)S(1)}, u32[]{:S(2)}, u32[]{:S(2)}) %collective-permute-start.22) | collective-permute-done | bytes 393248 | tf_op jit(solution)/shard_map/ppermute | solution.py:455
  133.7 6.2 %collective-permute-done.24 = f32[3,4,64,128]{3,2,1,0:T(8,128)S(1)} collective-permute-done((f32[3,4,64,128]{3,2,1,0:T(8,128)S(1)}, f32[3,4,64,128]{3,2,1,0:T(8,128)S(1)}, u32[]{:S(2)}, u32[]{:S(2)}) %collective-permute-start.24) | collective-permute-done | bytes 393248 | tf_op jit(solution)/shard_map/ppermute | solution.py:455
  141.7 4.3 %square.1 = (f32[3,4,64,128]{3,2,1,0:T(8,128)S(1)}, f32[3,4,64,128]{3,2,1,0:T(8,128)S(1)}, f32[3,4,64,128]{3,2,1,0:T(8,128)S(1)}) custom-call(s32[1]{0:T(128)} %bitcast.odd_ref, f32[3,4,64,128]{3,2,1,0:T(8,128)S(1)} %collective-permute-done.21.hb, f32[3,4,64,128]{3,2,1,0:T(8,128)S(1)} %add.35.sb, f32[3,4,64,128]{3,2,1,0:T(8,128)S(1)} %collective-permute-done.25.ha, ...), custom_call_target="tpu_custom_call" | custom-call | bytes 4194304 | tf_op jit(solution)/shard_map/square/pallas_call | solution.py:63
  156.0 5.3 %collective-permute-done.29 = f32[3,4,64,128]{3,2,1,0:T(8,128)S(1)} collective-permute-done((f32[3,4,64,128]{3,2,1,0:T(8,128)S(1)}, f32[3,4,64,128]{3,2,1,0:T(8,128)S(1)}, u32[]{:S(2)}, u32[]{:S(2)}) %collective-permute-start.29) | collective-permute-done | bytes 393248 | tf_op jit(solution)/shard_map/ppermute | solution.py:455
  162.9 4.4 %collective-permute-start.30 = (f32[3,4,64,128]{3,2,1,0:T(8,128)S(1)}, f32[3,4,64,128]{3,2,1,0:T(8,128)S(1)}, u32[]{:S(2)}, u32[]{:S(2)}) collective-permute-start(f32[3,4,64,128]{3,2,1,0:T(8,128)S(1)} %add.40.tm), channel_id=1, source_target_pairs={{1,2},{3,4},{5,6},{7,8},{9,10},{11,12},{13,14},{2,1},{4,3},{6,5},{... | collective-permute-start | bytes 1179656 | tf_op jit(solution)/shard_map/ppermute | solution.py:450
  169.7 7.3 %collective-permute-start.28 = (f32[3,4,64,128]{3,2,1,0:T(8,128)S(1)}, f32[3,4,64,128]{3,2,1,0:T(8,128)S(1)}, u32[]{:S(2)}, u32[]{:S(2)}) collective-permute-start(f32[3,4,64,128]{3,2,1,0:T(8,128)S(1)} %add.39.tb), channel_id=1, source_target_pairs={{1,2},{3,4},{5,6},{7,8},{9,10},{11,12},{13,14},{2,1},{4,3},{6,5},{... | collective-permute-start | bytes 1179656 | tf_op jit(solution)/shard_map/ppermute | solution.py:450
  178.6 6.9 %collective-permute-done.28.near_b = f32[3,4,64,128]{3,2,1,0:T(8,128)S(1)} collective-permute-done((f32[3,4,64,128]{3,2,1,0:T(8,128)S(1)}, f32[3,4,64,128]{3,2,1,0:T(8,128)S(1)}, u32[]{:S(2)}, u32[]{:S(2)}) %collective-permute-start.28) | collective-permute-done | bytes 393248 | tf_op jit(solution)/shard_map/ppermute | solution.py:450
  185.4 10.6 %fourth.1 = (f32[3,4,64,128]{3,2,1,0:T(8,128)S(1)}, f32[3,4,64,128]{3,2,1,0:T(8,128)S(1)}, f32[3,4,64,128]{3,2,1,0:T(8,128)S(1)}, f32[3,4,64,128]{3,2,1,0:T(8,12...) custom-call(s32[1]{0:T(128)} %bitcast.odd_ref, ...), custom_call_target="tpu_custom_call" | custom-call | bytes 4194304 | tf_op jit(solution)/shard_map/fourth/pallas_call | solution.py:63
  196.0 4.4 %collective-permute-start.37 = (f32[3,4,64,128]{3,2,1,0:T(8,128)S(1)}, f32[3,4,64,128]{3,2,1,0:T(8,128)S(1)}, u32[]{:S(2)}, u32[]{:S(2)}) collective-permute-start(f32[3,4,64,128]{3,2,1,0:T(8,128)S(1)} %get-tuple-element.99), channel_id=1, source_target_pairs={{0,64},{16,80},{32,96},{48,112},{64,0},{80,16},{96,32},{112,48},{1... | collective-permute-start | bytes 1179656 | tf_op jit(solution)/shard_map/ppermute | solution.py:455
  200.5 11.7 %collective-permute-done.37.moved = f32[3,4,64,128]{3,2,1,0:T(8,128)S(1)} collective-permute-done((f32[3,4,64,128]{3,2,1,0:T(8,128)S(1)}, f32[3,4,64,128]{3,2,1,0:T(8,128)S(1)}, u32[]{:S(2)}, u32[]{:S(2)}) %collective-permute-start.37) | collective-permute-done | bytes 393248 | tf_op jit(solution)/shard_map/ppermute | solution.py:455
  220.5 6.0 %collective-permute-done.40 = f32[3,4,64,128]{3,2,1,0:T(8,128)S(1)} collective-permute-done((f32[3,4,64,128]{3,2,1,0:T(8,128)S(1)}, f32[3,4,64,128]{3,2,1,0:T(8,128)S(1)}, u32[]{:S(2)}, u32[]{:S(2)}) %collective-permute-start.40) | collective-permute-done | bytes 393248 | tf_op jit(solution)/shard_map/ppermute | solution.py:455
  (97 shorter events, 78.1 us)
Async XLA Ops:
  16.7 14.9 %collective-permute-start.3 = (f32[12,64,128]{2,1,0:T(8,128)S(1)}, f32[12,64,128]{2,1,0:T(8,128)S(1)}, u32[]{:S(2)}, u32[]{:S(2)}) collective-permute-start(f32[12,64,128]{2,1,0:T(8,128)S(1)} %get-tuple-element.63), channel_id=1, source_target_pairs={{0,1},{1,0},{2,3},{3,2},{4,5},{5,4},{6,7},{7,6},{8,9},{9,8},{10,11... | collective-permute-start | bytes 1179656 | tf_op jit(solution)/shard_map/ppermute | solution.py:447
  17.3 15.6 %collective-permute-start.4 = (f32[12,64,128]{2,1,0:T(8,128)S(1)}, f32[12,64,128]{2,1,0:T(8,128)S(1)}, u32[]{:S(2)}, u32[]{:S(2)}) collective-permute-start(f32[12,64,128]{2,1,0:T(8,128)S(1)} %get-tuple-element.64), channel_id=1, source_target_pairs={{1,2},{3,4},{5,6},{7,8},{9,10},{11,12},{13,14},{2,1},{4,3},{6,5},{... | collective-permute-start | bytes 1179656 | tf_op jit(solution)/shard_map/ppermute | solution.py:450
  22.3 15.7 %collective-permute-start.2 = (f32[3,4,64,128]{3,2,1,0:T(8,128)S(1)}, f32[3,4,64,128]{3,2,1,0:T(8,128)S(1)}, u32[]{:S(2)}, u32[]{:S(2)}) collective-permute-start(f32[3,4,64,128]{3,2,1,0:T(8,128)S(1)} %get-tuple-element.62), channel_id=1, source_target_pairs={{0,16},{16,32},{32,48},{48,64},{64,80},{80,96},{96,112},{112,0},{1... | collective-permute-start | bytes 1179656 | tf_op jit(solution)/shard_map/ppermute | solution.py:455
  23.6 17.9 %collective-permute-start.9 = (f32[3,4,64,128]{3,2,1,0:T(8,128)S(1)}, f32[3,4,64,128]{3,2,1,0:T(8,128)S(1)}, u32[]{:S(2)}, u32[]{:S(2)}) collective-permute-start(f32[3,4,64,128]{3,2,1,0:T(8,128)S(1)} %first_middle.1.after), channel_id=1, source_target_pairs={{0,16},{16,32},{32,48},{64,80},{80,96},{96,112},{1,17},{17,33},{33... | collective-permute-start | bytes 1179656 | tf_op jit(solution)/shard_map/ppermute | solution.py:455
  26.7 21.9 %collective-permute-start.6 = (f32[3,4,64,128]{3,2,1,0:T(8,128)S(1)}, f32[3,4,64,128]{3,2,1,0:T(8,128)S(1)}, u32[]{:S(2)}, u32[]{:S(2)}) collective-permute-start(f32[3,4,64,128]{3,2,1,0:T(8,128)S(1)} %get-tuple-element.67), channel_id=1, source_target_pairs={{0,16},{16,32},{32,48},{48,64},{64,80},{80,96},{96,112},{112,0},{1... | collective-permute-start | bytes 1179656 | tf_op jit(solution)/shard_map/ppermute | solution.py:455
  31.6 23.0 %collective-permute-start.8 = (f32[3,4,64,128]{3,2,1,0:T(8,128)S(1)}, f32[3,4,64,128]{3,2,1,0:T(8,128)S(1)}, u32[]{:S(2)}, u32[]{:S(2)}) collective-permute-start(f32[3,4,64,128]{3,2,1,0:T(8,128)S(1)} %collective-permute-done.7), channel_id=1, source_target_pairs={{112,64},{48,0},{113,65},{49,1},{114,66},{50,2},{115,67},{51,3},{1... | collective-permute-start | bytes 1179656 | tf_op jit(solution)/shard_map/ppermute | solution.py:455
  38.0 18.5 %collective-permute-start.5 = (f32[3,4,64,128]{3,2,1,0:T(8,128)S(1)}, f32[3,4,64,128]{3,2,1,0:T(8,128)S(1)}, u32[]{:S(2)}, u32[]{:S(2)}) collective-permute-start(f32[3,4,64,128]{3,2,1,0:T(8,128)S(1)} %collective-permute-done.2.vb), channel_id=1, source_target_pairs={{1,2},{3,4},{5,6},{7,8},{9,10},{11,12},{13,14},{2,1},{4,3},{6,5},{... | collective-permute-start | bytes 1179656 | tf_op jit(solution)/shard_map/ppermute | solution.py:450
  62.5 24.8 %collective-permute-start.13 = (f32[3,4,64,128]{3,2,1,0:T(8,128)S(1)}, f32[3,4,64,128]{3,2,1,0:T(8,128)S(1)}, u32[]{:S(2)}, u32[]{:S(2)}) collective-permute-start(f32[3,4,64,128]{3,2,1,0:T(8,128)S(1)} %get-tuple-element.75), channel_id=1, source_target_pairs={{0,16},{16,32},{32,48},{48,64},{64,80},{80,96},{96,112},{112,0},{1... | collective-permute-start | bytes 1179656 | tf_op jit(solution)/shard_map/ppermute | solution.py:455
  62.6 32.6 %collective-permute-start.15 = (f32[3,4,64,128]{3,2,1,0:T(8,128)S(1)}, f32[3,4,64,128]{3,2,1,0:T(8,128)S(1)}, u32[]{:S(2)}, u32[]{:S(2)}) collective-permute-start(f32[3,4,64,128]{3,2,1,0:T(8,128)S(1)} %collective-permute-done.14), channel_id=1, source_target_pairs={{112,64},{48,0},{113,65},{49,1},{114,66},{50,2},{115,67},{51,3},{1... | collective-permute-start | bytes 1179656 | tf_op jit(solution)/shard_map/ppermute | solution.py:455
  63.9 40.3 %collective-permute-start.17 = (f32[3,4,64,128]{3,2,1,0:T(8,128)S(1)}, f32[3,4,64,128]{3,2,1,0:T(8,128)S(1)}, u32[]{:S(2)}, u32[]{:S(2)}) collective-permute-start(f32[3,4,64,128]{3,2,1,0:T(8,128)S(1)} %get-tuple-element.76), channel_id=1, source_target_pairs={{0,16},{16,32},{32,48},{64,80},{80,96},{96,112},{1,17},{17,33},{33... | collective-permute-start | bytes 1179656 | tf_op jit(solution)/shard_map/ppermute | solution.py:455
  76.7 27.5 %collective-permute-start.12 = (f32[3,4,64,128]{3,2,1,0:T(8,128)S(1)}, f32[3,4,64,128]{3,2,1,0:T(8,128)S(1)}, u32[]{:S(2)}, u32[]{:S(2)}) collective-permute-start(f32[3,4,64,128]{3,2,1,0:T(8,128)S(1)} %collective-permute-done.11.vb), channel_id=1, source_target_pairs={{1,2},{3,4},{5,6},{7,8},{9,10},{11,12},{13,14},{2,1},{4,3},{6,5},{... | collective-permute-start | bytes 1179656 | tf_op jit(solution)/shard_map/ppermute | solution.py:450
  109.7 14.8 %collective-permute-start.20 = (f32[3,4,64,128]{3,2,1,0:T(8,128)S(1)}, f32[3,4,64,128]{3,2,1,0:T(8,128)S(1)}, u32[]{:S(2)}, u32[]{:S(2)}) collective-permute-start(f32[3,4,64,128]{3,2,1,0:T(8,128)S(1)} %get-tuple-element.87), channel_id=1, source_target_pairs={{0,16},{16,32},{32,48},{48,64},{64,80},{80,96},{96,112},{112,0},{1... | collective-permute-start | bytes 1179656 | tf_op jit(solution)/shard_map/ppermute | solution.py:455
  109.8 23.9 %collective-permute-start.22 = (f32[3,4,64,128]{3,2,1,0:T(8,128)S(1)}, f32[3,4,64,128]{3,2,1,0:T(8,128)S(1)}, u32[]{:S(2)}, u32[]{:S(2)}) collective-permute-start(f32[3,4,64,128]{3,2,1,0:T(8,128)S(1)} %get-tuple-element.89), channel_id=1, source_target_pairs={{0,16},{16,32},{32,48},{48,64},{64,80},{80,96},{96,112},{112,0},{1... | collective-permute-start | bytes 1179656 | tf_op jit(solution)/shard_map/ppermute | solution.py:455
  109.9 30.0 %collective-permute-start.24 = (f32[3,4,64,128]{3,2,1,0:T(8,128)S(1)}, f32[3,4,64,128]{3,2,1,0:T(8,128)S(1)}, u32[]{:S(2)}, u32[]{:S(2)}) collective-permute-start(f32[3,4,64,128]{3,2,1,0:T(8,128)S(1)} %collective-permute-done.23), channel_id=1, source_target_pairs={{112,64},{48,0},{113,65},{49,1},{114,66},{50,2},{115,67},{51,3},{1... | collective-permute-start | bytes 1179656 | tf_op jit(solution)/shard_map/ppermute | solution.py:455
  111.2 28.8 %collective-permute-start.26 = (f32[3,4,64,128]{3,2,1,0:T(8,128)S(1)}, f32[3,4,64,128]{3,2,1,0:T(8,128)S(1)}, u32[]{:S(2)}, u32[]{:S(2)}) collective-permute-start(f32[3,4,64,128]{3,2,1,0:T(8,128)S(1)} %get-tuple-element.90), channel_id=1, source_target_pairs={{0,16},{16,32},{32,48},{64,80},{80,96},{96,112},{1,17},{17,33},{33... | collective-permute-start | bytes 1179656 | tf_op jit(solution)/shard_map/ppermute | solution.py:455
  124.5 17.1 %collective-permute-start.21 = (f32[3,4,64,128]{3,2,1,0:T(8,128)S(1)}, f32[3,4,64,128]{3,2,1,0:T(8,128)S(1)}, u32[]{:S(2)}, u32[]{:S(2)}) collective-permute-start(f32[3,4,64,128]{3,2,1,0:T(8,128)S(1)} %add.35.sb), channel_id=1, source_target_pairs={{1,2},{3,4},{5,6},{7,8},{9,10},{11,12},{13,14},{2,1},{4,3},{6,5},{... | collective-permute-start | bytes 1179656 | tf_op jit(solution)/shard_map/ppermute | solution.py:450
  148.5 21.1 %collective-permute-start.27 = (f32[3,4,64,128]{3,2,1,0:T(8,128)S(1)}, f32[3,4,64,128]{3,2,1,0:T(8,128)S(1)}, u32[]{:S(2)}, u32[]{:S(2)}) collective-permute-start(f32[3,4,64,128]{3,2,1,0:T(8,128)S(1)} %get-tuple-element.94), channel_id=1, source_target_pairs={{0,32},{16,48},{32,64},{48,80},{64,96},{80,112},{96,0},{112,16},{1... | collective-permute-start | bytes 1179656 | tf_op jit(solution)/shard_map/ppermute | solution.py:455
  151.3 25.8 %collective-permute-start.34 = (f32[3,4,64,128]{3,2,1,0:T(8,128)S(1)}, f32[3,4,64,128]{3,2,1,0:T(8,128)S(1)}, u32[]{:S(2)}, u32[]{:S(2)}) collective-permute-start(f32[3,4,64,128]{3,2,1,0:T(8,128)S(1)} %get-tuple-element.96), channel_id=1, source_target_pairs={{0,32},{16,48},{64,96},{80,112},{1,33},{17,49},{65,97},{81,113},{2... | collective-permute-start | bytes 1179656 | tf_op jit(solution)/shard_map/ppermute | solution.py:455
  154.7 22.4 %collective-permute-start.33 = (f32[3,4,64,128]{3,2,1,0:T(8,128)S(1)}, f32[3,4,64,128]{3,2,1,0:T(8,128)S(1)}, u32[]{:S(2)}, u32[]{:S(2)}) collective-permute-start(f32[3,4,64,128]{3,2,1,0:T(8,128)S(1)} %collective-permute-done.32), channel_id=1, source_target_pairs={{96,64},{112,80},{32,0},{48,16},{97,65},{113,81},{33,1},{49,17},{9... | collective-permute-start | bytes 1179656 | tf_op jit(solution)/shard_map/ppermute | solution.py:455
  161.3 24.1 %collective-permute-start.31 = (f32[3,4,64,128]{3,2,1,0:T(8,128)S(1)}, f32[3,4,64,128]{3,2,1,0:T(8,128)S(1)}, u32[]{:S(2)}, u32[]{:S(2)}) collective-permute-start(f32[3,4,64,128]{3,2,1,0:T(8,128)S(1)} %add.40.tm), channel_id=1, source_target_pairs={{0,1},{1,0},{2,3},{3,2},{4,5},{5,4},{6,7},{7,6},{8,9},{9,8},{10,11... | collective-permute-start | bytes 1179656 | tf_op jit(solution)/shard_map/ppermute | solution.py:447
  162.9 22.5 %collective-permute-start.30 = (f32[3,4,64,128]{3,2,1,0:T(8,128)S(1)}, f32[3,4,64,128]{3,2,1,0:T(8,128)S(1)}, u32[]{:S(2)}, u32[]{:S(2)}) collective-permute-start(f32[3,4,64,128]{3,2,1,0:T(8,128)S(1)} %add.40.tm), channel_id=1, source_target_pairs={{1,2},{3,4},{5,6},{7,8},{9,10},{11,12},{13,14},{2,1},{4,3},{6,5},{... | collective-permute-start | bytes 1179656 | tf_op jit(solution)/shard_map/ppermute | solution.py:450
  169.7 15.7 %collective-permute-start.28 = (f32[3,4,64,128]{3,2,1,0:T(8,128)S(1)}, f32[3,4,64,128]{3,2,1,0:T(8,128)S(1)}, u32[]{:S(2)}, u32[]{:S(2)}) collective-permute-start(f32[3,4,64,128]{3,2,1,0:T(8,128)S(1)} %add.39.tb), channel_id=1, source_target_pairs={{1,2},{3,4},{5,6},{7,8},{9,10},{11,12},{13,14},{2,1},{4,3},{6,5},{... | collective-permute-start | bytes 1179656 | tf_op jit(solution)/shard_map/ppermute | solution.py:450
  196.0 16.2 %collective-permute-start.37 = (f32[3,4,64,128]{3,2,1,0:T(8,128)S(1)}, f32[3,4,64,128]{3,2,1,0:T(8,128)S(1)}, u32[]{:S(2)}, u32[]{:S(2)}) collective-permute-start(f32[3,4,64,128]{3,2,1,0:T(8,128)S(1)} %get-tuple-element.99), channel_id=1, source_target_pairs={{0,64},{16,80},{32,96},{48,112},{64,0},{80,16},{96,32},{112,48},{1... | collective-permute-start | bytes 1179656 | tf_op jit(solution)/shard_map/ppermute | solution.py:455
  200.4 19.8 %collective-permute-start.36 = (f32[3,4,64,128]{3,2,1,0:T(8,128)S(1)}, f32[3,4,64,128]{3,2,1,0:T(8,128)S(1)}, u32[]{:S(2)}, u32[]{:S(2)}) collective-permute-start(f32[3,4,64,128]{3,2,1,0:T(8,128)S(1)} %get-tuple-element.97), channel_id=1, source_target_pairs={{0,64},{16,80},{32,96},{48,112},{64,0},{80,16},{96,32},{112,48},{1... | collective-permute-start | bytes 1179656 | tf_op jit(solution)/shard_map/ppermute | solution.py:455
  (25 other events, 143.0 us)

commit v11 on v10

--- a/solution.py
+++ b/solution.py
@@ -270,10 +270,10 @@
     for i in range(LX + 6):
         keep[i + 4] = keep_i[i]
         spread[i + 4] = spread_i[i]
-    for pack, high in ((ra, 1 - odd), (rb, odd)):
+    for pack, start, high in ((ra, 0, 1 - odd), (rb, 12, odd)):
         for k in range(4):
             at = high * (LX + 10) + k
-            cv, nv = materials(pack[k], cond_t, nu_t)
+            cv, nv = materials(pack[start + k], cond_t, nu_t)
             half = 0.5 * cv
             scale = 1.0 / (half + 6.0 * nv)
             keep[at] = half * scale
@@ -292,7 +292,7 @@
             x[c, 4 + (1 - odd) * 8 + k, ROWS] = a[c, k]
             x[c, 4 + odd * 8 + k, ROWS] = b[c, k]
             x[c, (1 - odd) * 16 + k, ROWS] = ha[c, k]
-            x[c, odd * 16 + k, ROWS] = hb[c, k]
+            x[c, odd * 16 + k, ROWS] = hb[c, k] if len(hb.shape) == 4 else hb[4 * c + k]
 
 
 def extend_force(odd, source, which, width, packs, start, f):
@@ -353,9 +353,9 @@
     fine_sweep(y, less, held, cond, nu, 2, 18, None, 1)
     kept = copy_all([(x.at[:, pl.ds(4, LX), ROWS], res_o.at[0])], sems)
     split(odd, x, 4, rb, ra, rm)
-    coarse_sweep(x, y, held, keep, spread, 3, 3, 17, True)
+    coarse_sweep(x, y, held, keep, spread, -1, 3, 17, True)
     wait_all(kept)
-    coarse_sweep(y, x, held, keep, spread, 3, 4, 16, False)
+    coarse_sweep(y, x, held, keep, spread, -1, 4, 16, False)
     split(odd, x, 4, lb, la, lm)
 
 
@@ -503,25 +503,24 @@
         (odd, hb, vb, ha, va, *vm, source, a1, b1, a2, b2, cond, nu),
         [planes(3, LX + 4), planes(3, 4), planes(3, 4), planes(3, 4)], [padded(3, n)] * 2 + [vmem(3, n)] * 3,
     )
-    sb3, sa3, ub = fence((sb3, sa3, ub))
     vb = later(ub, 1)
     va = later(ua, 1)
     around, plain = later_parts(um, 1)
     hb = from_b(vb)
-    b3 = from_b(sb3)
-    a3 = from_a(sa3)
-    wide_keep, wide_spread = call(
-        wide_kernel, "wide", (odd, *tables, keep, spread, a3, b3), [planes(LX + 14)] * 2, [],
-    )
     va, around = fence((va, around))
     ha = from_a(va)
     residual, lb, la, lm, rb, ra, rm = call(
         residual_kernel, "residual",
-        (odd, hb, vb, ha, va, around, plain, source, a2, b2, cond, nu, wide_keep, wide_spread, u0),
+        (odd, hb, vb, ha, va, around, plain, source, a2, b2, cond, nu, keep, spread, u0),
         [planes(1, 3, LX)] + [planes(3, 4)] * 6, [padded(3, n)] * 2 + [vmem(3, n)] * 2, 1, [ANY] + [VMEM] * 6,
     )
     sb = rb + later(lb, 1)
-    hb = from_b(sb)
+    hb = from_b(jnp.concatenate([sb.reshape(12, NY, NZ), sb3], axis=0))
+    sa3, sb = fence((sa3, sb))
+    a3 = from_a(sa3)
+    wide_keep, wide_spread = call(
+        wide_kernel, "wide", (odd, *tables, keep, spread, a3, hb), [planes(LX + 14)] * 2, [],
+    )
     around, plain = later_parts(lm, 1)
     moved, around = fence((later(la, 1), around))
     sa = ra + moved

time: 231 us -> 223 us (0.965)
  starting transfers between devices: 84 us -> 74.4 us
    ppermute x9 -> x8, starting transfers between devices: 37.3 us -> 31.6 us  [from_b(): return lax.ppermute(x, 'space', off_chip)]
    ppermute x23, starting transfers between devices: 41.2 us -> 38.9 us  [along(): return lax.ppermute(x, 'tm', pairs)]
    ppermute x9 -> x8, waiting for transfers between devices: 14.6 us -> 15.5 us  [from_b(): return lax.ppermute(x, 'space', off_chip)]
  transfers between devices with their start and end apart: 41 -> 40, of which waited for: 21 -> 23; matrix products, arithmetic and copies ran while one was open for 0% -> 0% of each run, Pallas kernels for 3% -> 3%
where the time goes in v11:
time: 223 us
  waiting for transfers between devices  104 us (47%)
  starting transfers between devices  74.4 us (33%)
  Pallas kernels  33.9 us (15%)
  local copies, waits for them, and re-layouts  8.44 us (4%)
    ppermute x23, waiting for transfers between devices, along(): return lax.ppermute(x, 'tm', pairs)  85.8 us
    ppermute x23, starting transfers between devices, along(): return lax.ppermute(x, 'tm', pairs)  38.9 us
    pallas_call x12, Pallas kernels, call(): pl.pallas_call(kernel, name=name, out_shape=outs, in_specs=in_specs, out_...  33.9 us
    ppermute x8, starting transfers between devices, from_b(): return lax.ppermute(x, 'space', off_chip)  31.6 us
    ppermute x8, waiting for transfers between devices, from_b(): return lax.ppermute(x, 'space', off_chip)  15.5 us
    unnamed x16, local copies, waits for them, and re-layouts  5.65 us
  transfers between devices with their start and end apart: 40, of which 23 were waited for; matrix products, arithmetic and copies ran while one was open for 0% of the time, Pallas kernels for 3%

profile of v11, /device:TPU:17, one launch (start us, length us, event | category | flops | bytes accessed | tf_op | source)
XLA Modules:
  0.0 222.5 jit_solution(4344622754582856976)
XLA Ops:
  26.7 4.9 %collective-permute-start.6 = (f32[3,4,64,128]{3,2,1,0:T(8,128)S(1)}, f32[3,4,64,128]{3,2,1,0:T(8,128)S(1)}, u32[]{:S(2)}, u32[]{:S(2)}) collective-permute-start(f32[3,4,64,128]{3,2,1,0:T(8,128)S(1)} %get-tuple-element.65), channel_id=1, source_target_pairs={{0,16},{16,32},{32,48},{48,64},{64,80},{80,96},{96,112},{112,0},{1... | collective-permute-start | bytes 1179656 | tf_op jit(solution)/shard_map/ppermute | solution.py:455
  33.9 4.1 %collective-permute-done.2.vb = f32[3,4,64,128]{3,2,1,0:T(8,128)S(1)} collective-permute-done((f32[3,4,64,128]{3,2,1,0:T(8,128)S(1)}, f32[3,4,64,128]{3,2,1,0:T(8,128)S(1)}, u32[]{:S(2)}, u32[]{:S(2)}) %collective-permute-start.2) | collective-permute-done | bytes 393248 | tf_op jit(solution)/shard_map/ppermute | solution.py:455
  41.5 7.1 %collective-permute-done.6.va = f32[3,4,64,128]{3,2,1,0:T(8,128)S(1)} collective-permute-done((f32[3,4,64,128]{3,2,1,0:T(8,128)S(1)}, f32[3,4,64,128]{3,2,1,0:T(8,128)S(1)}, u32[]{:S(2)}, u32[]{:S(2)}) %collective-permute-start.6) | collective-permute-done | bytes 393248 | tf_op jit(solution)/shard_map/ppermute | solution.py:455
  48.6 5.9 %collective-permute-done.8.vm = f32[3,4,64,128]{3,2,1,0:T(8,128)S(1)} collective-permute-done((f32[3,4,64,128]{3,2,1,0:T(8,128)S(1)}, f32[3,4,64,128]{3,2,1,0:T(8,128)S(1)}, u32[]{:S(2)}, u32[]{:S(2)}) %collective-permute-start.8) | collective-permute-done | bytes 393248 | tf_op jit(solution)/shard_map/ppermute | solution.py:455
  57.0 4.7 %second.1 = (f32[3,16,64,128]{3,2,1,0:T(8,128)S(1)}, f32[3,4,64,128]{3,2,1,0:T(8,128)S(1)}, f32[3,4,64,128]{3,2,1,0:T(8,128)S(1)}, f32[3,4,64,128]{3,2,1,0:T(8,128)S(1)}) custom-call(s32[1]{0:T(128)} %bitcast.odd_ref, f32[3,4,64,128]{3,2,1,0:T(8,128)S(1)} %collective-permute-done.5.hb, f32[3,4,64,128]{3,2,1,0:T(8,128)S(1)} %collective-permute-done.2.vb, ...), custom_call_target="tpu_custom_call" | custom-call | bytes 4194304 | tf_op jit(solution)/shard_map/second/pallas_call | solution.py:63
  63.9 5.3 %collective-permute-start.17 = (f32[3,4,64,128]{3,2,1,0:T(8,128)S(1)}, f32[3,4,64,128]{3,2,1,0:T(8,128)S(1)}, u32[]{:S(2)}, u32[]{:S(2)}) collective-permute-start(f32[3,4,64,128]{3,2,1,0:T(8,128)S(1)} %get-tuple-element.73), channel_id=1, source_target_pairs={{0,16},{16,32},{32,48},{64,80},{80,96},{96,112},{1,17},{17,33},{33... | collective-permute-start | bytes 1179656 | tf_op jit(solution)/shard_map/ppermute | solution.py:455
  69.3 7.4 %collective-permute-done.11.vb = f32[3,4,64,128]{3,2,1,0:T(8,128)S(1)} collective-permute-done((f32[3,4,64,128]{3,2,1,0:T(8,128)S(1)}, f32[3,4,64,128]{3,2,1,0:T(8,128)S(1)}, u32[]{:S(2)}, u32[]{:S(2)}) %collective-permute-start.11) | collective-permute-done | bytes 393248 | tf_op jit(solution)/shard_map/ppermute | solution.py:455
  76.7 6.1 %collective-permute-start.12 = (f32[3,4,64,128]{3,2,1,0:T(8,128)S(1)}, f32[3,4,64,128]{3,2,1,0:T(8,128)S(1)}, u32[]{:S(2)}, u32[]{:S(2)}) collective-permute-start(f32[3,4,64,128]{3,2,1,0:T(8,128)S(1)} %collective-permute-done.11.vb), channel_id=1, source_target_pairs={{1,2},{3,4},{5,6},{7,8},{9,10},{11,12},{13,14},{2,1},{4,3},{6,5},{... | collective-permute-start | bytes 1179656 | tf_op jit(solution)/shard_map/ppermute | solution.py:450
  82.9 4.4 %collective-permute-done.13.va = f32[3,4,64,128]{3,2,1,0:T(8,128)S(1)} collective-permute-done((f32[3,4,64,128]{3,2,1,0:T(8,128)S(1)}, f32[3,4,64,128]{3,2,1,0:T(8,128)S(1)}, u32[]{:S(2)}, u32[]{:S(2)}) %collective-permute-start.13) | collective-permute-done | bytes 393248 | tf_op jit(solution)/shard_map/ppermute | solution.py:455
  87.3 8.0 %collective-permute-done.15.vm = f32[3,4,64,128]{3,2,1,0:T(8,128)S(1)} collective-permute-done((f32[3,4,64,128]{3,2,1,0:T(8,128)S(1)}, f32[3,4,64,128]{3,2,1,0:T(8,128)S(1)}, u32[]{:S(2)}, u32[]{:S(2)}) %collective-permute-start.15) | collective-permute-done | bytes 393248 | tf_op jit(solution)/shard_map/ppermute | solution.py:455
  97.0 4.7 %residual.1 = (f32[1,3,12,64,128]{4,3,2,1,0:T(8,128)}, f32[3,4,64,128]{3,2,1,0:T(8,128)S(1)}, f32[3,4,64,128]{3,2,1,0:T(8,128)S(1)}, f32[3,4,64,128]{3,2,1,0:T(8...) custom-call(s32[1]{0:T(128)} %bitcast.odd_ref, ...), custom_call_target="tpu_custom_call" | custom-call | bytes 4194304 | tf_op jit(solution)/shard_map/residual/pallas_call | solution.py:63
  106.9 9.8 %collective-permute-done.18 = f32[3,4,64,128]{3,2,1,0:T(8,128)S(1)} collective-permute-done((f32[3,4,64,128]{3,2,1,0:T(8,128)S(1)}, f32[3,4,64,128]{3,2,1,0:T(8,128)S(1)}, u32[]{:S(2)}, u32[]{:S(2)}) %collective-permute-start.18) | collective-permute-done | bytes 393248 | tf_op jit(solution)/shard_map/ppermute | solution.py:455
  120.7 4.4 %collective-permute-done.20 = f32[3,4,64,128]{3,2,1,0:T(8,128)S(1)} collective-permute-done((f32[3,4,64,128]{3,2,1,0:T(8,128)S(1)}, f32[3,4,64,128]{3,2,1,0:T(8,128)S(1)}, u32[]{:S(2)}, u32[]{:S(2)}) %collective-permute-start.20) | collective-permute-done | bytes 393248 | tf_op jit(solution)/shard_map/ppermute | solution.py:455
  125.1 5.9 %collective-permute-done.22 = f32[3,4,64,128]{3,2,1,0:T(8,128)S(1)} collective-permute-done((f32[3,4,64,128]{3,2,1,0:T(8,128)S(1)}, f32[3,4,64,128]{3,2,1,0:T(8,128)S(1)}, u32[]{:S(2)}, u32[]{:S(2)}) %collective-permute-start.22) | collective-permute-done | bytes 393248 | tf_op jit(solution)/shard_map/ppermute | solution.py:455
  132.4 5.2 %collective-permute-done.19.hb.rb = f32[16,64,128]{2,1,0:T(8,128)S(1)} collective-permute-done((f32[16,64,128]{2,1,0:T(8,128)S(1)}, f32[16,64,128]{2,1,0:T(8,128)S(1)}, u32[]{:S(2)}, u32[]{:S(2)}) %collective-permute-start.19) | collective-permute-done | bytes 524320 | tf_op jit(solution)/shard_map/ppermute | solution.py:450
  137.6 4.3 %square.1 = (f32[3,4,64,128]{3,2,1,0:T(8,128)S(1)}, f32[3,4,64,128]{3,2,1,0:T(8,128)S(1)}, f32[3,4,64,128]{3,2,1,0:T(8,128)S(1)}) custom-call(s32[1]{0:T(128)} %bitcast.odd_ref, f32[16,64,128]{2,1,0:T(8,128)S(1)} %collective-permute-done.19.hb.rb, f32[3,4,64,128]{3,2,1,0:T(8,128)S(1)} %add.35.sb, f32[3,4,64,128]{3,2,1,0:T(8,128)S(1)} %collective-permute-done.23.ha, ...), custom_call_target="tpu_custom_call" | custom-call | bytes 4194304 | tf_op jit(solution)/shard_map/square/pallas_call | solution.py:63
  145.2 4.7 %collective-permute-start.32 = (f32[3,4,64,128]{3,2,1,0:T(8,128)S(1)}, f32[3,4,64,128]{3,2,1,0:T(8,128)S(1)}, u32[]{:S(2)}, u32[]{:S(2)}) collective-permute-start(f32[3,4,64,128]{3,2,1,0:T(8,128)S(1)} %get-tuple-element.91), channel_id=1, source_target_pairs={{0,32},{16,48},{64,96},{80,112},{1,33},{17,49},{65,97},{81,113},{2... | collective-permute-start | bytes 1179656 | tf_op jit(solution)/shard_map/ppermute | solution.py:455
  151.2 6.6 %collective-permute-done.27 = f32[3,4,64,128]{3,2,1,0:T(8,128)S(1)} collective-permute-done((f32[3,4,64,128]{3,2,1,0:T(8,128)S(1)}, f32[3,4,64,128]{3,2,1,0:T(8,128)S(1)}, u32[]{:S(2)}, u32[]{:S(2)}) %collective-permute-start.27) | collective-permute-done | bytes 393248 | tf_op jit(solution)/shard_map/ppermute | solution.py:455
  160.6 5.7 %collective-permute-done.25 = f32[3,4,64,128]{3,2,1,0:T(8,128)S(1)} collective-permute-done((f32[3,4,64,128]{3,2,1,0:T(8,128)S(1)}, f32[3,4,64,128]{3,2,1,0:T(8,128)S(1)}, u32[]{:S(2)}, u32[]{:S(2)}) %collective-permute-start.25) | collective-permute-done | bytes 393248 | tf_op jit(solution)/shard_map/ppermute | solution.py:455
  173.9 6.9 %collective-permute-done.26.near_b = f32[3,4,64,128]{3,2,1,0:T(8,128)S(1)} collective-permute-done((f32[3,4,64,128]{3,2,1,0:T(8,128)S(1)}, f32[3,4,64,128]{3,2,1,0:T(8,128)S(1)}, u32[]{:S(2)}, u32[]{:S(2)}) %collective-permute-start.26) | collective-permute-done | bytes 393248 | tf_op jit(solution)/shard_map/ppermute | solution.py:450
  180.8 10.6 %fourth.1 = (f32[3,4,64,128]{3,2,1,0:T(8,128)S(1)}, f32[3,4,64,128]{3,2,1,0:T(8,128)S(1)}, f32[3,4,64,128]{3,2,1,0:T(8,128)S(1)}, f32[3,4,64,128]{3,2,1,0:T(8,12...) custom-call(s32[1]{0:T(128)} %bitcast.odd_ref, ...), custom_call_target="tpu_custom_call" | custom-call | bytes 4194304 | tf_op jit(solution)/shard_map/fourth/pallas_call | solution.py:63
  194.5 10.7 %collective-permute-done.36.moved = f32[3,4,64,128]{3,2,1,0:T(8,128)S(1)} collective-permute-done((f32[3,4,64,128]{3,2,1,0:T(8,128)S(1)}, f32[3,4,64,128]{3,2,1,0:T(8,128)S(1)}, u32[]{:S(2)}, u32[]{:S(2)}) %collective-permute-start.36) | collective-permute-done | bytes 393248 | tf_op jit(solution)/shard_map/ppermute | solution.py:455
  205.2 4.4 %collective-permute-start.37 = (f32[3,2,64,128]{3,2,1,0:T(8,128)S(1)}, f32[3,2,64,128]{3,2,1,0:T(8,128)S(1)}, u32[]{:S(2)}, u32[]{:S(2)}) collective-permute-start(f32[3,2,64,128]{3,2,1,0:T(8,128)S(1)} %get-tuple-element.98), channel_id=1, source_target_pairs={{1,2},{3,4},{5,6},{7,8},{9,10},{11,12},{13,14},{2,1},{4,3},{6,5},{... | collective-permute-start | bytes 589832 | tf_op jit(solution)/shard_map/ppermute | solution.py:450
  214.5 4.8 %collective-permute-done.39 = f32[3,4,64,128]{3,2,1,0:T(8,128)S(1)} collective-permute-done((f32[3,4,64,128]{3,2,1,0:T(8,128)S(1)}, f32[3,4,64,128]{3,2,1,0:T(8,128)S(1)}, u32[]{:S(2)}, u32[]{:S(2)}) %collective-permute-start.39) | collective-permute-done | bytes 393248 | tf_op jit(solution)/shard_map/ppermute | solution.py:455
  (96 shorter events, 74.6 us)
Async XLA Ops:
  16.7 14.9 %collective-permute-start.3 = (f32[12,64,128]{2,1,0:T(8,128)S(1)}, f32[12,64,128]{2,1,0:T(8,128)S(1)}, u32[]{:S(2)}, u32[]{:S(2)}) collective-permute-start(f32[12,64,128]{2,1,0:T(8,128)S(1)} %get-tuple-element.61), channel_id=1, source_target_pairs={{0,1},{1,0},{2,3},{3,2},{4,5},{5,4},{6,7},{7,6},{8,9},{9,8},{10,11... | collective-permute-start | bytes 1179656 | tf_op jit(solution)/shard_map/ppermute | solution.py:447
  17.3 15.6 %collective-permute-start.4 = (f32[12,64,128]{2,1,0:T(8,128)S(1)}, f32[12,64,128]{2,1,0:T(8,128)S(1)}, u32[]{:S(2)}, u32[]{:S(2)}) collective-permute-start(f32[12,64,128]{2,1,0:T(8,128)S(1)} %get-tuple-element.62), channel_id=1, source_target_pairs={{1,2},{3,4},{5,6},{7,8},{9,10},{11,12},{13,14},{2,1},{4,3},{6,5},{... | collective-permute-start | bytes 1179656 | tf_op jit(solution)/shard_map/ppermute | solution.py:450
  22.3 15.7 %collective-permute-start.2 = (f32[3,4,64,128]{3,2,1,0:T(8,128)S(1)}, f32[3,4,64,128]{3,2,1,0:T(8,128)S(1)}, u32[]{:S(2)}, u32[]{:S(2)}) collective-permute-start(f32[3,4,64,128]{3,2,1,0:T(8,128)S(1)} %get-tuple-element.60), channel_id=1, source_target_pairs={{0,16},{16,32},{32,48},{48,64},{64,80},{80,96},{96,112},{112,0},{1... | collective-permute-start | bytes 1179656 | tf_op jit(solution)/shard_map/ppermute | solution.py:455
  23.6 17.9 %collective-permute-start.9 = (f32[3,4,64,128]{3,2,1,0:T(8,128)S(1)}, f32[3,4,64,128]{3,2,1,0:T(8,128)S(1)}, u32[]{:S(2)}, u32[]{:S(2)}) collective-permute-start(f32[3,4,64,128]{3,2,1,0:T(8,128)S(1)} %first_middle.1.after), channel_id=1, source_target_pairs={{0,16},{16,32},{32,48},{64,80},{80,96},{96,112},{1,17},{17,33},{33... | collective-permute-start | bytes 1179656 | tf_op jit(solution)/shard_map/ppermute | solution.py:455
  26.7 21.9 %collective-permute-start.6 = (f32[3,4,64,128]{3,2,1,0:T(8,128)S(1)}, f32[3,4,64,128]{3,2,1,0:T(8,128)S(1)}, u32[]{:S(2)}, u32[]{:S(2)}) collective-permute-start(f32[3,4,64,128]{3,2,1,0:T(8,128)S(1)} %get-tuple-element.65), channel_id=1, source_target_pairs={{0,16},{16,32},{32,48},{48,64},{64,80},{80,96},{96,112},{112,0},{1... | collective-permute-start | bytes 1179656 | tf_op jit(solution)/shard_map/ppermute | solution.py:455
  31.6 23.0 %collective-permute-start.8 = (f32[3,4,64,128]{3,2,1,0:T(8,128)S(1)}, f32[3,4,64,128]{3,2,1,0:T(8,128)S(1)}, u32[]{:S(2)}, u32[]{:S(2)}) collective-permute-start(f32[3,4,64,128]{3,2,1,0:T(8,128)S(1)} %collective-permute-done.7), channel_id=1, source_target_pairs={{112,64},{48,0},{113,65},{49,1},{114,66},{50,2},{115,67},{51,3},{1... | collective-permute-start | bytes 1179656 | tf_op jit(solution)/shard_map/ppermute | solution.py:455
  38.0 18.5 %collective-permute-start.5 = (f32[3,4,64,128]{3,2,1,0:T(8,128)S(1)}, f32[3,4,64,128]{3,2,1,0:T(8,128)S(1)}, u32[]{:S(2)}, u32[]{:S(2)}) collective-permute-start(f32[3,4,64,128]{3,2,1,0:T(8,128)S(1)} %collective-permute-done.2.vb), channel_id=1, source_target_pairs={{1,2},{3,4},{5,6},{7,8},{9,10},{11,12},{13,14},{2,1},{4,3},{6,5},{... | collective-permute-start | bytes 1179656 | tf_op jit(solution)/shard_map/ppermute | solution.py:450
  62.5 14.3 %collective-permute-start.11 = (f32[3,4,64,128]{3,2,1,0:T(8,128)S(1)}, f32[3,4,64,128]{3,2,1,0:T(8,128)S(1)}, u32[]{:S(2)}, u32[]{:S(2)}) collective-permute-start(f32[3,4,64,128]{3,2,1,0:T(8,128)S(1)} %get-tuple-element.71), channel_id=1, source_target_pairs={{0,16},{16,32},{32,48},{48,64},{64,80},{80,96},{96,112},{112,0},{1... | collective-permute-start | bytes 1179656 | tf_op jit(solution)/shard_map/ppermute | solution.py:455
  62.5 24.8 %collective-permute-start.13 = (f32[3,4,64,128]{3,2,1,0:T(8,128)S(1)}, f32[3,4,64,128]{3,2,1,0:T(8,128)S(1)}, u32[]{:S(2)}, u32[]{:S(2)}) collective-permute-start(f32[3,4,64,128]{3,2,1,0:T(8,128)S(1)} %get-tuple-element.72), channel_id=1, source_target_pairs={{0,16},{16,32},{32,48},{48,64},{64,80},{80,96},{96,112},{112,0},{1... | collective-permute-start | bytes 1179656 | tf_op jit(solution)/shard_map/ppermute | solution.py:455
  62.6 32.6 %collective-permute-start.15 = (f32[3,4,64,128]{3,2,1,0:T(8,128)S(1)}, f32[3,4,64,128]{3,2,1,0:T(8,128)S(1)}, u32[]{:S(2)}, u32[]{:S(2)}) collective-permute-start(f32[3,4,64,128]{3,2,1,0:T(8,128)S(1)} %collective-permute-done.14), channel_id=1, source_target_pairs={{112,64},{48,0},{113,65},{49,1},{114,66},{50,2},{115,67},{51,3},{1... | collective-permute-start | bytes 1179656 | tf_op jit(solution)/shard_map/ppermute | solution.py:455
  63.9 31.3 %collective-permute-start.17 = (f32[3,4,64,128]{3,2,1,0:T(8,128)S(1)}, f32[3,4,64,128]{3,2,1,0:T(8,128)S(1)}, u32[]{:S(2)}, u32[]{:S(2)}) collective-permute-start(f32[3,4,64,128]{3,2,1,0:T(8,128)S(1)} %get-tuple-element.73), channel_id=1, source_target_pairs={{0,16},{16,32},{32,48},{64,80},{80,96},{96,112},{1,17},{17,33},{33... | collective-permute-start | bytes 1179656 | tf_op jit(solution)/shard_map/ppermute | solution.py:455
  76.7 19.3 %collective-permute-start.12 = (f32[3,4,64,128]{3,2,1,0:T(8,128)S(1)}, f32[3,4,64,128]{3,2,1,0:T(8,128)S(1)}, u32[]{:S(2)}, u32[]{:S(2)}) collective-permute-start(f32[3,4,64,128]{3,2,1,0:T(8,128)S(1)} %collective-permute-done.11.vb), channel_id=1, source_target_pairs={{1,2},{3,4},{5,6},{7,8},{9,10},{11,12},{13,14},{2,1},{4,3},{6,5},{... | collective-permute-start | bytes 1179656 | tf_op jit(solution)/shard_map/ppermute | solution.py:450
  102.5 22.6 %collective-permute-start.20 = (f32[3,4,64,128]{3,2,1,0:T(8,128)S(1)}, f32[3,4,64,128]{3,2,1,0:T(8,128)S(1)}, u32[]{:S(2)}, u32[]{:S(2)}) collective-permute-start(f32[3,4,64,128]{3,2,1,0:T(8,128)S(1)} %get-tuple-element.84), channel_id=1, source_target_pairs={{0,16},{16,32},{32,48},{48,64},{64,80},{80,96},{96,112},{112,0},{1... | collective-permute-start | bytes 1179656 | tf_op jit(solution)/shard_map/ppermute | solution.py:455
  102.6 28.4 %collective-permute-start.22 = (f32[3,4,64,128]{3,2,1,0:T(8,128)S(1)}, f32[3,4,64,128]{3,2,1,0:T(8,128)S(1)}, u32[]{:S(2)}, u32[]{:S(2)}) collective-permute-start(f32[3,4,64,128]{3,2,1,0:T(8,128)S(1)} %collective-permute-done.21), channel_id=1, source_target_pairs={{112,64},{48,0},{113,65},{49,1},{114,66},{50,2},{115,67},{51,3},{1... | collective-permute-start | bytes 1179656 | tf_op jit(solution)/shard_map/ppermute | solution.py:455
  103.9 28.5 %collective-permute-start.24 = (f32[3,4,64,128]{3,2,1,0:T(8,128)S(1)}, f32[3,4,64,128]{3,2,1,0:T(8,128)S(1)}, u32[]{:S(2)}, u32[]{:S(2)}) collective-permute-start(f32[3,4,64,128]{3,2,1,0:T(8,128)S(1)} %get-tuple-element.85), channel_id=1, source_target_pairs={{0,16},{16,32},{32,48},{64,80},{80,96},{96,112},{1,17},{17,33},{33... | collective-permute-start | bytes 1179656 | tf_op jit(solution)/shard_map/ppermute | solution.py:455
  116.8 20.9 %collective-permute-start.19 = (f32[16,64,128]{2,1,0:T(8,128)S(1)}, f32[16,64,128]{2,1,0:T(8,128)S(1)}, u32[]{:S(2)}, u32[]{:S(2)}) collective-permute-start(f32[16,64,128]{2,1,0:T(8,128)S(1)} %pad_maximum_fusion), channel_id=1, source_target_pairs={{1,2},{3,4},{5,6},{7,8},{9,10},{11,12},{13,14},{2,1},{4,3},{6,5},{... | collective-permute-start | bytes 1572872 | tf_op jit(solution)/shard_map/ppermute | solution.py:450
  142.6 15.2 %collective-permute-start.27 = (f32[3,4,64,128]{3,2,1,0:T(8,128)S(1)}, f32[3,4,64,128]{3,2,1,0:T(8,128)S(1)}, u32[]{:S(2)}, u32[]{:S(2)}) collective-permute-start(f32[3,4,64,128]{3,2,1,0:T(8,128)S(1)} %get-tuple-element.90), channel_id=1, source_target_pairs={{0,32},{16,48},{32,64},{48,80},{64,96},{80,112},{96,0},{112,16},{1... | collective-permute-start | bytes 1179656 | tf_op jit(solution)/shard_map/ppermute | solution.py:455
  145.1 21.2 %collective-permute-start.25 = (f32[3,4,64,128]{3,2,1,0:T(8,128)S(1)}, f32[3,4,64,128]{3,2,1,0:T(8,128)S(1)}, u32[]{:S(2)}, u32[]{:S(2)}) collective-permute-start(f32[3,4,64,128]{3,2,1,0:T(8,128)S(1)} %get-tuple-element.89), channel_id=1, source_target_pairs={{0,32},{16,48},{32,64},{48,80},{64,96},{80,112},{96,0},{112,16},{1... | collective-permute-start | bytes 1179656 | tf_op jit(solution)/shard_map/ppermute | solution.py:455
  145.2 25.2 %collective-permute-start.32 = (f32[3,4,64,128]{3,2,1,0:T(8,128)S(1)}, f32[3,4,64,128]{3,2,1,0:T(8,128)S(1)}, u32[]{:S(2)}, u32[]{:S(2)}) collective-permute-start(f32[3,4,64,128]{3,2,1,0:T(8,128)S(1)} %get-tuple-element.91), channel_id=1, source_target_pairs={{0,32},{16,48},{64,96},{80,112},{1,33},{17,49},{65,97},{81,113},{2... | collective-permute-start | bytes 1179656 | tf_op jit(solution)/shard_map/ppermute | solution.py:455
  149.9 21.1 %collective-permute-start.31 = (f32[3,4,64,128]{3,2,1,0:T(8,128)S(1)}, f32[3,4,64,128]{3,2,1,0:T(8,128)S(1)}, u32[]{:S(2)}, u32[]{:S(2)}) collective-permute-start(f32[3,4,64,128]{3,2,1,0:T(8,128)S(1)} %collective-permute-done.30), channel_id=1, source_target_pairs={{96,64},{112,80},{32,0},{48,16},{97,65},{113,81},{33,1},{49,17},{9... | collective-permute-start | bytes 1179656 | tf_op jit(solution)/shard_map/ppermute | solution.py:455
  157.8 23.0 %collective-permute-start.29 = (f32[3,4,64,128]{3,2,1,0:T(8,128)S(1)}, f32[3,4,64,128]{3,2,1,0:T(8,128)S(1)}, u32[]{:S(2)}, u32[]{:S(2)}) collective-permute-start(f32[3,4,64,128]{3,2,1,0:T(8,128)S(1)} %add.40.tm), channel_id=1, source_target_pairs={{0,1},{1,0},{2,3},{3,2},{4,5},{5,4},{6,7},{7,6},{8,9},{9,8},{10,11... | collective-permute-start | bytes 1179656 | tf_op jit(solution)/shard_map/ppermute | solution.py:447
  157.9 22.9 %collective-permute-start.28 = (f32[3,4,64,128]{3,2,1,0:T(8,128)S(1)}, f32[3,4,64,128]{3,2,1,0:T(8,128)S(1)}, u32[]{:S(2)}, u32[]{:S(2)}) collective-permute-start(f32[3,4,64,128]{3,2,1,0:T(8,128)S(1)} %add.40.tm), channel_id=1, source_target_pairs={{1,2},{3,4},{5,6},{7,8},{9,10},{11,12},{13,14},{2,1},{4,3},{6,5},{... | collective-permute-start | bytes 1179656 | tf_op jit(solution)/shard_map/ppermute | solution.py:450
  166.3 14.5 %collective-permute-start.26 = (f32[3,4,64,128]{3,2,1,0:T(8,128)S(1)}, f32[3,4,64,128]{3,2,1,0:T(8,128)S(1)}, u32[]{:S(2)}, u32[]{:S(2)}) collective-permute-start(f32[3,4,64,128]{3,2,1,0:T(8,128)S(1)} %add.39.tb), channel_id=1, source_target_pairs={{1,2},{3,4},{5,6},{7,8},{9,10},{11,12},{13,14},{2,1},{4,3},{6,5},{... | collective-permute-start | bytes 1179656 | tf_op jit(solution)/shard_map/ppermute | solution.py:450
  193.7 18.8 %collective-permute-start.35 = (f32[3,4,64,128]{3,2,1,0:T(8,128)S(1)}, f32[3,4,64,128]{3,2,1,0:T(8,128)S(1)}, u32[]{:S(2)}, u32[]{:S(2)}) collective-permute-start(f32[3,4,64,128]{3,2,1,0:T(8,128)S(1)} %get-tuple-element.95), channel_id=1, source_target_pairs={{0,64},{16,80},{32,96},{48,112},{64,0},{80,16},{96,32},{112,48},{1... | collective-permute-start | bytes 1179656 | tf_op jit(solution)/shard_map/ppermute | solution.py:455
  (24 other events, 130.5 us)

commit v12 on v11

--- a/solution.py
+++ b/solution.py
@@ -127,7 +127,7 @@
                 fixed = held[c, i]
             store(c, i, fixed * keep + neighbours(src, c, i) * spread)
 
-    over_layers(lo, hi, step, 6)
+    over_layers(lo, hi, step, (hi - lo) // 2 if hi - lo >= 12 else 6)
 
 
 def coarse_sweep(src, dst, held, keep, spread, off, lo, hi, first):
@@ -142,7 +142,7 @@
                 fixed = held[c, i]
             dst[c, i, ROWS] = fixed + s * neighbours(src, c, i)
 
-    over_layers(lo, hi, step, 6)
+    over_layers(lo, hi, step, (hi - lo) // 2 if hi - lo >= 12 else 6)
 
 
 def lookup(code, table):

time: 223 us -> 223 us (level)
  no operation moved by 1% of the time
where the time goes in v12:
time: 223 us; the launch traced here: 222 us
  waiting for transfers between devices  105 us (47%)
  starting transfers between devices  73.9 us (33%)
  Pallas kernels  33.2 us (15%)
  local copies, waits for them, and re-layouts  8.44 us (4%)
    ppermute x23, waiting for transfers between devices, along(): return lax.ppermute(x, 'tm', pairs)  86.3 us
    ppermute x23, starting transfers between devices, along(): return lax.ppermute(x, 'tm', pairs)  38.7 us
    pallas_call x12, Pallas kernels, call(): pl.pallas_call(kernel, name=name, out_shape=outs, in_specs=in_specs, out_...  33.2 us
    ppermute x8, starting transfers between devices, from_b(): return lax.ppermute(x, 'space', off_chip)  31.4 us
    ppermute x8, waiting for transfers between devices, from_b(): return lax.ppermute(x, 'space', off_chip)  15.4 us
    unnamed x16, local copies, waits for them, and re-layouts  5.65 us
  transfers between devices with their start and end apart: 40, of which 23 were waited for; matrix products, arithmetic and copies ran while one was open for 0% of the time, Pallas kernels for 3%

profile of v12, /device:TPU:17, one launch (start us, length us, event | category | flops | bytes accessed | tf_op | source)
XLA Modules:
  0.0 221.9 jit_solution(13322651611653068228)
XLA Ops:
  26.7 4.9 %collective-permute-start.6 = (f32[3,4,64,128]{3,2,1,0:T(8,128)S(1)}, f32[3,4,64,128]{3,2,1,0:T(8,128)S(1)}, u32[]{:S(2)}, u32[]{:S(2)}) collective-permute-start(f32[3,4,64,128]{3,2,1,0:T(8,128)S(1)} %get-tuple-element.65), channel_id=1, source_target_pairs={{0,16},{16,32},{32,48},{48,64},{64,80},{80,96},{96,112},{112,0},{1... | collective-permute-start | bytes 1179656 | tf_op jit(solution)/shard_map/ppermute | solution.py:455
  33.9 4.1 %collective-permute-done.2.vb = f32[3,4,64,128]{3,2,1,0:T(8,128)S(1)} collective-permute-done((f32[3,4,64,128]{3,2,1,0:T(8,128)S(1)}, f32[3,4,64,128]{3,2,1,0:T(8,128)S(1)}, u32[]{:S(2)}, u32[]{:S(2)}) %collective-permute-start.2) | collective-permute-done | bytes 393248 | tf_op jit(solution)/shard_map/ppermute | solution.py:455
  41.5 7.1 %collective-permute-done.6.va = f32[3,4,64,128]{3,2,1,0:T(8,128)S(1)} collective-permute-done((f32[3,4,64,128]{3,2,1,0:T(8,128)S(1)}, f32[3,4,64,128]{3,2,1,0:T(8,128)S(1)}, u32[]{:S(2)}, u32[]{:S(2)}) %collective-permute-start.6) | collective-permute-done | bytes 393248 | tf_op jit(solution)/shard_map/ppermute | solution.py:455
  48.6 5.9 %collective-permute-done.8.vm = f32[3,4,64,128]{3,2,1,0:T(8,128)S(1)} collective-permute-done((f32[3,4,64,128]{3,2,1,0:T(8,128)S(1)}, f32[3,4,64,128]{3,2,1,0:T(8,128)S(1)}, u32[]{:S(2)}, u32[]{:S(2)}) %collective-permute-start.8) | collective-permute-done | bytes 393248 | tf_op jit(solution)/shard_map/ppermute | solution.py:455
  57.0 4.8 %second.1 = (f32[3,16,64,128]{3,2,1,0:T(8,128)S(1)}, f32[3,4,64,128]{3,2,1,0:T(8,128)S(1)}, f32[3,4,64,128]{3,2,1,0:T(8,128)S(1)}, f32[3,4,64,128]{3,2,1,0:T(8,128)S(1)}) custom-call(s32[1]{0:T(128)} %bitcast.odd_ref, f32[3,4,64,128]{3,2,1,0:T(8,128)S(1)} %collective-permute-done.5.hb, f32[3,4,64,128]{3,2,1,0:T(8,128)S(1)} %collective-permute-done.2.vb, ...), custom_call_target="tpu_custom_call" | custom-call | bytes 4194304 | tf_op jit(solution)/shard_map/second/pallas_call | solution.py:63
  64.0 5.3 %collective-permute-start.17 = (f32[3,4,64,128]{3,2,1,0:T(8,128)S(1)}, f32[3,4,64,128]{3,2,1,0:T(8,128)S(1)}, u32[]{:S(2)}, u32[]{:S(2)}) collective-permute-start(f32[3,4,64,128]{3,2,1,0:T(8,128)S(1)} %get-tuple-element.73), channel_id=1, source_target_pairs={{0,16},{16,32},{32,48},{64,80},{80,96},{96,112},{1,17},{17,33},{33... | collective-permute-start | bytes 1179656 | tf_op jit(solution)/shard_map/ppermute | solution.py:455
  69.3 7.4 %collective-permute-done.11.vb = f32[3,4,64,128]{3,2,1,0:T(8,128)S(1)} collective-permute-done((f32[3,4,64,128]{3,2,1,0:T(8,128)S(1)}, f32[3,4,64,128]{3,2,1,0:T(8,128)S(1)}, u32[]{:S(2)}, u32[]{:S(2)}) %collective-permute-start.11) | collective-permute-done | bytes 393248 | tf_op jit(solution)/shard_map/ppermute | solution.py:455
  76.8 6.1 %collective-permute-start.12 = (f32[3,4,64,128]{3,2,1,0:T(8,128)S(1)}, f32[3,4,64,128]{3,2,1,0:T(8,128)S(1)}, u32[]{:S(2)}, u32[]{:S(2)}) collective-permute-start(f32[3,4,64,128]{3,2,1,0:T(8,128)S(1)} %collective-permute-done.11.vb), channel_id=1, source_target_pairs={{1,2},{3,4},{5,6},{7,8},{9,10},{11,12},{13,14},{2,1},{4,3},{6,5},{... | collective-permute-start | bytes 1179656 | tf_op jit(solution)/shard_map/ppermute | solution.py:450
  82.9 4.4 %collective-permute-done.13.va = f32[3,4,64,128]{3,2,1,0:T(8,128)S(1)} collective-permute-done((f32[3,4,64,128]{3,2,1,0:T(8,128)S(1)}, f32[3,4,64,128]{3,2,1,0:T(8,128)S(1)}, u32[]{:S(2)}, u32[]{:S(2)}) %collective-permute-start.13) | collective-permute-done | bytes 393248 | tf_op jit(solution)/shard_map/ppermute | solution.py:455
  87.3 8.0 %collective-permute-done.15.vm = f32[3,4,64,128]{3,2,1,0:T(8,128)S(1)} collective-permute-done((f32[3,4,64,128]{3,2,1,0:T(8,128)S(1)}, f32[3,4,64,128]{3,2,1,0:T(8,128)S(1)}, u32[]{:S(2)}, u32[]{:S(2)}) %collective-permute-start.15) | collective-permute-done | bytes 393248 | tf_op jit(solution)/shard_map/ppermute | solution.py:455
  97.0 4.7 %residual.1 = (f32[1,3,12,64,128]{4,3,2,1,0:T(8,128)}, f32[3,4,64,128]{3,2,1,0:T(8,128)S(1)}, f32[3,4,64,128]{3,2,1,0:T(8,128)S(1)}, f32[3,4,64,128]{3,2,1,0:T(8...) custom-call(s32[1]{0:T(128)} %bitcast.odd_ref, ...), custom_call_target="tpu_custom_call" | custom-call | bytes 4194304 | tf_op jit(solution)/shard_map/residual/pallas_call | solution.py:63
  107.0 9.9 %collective-permute-done.18 = f32[3,4,64,128]{3,2,1,0:T(8,128)S(1)} collective-permute-done((f32[3,4,64,128]{3,2,1,0:T(8,128)S(1)}, f32[3,4,64,128]{3,2,1,0:T(8,128)S(1)}, u32[]{:S(2)}, u32[]{:S(2)}) %collective-permute-start.18) | collective-permute-done | bytes 393248 | tf_op jit(solution)/shard_map/ppermute | solution.py:455
  120.9 4.4 %collective-permute-done.20 = f32[3,4,64,128]{3,2,1,0:T(8,128)S(1)} collective-permute-done((f32[3,4,64,128]{3,2,1,0:T(8,128)S(1)}, f32[3,4,64,128]{3,2,1,0:T(8,128)S(1)}, u32[]{:S(2)}, u32[]{:S(2)}) %collective-permute-start.20) | collective-permute-done | bytes 393248 | tf_op jit(solution)/shard_map/ppermute | solution.py:455
  125.3 5.9 %collective-permute-done.22 = f32[3,4,64,128]{3,2,1,0:T(8,128)S(1)} collective-permute-done((f32[3,4,64,128]{3,2,1,0:T(8,128)S(1)}, f32[3,4,64,128]{3,2,1,0:T(8,128)S(1)}, u32[]{:S(2)}, u32[]{:S(2)}) %collective-permute-start.22) | collective-permute-done | bytes 393248 | tf_op jit(solution)/shard_map/ppermute | solution.py:455
  132.6 5.2 %collective-permute-done.19.hb.rb = f32[16,64,128]{2,1,0:T(8,128)S(1)} collective-permute-done((f32[16,64,128]{2,1,0:T(8,128)S(1)}, f32[16,64,128]{2,1,0:T(8,128)S(1)}, u32[]{:S(2)}, u32[]{:S(2)}) %collective-permute-start.19) | collective-permute-done | bytes 524320 | tf_op jit(solution)/shard_map/ppermute | solution.py:450
  137.8 4.1 %square.1 = (f32[3,4,64,128]{3,2,1,0:T(8,128)S(1)}, f32[3,4,64,128]{3,2,1,0:T(8,128)S(1)}, f32[3,4,64,128]{3,2,1,0:T(8,128)S(1)}) custom-call(s32[1]{0:T(128)} %bitcast.odd_ref, f32[16,64,128]{2,1,0:T(8,128)S(1)} %collective-permute-done.19.hb.rb, f32[3,4,64,128]{3,2,1,0:T(8,128)S(1)} %add.35.sb, f32[3,4,64,128]{3,2,1,0:T(8,128)S(1)} %collective-permute-done.23.ha, ...), custom_call_target="tpu_custom_call" | custom-call | bytes 4194304 | tf_op jit(solution)/shard_map/square/pallas_call | solution.py:63
  145.1 4.9 %collective-permute-start.32 = (f32[3,4,64,128]{3,2,1,0:T(8,128)S(1)}, f32[3,4,64,128]{3,2,1,0:T(8,128)S(1)}, u32[]{:S(2)}, u32[]{:S(2)}) collective-permute-start(f32[3,4,64,128]{3,2,1,0:T(8,128)S(1)} %get-tuple-element.91), channel_id=1, source_target_pairs={{0,32},{16,48},{64,96},{80,112},{1,33},{17,49},{65,97},{81,113},{2... | collective-permute-start | bytes 1179656 | tf_op jit(solution)/shard_map/ppermute | solution.py:455
  151.2 6.6 %collective-permute-done.27 = f32[3,4,64,128]{3,2,1,0:T(8,128)S(1)} collective-permute-done((f32[3,4,64,128]{3,2,1,0:T(8,128)S(1)}, f32[3,4,64,128]{3,2,1,0:T(8,128)S(1)}, u32[]{:S(2)}, u32[]{:S(2)}) %collective-permute-start.27) | collective-permute-done | bytes 393248 | tf_op jit(solution)/shard_map/ppermute | solution.py:455
  160.7 5.8 %collective-permute-done.25 = f32[3,4,64,128]{3,2,1,0:T(8,128)S(1)} collective-permute-done((f32[3,4,64,128]{3,2,1,0:T(8,128)S(1)}, f32[3,4,64,128]{3,2,1,0:T(8,128)S(1)}, u32[]{:S(2)}, u32[]{:S(2)}) %collective-permute-start.25) | collective-permute-done | bytes 393248 | tf_op jit(solution)/shard_map/ppermute | solution.py:455
  174.1 6.7 %collective-permute-done.26.near_b = f32[3,4,64,128]{3,2,1,0:T(8,128)S(1)} collective-permute-done((f32[3,4,64,128]{3,2,1,0:T(8,128)S(1)}, f32[3,4,64,128]{3,2,1,0:T(8,128)S(1)}, u32[]{:S(2)}, u32[]{:S(2)}) %collective-permute-start.26) | collective-permute-done | bytes 393248 | tf_op jit(solution)/shard_map/ppermute | solution.py:450
  180.8 9.9 %fourth.1 = (f32[3,4,64,128]{3,2,1,0:T(8,128)S(1)}, f32[3,4,64,128]{3,2,1,0:T(8,128)S(1)}, f32[3,4,64,128]{3,2,1,0:T(8,128)S(1)}, f32[3,4,64,128]{3,2,1,0:T(8,12...) custom-call(s32[1]{0:T(128)} %bitcast.odd_ref, ...), custom_call_target="tpu_custom_call" | custom-call | bytes 4194304 | tf_op jit(solution)/shard_map/fourth/pallas_call | solution.py:63
  193.8 11.0 %collective-permute-done.36.moved = f32[3,4,64,128]{3,2,1,0:T(8,128)S(1)} collective-permute-done((f32[3,4,64,128]{3,2,1,0:T(8,128)S(1)}, f32[3,4,64,128]{3,2,1,0:T(8,128)S(1)}, u32[]{:S(2)}, u32[]{:S(2)}) %collective-permute-start.36) | collective-permute-done | bytes 393248 | tf_op jit(solution)/shard_map/ppermute | solution.py:455
  204.9 4.2 %collective-permute-start.37 = (f32[3,2,64,128]{3,2,1,0:T(8,128)S(1)}, f32[3,2,64,128]{3,2,1,0:T(8,128)S(1)}, u32[]{:S(2)}, u32[]{:S(2)}) collective-permute-start(f32[3,2,64,128]{3,2,1,0:T(8,128)S(1)} %get-tuple-element.98), channel_id=1, source_target_pairs={{1,2},{3,4},{5,6},{7,8},{9,10},{11,12},{13,14},{2,1},{4,3},{6,5},{... | collective-permute-start | bytes 589832 | tf_op jit(solution)/shard_map/ppermute | solution.py:450
  214.1 4.5 %collective-permute-done.39 = f32[3,4,64,128]{3,2,1,0:T(8,128)S(1)} collective-permute-done((f32[3,4,64,128]{3,2,1,0:T(8,128)S(1)}, f32[3,4,64,128]{3,2,1,0:T(8,128)S(1)}, u32[]{:S(2)}, u32[]{:S(2)}) %collective-permute-start.39) | collective-permute-done | bytes 393248 | tf_op jit(solution)/shard_map/ppermute | solution.py:455
  (96 shorter events, 74.7 us)
Async XLA Ops:
  16.7 14.9 %collective-permute-start.3 = (f32[12,64,128]{2,1,0:T(8,128)S(1)}, f32[12,64,128]{2,1,0:T(8,128)S(1)}, u32[]{:S(2)}, u32[]{:S(2)}) collective-permute-start(f32[12,64,128]{2,1,0:T(8,128)S(1)} %get-tuple-element.61), channel_id=1, source_target_pairs={{0,1},{1,0},{2,3},{3,2},{4,5},{5,4},{6,7},{7,6},{8,9},{9,8},{10,11... | collective-permute-start | bytes 1179656 | tf_op jit(solution)/shard_map/ppermute | solution.py:447
  17.3 15.6 %collective-permute-start.4 = (f32[12,64,128]{2,1,0:T(8,128)S(1)}, f32[12,64,128]{2,1,0:T(8,128)S(1)}, u32[]{:S(2)}, u32[]{:S(2)}) collective-permute-start(f32[12,64,128]{2,1,0:T(8,128)S(1)} %get-tuple-element.62), channel_id=1, source_target_pairs={{1,2},{3,4},{5,6},{7,8},{9,10},{11,12},{13,14},{2,1},{4,3},{6,5},{... | collective-permute-start | bytes 1179656 | tf_op jit(solution)/shard_map/ppermute | solution.py:450
  22.3 15.7 %collective-permute-start.2 = (f32[3,4,64,128]{3,2,1,0:T(8,128)S(1)}, f32[3,4,64,128]{3,2,1,0:T(8,128)S(1)}, u32[]{:S(2)}, u32[]{:S(2)}) collective-permute-start(f32[3,4,64,128]{3,2,1,0:T(8,128)S(1)} %get-tuple-element.60), channel_id=1, source_target_pairs={{0,16},{16,32},{32,48},{48,64},{64,80},{80,96},{96,112},{112,0},{1... | collective-permute-start | bytes 1179656 | tf_op jit(solution)/shard_map/ppermute | solution.py:455
  23.6 17.9 %collective-permute-start.9 = (f32[3,4,64,128]{3,2,1,0:T(8,128)S(1)}, f32[3,4,64,128]{3,2,1,0:T(8,128)S(1)}, u32[]{:S(2)}, u32[]{:S(2)}) collective-permute-start(f32[3,4,64,128]{3,2,1,0:T(8,128)S(1)} %first_middle.1.after), channel_id=1, source_target_pairs={{0,16},{16,32},{32,48},{64,80},{80,96},{96,112},{1,17},{17,33},{33... | collective-permute-start | bytes 1179656 | tf_op jit(solution)/shard_map/ppermute | solution.py:455
  26.7 21.9 %collective-permute-start.6 = (f32[3,4,64,128]{3,2,1,0:T(8,128)S(1)}, f32[3,4,64,128]{3,2,1,0:T(8,128)S(1)}, u32[]{:S(2)}, u32[]{:S(2)}) collective-permute-start(f32[3,4,64,128]{3,2,1,0:T(8,128)S(1)} %get-tuple-element.65), channel_id=1, source_target_pairs={{0,16},{16,32},{32,48},{48,64},{64,80},{80,96},{96,112},{112,0},{1... | collective-permute-start | bytes 1179656 | tf_op jit(solution)/shard_map/ppermute | solution.py:455
  31.6 23.0 %collective-permute-start.8 = (f32[3,4,64,128]{3,2,1,0:T(8,128)S(1)}, f32[3,4,64,128]{3,2,1,0:T(8,128)S(1)}, u32[]{:S(2)}, u32[]{:S(2)}) collective-permute-start(f32[3,4,64,128]{3,2,1,0:T(8,128)S(1)} %collective-permute-done.7), channel_id=1, source_target_pairs={{112,64},{48,0},{113,65},{49,1},{114,66},{50,2},{115,67},{51,3},{1... | collective-permute-start | bytes 1179656 | tf_op jit(solution)/shard_map/ppermute | solution.py:455
  38.0 18.5 %collective-permute-start.5 = (f32[3,4,64,128]{3,2,1,0:T(8,128)S(1)}, f32[3,4,64,128]{3,2,1,0:T(8,128)S(1)}, u32[]{:S(2)}, u32[]{:S(2)}) collective-permute-start(f32[3,4,64,128]{3,2,1,0:T(8,128)S(1)} %collective-permute-done.2.vb), channel_id=1, source_target_pairs={{1,2},{3,4},{5,6},{7,8},{9,10},{11,12},{13,14},{2,1},{4,3},{6,5},{... | collective-permute-start | bytes 1179656 | tf_op jit(solution)/shard_map/ppermute | solution.py:450
  62.5 14.3 %collective-permute-start.11 = (f32[3,4,64,128]{3,2,1,0:T(8,128)S(1)}, f32[3,4,64,128]{3,2,1,0:T(8,128)S(1)}, u32[]{:S(2)}, u32[]{:S(2)}) collective-permute-start(f32[3,4,64,128]{3,2,1,0:T(8,128)S(1)} %get-tuple-element.71), channel_id=1, source_target_pairs={{0,16},{16,32},{32,48},{48,64},{64,80},{80,96},{96,112},{112,0},{1... | collective-permute-start | bytes 1179656 | tf_op jit(solution)/shard_map/ppermute | solution.py:455
  62.6 24.8 %collective-permute-start.13 = (f32[3,4,64,128]{3,2,1,0:T(8,128)S(1)}, f32[3,4,64,128]{3,2,1,0:T(8,128)S(1)}, u32[]{:S(2)}, u32[]{:S(2)}) collective-permute-start(f32[3,4,64,128]{3,2,1,0:T(8,128)S(1)} %get-tuple-element.72), channel_id=1, source_target_pairs={{0,16},{16,32},{32,48},{48,64},{64,80},{80,96},{96,112},{112,0},{1... | collective-permute-start | bytes 1179656 | tf_op jit(solution)/shard_map/ppermute | solution.py:455
  62.7 32.6 %collective-permute-start.15 = (f32[3,4,64,128]{3,2,1,0:T(8,128)S(1)}, f32[3,4,64,128]{3,2,1,0:T(8,128)S(1)}, u32[]{:S(2)}, u32[]{:S(2)}) collective-permute-start(f32[3,4,64,128]{3,2,1,0:T(8,128)S(1)} %collective-permute-done.14), channel_id=1, source_target_pairs={{112,64},{48,0},{113,65},{49,1},{114,66},{50,2},{115,67},{51,3},{1... | collective-permute-start | bytes 1179656 | tf_op jit(solution)/shard_map/ppermute | solution.py:455
  64.0 31.3 %collective-permute-start.17 = (f32[3,4,64,128]{3,2,1,0:T(8,128)S(1)}, f32[3,4,64,128]{3,2,1,0:T(8,128)S(1)}, u32[]{:S(2)}, u32[]{:S(2)}) collective-permute-start(f32[3,4,64,128]{3,2,1,0:T(8,128)S(1)} %get-tuple-element.73), channel_id=1, source_target_pairs={{0,16},{16,32},{32,48},{64,80},{80,96},{96,112},{1,17},{17,33},{33... | collective-permute-start | bytes 1179656 | tf_op jit(solution)/shard_map/ppermute | solution.py:455
  76.8 19.3 %collective-permute-start.12 = (f32[3,4,64,128]{3,2,1,0:T(8,128)S(1)}, f32[3,4,64,128]{3,2,1,0:T(8,128)S(1)}, u32[]{:S(2)}, u32[]{:S(2)}) collective-permute-start(f32[3,4,64,128]{3,2,1,0:T(8,128)S(1)} %collective-permute-done.11.vb), channel_id=1, source_target_pairs={{1,2},{3,4},{5,6},{7,8},{9,10},{11,12},{13,14},{2,1},{4,3},{6,5},{... | collective-permute-start | bytes 1179656 | tf_op jit(solution)/shard_map/ppermute | solution.py:450
  102.7 22.6 %collective-permute-start.20 = (f32[3,4,64,128]{3,2,1,0:T(8,128)S(1)}, f32[3,4,64,128]{3,2,1,0:T(8,128)S(1)}, u32[]{:S(2)}, u32[]{:S(2)}) collective-permute-start(f32[3,4,64,128]{3,2,1,0:T(8,128)S(1)} %get-tuple-element.84), channel_id=1, source_target_pairs={{0,16},{16,32},{32,48},{48,64},{64,80},{80,96},{96,112},{112,0},{1... | collective-permute-start | bytes 1179656 | tf_op jit(solution)/shard_map/ppermute | solution.py:455
  102.8 28.4 %collective-permute-start.22 = (f32[3,4,64,128]{3,2,1,0:T(8,128)S(1)}, f32[3,4,64,128]{3,2,1,0:T(8,128)S(1)}, u32[]{:S(2)}, u32[]{:S(2)}) collective-permute-start(f32[3,4,64,128]{3,2,1,0:T(8,128)S(1)} %collective-permute-done.21), channel_id=1, source_target_pairs={{112,64},{48,0},{113,65},{49,1},{114,66},{50,2},{115,67},{51,3},{1... | collective-permute-start | bytes 1179656 | tf_op jit(solution)/shard_map/ppermute | solution.py:455
  104.1 28.5 %collective-permute-start.24 = (f32[3,4,64,128]{3,2,1,0:T(8,128)S(1)}, f32[3,4,64,128]{3,2,1,0:T(8,128)S(1)}, u32[]{:S(2)}, u32[]{:S(2)}) collective-permute-start(f32[3,4,64,128]{3,2,1,0:T(8,128)S(1)} %get-tuple-element.85), channel_id=1, source_target_pairs={{0,16},{16,32},{32,48},{64,80},{80,96},{96,112},{1,17},{17,33},{33... | collective-permute-start | bytes 1179656 | tf_op jit(solution)/shard_map/ppermute | solution.py:455
  117.0 20.9 %collective-permute-start.19 = (f32[16,64,128]{2,1,0:T(8,128)S(1)}, f32[16,64,128]{2,1,0:T(8,128)S(1)}, u32[]{:S(2)}, u32[]{:S(2)}) collective-permute-start(f32[16,64,128]{2,1,0:T(8,128)S(1)} %pad_maximum_fusion), channel_id=1, source_target_pairs={{1,2},{3,4},{5,6},{7,8},{9,10},{11,12},{13,14},{2,1},{4,3},{6,5},{... | collective-permute-start | bytes 1572872 | tf_op jit(solution)/shard_map/ppermute | solution.py:450
  142.7 15.2 %collective-permute-start.27 = (f32[3,4,64,128]{3,2,1,0:T(8,128)S(1)}, f32[3,4,64,128]{3,2,1,0:T(8,128)S(1)}, u32[]{:S(2)}, u32[]{:S(2)}) collective-permute-start(f32[3,4,64,128]{3,2,1,0:T(8,128)S(1)} %get-tuple-element.90), channel_id=1, source_target_pairs={{0,32},{16,48},{32,64},{48,80},{64,96},{80,112},{96,0},{112,16},{1... | collective-permute-start | bytes 1179656 | tf_op jit(solution)/shard_map/ppermute | solution.py:455
  145.0 21.4 %collective-permute-start.25 = (f32[3,4,64,128]{3,2,1,0:T(8,128)S(1)}, f32[3,4,64,128]{3,2,1,0:T(8,128)S(1)}, u32[]{:S(2)}, u32[]{:S(2)}) collective-permute-start(f32[3,4,64,128]{3,2,1,0:T(8,128)S(1)} %get-tuple-element.89), channel_id=1, source_target_pairs={{0,32},{16,48},{32,64},{48,80},{64,96},{80,112},{96,0},{112,16},{1... | collective-permute-start | bytes 1179656 | tf_op jit(solution)/shard_map/ppermute | solution.py:455
  145.1 25.5 %collective-permute-start.32 = (f32[3,4,64,128]{3,2,1,0:T(8,128)S(1)}, f32[3,4,64,128]{3,2,1,0:T(8,128)S(1)}, u32[]{:S(2)}, u32[]{:S(2)}) collective-permute-start(f32[3,4,64,128]{3,2,1,0:T(8,128)S(1)} %get-tuple-element.91), channel_id=1, source_target_pairs={{0,32},{16,48},{64,96},{80,112},{1,33},{17,49},{65,97},{81,113},{2... | collective-permute-start | bytes 1179656 | tf_op jit(solution)/shard_map/ppermute | solution.py:455
  149.9 21.3 %collective-permute-start.31 = (f32[3,4,64,128]{3,2,1,0:T(8,128)S(1)}, f32[3,4,64,128]{3,2,1,0:T(8,128)S(1)}, u32[]{:S(2)}, u32[]{:S(2)}) collective-permute-start(f32[3,4,64,128]{3,2,1,0:T(8,128)S(1)} %collective-permute-done.30), channel_id=1, source_target_pairs={{96,64},{112,80},{32,0},{48,16},{97,65},{113,81},{33,1},{49,17},{9... | collective-permute-start | bytes 1179656 | tf_op jit(solution)/shard_map/ppermute | solution.py:455
  157.9 22.9 %collective-permute-start.29 = (f32[3,4,64,128]{3,2,1,0:T(8,128)S(1)}, f32[3,4,64,128]{3,2,1,0:T(8,128)S(1)}, u32[]{:S(2)}, u32[]{:S(2)}) collective-permute-start(f32[3,4,64,128]{3,2,1,0:T(8,128)S(1)} %add.40.tm), channel_id=1, source_target_pairs={{0,1},{1,0},{2,3},{3,2},{4,5},{5,4},{6,7},{7,6},{8,9},{9,8},{10,11... | collective-permute-start | bytes 1179656 | tf_op jit(solution)/shard_map/ppermute | solution.py:447
  158.0 22.8 %collective-permute-start.28 = (f32[3,4,64,128]{3,2,1,0:T(8,128)S(1)}, f32[3,4,64,128]{3,2,1,0:T(8,128)S(1)}, u32[]{:S(2)}, u32[]{:S(2)}) collective-permute-start(f32[3,4,64,128]{3,2,1,0:T(8,128)S(1)} %add.40.tm), channel_id=1, source_target_pairs={{1,2},{3,4},{5,6},{7,8},{9,10},{11,12},{13,14},{2,1},{4,3},{6,5},{... | collective-permute-start | bytes 1179656 | tf_op jit(solution)/shard_map/ppermute | solution.py:450
  166.5 14.3 %collective-permute-start.26 = (f32[3,4,64,128]{3,2,1,0:T(8,128)S(1)}, f32[3,4,64,128]{3,2,1,0:T(8,128)S(1)}, u32[]{:S(2)}, u32[]{:S(2)}) collective-permute-start(f32[3,4,64,128]{3,2,1,0:T(8,128)S(1)} %add.39.tb), channel_id=1, source_target_pairs={{1,2},{3,4},{5,6},{7,8},{9,10},{11,12},{13,14},{2,1},{4,3},{6,5},{... | collective-permute-start | bytes 1179656 | tf_op jit(solution)/shard_map/ppermute | solution.py:450
  193.1 19.0 %collective-permute-start.35 = (f32[3,4,64,128]{3,2,1,0:T(8,128)S(1)}, f32[3,4,64,128]{3,2,1,0:T(8,128)S(1)}, u32[]{:S(2)}, u32[]{:S(2)}) collective-permute-start(f32[3,4,64,128]{3,2,1,0:T(8,128)S(1)} %get-tuple-element.95), channel_id=1, source_target_pairs={{0,64},{16,80},{32,96},{48,112},{64,0},{80,16},{96,32},{112,48},{1... | collective-permute-start | bytes 1179656 | tf_op jit(solution)/shard_map/ppermute | solution.py:455
  (24 other events, 130.3 us)

commit v13 on v12

--- a/solution.py
+++ b/solution.py
@@ -534,8 +534,7 @@
     near_b = from_b(tb)
     tm = sm + later(lm, 2)
     far_b = from_b(tm)
-    around, plain = later_parts(la, 2)
-    ta = sa + (around + plain)
+    ta = sa + later(la, 2)
     near_a = from_a(ta)
     far_a = from_a(tm)
     lb, la, lm, bb, ba, bm = call(

time: 223 us -> 230 us (1.031)
  waiting for transfers between devices: 105 us -> 114 us
    ppermute x23 -> x21, waiting for transfers between devices: 86.3 us -> 93.7 us  [along(): return lax.ppermute(x, 'tm', pairs)]
    ppermute x23 -> x21, starting transfers between devices: 38.7 us -> 34 us  [along(): return lax.ppermute(x, 'tm', pairs)]
    ppermute x8, starting transfers between devices: 31.4 us -> 34 us  [from_b(): return lax.ppermute(x, 'space', off_chip)]
  transfers between devices with their start and end apart: 40 -> 38, of which waited for: 23 -> 22; matrix products, arithmetic and copies ran while one was open for 0% -> 0% of each run, Pallas kernels for 3% -> 3%
where the time goes in v13:
time: 230 us; the launch traced here: 229 us
  waiting for transfers between devices  114 us (50%)
  starting transfers between devices  71.7 us (31%)
  Pallas kernels  33.2 us (14%)
  local copies, waits for them, and re-layouts  8.44 us (4%)
    ppermute x21, waiting for transfers between devices, along(): return lax.ppermute(x, 'tm', pairs)  93.7 us
    ppermute x21, starting transfers between devices, along(): return lax.ppermute(x, 'tm', pairs)  34 us
    ppermute x8, starting transfers between devices, from_b(): return lax.ppermute(x, 'space', off_chip)  34 us
    pallas_call x12, Pallas kernels, call(): pl.pallas_call(kernel, name=name, out_shape=outs, in_specs=in_specs, out_...  33.2 us
    ppermute x8, waiting for transfers between devices, from_b(): return lax.ppermute(x, 'space', off_chip)  17.2 us
    unnamed x16, local copies, waits for them, and re-layouts  5.65 us
  transfers between devices with their start and end apart: 38, of which 22 were waited for; matrix products, arithmetic and copies ran while one was open for 0% of the time, Pallas kernels for 3%

profile of v13, /device:TPU:17, one launch (start us, length us, event | category | flops | bytes accessed | tf_op | source)
XLA Modules:
  0.0 228.8 jit_solution(14345124587678050806)
XLA Ops:
  26.7 4.9 %collective-permute-start.6 = (f32[3,4,64,128]{3,2,1,0:T(8,128)S(1)}, f32[3,4,64,128]{3,2,1,0:T(8,128)S(1)}, u32[]{:S(2)}, u32[]{:S(2)}) collective-permute-start(f32[3,4,64,128]{3,2,1,0:T(8,128)S(1)} %get-tuple-element.65), channel_id=1, source_target_pairs={{0,16},{16,32},{32,48},{48,64},{64,80},{80,96},{96,112},{112,0},{1... | collective-permute-start | bytes 1179656 | tf_op jit(solution)/shard_map/ppermute | solution.py:455
  41.5 7.1 %collective-permute-done.6.va = f32[3,4,64,128]{3,2,1,0:T(8,128)S(1)} collective-permute-done((f32[3,4,64,128]{3,2,1,0:T(8,128)S(1)}, f32[3,4,64,128]{3,2,1,0:T(8,128)S(1)}, u32[]{:S(2)}, u32[]{:S(2)}) %collective-permute-start.6) | collective-permute-done | bytes 393248 | tf_op jit(solution)/shard_map/ppermute | solution.py:455
  48.6 5.9 %collective-permute-done.8.vm = f32[3,4,64,128]{3,2,1,0:T(8,128)S(1)} collective-permute-done((f32[3,4,64,128]{3,2,1,0:T(8,128)S(1)}, f32[3,4,64,128]{3,2,1,0:T(8,128)S(1)}, u32[]{:S(2)}, u32[]{:S(2)}) %collective-permute-start.8) | collective-permute-done | bytes 393248 | tf_op jit(solution)/shard_map/ppermute | solution.py:455
  57.0 4.8 %second.1 = (f32[3,16,64,128]{3,2,1,0:T(8,128)S(1)}, f32[3,4,64,128]{3,2,1,0:T(8,128)S(1)}, f32[3,4,64,128]{3,2,1,0:T(8,128)S(1)}, f32[3,4,64,128]{3,2,1,0:T(8,128)S(1)}) custom-call(s32[1]{0:T(128)} %bitcast.odd_ref, f32[3,4,64,128]{3,2,1,0:T(8,128)S(1)} %collective-permute-done.5.hb, f32[3,4,64,128]{3,2,1,0:T(8,128)S(1)} %collective-permute-done.2.vb, ...), custom_call_target="tpu_custom_call" | custom-call | bytes 4194304 | tf_op jit(solution)/shard_map/second/pallas_call | solution.py:63
  64.0 5.3 %collective-permute-start.17 = (f32[3,4,64,128]{3,2,1,0:T(8,128)S(1)}, f32[3,4,64,128]{3,2,1,0:T(8,128)S(1)}, u32[]{:S(2)}, u32[]{:S(2)}) collective-permute-start(f32[3,4,64,128]{3,2,1,0:T(8,128)S(1)} %get-tuple-element.73), channel_id=1, source_target_pairs={{0,16},{16,32},{32,48},{64,80},{80,96},{96,112},{1,17},{17,33},{33... | collective-permute-start | bytes 1179656 | tf_op jit(solution)/shard_map/ppermute | solution.py:455
  69.3 7.4 %collective-permute-done.11.vb = f32[3,4,64,128]{3,2,1,0:T(8,128)S(1)} collective-permute-done((f32[3,4,64,128]{3,2,1,0:T(8,128)S(1)}, f32[3,4,64,128]{3,2,1,0:T(8,128)S(1)}, u32[]{:S(2)}, u32[]{:S(2)}) %collective-permute-start.11) | collective-permute-done | bytes 393248 | tf_op jit(solution)/shard_map/ppermute | solution.py:455
  76.8 6.1 %collective-permute-start.12 = (f32[3,4,64,128]{3,2,1,0:T(8,128)S(1)}, f32[3,4,64,128]{3,2,1,0:T(8,128)S(1)}, u32[]{:S(2)}, u32[]{:S(2)}) collective-permute-start(f32[3,4,64,128]{3,2,1,0:T(8,128)S(1)} %collective-permute-done.11.vb), channel_id=1, source_target_pairs={{1,2},{3,4},{5,6},{7,8},{9,10},{11,12},{13,14},{2,1},{4,3},{6,5},{... | collective-permute-start | bytes 1179656 | tf_op jit(solution)/shard_map/ppermute | solution.py:450
  82.9 4.4 %collective-permute-done.13.va = f32[3,4,64,128]{3,2,1,0:T(8,128)S(1)} collective-permute-done((f32[3,4,64,128]{3,2,1,0:T(8,128)S(1)}, f32[3,4,64,128]{3,2,1,0:T(8,128)S(1)}, u32[]{:S(2)}, u32[]{:S(2)}) %collective-permute-start.13) | collective-permute-done | bytes 393248 | tf_op jit(solution)/shard_map/ppermute | solution.py:455
  87.3 8.0 %collective-permute-done.15.vm = f32[3,4,64,128]{3,2,1,0:T(8,128)S(1)} collective-permute-done((f32[3,4,64,128]{3,2,1,0:T(8,128)S(1)}, f32[3,4,64,128]{3,2,1,0:T(8,128)S(1)}, u32[]{:S(2)}, u32[]{:S(2)}) %collective-permute-start.15) | collective-permute-done | bytes 393248 | tf_op jit(solution)/shard_map/ppermute | solution.py:455
  97.0 4.7 %residual.1 = (f32[1,3,12,64,128]{4,3,2,1,0:T(8,128)}, f32[3,4,64,128]{3,2,1,0:T(8,128)S(1)}, f32[3,4,64,128]{3,2,1,0:T(8,128)S(1)}, f32[3,4,64,128]{3,2,1,0:T(8...) custom-call(s32[1]{0:T(128)} %bitcast.odd_ref, ...), custom_call_target="tpu_custom_call" | custom-call | bytes 4194304 | tf_op jit(solution)/shard_map/residual/pallas_call | solution.py:63
  107.0 9.9 %collective-permute-done.18 = f32[3,4,64,128]{3,2,1,0:T(8,128)S(1)} collective-permute-done((f32[3,4,64,128]{3,2,1,0:T(8,128)S(1)}, f32[3,4,64,128]{3,2,1,0:T(8,128)S(1)}, u32[]{:S(2)}, u32[]{:S(2)}) %collective-permute-start.18) | collective-permute-done | bytes 393248 | tf_op jit(solution)/shard_map/ppermute | solution.py:455
  120.9 4.4 %collective-permute-done.20 = f32[3,4,64,128]{3,2,1,0:T(8,128)S(1)} collective-permute-done((f32[3,4,64,128]{3,2,1,0:T(8,128)S(1)}, f32[3,4,64,128]{3,2,1,0:T(8,128)S(1)}, u32[]{:S(2)}, u32[]{:S(2)}) %collective-permute-start.20) | collective-permute-done | bytes 393248 | tf_op jit(solution)/shard_map/ppermute | solution.py:455
  125.3 5.9 %collective-permute-done.22 = f32[3,4,64,128]{3,2,1,0:T(8,128)S(1)} collective-permute-done((f32[3,4,64,128]{3,2,1,0:T(8,128)S(1)}, f32[3,4,64,128]{3,2,1,0:T(8,128)S(1)}, u32[]{:S(2)}, u32[]{:S(2)}) %collective-permute-start.22) | collective-permute-done | bytes 393248 | tf_op jit(solution)/shard_map/ppermute | solution.py:455
  132.6 5.2 %collective-permute-done.19.hb.rb = f32[16,64,128]{2,1,0:T(8,128)S(1)} collective-permute-done((f32[16,64,128]{2,1,0:T(8,128)S(1)}, f32[16,64,128]{2,1,0:T(8,128)S(1)}, u32[]{:S(2)}, u32[]{:S(2)}) %collective-permute-start.19) | collective-permute-done | bytes 524320 | tf_op jit(solution)/shard_map/ppermute | solution.py:450
  137.8 4.1 %square.1 = (f32[3,4,64,128]{3,2,1,0:T(8,128)S(1)}, f32[3,4,64,128]{3,2,1,0:T(8,128)S(1)}, f32[3,4,64,128]{3,2,1,0:T(8,128)S(1)}) custom-call(s32[1]{0:T(128)} %bitcast.odd_ref, f32[16,64,128]{2,1,0:T(8,128)S(1)} %collective-permute-done.19.hb.rb, f32[3,4,64,128]{3,2,1,0:T(8,128)S(1)} %add.32.sb, f32[3,4,64,128]{3,2,1,0:T(8,128)S(1)} %collective-permute-done.23.ha, ...), custom_call_target="tpu_custom_call" | custom-call | bytes 4194304 | tf_op jit(solution)/shard_map/square/pallas_call | solution.py:63
  145.8 11.4 %collective-permute-done.27 = f32[3,4,64,128]{3,2,1,0:T(8,128)S(1)} collective-permute-done((f32[3,4,64,128]{3,2,1,0:T(8,128)S(1)}, f32[3,4,64,128]{3,2,1,0:T(8,128)S(1)}, u32[]{:S(2)}, u32[]{:S(2)}) %collective-permute-start.27) | collective-permute-done | bytes 393248 | tf_op jit(solution)/shard_map/ppermute | solution.py:455
  160.0 6.6 %collective-permute-done.25 = f32[3,4,64,128]{3,2,1,0:T(8,128)S(1)} collective-permute-done((f32[3,4,64,128]{3,2,1,0:T(8,128)S(1)}, f32[3,4,64,128]{3,2,1,0:T(8,128)S(1)}, u32[]{:S(2)}, u32[]{:S(2)}) %collective-permute-start.25) | collective-permute-done | bytes 393248 | tf_op jit(solution)/shard_map/ppermute | solution.py:455
  166.6 4.4 %collective-permute-start.26 = (f32[3,4,64,128]{3,2,1,0:T(8,128)S(1)}, f32[3,4,64,128]{3,2,1,0:T(8,128)S(1)}, u32[]{:S(2)}, u32[]{:S(2)}) collective-permute-start(f32[3,4,64,128]{3,2,1,0:T(8,128)S(1)} %add.36.tb), channel_id=1, source_target_pairs={{1,2},{3,4},{5,6},{7,8},{9,10},{11,12},{13,14},{2,1},{4,3},{6,5},{... | collective-permute-start | bytes 1179656 | tf_op jit(solution)/shard_map/ppermute | solution.py:450
  177.8 8.8 %collective-permute-done.26.near_b = f32[3,4,64,128]{3,2,1,0:T(8,128)S(1)} collective-permute-done((f32[3,4,64,128]{3,2,1,0:T(8,128)S(1)}, f32[3,4,64,128]{3,2,1,0:T(8,128)S(1)}, u32[]{:S(2)}, u32[]{:S(2)}) %collective-permute-start.26) | collective-permute-done | bytes 393248 | tf_op jit(solution)/shard_map/ppermute | solution.py:450
  186.5 9.9 %fourth.1 = (f32[3,4,64,128]{3,2,1,0:T(8,128)S(1)}, f32[3,4,64,128]{3,2,1,0:T(8,128)S(1)}, f32[3,4,64,128]{3,2,1,0:T(8,128)S(1)}, f32[3,4,64,128]{3,2,1,0:T(8,12...) custom-call(s32[1]{0:T(128)} %bitcast.odd_ref, ...), custom_call_target="tpu_custom_call" | custom-call | bytes 4194304 | tf_op jit(solution)/shard_map/fourth/pallas_call | solution.py:63
  196.5 4.4 %collective-permute-start.34 = (f32[3,4,64,128]{3,2,1,0:T(8,128)S(1)}, f32[3,4,64,128]{3,2,1,0:T(8,128)S(1)}, u32[]{:S(2)}, u32[]{:S(2)}) collective-permute-start(f32[3,4,64,128]{3,2,1,0:T(8,128)S(1)} %get-tuple-element.97), channel_id=1, source_target_pairs={{0,64},{16,80},{32,96},{48,112},{64,0},{80,16},{96,32},{112,48},{1... | collective-permute-start | bytes 1179656 | tf_op jit(solution)/shard_map/ppermute | solution.py:455
  200.9 9.2 %collective-permute-done.34.moved = f32[3,4,64,128]{3,2,1,0:T(8,128)S(1)} collective-permute-done((f32[3,4,64,128]{3,2,1,0:T(8,128)S(1)}, f32[3,4,64,128]{3,2,1,0:T(8,128)S(1)}, u32[]{:S(2)}, u32[]{:S(2)}) %collective-permute-start.34) | collective-permute-done | bytes 393248 | tf_op jit(solution)/shard_map/ppermute | solution.py:455
  210.2 6.4 %collective-permute-start.35 = (f32[3,2,64,128]{3,2,1,0:T(8,128)S(1)}, f32[3,2,64,128]{3,2,1,0:T(8,128)S(1)}, u32[]{:S(2)}, u32[]{:S(2)}) collective-permute-start(f32[3,2,64,128]{3,2,1,0:T(8,128)S(1)} %get-tuple-element.98), channel_id=1, source_target_pairs={{1,2},{3,4},{5,6},{7,8},{9,10},{11,12},{13,14},{2,1},{4,3},{6,5},{... | collective-permute-start | bytes 589832 | tf_op jit(solution)/shard_map/ppermute | solution.py:450
  220.2 5.4 %collective-permute-done.37 = f32[3,4,64,128]{3,2,1,0:T(8,128)S(1)} collective-permute-done((f32[3,4,64,128]{3,2,1,0:T(8,128)S(1)}, f32[3,4,64,128]{3,2,1,0:T(8,128)S(1)}, u32[]{:S(2)}, u32[]{:S(2)}) %collective-permute-start.37) | collective-permute-done | bytes 393248 | tf_op jit(solution)/shard_map/ppermute | solution.py:455
  (92 shorter events, 72.9 us)
Async XLA Ops:
  16.7 14.9 %collective-permute-start.3 = (f32[12,64,128]{2,1,0:T(8,128)S(1)}, f32[12,64,128]{2,1,0:T(8,128)S(1)}, u32[]{:S(2)}, u32[]{:S(2)}) collective-permute-start(f32[12,64,128]{2,1,0:T(8,128)S(1)} %get-tuple-element.61), channel_id=1, source_target_pairs={{0,1},{1,0},{2,3},{3,2},{4,5},{5,4},{6,7},{7,6},{8,9},{9,8},{10,11... | collective-permute-start | bytes 1179656 | tf_op jit(solution)/shard_map/ppermute | solution.py:447
  17.3 15.6 %collective-permute-start.4 = (f32[12,64,128]{2,1,0:T(8,128)S(1)}, f32[12,64,128]{2,1,0:T(8,128)S(1)}, u32[]{:S(2)}, u32[]{:S(2)}) collective-permute-start(f32[12,64,128]{2,1,0:T(8,128)S(1)} %get-tuple-element.62), channel_id=1, source_target_pairs={{1,2},{3,4},{5,6},{7,8},{9,10},{11,12},{13,14},{2,1},{4,3},{6,5},{... | collective-permute-start | bytes 1179656 | tf_op jit(solution)/shard_map/ppermute | solution.py:450
  22.3 15.7 %collective-permute-start.2 = (f32[3,4,64,128]{3,2,1,0:T(8,128)S(1)}, f32[3,4,64,128]{3,2,1,0:T(8,128)S(1)}, u32[]{:S(2)}, u32[]{:S(2)}) collective-permute-start(f32[3,4,64,128]{3,2,1,0:T(8,128)S(1)} %get-tuple-element.60), channel_id=1, source_target_pairs={{0,16},{16,32},{32,48},{48,64},{64,80},{80,96},{96,112},{112,0},{1... | collective-permute-start | bytes 1179656 | tf_op jit(solution)/shard_map/ppermute | solution.py:455
  23.6 17.9 %collective-permute-start.9 = (f32[3,4,64,128]{3,2,1,0:T(8,128)S(1)}, f32[3,4,64,128]{3,2,1,0:T(8,128)S(1)}, u32[]{:S(2)}, u32[]{:S(2)}) collective-permute-start(f32[3,4,64,128]{3,2,1,0:T(8,128)S(1)} %first_middle.1.after), channel_id=1, source_target_pairs={{0,16},{16,32},{32,48},{64,80},{80,96},{96,112},{1,17},{17,33},{33... | collective-permute-start | bytes 1179656 | tf_op jit(solution)/shard_map/ppermute | solution.py:455
  26.7 21.9 %collective-permute-start.6 = (f32[3,4,64,128]{3,2,1,0:T(8,128)S(1)}, f32[3,4,64,128]{3,2,1,0:T(8,128)S(1)}, u32[]{:S(2)}, u32[]{:S(2)}) collective-permute-start(f32[3,4,64,128]{3,2,1,0:T(8,128)S(1)} %get-tuple-element.65), channel_id=1, source_target_pairs={{0,16},{16,32},{32,48},{48,64},{64,80},{80,96},{96,112},{112,0},{1... | collective-permute-start | bytes 1179656 | tf_op jit(solution)/shard_map/ppermute | solution.py:455
  31.6 23.0 %collective-permute-start.8 = (f32[3,4,64,128]{3,2,1,0:T(8,128)S(1)}, f32[3,4,64,128]{3,2,1,0:T(8,128)S(1)}, u32[]{:S(2)}, u32[]{:S(2)}) collective-permute-start(f32[3,4,64,128]{3,2,1,0:T(8,128)S(1)} %collective-permute-done.7), channel_id=1, source_target_pairs={{112,64},{48,0},{113,65},{49,1},{114,66},{50,2},{115,67},{51,3},{1... | collective-permute-start | bytes 1179656 | tf_op jit(solution)/shard_map/ppermute | solution.py:455
  38.0 18.5 %collective-permute-start.5 = (f32[3,4,64,128]{3,2,1,0:T(8,128)S(1)}, f32[3,4,64,128]{3,2,1,0:T(8,128)S(1)}, u32[]{:S(2)}, u32[]{:S(2)}) collective-permute-start(f32[3,4,64,128]{3,2,1,0:T(8,128)S(1)} %collective-permute-done.2.vb), channel_id=1, source_target_pairs={{1,2},{3,4},{5,6},{7,8},{9,10},{11,12},{13,14},{2,1},{4,3},{6,5},{... | collective-permute-start | bytes 1179656 | tf_op jit(solution)/shard_map/ppermute | solution.py:450
  62.5 14.3 %collective-permute-start.11 = (f32[3,4,64,128]{3,2,1,0:T(8,128)S(1)}, f32[3,4,64,128]{3,2,1,0:T(8,128)S(1)}, u32[]{:S(2)}, u32[]{:S(2)}) collective-permute-start(f32[3,4,64,128]{3,2,1,0:T(8,128)S(1)} %get-tuple-element.71), channel_id=1, source_target_pairs={{0,16},{16,32},{32,48},{48,64},{64,80},{80,96},{96,112},{112,0},{1... | collective-permute-start | bytes 1179656 | tf_op jit(solution)/shard_map/ppermute | solution.py:455
  62.6 24.8 %collective-permute-start.13 = (f32[3,4,64,128]{3,2,1,0:T(8,128)S(1)}, f32[3,4,64,128]{3,2,1,0:T(8,128)S(1)}, u32[]{:S(2)}, u32[]{:S(2)}) collective-permute-start(f32[3,4,64,128]{3,2,1,0:T(8,128)S(1)} %get-tuple-element.72), channel_id=1, source_target_pairs={{0,16},{16,32},{32,48},{48,64},{64,80},{80,96},{96,112},{112,0},{1... | collective-permute-start | bytes 1179656 | tf_op jit(solution)/shard_map/ppermute | solution.py:455
  62.7 32.6 %collective-permute-start.15 = (f32[3,4,64,128]{3,2,1,0:T(8,128)S(1)}, f32[3,4,64,128]{3,2,1,0:T(8,128)S(1)}, u32[]{:S(2)}, u32[]{:S(2)}) collective-permute-start(f32[3,4,64,128]{3,2,1,0:T(8,128)S(1)} %collective-permute-done.14), channel_id=1, source_target_pairs={{112,64},{48,0},{113,65},{49,1},{114,66},{50,2},{115,67},{51,3},{1... | collective-permute-start | bytes 1179656 | tf_op jit(solution)/shard_map/ppermute | solution.py:455
  64.0 31.3 %collective-permute-start.17 = (f32[3,4,64,128]{3,2,1,0:T(8,128)S(1)}, f32[3,4,64,128]{3,2,1,0:T(8,128)S(1)}, u32[]{:S(2)}, u32[]{:S(2)}) collective-permute-start(f32[3,4,64,128]{3,2,1,0:T(8,128)S(1)} %get-tuple-element.73), channel_id=1, source_target_pairs={{0,16},{16,32},{32,48},{64,80},{80,96},{96,112},{1,17},{17,33},{33... | collective-permute-start | bytes 1179656 | tf_op jit(solution)/shard_map/ppermute | solution.py:455
  76.8 19.3 %collective-permute-start.12 = (f32[3,4,64,128]{3,2,1,0:T(8,128)S(1)}, f32[3,4,64,128]{3,2,1,0:T(8,128)S(1)}, u32[]{:S(2)}, u32[]{:S(2)}) collective-permute-start(f32[3,4,64,128]{3,2,1,0:T(8,128)S(1)} %collective-permute-done.11.vb), channel_id=1, source_target_pairs={{1,2},{3,4},{5,6},{7,8},{9,10},{11,12},{13,14},{2,1},{4,3},{6,5},{... | collective-permute-start | bytes 1179656 | tf_op jit(solution)/shard_map/ppermute | solution.py:450
  102.6 14.3 %collective-permute-start.18 = (f32[3,4,64,128]{3,2,1,0:T(8,128)S(1)}, f32[3,4,64,128]{3,2,1,0:T(8,128)S(1)}, u32[]{:S(2)}, u32[]{:S(2)}) collective-permute-start(f32[3,4,64,128]{3,2,1,0:T(8,128)S(1)} %get-tuple-element.80), channel_id=1, source_target_pairs={{0,16},{16,32},{32,48},{48,64},{64,80},{80,96},{96,112},{112,0},{1... | collective-permute-start | bytes 1179656 | tf_op jit(solution)/shard_map/ppermute | solution.py:455
  102.7 22.6 %collective-permute-start.20 = (f32[3,4,64,128]{3,2,1,0:T(8,128)S(1)}, f32[3,4,64,128]{3,2,1,0:T(8,128)S(1)}, u32[]{:S(2)}, u32[]{:S(2)}) collective-permute-start(f32[3,4,64,128]{3,2,1,0:T(8,128)S(1)} %get-tuple-element.84), channel_id=1, source_target_pairs={{0,16},{16,32},{32,48},{48,64},{64,80},{80,96},{96,112},{112,0},{1... | collective-permute-start | bytes 1179656 | tf_op jit(solution)/shard_map/ppermute | solution.py:455
  102.8 28.4 %collective-permute-start.22 = (f32[3,4,64,128]{3,2,1,0:T(8,128)S(1)}, f32[3,4,64,128]{3,2,1,0:T(8,128)S(1)}, u32[]{:S(2)}, u32[]{:S(2)}) collective-permute-start(f32[3,4,64,128]{3,2,1,0:T(8,128)S(1)} %collective-permute-done.21), channel_id=1, source_target_pairs={{112,64},{48,0},{113,65},{49,1},{114,66},{50,2},{115,67},{51,3},{1... | collective-permute-start | bytes 1179656 | tf_op jit(solution)/shard_map/ppermute | solution.py:455
  104.1 28.5 %collective-permute-start.24 = (f32[3,4,64,128]{3,2,1,0:T(8,128)S(1)}, f32[3,4,64,128]{3,2,1,0:T(8,128)S(1)}, u32[]{:S(2)}, u32[]{:S(2)}) collective-permute-start(f32[3,4,64,128]{3,2,1,0:T(8,128)S(1)} %get-tuple-element.85), channel_id=1, source_target_pairs={{0,16},{16,32},{32,48},{64,80},{80,96},{96,112},{1,17},{17,33},{33... | collective-permute-start | bytes 1179656 | tf_op jit(solution)/shard_map/ppermute | solution.py:455
  117.0 20.9 %collective-permute-start.19 = (f32[16,64,128]{2,1,0:T(8,128)S(1)}, f32[16,64,128]{2,1,0:T(8,128)S(1)}, u32[]{:S(2)}, u32[]{:S(2)}) collective-permute-start(f32[16,64,128]{2,1,0:T(8,128)S(1)} %pad_maximum_fusion), channel_id=1, source_target_pairs={{1,2},{3,4},{5,6},{7,8},{9,10},{11,12},{13,14},{2,1},{4,3},{6,5},{... | collective-permute-start | bytes 1572872 | tf_op jit(solution)/shard_map/ppermute | solution.py:450
  142.0 15.2 %collective-permute-start.27 = (f32[3,4,64,128]{3,2,1,0:T(8,128)S(1)}, f32[3,4,64,128]{3,2,1,0:T(8,128)S(1)}, u32[]{:S(2)}, u32[]{:S(2)}) collective-permute-start(f32[3,4,64,128]{3,2,1,0:T(8,128)S(1)} %get-tuple-element.90), channel_id=1, source_target_pairs={{0,32},{16,48},{32,64},{48,80},{64,96},{80,112},{96,0},{112,16},{1... | collective-permute-start | bytes 1179656 | tf_op jit(solution)/shard_map/ppermute | solution.py:455
  142.1 24.5 %collective-permute-start.25 = (f32[3,4,64,128]{3,2,1,0:T(8,128)S(1)}, f32[3,4,64,128]{3,2,1,0:T(8,128)S(1)}, u32[]{:S(2)}, u32[]{:S(2)}) collective-permute-start(f32[3,4,64,128]{3,2,1,0:T(8,128)S(1)} %get-tuple-element.89), channel_id=1, source_target_pairs={{0,32},{16,48},{32,64},{48,80},{64,96},{80,112},{96,0},{112,16},{1... | collective-permute-start | bytes 1179656 | tf_op jit(solution)/shard_map/ppermute | solution.py:455
  144.4 30.6 %collective-permute-start.30 = (f32[3,4,64,128]{3,2,1,0:T(8,128)S(1)}, f32[3,4,64,128]{3,2,1,0:T(8,128)S(1)}, u32[]{:S(2)}, u32[]{:S(2)}) collective-permute-start(f32[3,4,64,128]{3,2,1,0:T(8,128)S(1)} %get-tuple-element.91), channel_id=1, source_target_pairs={{0,32},{16,48},{32,64},{48,80},{64,96},{80,112},{96,0},{112,16},{1... | collective-permute-start | bytes 1179656 | tf_op jit(solution)/shard_map/ppermute | solution.py:455
  157.2 29.3 %collective-permute-start.29 = (f32[3,4,64,128]{3,2,1,0:T(8,128)S(1)}, f32[3,4,64,128]{3,2,1,0:T(8,128)S(1)}, u32[]{:S(2)}, u32[]{:S(2)}) collective-permute-start(f32[3,4,64,128]{3,2,1,0:T(8,128)S(1)} %add.37.tm), channel_id=1, source_target_pairs={{0,1},{1,0},{2,3},{3,2},{4,5},{5,4},{6,7},{7,6},{8,9},{9,8},{10,11... | collective-permute-start | bytes 1179656 | tf_op jit(solution)/shard_map/ppermute | solution.py:447
  157.3 29.2 %collective-permute-start.28 = (f32[3,4,64,128]{3,2,1,0:T(8,128)S(1)}, f32[3,4,64,128]{3,2,1,0:T(8,128)S(1)}, u32[]{:S(2)}, u32[]{:S(2)}) collective-permute-start(f32[3,4,64,128]{3,2,1,0:T(8,128)S(1)} %add.37.tm), channel_id=1, source_target_pairs={{1,2},{3,4},{5,6},{7,8},{9,10},{11,12},{13,14},{2,1},{4,3},{6,5},{... | collective-permute-start | bytes 1179656 | tf_op jit(solution)/shard_map/ppermute | solution.py:450
  166.6 19.9 %collective-permute-start.26 = (f32[3,4,64,128]{3,2,1,0:T(8,128)S(1)}, f32[3,4,64,128]{3,2,1,0:T(8,128)S(1)}, u32[]{:S(2)}, u32[]{:S(2)}) collective-permute-start(f32[3,4,64,128]{3,2,1,0:T(8,128)S(1)} %add.36.tb), channel_id=1, source_target_pairs={{1,2},{3,4},{5,6},{7,8},{9,10},{11,12},{13,14},{2,1},{4,3},{6,5},{... | collective-permute-start | bytes 1179656 | tf_op jit(solution)/shard_map/ppermute | solution.py:450
  200.8 17.6 %collective-permute-start.33 = (f32[3,4,64,128]{3,2,1,0:T(8,128)S(1)}, f32[3,4,64,128]{3,2,1,0:T(8,128)S(1)}, u32[]{:S(2)}, u32[]{:S(2)}) collective-permute-start(f32[3,4,64,128]{3,2,1,0:T(8,128)S(1)} %get-tuple-element.95), channel_id=1, source_target_pairs={{0,64},{16,80},{32,96},{48,112},{64,0},{80,16},{96,32},{112,48},{1... | collective-permute-start | bytes 1179656 | tf_op jit(solution)/shard_map/ppermute | solution.py:455
  (22 other events, 111.0 us)
